TPU v7x, 128 devices: a whole 4x4x4 slice. The times are simulated.
128 devices in a mesh: row: 16 (over y, z), col: 8 (over x, core).
Axes of the slice: x: 4, y: 4, z: 4, core: 2. Of those that a mesh axis runs over, the one named last changes fastest.
Arguments:
- matrix: float32 [18432, 18432], P('row', 'col'), as said below
Outputs:
- updated: float32 [18432, 18432], P('row', 'col')
- reflectors: float32 [18432, 512], P('row')
Inputs may be any that keep to these rules, and one draw needn't show every extreme that they name: matrix is symmetric.
All inputs are finite; a program needn't handle non-finite values.
Results may differ from a plain program's by a relative error of at most 0.00016.
Values sent between devices are 32-bit elements; how exact they have to be, the bound alone decides.
A program may use at most 128 MiB of HBM per device.

v0:
```python
import jax
import jax.numpy as jnp
from jax import lax
from jax.sharding import PartitionSpec as P

BAND = 256
PANELS = 2


def spread(array, axis, root):
    mine = lax.axis_index(axis) == root
    return lax.psum(jnp.where(mine, array, jnp.zeros_like(array)), axis)


def contract_first(left, right):
    return lax.dot_general(left, right, (((0,), (0,)), ((), ())), precision=lax.Precision.HIGHEST)


def body(matrix):
    high = lax.Precision.HIGHEST
    current = matrix
    row_count = matrix.shape[0]
    col_count = matrix.shape[1]
    row_start = lax.axis_index("row") * row_count
    col_start = lax.axis_index("col") * col_count
    row_places = row_start + jnp.arange(row_count, dtype=jnp.int32)
    col_places = col_start + jnp.arange(col_count, dtype=jnp.int32)
    columns = jnp.arange(BAND, dtype=jnp.int32)
    identity = jnp.eye(BAND, dtype=jnp.float32)
    stored = []
    history = []
    for which_panel in range(PANELS):
        start = (which_panel + 1) * BAND
        low_edge = which_panel * BAND
        high_edge = (which_panel + 1) * BAND
        local_panel = current[:, low_edge:high_edge]
        panel_rows = spread(local_panel, "col", 0)
        row_strip = spread(current[low_edge:high_edge, :], "row", 0)
        panel_rows = jnp.where(row_places[:, None] >= start, panel_rows, 0.0)
        unit_rows = (row_places[:, None] - start == columns[None, :]).astype(jnp.float32)
        gram_sum, top_block = lax.psum(
            (contract_first(panel_rows, panel_rows), contract_first(unit_rows, panel_rows)), "row"
        )
        factor_low = jnp.linalg.cholesky(gram_sum)
        rows_vec_t = (
            jax.scipy.linalg.solve_triangular(factor_low, panel_rows.T, lower=True) + unit_rows.T
        )
        q_top = jax.scipy.linalg.solve_triangular(factor_low, top_block.T, lower=True).T
        shifted = identity + q_top
        factor_two = jnp.linalg.cholesky(jnp.dot(shifted, shifted.T, precision=high))
        inner = jax.scipy.linalg.solve_triangular(factor_two, identity, lower=True)
        transform = jnp.dot(shifted.T, jnp.dot(inner.T, inner, precision=high), precision=high)
        row_strip = jnp.where(col_places[None, :] >= start, row_strip, 0.0)
        unit_cols = (columns[:, None] == col_places[None, :] - start).astype(jnp.float32)
        cols_vec_t = (
            jax.scipy.linalg.solve_triangular(factor_low, row_strip, lower=True) + unit_cols
        )
        stored.append(rows_vec_t)
        image_part = jnp.dot(rows_vec_t, current, precision=high)
        image_cols = lax.psum(image_part, "row")
        curvature = lax.psum(jnp.dot(image_cols, cols_vec_t.T, precision=high), "col")
        row_part = lax.dot_general(cols_vec_t, current, (((1,), (1,)), ((), ())), precision=high)
        image_rows = lax.psum(row_part, "col")
        middle = jnp.dot(jnp.dot(transform, curvature, precision=high), transform.T, precision=high)
        w_cols = jnp.dot(transform, image_cols, precision=high) - 0.5 * jnp.dot(
            middle.T, cols_vec_t, precision=high
        )
        w_rows = jnp.dot(transform, image_rows, precision=high) - 0.5 * jnp.dot(
            middle.T, rows_vec_t, precision=high
        )
        current = current - contract_first(rows_vec_t, w_cols) - contract_first(w_rows, cols_vec_t)
        history.append((rows_vec_t, w_rows, w_cols, cols_vec_t))
    return (current, jnp.concatenate(stored, axis=0).T)


def solution(mesh):
    placed = (P("row", "col"),)
    return jax.shard_map(
        body,
        mesh=mesh,
        in_specs=placed,
        out_specs=(P("row", "col"), P("row", None)),
        check_vma=False,
    )
```

profile of v0, /device:TPU:1, one launch (start us, length us, event | category | flops | bytes accessed | tf_op | source)
XLA Modules:
  0.0 1101.6 jit_solution(8772189510013273424)
XLA Ops:
  7.2 2.4 slice_select_fusion.3
  9.7 3.2 slice_select_fusion.1
  12.9 62.1 %all-reduce.14.cloned.1.call-done = f32[1152,256]{1,0:T(8,128)} async-done(((f32[1152,256]{1,0:T(8,128)}), f32[1152,256]{1,0:T(8,128)}) %all-reduce.14.cloned.1.call-update) | async-done | bytes 1179664 | tf_op jit(solution)/shard_map/psum | solution.py:12
  75.1 4.9 fusion.14
  80.8 2.1 fusion.8
  82.9 81.7 %all-reduce.16.cloned.1.call-done = f32[256,256]{0,1:T(8,128)} async-done(((f32[256,256]{0,1:T(8,128)}), f32[256,256]{0,1:T(8,128)}) %all-reduce.16.cloned.1.call-update) | async-done | bytes 262160 | tf_op jit(solution)/shard_map/psum | solution.py:41
  166.7 11.7 %cholesky.214 = f32[128,128]{1,0:T(8,128)S(1)} custom-call(f32[128,128]{1,0:T(8,128)S(1)} %cholesky.346), custom_call_target="Cholesky" | custom-call | tf_op jit(solution)/shard_map/jit(cholesky)/cholesky | solution.py:44
  178.5 9.8 custom-call.25
  188.8 11.7 %cholesky.231 = f32[128,128]{1,0:T(8,128)S(1)} custom-call(f32[128,128]{1,0:T(8,128)S(1)} %convolution_subtract_fusion.15), custom_call_target="Cholesky" | custom-call | tf_op jit(solution)/shard_map/jit(cholesky)/cholesky | solution.py:44
  202.7 4.1 while.16
  207.3 19.7 %custom-call.26 = f32[2,128,128]{1,2,0:T(8,128)S(1)} custom-call(f32[2,128,128]{2,1,0:T(8,128)S(1)} %get-tuple-element.60), custom_call_target="InvertDiagBlocksLowerTriangular" | custom-call | tf_op jit(solution)/shard_map/jit(_solve_triangular)/triangular_solve | solution.py:46
  229.7 13.3 %fusion.123 = f32[256,2304]{1,0:T(8,128)} fusion(f32[256,1152]{1,0:T(8,128)S(1)} %maximum_add_fusion.2, f32[1152,2304]{1,0:T(8,128)} %param.8), kind=kOutput, calls=%fused_computation.219 | convolution fusion | flops 8153726976 | bytes 14155776 | tf_op jit(solution)/shard_map/dot_general | solution.py:59
  244.4 110.3 %all-reduce.24.cloned.1.call-done = (f32[256,256]{1,0:T(8,128)}, f32[256,2304]{1,0:T(8,128)}, f32[256,2304]{1,0:T(8,128)}) async-done(((f32[256,256]{1,0:T(8,128)}, f32[256,2304]{1,0:T(8,128)}, f32[256,2304]{1,0:T(8,128)}), (f32[256,256]{1,0:T(8,128)}, f32[256,2304]{1,0:T(8,128)}, f32[256,2304]{1,0:T(8,128)})) %all-reduce.24.cloned.1.call-update) | async-done | bytes 4980752 | tf_op jit(solution)/shard_map/psum | solution.py:41
  354.8 1.8 broadcast_select_fusion.1
  360.1 14.0 %fusion.47 = f32[256,1152]{1,0:T(8,128)} fusion(f32[1152,2304]{1,0:T(8,128)} %param.8, f32[128,2304]{1,0:T(8,128)S(1)} %fusion.81, f32[128,2304]{1,0:T(8,128)S(1)} %fusion.6, s32[2304]{0:T(1024)S(1)} %fusion.95), kind=kOutput, calls=%fused_computation.106 | convolution fusion | flops 8156086272 | bytes 14164992 | tf_op jit(solution)/shard_map/dot_general | solution.py:62
  374.1 3.1 fusion.48
  382.8 1.8 copy.5
  387.0 13.2 %cholesky.248 = f32[128,128]{1,0:T(8,128)} custom-call(f32[128,128]{1,0:T(8,128)} %cholesky.349), custom_call_target="Cholesky" | custom-call | tf_op jit(solution)/shard_map/jit(cholesky)/cholesky | solution.py:50
  400.2 2.0 select_reduce_fusion.5
  403.8 11.3 %custom-call.28 = f32[1,128,128]{1,2,0:T(8,128)} custom-call(f32[1,128,128]{2,1,0:T(8,128)} %get-tuple-element.131), custom_call_target="InvertDiagBlocksLowerTriangular" | custom-call | tf_op jit(solution)/shard_map/jit(cholesky)/cholesky | solution.py:50
  415.0 1.7 constant_dynamic-update-slice_fusion.4
  416.7 1.7 convolution_subtract_fusion.14
  418.5 13.3 %cholesky.265 = f32[128,128]{1,0:T(8,128)} custom-call(f32[128,128]{1,0:T(8,128)} %convolution_subtract_fusion.14), custom_call_target="Cholesky" | custom-call | tf_op jit(solution)/shard_map/jit(cholesky)/cholesky | solution.py:50
  436.6 1.7 select_select_fusion.2
  439.0 8.3 while.17
  440.3 2.9 bitcast_dynamic-update-slice_fusion.9
  444.5 2.9 bitcast_dynamic-update-slice_fusion.9
  447.3 21.1 %custom-call.29 = f32[2,128,128]{1,2,0:T(8,128)} custom-call(f32[2,128,128]{2,1,0:T(8,128)} %get-tuple-element.62), custom_call_target="InvertDiagBlocksLowerTriangular" | custom-call | tf_op jit(solution)/shard_map/jit(_solve_triangular)/triangular_solve | solution.py:51
  470.4 2.0 convolution_subtract_fusion.10
  473.7 1.6 fusion.31
  477.3 5.2 fusion.124
  482.5 51.4 %all-reduce.28.cloned.1.call-done = (f32[256,256]{1,0:T(8,128)}, f32[256,1152]{1,0:T(8,128)}) async-done(((f32[256,256]{1,0:T(8,128)}, f32[256,1152]{1,0:T(8,128)}), (f32[256,256]{1,0:T(8,128)}, f32[256,1152]{1,0:T(8,128)})) %all-reduce.28.cloned.1.call-update) | async-done | bytes 1441808 | tf_op jit(solution)/shard_map/psum | solution.py:61
  533.9 2.6 fusion.127
  539.0 2.6 fusion.1
  541.6 12.7 %convolution_subtract_fusion.3 = f32[1152,2304]{1,0:T(8,128)S(1)} fusion(f32[1152,2304]{1,0:T(8,128)} %param.8, f32[256,1152]{1,0:T(8,128)S(1)} %maximum_add_fusion.2, f32[256,2304]{1,0:T(8,128)S(1)} %fusion.1), kind=kOutput, calls=%fused_computation.11 | convolution fusion | flops 8156381184 | bytes 24772608 | tf_op jit(solution)/shard_map/dot_general | solution.py:16
  554.3 10.0 convolution_subtract_fusion.2
  564.3 4.1 copy-done
  569.6 3.2 slice_select_fusion
  572.8 59.1 %all-reduce.18.cloned.1.call-done = f32[1152,256]{1,0:T(8,128)} async-done(((f32[1152,256]{1,0:T(8,128)}), f32[1152,256]{1,0:T(8,128)}) %all-reduce.18.cloned.1.call-update) | async-done | bytes 1179664 | tf_op jit(solution)/shard_map/psum | solution.py:12
  631.9 4.9 fusion.11
  637.5 2.2 fusion.9
  639.7 81.8 %all-reduce.20.cloned.1.call-done = f32[256,256]{0,1:T(8,128)} async-done(((f32[256,256]{0,1:T(8,128)}), f32[256,256]{0,1:T(8,128)}) %all-reduce.20.cloned.1.call-update) | async-done | bytes 262160 | tf_op jit(solution)/shard_map/psum | solution.py:41
  723.6 11.7 %cholesky.282 = f32[128,128]{1,0:T(8,128)S(1)} custom-call(f32[128,128]{1,0:T(8,128)S(1)} %cholesky.352), custom_call_target="Cholesky" | custom-call | tf_op jit(solution)/shard_map/jit(cholesky)/cholesky | solution.py:44
  735.4 9.8 custom-call.31
  745.7 11.7 %cholesky.299 = f32[128,128]{1,0:T(8,128)S(1)} custom-call(f32[128,128]{1,0:T(8,128)S(1)} %convolution_subtract_fusion.13), custom_call_target="Cholesky" | custom-call | tf_op jit(solution)/shard_map/jit(cholesky)/cholesky | solution.py:44
  760.2 4.5 while.18
  764.6 19.7 %custom-call.32 = f32[2,128,128]{1,2,0:T(8,128)S(1)} custom-call(f32[2,128,128]{2,1,0:T(8,128)S(1)} %get-tuple-element.64), custom_call_target="InvertDiagBlocksLowerTriangular" | custom-call | tf_op jit(solution)/shard_map/jit(_solve_triangular)/triangular_solve | solution.py:46
  787.1 13.7 %fusion.128 = f32[256,2304]{1,0:T(8,128)} fusion(f32[256,1152]{1,0:T(8,128)S(1)} %maximum_add_fusion.3, f32[1152,2304]{1,0:T(8,128)} %copy-done), kind=kOutput, calls=%fused_computation.224 | convolution fusion | flops 8153726976 | bytes 14155776 | tf_op jit(solution)/shard_map/dot_general | solution.py:59
  802.5 3.0 copy.9
  805.5 107.1 %all-reduce.22.cloned.1.call-done = (f32[256,256]{1,0:T(8,128)}, f32[256,2304]{1,0:T(8,128)}, f32[256,2304]{1,0:T(8,128)}) async-done(((f32[256,256]{1,0:T(8,128)}, f32[256,2304]{1,0:T(8,128)}, f32[256,2304]{1,0:T(8,128)}), (f32[256,256]{1,0:T(8,128)}, f32[256,2304]{1,0:T(8,128)}, f32[256,2304]{1,0:T(8,128)})) %all-reduce.22.cloned.1.call-update) | async-done | bytes 4980752 | tf_op jit(solution)/shard_map/psum | solution.py:41
  912.6 1.9 broadcast_select_fusion
  918.0 13.8 %fusion.45 = f32[256,1152]{1,0:T(8,128)} fusion(f32[1152,2304]{1,0:T(8,128)} %copy-done, f32[128,2304]{1,0:T(8,128)S(1)} %fusion.84, f32[128,2304]{1,0:T(8,128)S(1)} %fusion.4, s32[2304]{0:T(1024)S(1)} %fusion.93), kind=kOutput, calls=%fused_computation.104 | convolution fusion | flops 8156086272 | bytes 14164992 | tf_op jit(solution)/shard_map/dot_general | solution.py:62
  931.8 3.1 fusion.46
  937.3 11.7 %cholesky.316 = f32[128,128]{1,0:T(8,128)S(1)} custom-call(f32[128,128]{1,0:T(8,128)S(1)} %cholesky.355), custom_call_target="Cholesky" | custom-call | tf_op jit(solution)/shard_map/jit(cholesky)/cholesky | solution.py:50
  949.1 9.8 custom-call.34
  961.0 11.9 %cholesky.333 = f32[128,128]{1,0:T(8,128)S(1)} custom-call(f32[128,128]{1,0:T(8,128)S(1)} %convolution_subtract_fusion.12), custom_call_target="Cholesky" | custom-call | tf_op jit(solution)/shard_map/jit(cholesky)/cholesky | solution.py:50
  975.7 4.1 while.19
  979.8 19.7 %custom-call.35 = f32[2,128,128]{1,2,0:T(8,128)S(1)} custom-call(f32[2,128,128]{2,1,0:T(8,128)S(1)} %get-tuple-element.66), custom_call_target="InvertDiagBlocksLowerTriangular" | custom-call | tf_op jit(solution)/shard_map/jit(_solve_triangular)/triangular_solve | solution.py:51
  1001.6 5.2 fusion.129
  1006.7 55.0 %all-reduce.26.cloned.1.call-done = (f32[256,256]{1,0:T(8,128)}, f32[256,1152]{1,0:T(8,128)}) async-done(((f32[256,256]{1,0:T(8,128)}, f32[256,1152]{1,0:T(8,128)}), (f32[256,256]{1,0:T(8,128)}, f32[256,1152]{1,0:T(8,128)})) %all-reduce.26.cloned.1.call-update) | async-done | bytes 1441808 | tf_op jit(solution)/shard_map/psum | solution.py:61
  1061.7 2.6 fusion.132
  1067.2 2.5 fusion
  1069.7 12.6 %convolution_subtract_fusion.1 = f32[1152,2304]{1,0:T(8,128)S(1)} fusion(f32[1152,2304]{1,0:T(8,128)} %copy-done, f32[256,1152]{1,0:T(8,128)S(1)} %copy-done.2, f32[256,2304]{1,0:T(8,128)S(1)} %fusion), kind=kOutput, calls=%fused_computation.9 | convolution fusion | flops 8156381184 | bytes 24772608 | tf_op jit(solution)/shard_map/dot_general | solution.py:16
  1082.3 12.2 %convolution_subtract_fusion = f32[1152,2304]{1,0:T(8,128)} fusion(f32[1152,2304]{1,0:T(8,128)S(1)} %convolution_subtract_fusion.1, f32[256,1152]{1,0:T(8,128)S(1)} %fusion.2, f32[128,2304]{1,0:T(8,128)S(1)} %fusion.84, f32[128,2304]{1,0:T(8,128)S(1)} %fusion.4, s32[2304]{0:T(1024)S(1)} %fusion.93), kind=kOutput, calls=%fused_computation.8 | convolution fusion | flops 8158740480 | bytes 24781824 | tf_op jit(solution)/shard_map/dot_general | solution.py:16
  (190 shorter events, 72.9 us)
Async XLA Ops:
  7.2 67.9 %all-reduce.14.cloned.1.call-start = ((), (), s32[]{:S(2)}) async-start(), calls=%async_computation | async-start | bytes 2359296 | tf_op jit(solution)/shard_map/psum | solution.py:12
  9.6 155.0 %all-reduce.16.cloned.1.call-start = ((), (), s32[]{:S(2)}) async-start(), calls=%async_computation.1 | async-start | bytes 524288 | tf_op jit(solution)/shard_map/psum | solution.py:41
  75.0 5.5 copy-start.3
  80.0 274.8 %all-reduce.24.cloned.1.call-start = ((), (), s32[]{:S(2)}) async-start(), calls=%async_computation.5 | async-start | bytes 9961472 | tf_op jit(solution)/shard_map/psum | solution.py:41
  206.8 0.5 copy-start.28
  207.3 150.4 %copy-start.11 = (f32[256,256]{1,0:T(8,128)}, f32[256,256]{1,0:T(8,128)S(1)}, u32[]{:S(2)}) copy-start(f32[256,256]{1,0:T(8,128)S(1)} %get-tuple-element.366) | copy-start | bytes 786436
  227.0 129.6 %copy-start.16 = (f32[2,128,128]{1,2,0:T(8,128)}, f32[2,128,128]{1,2,0:T(8,128)S(1)}, u32[]{:S(2)}) copy-start(f32[2,128,128]{1,2,0:T(8,128)S(1)} %custom-call.26) | copy-start | bytes 393220
  243.0 290.9 %all-reduce.28.cloned.1.call-start = ((), (), s32[]{:S(2)}) async-start(), calls=%async_computation.7 | async-start | bytes 2883584 | tf_op jit(solution)/shard_map/psum | solution.py:61
  357.8 1.2 copy-start.17
  360.1 14.0 %copy-start.5 = (f32[256,2304]{1,0:T(8,128)S(1)}, f32[256,2304]{1,0:T(8,128)}, u32[]{:S(2)}) copy-start(f32[256,2304]{1,0:T(8,128)} %get-tuple-element.106) | copy-start | bytes 7077892
  378.4 2.4 copy-start.15
  380.9 0.7 copy-start.21
  385.7 0.7 copy-start.22
  469.7 0.7 copy-start.20
  472.4 159.6 %all-reduce.18.cloned.1.call-start = ((), (), s32[]{:S(2)}) async-start(), calls=%async_computation.2 | async-start | bytes 2359296 | tf_op jit(solution)/shard_map/psum | solution.py:12
  476.6 0.7 copy-start.9
  533.9 2.7 copy-start.10
  533.9 2.7 copy-start.24
  537.3 1.7 copy-start.7
  564.3 4.1 copy-start
  569.5 152.0 %all-reduce.20.cloned.1.call-start = ((), (), s32[]{:S(2)}) async-start(), calls=%async_computation.3 | async-start | bytes 524288 | tf_op jit(solution)/shard_map/psum | solution.py:41
  631.9 5.2 copy-start.4
  636.8 0.7 copy-start.27
  636.8 275.7 %all-reduce.22.cloned.1.call-start = ((), (), s32[]{:S(2)}) async-start(), calls=%async_computation.4 | async-start | bytes 9961472 | tf_op jit(solution)/shard_map/psum | solution.py:41
  722.6 37.6 %copy-start.29 = (s32[2,2]{1,0:T(2,128)S(1)}, s32[2,2]{1,0:T(2,128)}, u32[]{:S(2)}) copy-start(s32[2,2]{1,0:T(2,128)} %get-tuple-element.391) | copy-start | bytes 52
  764.6 21.5 %copy-start.12 = (f32[256,256]{1,0:T(8,128)}, f32[256,256]{1,0:T(8,128)S(1)}, u32[]{:S(2)}) copy-start(f32[256,256]{1,0:T(8,128)S(1)} %get-tuple-element.367) | copy-start | bytes 786436
  784.3 1.9 copy-start.18
  787.0 13.9 %copy-start.1 = (f32[256,1152]{1,0:T(8,128)}, f32[256,1152]{1,0:T(8,128)S(1)}, u32[]{:S(2)}) copy-start(f32[256,1152]{1,0:T(8,128)S(1)} %maximum_add_fusion.3) | copy-start | bytes 3538948
  800.8 260.9 %all-reduce.26.cloned.1.call-start = ((), (), s32[]{:S(2)}) async-start(), calls=%async_computation.6 | async-start | bytes 2883584 | tf_op jit(solution)/shard_map/psum | solution.py:61
  912.6 1.9 copy-start.19
  914.5 1.2 copy-start.13
  917.9 13.8 %copy-start.6 = (f32[256,2304]{1,0:T(8,128)S(1)}, f32[256,2304]{1,0:T(8,128)}, u32[]{:S(2)}) copy-start(f32[256,2304]{1,0:T(8,128)} %get-tuple-element.103) | copy-start | bytes 7077892
  931.8 3.1 copy-start.26
  936.6 0.7 copy-start.23
  949.0 50.5 %copy-start.14 = (f32[256,256]{0,1:T(8,128)S(1)}, f32[256,256]{0,1:T(8,128)}, u32[]{:S(2)}) copy-start(f32[256,256]{0,1:T(8,128)} %fusion.44) | copy-start | bytes 786436
  1061.7 2.6 copy-start.25
  1064.3 1.3 copy-start.2
  1065.5 1.7 copy-start.8
Sparse Core Ops, SparseCore 0:
  10.9 64.0 all-reduce.13
  80.1 84.5 all-reduce.15
  243.1 111.6 all-reduce.23
  472.5 61.3 all-reduce.27
  569.6 62.2 all-reduce.17
  637.0 84.4 all-reduce.19
  800.9 111.5 all-reduce.21
  1000.4 61.2 all-reduce.25
where the time goes:
time: 1110 us; the launch traced here: 1100 us
  waiting for transfers between devices  609 us (55%)
  other arithmetic  249 us (22%)
  matrix products  182 us (16%)
  local copies, waits for them, and re-layouts  39.9 us (4%)
  between operations  20.6 us (2%)
    psum x4, waiting for transfers between devices, body(): lax.psum((contract_first(panel_rows, panel_rows), contract_first(unit_row...  381 us
    psum x2, waiting for transfers between devices, spread(): return lax.psum(jnp.where(mine, array, jnp.zeros_like(array)), axis)  121 us
    psum x2, waiting for transfers between devices, body(): lax.psum(jnp.dot(image_cols, cols_vec_t.T, precision=high), 'col')  106 us
    another operation x14, other arithmetic, body(): jnp.linalg.cholesky(jnp.dot(shifted, shifted.T, precision=high))  78.2 us
    another operation x13, other arithmetic, body(): factor_low = jnp.linalg.cholesky(gram_sum)  68.7 us
    dot_general x8, matrix products, contract_first(): lax.dot_general(left, right, (((0,), (0,)), ((), ())), precision=lax.Prec...  61.5 us
    another operation x4, other arithmetic, body(): inner = jax.scipy.linalg.solve_triangular(factor_two, identity, lower=True)  42.5 us
    another operation x5, other arithmetic, body(): jax.scipy.linalg.solve_triangular(factor_low, panel_rows.T, lower=True)  39.4 us
  transfers between devices with their start and end apart: 8, of which 8 were waited for; matrix products, arithmetic and copies ran while one was open for 3% of the time, Pallas kernels for 0%

commit v1 on v0

v1 whole, which is shorter than its diff:
```python
import jax
import jax.numpy as jnp
from jax import lax
from jax.sharding import PartitionSpec as P

BAND = 256
PANELS = 2
HIGH = lax.Precision.HIGHEST


def mm(a, b):
    return jnp.dot(a, b, precision=HIGH)


def mm_tn(a, b):
    return lax.dot_general(a, b, (((0,), (0,)), ((), ())), precision=HIGH)


def mm_nt(a, b):
    return lax.dot_general(a, b, (((1,), (1,)), ((), ())), precision=HIGH)


def transpose_exchange(x, rows, cols):
    both = ("row", "col")
    first = []
    second = []
    for s in range(rows):
        for j in range(cols):
            src = s * cols + j
            first.append((src, (2 * j + s % 2) * cols + s // 2))
            second.append((src, (2 * j + 1 - s % 2) * cols + s // 2))
    got1 = lax.ppermute(x, both, first)
    got2 = lax.ppermute(x, both, second)
    odd_row = lax.axis_index("row") % 2 == 1
    even = jnp.where(odd_row, got2, got1)
    odd = jnp.where(odd_row, got1, got2)
    return jnp.concatenate([even, odd], axis=0)


def small_factors(gram, top):
    identity = jnp.eye(BAND, dtype=jnp.float32)
    low = jnp.linalg.cholesky(gram)
    low_inv = jax.scipy.linalg.solve_triangular(low, identity, lower=True)
    shifted = identity + mm_nt(top, low_inv)
    second = jnp.linalg.cholesky(mm_nt(shifted, shifted))
    second_inv = jax.scipy.linalg.solve_triangular(second, identity, lower=True)
    transform = mm_tn(shifted, mm_tn(second_inv, second_inv))
    return low_inv, transform


def body(a):
    rows = lax.psum(1, "row")
    cols = lax.psum(1, "col")
    row_count, col_count = a.shape
    r = lax.axis_index("row")
    c = lax.axis_index("col")
    row_pos = r * row_count + jnp.arange(row_count, dtype=jnp.int32)
    col_pos = c * col_count + jnp.arange(col_count, dtype=jnp.int32)
    band_idx = jnp.arange(BAND, dtype=jnp.int32)
    width = PANELS * BAND

    col_zero = c == 0
    colb = lax.psum(jnp.where(col_zero, a[:, :width], 0.0), "col")
    strip_t = transpose_exchange(colb, rows, cols)

    lo = BAND
    p0_loc = jnp.where(row_pos[:, None] >= lo, a[:, :BAND], 0.0)
    g_loc = jnp.where(col_zero, mm_tn(p0_loc, p0_loc), 0.0)
    top_loc = jnp.where(col_zero & (r == 0), a[lo:lo + BAND, :BAND], 0.0)
    gram0, top0 = lax.psum((g_loc, top_loc), ("row", "col"))

    stored = []
    current = a
    prev = None
    for k in range(PANELS):
        lo = (k + 1) * BAND
        if k == 0:
            gram, top = gram0, top0
            pr = jnp.where(row_pos[:, None] >= lo, colb[:, :BAND], 0.0)
            pc = jnp.where(col_pos[:, None] >= lo, strip_t[:, :BAND], 0.0)
        else:
            y_r0, w_r0, y_c0, w_c0, y_e0, w_e0 = prev
            pr = colb[:, k * BAND:(k + 1) * BAND] - mm_nt(y_r0, w_e0) - mm_nt(w_r0, y_e0)
            pc = strip_t[:, k * BAND:(k + 1) * BAND] - mm_nt(y_c0, w_e0) - mm_nt(w_c0, y_e0)
            pr = jnp.where(row_pos[:, None] >= lo, pr, 0.0)
            pc = jnp.where(col_pos[:, None] >= lo, pc, 0.0)
            g_part = mm_tn(pc, pc)
            top_part = jnp.where(col_zero, pc[lo:lo + BAND], 0.0)
            gram, top = lax.psum((g_part, top_part), "col")
        low_inv, transform = small_factors(gram, top)
        unit_r = (row_pos[:, None] - lo == band_idx[None, :]).astype(jnp.float32)
        unit_c = (col_pos[:, None] - lo == band_idx[None, :]).astype(jnp.float32)
        y_r = mm_nt(pr, low_inv) + unit_r
        y_c = mm_nt(pc, low_inv) + unit_c
        stored.append(y_r)

        xp = mm(current, y_c)
        if k + 1 < PANELS:
            nlo = (k + 1) * BAND
            ext = mm_tn(strip_t[:, nlo:nlo + BAND], y_c)
            x_r, x_e = lax.psum((xp, ext), "col")
        else:
            x_r = lax.psum(xp, "col")
        curv = lax.psum(mm_tn(y_r, xp), ("row", "col"))
        x_c = transpose_exchange(x_r, rows, cols)
        middle = mm_nt(mm(transform, curv), transform)
        w_r = mm_nt(x_r, transform) - 0.5 * mm(y_r, middle)
        w_c = mm_nt(x_c, transform) - 0.5 * mm(y_c, middle)
        current = current - mm_nt(y_r, w_c) - mm_nt(w_r, y_c)
        if k + 1 < PANELS:
            y_e = mm_nt(top, low_inv) + jnp.eye(BAND, dtype=jnp.float32)
            w_e = mm_nt(x_e, transform) - 0.5 * mm(y_e, middle)
            prev = (y_r, w_r, y_c, w_c, y_e, w_e)
    return current, jnp.concatenate(stored, axis=1)


def solution(mesh):
    return jax.shard_map(
        body,
        mesh=mesh,
        in_specs=(P("row", "col"),),
        out_specs=(P("row", "col"), P("row", None)),
        check_vma=False,
    )
```

time: 1110 us -> 1380 us (1.24)
  waiting for transfers between devices: 609 us -> 835 us
  starting transfers between devices: 1.03 us -> 21.4 us
    psum x8 -> x7, waiting for transfers between devices: 609 us -> 804 us  [the longest x2 430 us: body(): gram0, top0 = lax.psum((g_loc, top_loc), ('row', 'col'))]
    ppermute x0 -> x6, waiting for transfers between devices: none -> 30.3 us  [the longest x3 18.9 us: transpose_exchange(): got1 = lax.ppermute(x, both, first)]
    ppermute x0 -> x6, starting transfers between devices: none -> 20.9 us  [the longest x3 18.6 us: transpose_exchange(): got1 = lax.ppermute(x, both, first)]
    dot_general x32 -> x41, matrix products: 153 us -> 169 us  [the longest x23 108 us: mm_nt(): return lax.dot_general(a, b, (((1,), (1,)), ((), ())), precision=HIGH)]
    another operation x32 -> x20, matrix products: 28.5 us -> 16.9 us  [the longest x6 4.53 us: small_factors(): low_inv = jax.scipy.linalg.solve_triangular(low, identity, lower=True)]
  transfers between devices with their start and end apart: 8 -> 13, of which waited for: 8 -> 9; matrix products, arithmetic and copies ran while one was open for 3% -> 20% of each run, Pallas kernels for 0% -> 0%
where the time goes in v1:
time: 1380 us; the launch traced here: 1370 us
  waiting for transfers between devices  835 us (61%)
  other arithmetic  255 us (18%)
  matrix products  185 us (13%)
  local copies, waits for them, and re-layouts  51.6 us (4%)
  starting transfers between devices  21.4 us (2%)
  between operations  20.9 us (2%)
    psum x2, waiting for transfers between devices, body(): gram0, top0 = lax.psum((g_loc, top_loc), ('row', 'col'))  430 us
    psum x2, waiting for transfers between devices, body(): gram, top = lax.psum((g_part, top_part), 'col')  170 us
    psum x1, waiting for transfers between devices, body(): curv = lax.psum(mm_tn(y_r, xp), ('row', 'col'))  163 us
    dot_general x23, matrix products, mm_nt(): return lax.dot_general(a, b, (((1,), (1,)), ((), ())), precision=HIGH)  108 us
    another operation x14, other arithmetic, small_factors(): second = jnp.linalg.cholesky(mm_nt(shifted, shifted))  76.6 us
    another operation x13, other arithmetic, small_factors(): low = jnp.linalg.cholesky(gram)  75.8 us
    dot_general x9, matrix products, mm(): return jnp.dot(a, b, precision=HIGH)  44.4 us
    another operation x4, other arithmetic, small_factors(): second_inv = jax.scipy.linalg.solve_triangular(second, identity, lower=True)  42.7 us
  transfers between devices with their start and end apart: 13, of which 9 were waited for; matrix products, arithmetic and copies ran while one was open for 20% of the time, Pallas kernels for 0%

profile of v1, /device:TPU:1, one launch (start us, length us, event | category | flops | bytes accessed | tf_op | source)
XLA Modules:
  0.0 1369.1 jit_solution(15635334820634010336)
XLA Ops:
  8.8 2.0 fusion.18
  12.5 1.9 copy.20
  21.0 137.2 %all-reduce.14.cloned.1.call-done = f32[256,256]{0,1:T(8,128)} async-done(((f32[256,256]{0,1:T(8,128)}), f32[256,256]{0,1:T(8,128)}) %all-reduce.14.cloned.1.call-update) | async-done | bytes 262160 | tf_op jit(solution)/shard_map/psum | solution.py:70
  160.3 11.7 cholesky.214
  172.0 9.8 custom-call.17
  182.1 41.3 %all-reduce.12.cloned.1.call-done = f32[1152,512]{0,1:T(8,128)} async-done(((f32[1152,512]{0,1:T(8,128)}), f32[1152,512]{0,1:T(8,128)}) %all-reduce.12.cloned.1.call-update) | async-done | bytes 2359312 | tf_op jit(solution)/shard_map/psum | solution.py:63
  223.4 7.2 collective-permute-start.1
  231.2 11.7 cholesky.231
  245.0 4.0 while.8
  249.6 19.7 %custom-call.18 = f32[2,128,128]{1,2,0:T(8,128)S(1)} custom-call(f32[2,128,128]{2,1,0:T(8,128)S(1)} %get-tuple-element.30), custom_call_target="InvertDiagBlocksLowerTriangular" | custom-call | tf_op jit(solution)/shard_map/jit(_solve_triangular)/triangular_solve | solution.py:43
  270.2 2.7 convolution_add_fusion.3
  272.9 9.8 collective-permute-done
  282.7 2.7 broadcast_select_fusion.1
  285.4 4.2 convolution_add_fusion.1
  289.7 21.5 %fusion.94 = f32[256,1152]{1,0:T(8,128)S(1)} fusion(f32[2304,256]{1,0:T(8,128)S(1)} %convolution_add_fusion.1, f32[1152,2304]{1,0:T(8,128)} %param.4), kind=kOutput, calls=%fused_computation.198 | convolution fusion | flops 8153726976 | bytes 14155776 | tf_op jit(solution)/shard_map/dot_general | solution.py:12
  312.2 1.9 fusion.97
  314.2 4.5 fusion.22
  318.9 293.3 %all-reduce.20.cloned.1.call-done = (f32[256,256]{0,1:T(8,128)}, f32[256,256]{1,0:T(8,128)}) async-done(((f32[256,256]{0,1:T(8,128)}, f32[256,256]{1,0:T(8,128)}), (f32[256,256]{0,1:T(8,128)}, f32[256,256]{1,0:T(8,128)})) %all-reduce.20.cloned.1.call-update) | async-done | bytes 524304 | tf_op jit(solution)/shard_map/psum | solution.py:70
  619.9 13.2 cholesky.248
  635.2 11.3 custom-call.19
  651.5 13.2 cholesky.265
  670.4 7.2 while.9
  671.3 2.9 bitcast_dynamic-update-slice_fusion.9
  674.8 2.8 bitcast_dynamic-update-slice_fusion.9
  677.6 21.1 %custom-call.20 = f32[2,128,128]{1,2,0:T(8,128)} custom-call(f32[2,128,128]{2,1,0:T(8,128)} %get-tuple-element.31), custom_call_target="InvertDiagBlocksLowerTriangular" | custom-call | tf_op jit(solution)/shard_map/jit(_solve_triangular)/triangular_solve | solution.py:46
  706.4 3.4 convolution_multiply_fusion.1
  709.8 3.5 fusion.100
  713.3 4.2 collective-permute-start.3
  719.8 2.0 fusion.4
  723.3 2.5 fusion.3
  725.7 18.9 %collective-permute-done.3 = f32[1152,256]{0,1:T(8,128)S(1)} collective-permute-done((f32[1152,256]{0,1:T(8,128)S(1)}, f32[1152,256]{0,1:T(8,128)S(1)}, u32[]{:S(2)}, u32[]{:S(2)}) %collective-permute-start.3) | collective-permute-done | bytes 1179680 | tf_op jit(solution)/shard_map/ppermute | solution.py:32
  746.4 4.1 convolution_subtract_fusion.6
  750.4 2.3 fusion.102
  752.8 19.4 %convolution_subtract_fusion.3 = f32[1152,2304]{1,0:T(8,128)} fusion(f32[1152,2304]{1,0:T(8,128)S(1)} %bitcast.193, f32[1152,256]{0,1:T(8,128)S(1)} %convolution_add_fusion.3, f32[2304,256]{1,0:T(8,128)S(1)} %convolution_subtract_fusion.6), kind=kOutput, calls=%fused_computation.11 | convolution fusion | flops 8156381184 | bytes 24772608 | tf_op jit(solution)/shard_map/dot_general | solution.py:20
  772.2 2.6 fusion.1
  776.2 2.8 fusion.103
  779.0 13.9 %convolution_subtract_fusion.2 = f32[1152,2304]{1,0:T(8,128)} fusion(f32[1152,2304]{1,0:T(8,128)} %convolution_subtract_fusion.3, f32[1152,256]{1,0:T(8,128)} %copy-done.13, f32[2304,256]{1,0:T(8,128)S(1)} %convolution_add_fusion.1), kind=kOutput, calls=%fused_computation.10 | convolution fusion | flops 8156381184 | bytes 24772608 | tf_op jit(solution)/shard_map/dot_general | solution.py:20
  794.7 116.0 %all-reduce.16.cloned.1.call-done = f32[256,256]{0,1:T(8,128)} async-done(((f32[256,256]{0,1:T(8,128)}), f32[256,256]{0,1:T(8,128)}) %all-reduce.16.cloned.1.call-update) | async-done | bytes 262160 | tf_op jit(solution)/shard_map/psum | solution.py:89
  915.0 13.2 cholesky.282
  930.3 11.3 custom-call.21
  946.6 13.2 cholesky.299
  965.5 6.8 while.10
  966.1 2.8 bitcast_dynamic-update-slice_fusion.10
  969.5 2.8 bitcast_dynamic-update-slice_fusion.10
  972.3 21.3 %custom-call.22 = f32[2,128,128]{1,2,0:T(8,128)} custom-call(f32[2,128,128]{2,1,0:T(8,128)} %get-tuple-element.32), custom_call_target="InvertDiagBlocksLowerTriangular" | custom-call | tf_op jit(solution)/shard_map/jit(_solve_triangular)/triangular_solve | solution.py:43
  997.9 4.4 convolution_add_fusion
  1003.7 11.2 fusion.104
  1016.4 2.6 convolution_add_fusion.2
  1020.8 3.0 copy.15
  1023.8 1.9 fusion.107
  1025.8 53.7 %all-reduce.22.cloned.1.call-done = (f32[256,256]{0,1:T(8,128)}, f32[1152,256]{0,1:T(8,128)}) async-done(((f32[256,256]{0,1:T(8,128)}, f32[1152,256]{0,1:T(8,128)}), (f32[256,256]{0,1:T(8,128)}, f32[1152,256]{0,1:T(8,128)})) %all-reduce.22.cloned.1.call-update) | async-done | bytes 1441808 | tf_op jit(solution)/shard_map/psum | solution.py:89
  1079.4 7.2 collective-permute-start.5
  1089.4 11.7 cholesky.316
  1101.8 9.8 custom-call.23
  1112.1 11.7 cholesky.333
  1126.0 4.2 while.11
  1130.3 19.8 %custom-call.24 = f32[2,128,128]{1,2,0:T(8,128)S(1)} custom-call(f32[2,128,128]{2,1,0:T(8,128)S(1)} %get-tuple-element.33), custom_call_target="InvertDiagBlocksLowerTriangular" | custom-call | tf_op jit(solution)/shard_map/jit(_solve_triangular)/triangular_solve | solution.py:46
  1152.3 163.1 %all-reduce.18.cloned.1.call-done = f32[256,256]{1,0:T(8,128)} async-done(((f32[256,256]{1,0:T(8,128)}), f32[256,256]{1,0:T(8,128)}) %all-reduce.18.cloned.1.call-update) | async-done | bytes 262160 | tf_op jit(solution)/shard_map/psum | solution.py:104
  1318.3 3.5 fusion.110
  1321.8 2.0 fusion.2
  1323.8 2.1 convolution_multiply_fusion
  1327.9 4.3 convolution_subtract_fusion.4
  1332.3 18.1 %convolution_subtract_fusion.1 = f32[1152,2304]{1,0:T(8,128)S(1)} fusion(f32[1152,2304]{1,0:T(8,128)S(1)} %bitcast.191, f32[1152,256]{0,1:T(8,128)S(1)} %copy-done.9, f32[2304,256]{1,0:T(8,128)S(1)} %convolution_subtract_fusion.4), kind=kOutput, calls=%fused_computation.9 | convolution fusion | flops 8156381184 | bytes 24772608 | tf_op jit(solution)/shard_map/dot_general | solution.py:20
  1350.3 11.5 convolution_subtract_fusion
  (239 shorter events, 98.7 us)
Async XLA Ops:
  7.2 1.3 slice-start.6
  7.2 151.0 %all-reduce.14.cloned.1.call-start = ((), (), s32[]{:S(2)}) async-start(), calls=%async_computation.1 | async-start | bytes 524288 | tf_op jit(solution)/shard_map/psum | solution.py:70
  10.8 1.7 slice-start.7
  10.8 212.5 %all-reduce.12.cloned.1.call-start = ((), (), s32[]{:S(2)}) async-start(), calls=%async_computation | async-start | bytes 4718592 | tf_op jit(solution)/shard_map/psum | solution.py:63
  16.0 596.2 %all-reduce.20.cloned.1.call-start = ((), (), s32[]{:S(2)}) async-start(), calls=%async_computation.4 | async-start | bytes 1048576 | tf_op jit(solution)/shard_map/psum | solution.py:70
  20.2 249.3 %copy-start.19 = (f32[256,256]{1,0:T(8,128)}, f32[256,256]{1,0:T(8,128)S(1)}, u32[]{:S(2)}) copy-start(f32[256,256]{1,0:T(8,128)S(1)} %fusion.39) | copy-start | bytes 786436
  223.4 49.5 %collective-permute-start.1 = (f32[1152,512]{0,1:T(8,128)}, f32[1152,512]{0,1:T(8,128)}, u32[]{:S(2)}, u32[]{:S(2)}) collective-permute-start(f32[1152,512]{0,1:T(8,128)} %all-reduce.12.cloned.1.call-done), channel_id=1, source_target_pairs={{0,0},{1,16},{2,32},{3,48},{4,64},{5,80},{6,96},{7,112},{8,8},{9,2... | collective-permute-start | bytes 7077896 | tf_op jit(solution)/shard_map/ppermute | solution.py:32
  230.6 52.1 %collective-permute-start = (f32[1152,512]{0,1:T(8,128)}, f32[1152,512]{0,1:T(8,128)}, u32[]{:S(2)}, u32[]{:S(2)}) collective-permute-start(f32[1152,512]{0,1:T(8,128)} %all-reduce.12.cloned.1.call-done), channel_id=1, source_target_pairs={{0,8},{1,24},{2,40},{3,56},{4,72},{5,88},{6,104},{7,120},{8,0},{9,... | collective-permute-start | bytes 7077896 | tf_op jit(solution)/shard_map/ppermute | solution.py:33
  249.0 0.6 copy-start.40
  269.6 15.8 %copy-start.23 = (f32[128,256]{1,0:T(8,128)}, f32[128,256]{1,0:T(8,128)S(1)}, u32[]{:S(2)}) copy-start(f32[128,256]{1,0:T(8,128)S(1)} %fusion.46) | copy-start | bytes 393220
  270.2 15.2 %copy-start.27 = (f32[128,256]{1,0:T(8,128)}, f32[128,256]{1,0:T(8,128)S(1)}, u32[]{:S(2)}) copy-start(f32[128,256]{1,0:T(8,128)S(1)} %fusion.61) | copy-start | bytes 393220
  272.9 12.6 copy-start.37
  285.4 4.3 copy-start.4
  285.4 4.3 copy-start.6
  311.2 1.0 copy-start.12
  314.2 395.6 %all-reduce.24.cloned.1.call-start = ((), (), s32[]{:S(2)}) async-start(), calls=%async_computation.6 | async-start | bytes 2883584 | tf_op jit(solution)/shard_map/psum | solution.py:101
  318.7 591.9 %all-reduce.16.cloned.1.call-start = ((), (), s32[]{:S(2)}) async-start(), calls=%async_computation.2 | async-start | bytes 524288 | tf_op jit(solution)/shard_map/psum | solution.py:89
  612.2 58.2 %copy-start.41 = (s32[2,2]{1,0:T(2,128)S(1)}, s32[2,2]{1,0:T(2,128)}, u32[]{:S(2)}) copy-start(s32[2,2]{1,0:T(2,128)} %copy-done.40) | copy-start | bytes 52
  613.9 0.7 copy-start.10
  618.6 0.7 copy-start.31
  698.7 5.8 copy-start.34
  704.5 0.7 copy-start.14
  705.7 0.7 copy-start.21
  709.8 3.5 copy-start.30
  709.8 9.2 copy-start.15
  709.8 9.2 copy-start.33
  709.8 9.6 copy-start.11
  709.8 9.6 copy-start.22
  713.3 31.4 %collective-permute-start.3 = (f32[1152,256]{0,1:T(8,128)S(1)}, f32[1152,256]{0,1:T(8,128)S(1)}, u32[]{:S(2)}, u32[]{:S(2)}) collective-permute-start(f32[1152,256]{0,1:T(8,128)S(1)} %copy-done.30), channel_id=1, source_target_pairs={{0,0},{1,16},{2,32},{3,48},{4,64},{5,80},{6,96},{7,112},{8,8},{9,2... | collective-permute-start | bytes 3538952 | tf_op jit(solution)/shard_map/ppermute | solution.py:32
  717.5 28.7 %collective-permute-start.2 = (f32[1152,256]{0,1:T(8,128)S(1)}, f32[1152,256]{0,1:T(8,128)S(1)}, u32[]{:S(2)}, u32[]{:S(2)}) collective-permute-start(f32[1152,256]{0,1:T(8,128)S(1)} %copy-done.30), channel_id=1, source_target_pairs={{0,8},{1,24},{2,40},{3,56},{4,72},{5,88},{6,104},{7,120},{8,0},{9,... | collective-permute-start | bytes 3538952 | tf_op jit(solution)/shard_map/ppermute | solution.py:33
  719.4 2.5 copy-start.26
  721.9 1.4 copy-start.13
  721.9 1.4 copy-start.39
  723.3 23.1 %copy-start.16 = (f32[2304,256]{1,0:T(8,128)S(1)}, f32[2304,256]{1,0:T(8,128)}, u32[]{:S(2)}) copy-start(f32[2304,256]{1,0:T(8,128)} %convolution_multiply_fusion.1) | copy-start | bytes 7077892
  723.3 29.5 %slice-start.3 = ((s8[10616832]{0:T(1024)(128)(4,1)}), s8[4194304]{0:T(1024)(128)(4,1)S(1)}, s32[]{:S(2)}) async-start(s8[10616832]{0:T(1024)(128)(4,1)} %bitcast.192), calls=%async_computation.10 | async-start | bytes 8388608
  725.7 27.0 %slice-start.4 = ((s8[10616832]{0:T(1024)(128)(4,1)}), s8[4194304]{0:T(1024)(128)(4,1)S(1)}, s32[]{:S(2)}) async-start(s8[10616832]{0:T(1024)(128)(4,1)} %bitcast.192), calls=%async_computation.11 | async-start | bytes 8388608
  746.4 6.4 slice-start.5
  752.8 19.4 %copy-start.5 = (f32[1152,512]{0,1:T(8,128)S(1)}, f32[1152,512]{0,1:T(8,128)}, u32[]{:S(2)}) copy-start(f32[1152,512]{0,1:T(8,128)} %copy-done.4) | copy-start | bytes 7077892
  752.8 19.4 %copy-start.7 = (f32[1152,512]{0,1:T(8,128)S(1)}, f32[1152,512]{0,1:T(8,128)}, u32[]{:S(2)}) copy-start(f32[1152,512]{0,1:T(8,128)} %copy-done.6) | copy-start | bytes 7077892
  752.8 19.4 %copy-start.38 = (pred[2304]{0:T(1024)(128)(4,1)S(1)}, pred[2304]{0:T(1024)(128)(4,1)}, u32[]{:S(2)}) copy-start(pred[2304]{0:T(1024)(128)(4,1)} %fusion.69) | copy-start | bytes 6916
  774.7 1.4 copy-start
  779.0 300.5 %all-reduce.22.cloned.1.call-start = ((), (), s32[]{:S(2)}) async-start(), calls=%async_computation.5 | async-start | bytes 2883584 | tf_op jit(solution)/shard_map/psum | solution.py:89
  912.4 85.5 %copy-start.1 = (f32[2304,256]{0,1:T(8,128)S(1)}, f32[2304,256]{0,1:T(8,128)}, u32[]{:S(2)}) copy-start(f32[2304,256]{0,1:T(8,128)} %copy-done) | copy-start | bytes 7077892
  912.4 85.5 %copy-start.35 = (s32[2304]{0:T(1024)S(1)}, s32[2304]{0:T(1024)}, u32[]{:S(2)}) copy-start(s32[2304]{0:T(1024)} %fusion.68) | copy-start | bytes 27652
  913.6 0.7 copy-start.32
  994.8 2.4 copy-start.24
  997.2 0.7 copy-start.28
  1002.3 1.4 copy-start.2
  1014.9 1.5 copy-start.36
  1016.3 299.0 %all-reduce.18.cloned.1.call-start = ((), (), s32[]{:S(2)}) async-start(), calls=%async_computation.3 | async-start | bytes 524288 | tf_op jit(solution)/shard_map/psum | solution.py:104
  1019.0 4.8 copy-start.8
  1023.8 63.4 %copy-start.25 = (f32[128,256]{1,0:T(8,128)S(1)}, f32[128,256]{1,0:T(8,128)}, u32[]{:S(2)}) copy-start(f32[128,256]{1,0:T(8,128)} %copy-done.24) | copy-start | bytes 393220
  1023.8 63.4 %copy-start.29 = (f32[128,256]{1,0:T(8,128)S(1)}, f32[128,256]{1,0:T(8,128)}, u32[]{:S(2)}) copy-start(f32[128,256]{1,0:T(8,128)} %copy-done.28) | copy-start | bytes 393220
  1079.4 246.6 %collective-permute-start.5 = (f32[1152,256]{0,1:T(8,128)}, f32[1152,256]{0,1:T(8,128)}, u32[]{:S(2)}, u32[]{:S(2)}) collective-permute-start(f32[1152,256]{0,1:T(8,128)} %get-tuple-element.71), channel_id=1, source_target_pairs={{0,0},{1,16},{2,32},{3,48},{4,64},{5,80},{6,96},{7,112},{8,8},{9,2... | collective-permute-start | bytes 3538952 | tf_op jit(solution)/shard_map/ppermute | solution.py:32
  1086.7 239.3 %collective-permute-start.4 = (f32[1152,256]{0,1:T(8,128)}, f32[1152,256]{0,1:T(8,128)}, u32[]{:S(2)}, u32[]{:S(2)}) collective-permute-start(f32[1152,256]{0,1:T(8,128)} %get-tuple-element.71), channel_id=1, source_target_pairs={{0,8},{1,24},{2,40},{3,56},{4,72},{5,88},{6,104},{7,120},{8,0},{9,... | collective-permute-start | bytes 3538952 | tf_op jit(solution)/shard_map/ppermute | solution.py:33
  1088.8 61.4 %copy-start.20 = (f32[256,256]{1,0:T(8,128)S(1)}, f32[256,256]{1,0:T(8,128)}, u32[]{:S(2)}) copy-start(f32[256,256]{1,0:T(8,128)} %copy-done.19) | copy-start | bytes 786436
  1151.6 170.1 %copy-start.9 = (f32[1152,256]{0,1:T(8,128)S(1)}, f32[1152,256]{0,1:T(8,128)}, u32[]{:S(2)}) copy-start(f32[1152,256]{0,1:T(8,128)} %copy-done.8) | copy-start | bytes 3538948
  1152.2 163.1 %copy-start.17 = (f32[256,256]{1,0:T(8,128)}, f32[256,256]{1,0:T(8,128)S(1)}, u32[]{:S(2)}) copy-start(f32[256,256]{1,0:T(8,128)S(1)} %fusion.106) | copy-start | bytes 786436
  1316.7 7.1 copy-start.3
  1318.2 14.0 %slice-start = ((s8[10616832]{0:T(1024)(128)(4,1)}), s8[4194304]{0:T(1024)(128)(4,1)S(1)}, s32[]{:S(2)}) async-start(s8[10616832]{0:T(1024)(128)(4,1)} %bitcast.190), calls=%async_computation.7 | async-start | bytes 8388608
  1323.8 8.4 slice-start.1
  1326.0 2.0 copy-start.18
  1326.0 6.3 slice-start.2
Sparse Core Ops, SparseCore 0:
  13.3 144.8 all-reduce.13
  161.1 62.1 all-reduce.11
  314.3 297.8 all-reduce.19
  615.3 60.7 all-reduce.23
  779.1 131.4 all-reduce.15
  1016.5 62.9 all-reduce.21
  1084.2 231.1 all-reduce.17

commit v2 on v1

--- a/solution.py
+++ b/solution.py
@@ -1,11 +1,17 @@
+import functools
+import itertools
+
 import jax
 import jax.numpy as jnp
 from jax import lax
+from jax.experimental import pallas as pl
+from jax.experimental.pallas import tpu as pltpu
 from jax.sharding import PartitionSpec as P
 
 BAND = 256
 PANELS = 2
 HIGH = lax.Precision.HIGHEST
+MESH_ID = pl.DeviceIdType.MESH
 
 
 def mm(a, b):
@@ -18,6 +24,72 @@
 
 def mm_nt(a, b):
     return lax.dot_general(a, b, (((1,), (1,)), ((), ())), precision=HIGH)
+
+
+def _a2a_kernel(axis, groups, x_ref, o_ref, local_sem, send_sems, recv_sems):
+    me = lax.axis_index(axis)
+    barrier = pltpu.get_barrier_semaphore()
+    for k in range(1, groups):
+        peer = (me + k) % groups
+        pl.semaphore_signal(barrier, 1, device_id={axis: peer}, device_id_type=MESH_ID)
+    pl.semaphore_wait(barrier, groups - 1)
+    local = pltpu.make_async_copy(x_ref.at[me], o_ref.at[me], local_sem)
+    local.start()
+    copies = []
+    for k in range(1, groups):
+        peer = (me + k) % groups
+        copy = pltpu.make_async_remote_copy(
+            src_ref=x_ref.at[peer],
+            dst_ref=o_ref.at[me],
+            send_sem=send_sems.at[k],
+            recv_sem=recv_sems.at[k],
+            device_id={axis: peer},
+            device_id_type=MESH_ID,
+        )
+        copy.start()
+        copies.append(copy)
+    for copy in copies:
+        copy.wait_send()
+    for copy in copies:
+        copy.wait_recv()
+    local.wait()
+
+
+class Comm:
+    def __init__(self):
+        self.ids = itertools.count()
+
+    def a2a(self, x, axis):
+        groups = x.shape[0]
+        return pl.pallas_call(
+            functools.partial(_a2a_kernel, axis, groups),
+            out_shape=jax.ShapeDtypeStruct(x.shape, x.dtype),
+            in_specs=[pl.BlockSpec(memory_space=pl.ANY)],
+            out_specs=pl.BlockSpec(memory_space=pl.ANY),
+            scratch_shapes=[
+                pltpu.SemaphoreType.DMA,
+                pltpu.SemaphoreType.DMA((groups,)),
+                pltpu.SemaphoreType.DMA((groups,)),
+            ],
+            compiler_params=pltpu.CompilerParams(
+                collective_id=next(self.ids), has_side_effects=True
+            ),
+        )(x)
+
+    def reduce_scatter(self, x, axis, groups):
+        parts = self.a2a(x.reshape(groups, x.shape[0] // groups, *x.shape[1:]), axis)
+        return jnp.sum(parts, axis=0)
+
+    def all_gather(self, x, axis, groups):
+        got = self.a2a(jnp.broadcast_to(x[None], (groups,) + x.shape), axis)
+        return got.reshape(groups * x.shape[0], *x.shape[1:])
+
+    def psum(self, x, axis, groups):
+        return self.all_gather(self.reduce_scatter(x, axis, groups), axis, groups)
+
+    def broadcast(self, x, axis, groups, root):
+        parts = self.a2a(x.reshape(groups, x.shape[0] // groups, *x.shape[1:]), axis)
+        return self.all_gather(parts[root], axis, groups)
 
 
 def transpose_exchange(x, rows, cols):
@@ -49,6 +121,7 @@
 
 
 def body(a):
+    comm = Comm()
     rows = lax.psum(1, "row")
     cols = lax.psum(1, "col")
     row_count, col_count = a.shape
@@ -59,15 +132,13 @@
     band_idx = jnp.arange(BAND, dtype=jnp.int32)
     width = PANELS * BAND
 
-    col_zero = c == 0
-    colb = lax.psum(jnp.where(col_zero, a[:, :width], 0.0), "col")
+    colb = comm.broadcast(a[:, :width], "col", cols, 0)
+    lo = BAND
+    p0 = jnp.where(row_pos[:, None] >= lo, colb[:, :BAND], 0.0)
+    top_part = jnp.where(r == 0, colb[lo:lo + BAND, :BAND], 0.0)
+    summed = comm.psum(jnp.concatenate([mm_tn(p0, p0), top_part], axis=0), "row", rows)
+    gram0, top0 = summed[:BAND], summed[BAND:]
     strip_t = transpose_exchange(colb, rows, cols)
-
-    lo = BAND
-    p0_loc = jnp.where(row_pos[:, None] >= lo, a[:, :BAND], 0.0)
-    g_loc = jnp.where(col_zero, mm_tn(p0_loc, p0_loc), 0.0)
-    top_loc = jnp.where(col_zero & (r == 0), a[lo:lo + BAND, :BAND], 0.0)
-    gram0, top0 = lax.psum((g_loc, top_loc), ("row", "col"))
 
     stored = []
     current = a
@@ -76,7 +147,7 @@
         lo = (k + 1) * BAND
         if k == 0:
             gram, top = gram0, top0
-            pr = jnp.where(row_pos[:, None] >= lo, colb[:, :BAND], 0.0)
+            pr = p0
             pc = jnp.where(col_pos[:, None] >= lo, strip_t[:, :BAND], 0.0)
         else:
             y_r0, w_r0, y_c0, w_c0, y_e0, w_e0 = prev
@@ -84,9 +155,9 @@
             pc = strip_t[:, k * BAND:(k + 1) * BAND] - mm_nt(y_c0, w_e0) - mm_nt(w_c0, y_e0)
             pr = jnp.where(row_pos[:, None] >= lo, pr, 0.0)
             pc = jnp.where(col_pos[:, None] >= lo, pc, 0.0)
-            g_part = mm_tn(pc, pc)
-            top_part = jnp.where(col_zero, pc[lo:lo + BAND], 0.0)
-            gram, top = lax.psum((g_part, top_part), "col")
+            top_part = jnp.where(c == 0, pc[lo:lo + BAND], 0.0)
+            summed = comm.psum(jnp.concatenate([mm_tn(pc, pc), top_part], axis=0), "col", cols)
+            gram, top = summed[:BAND], summed[BAND:]
         low_inv, transform = small_factors(gram, top)
         unit_r = (row_pos[:, None] - lo == band_idx[None, :]).astype(jnp.float32)
         unit_c = (col_pos[:, None] - lo == band_idx[None, :]).astype(jnp.float32)
@@ -95,19 +166,20 @@
         stored.append(y_r)
 
         xp = mm(current, y_c)
+        parts = [xp, mm_tn(y_r, xp)]
         if k + 1 < PANELS:
             nlo = (k + 1) * BAND
-            ext = mm_tn(strip_t[:, nlo:nlo + BAND], y_c)
-            x_r, x_e = lax.psum((xp, ext), "col")
-        else:
-            x_r = lax.psum(xp, "col")
-        curv = lax.psum(mm_tn(y_r, xp), ("row", "col"))
+            parts.append(mm_tn(strip_t[:, nlo:nlo + BAND], y_c))
+        summed = comm.psum(jnp.concatenate(parts, axis=0), "col", cols)
+        x_r = summed[:row_count]
+        curv = comm.psum(summed[row_count:row_count + BAND], "row", rows)
         x_c = transpose_exchange(x_r, rows, cols)
         middle = mm_nt(mm(transform, curv), transform)
         w_r = mm_nt(x_r, transform) - 0.5 * mm(y_r, middle)
         w_c = mm_nt(x_c, transform) - 0.5 * mm(y_c, middle)
         current = current - mm_nt(y_r, w_c) - mm_nt(w_r, y_c)
         if k + 1 < PANELS:
+            x_e = summed[row_count + BAND:]
             y_e = mm_nt(top, low_inv) + jnp.eye(BAND, dtype=jnp.float32)
             w_e = mm_nt(x_e, transform) - 0.5 * mm(y_e, middle)
             prev = (y_r, w_r, y_c, w_c, y_e, w_e)

time: 1380 us -> 1060 us (0.77)
  waiting for transfers between devices: 835 us -> 0.02 us
  Pallas kernels: 0 us -> 536 us
  matrix products: 185 us -> 167 us
    psum x7 -> x0, waiting for transfers between devices: 804 us -> none  [the longest x2 430 us: body(): gram0, top0 = lax.psum((g_loc, top_loc), ('row', 'col'))]
    pallas_call x0 -> x14, Pallas kernels: none -> 536 us  [a2a(): pl.pallas_call(functools.partial(_a2a_kernel, axis, groups), out_shape=ja...]
    ppermute x3, waiting for transfers between devices: 18.9 us -> 0.01 us  [transpose_exchange(): got1 = lax.ppermute(x, both, first)]
    dot_general x23, matrix products: 108 us -> 92.7 us  [mm_nt(): return lax.dot_general(a, b, (((1,), (1,)), ((), ())), precision=HIGH)]
    another operation x13 -> x14, other arithmetic: 75.8 us -> 77.3 us  [small_factors(): low = jnp.linalg.cholesky(gram)]
  transfers between devices with their start and end apart: 13 -> 6, of which waited for: 9 -> 0; matrix products, arithmetic and copies ran while one was open for 20% -> 23% of each run, Pallas kernels for 0% -> 35%
where the time goes in v2:
time: 1060 us; the launch traced here: 1040 us
  Pallas kernels  536 us (51%)
  other arithmetic  255 us (24%)
  matrix products  167 us (16%)
  local copies, waits for them, and re-layouts  59.1 us (6%)
  starting transfers between devices  15.4 us (1%)
    pallas_call x14, Pallas kernels, a2a(): pl.pallas_call(functools.partial(_a2a_kernel, axis, groups), out_shape=ja...  536 us
    dot_general x23, matrix products, mm_nt(): return lax.dot_general(a, b, (((1,), (1,)), ((), ())), precision=HIGH)  92.7 us
    another operation x14, other arithmetic, small_factors(): low = jnp.linalg.cholesky(gram)  77.3 us
    another operation x14, other arithmetic, small_factors(): second = jnp.linalg.cholesky(mm_nt(shifted, shifted))  69.3 us
    another operation x5, other arithmetic, small_factors(): low_inv = jax.scipy.linalg.solve_triangular(low, identity, lower=True)  42.5 us
    dot_general x9, matrix products, mm(): return jnp.dot(a, b, precision=HIGH)  41.7 us
    another operation x4, other arithmetic, small_factors(): second_inv = jax.scipy.linalg.solve_triangular(second, identity, lower=True)  39.6 us
  transfers between devices with their start and end apart: 6, of which 0 were waited for; matrix products, arithmetic and copies ran while one was open for 23% of the time, Pallas kernels for 35%

profile of v2, /device:TPU:1, one launch (start us, length us, event | category | flops | bytes accessed | tf_op | source)
XLA Modules:
  0.0 1040.8 jit_solution(10880050841079641914)
XLA Ops:
  0.6 3.3 slice.97
  3.9 31.8 %shard_map.30 = f32[8,144,512]{2,1,0:T(8,128)} custom-call(f32[8,144,512]{2,1,0:T(8,128)} %bitcast.225), custom_call_target="tpu_custom_call" | custom-call | tf_op jit(solution)/shard_map/pallas_call | solution.py:64
  38.4 29.7 %shard_map.31 = f32[8,144,512]{2,1,0:T(8,128)} custom-call(f32[8,144,512]{2,1,0:T(8,128)} %broadcast_in_dim.99.x_ref), custom_call_target="tpu_custom_call" | custom-call | tf_op jit(solution)/shard_map/pallas_call | solution.py:64
  68.1 2.8 collective-permute-start
  70.9 2.9 collective-permute-start.1
  75.5 4.2 fusion.17
  80.6 199.7 %shard_map.32 = f32[16,32,256]{2,1,0:T(8,128)} custom-call(f32[16,32,256]{2,1,0:T(8,128)} %bitcast.230), custom_call_target="tpu_custom_call" | custom-call | tf_op jit(solution)/shard_map/pallas_call | solution.py:64
  282.2 14.0 %shard_map.33 = f32[16,32,256]{2,1,0:T(8,128)} custom-call(f32[16,32,256]{2,1,0:T(8,128)} %broadcast_in_dim.102.x_ref), custom_call_target="tpu_custom_call" | custom-call | tf_op jit(solution)/shard_map/pallas_call | solution.py:64
  297.5 11.7 %cholesky.214 = f32[128,128]{1,0:T(8,128)S(1)} custom-call(f32[128,128]{1,0:T(8,128)S(1)} %cholesky.346), custom_call_target="Cholesky" | custom-call | tf_op jit(solution)/shard_map/jit(cholesky)/cholesky | solution.py:114
  309.2 9.8 custom-call.17
  319.5 12.0 %cholesky.231 = f32[128,128]{1,0:T(8,128)S(1)} custom-call(f32[128,128]{1,0:T(8,128)S(1)} %convolution_subtract_fusion.16), custom_call_target="Cholesky" | custom-call | tf_op jit(solution)/shard_map/jit(cholesky)/cholesky | solution.py:114
  334.4 4.1 while.8
  338.5 19.7 %custom-call.18 = f32[2,128,128]{1,2,0:T(8,128)S(1)} custom-call(f32[2,128,128]{2,1,0:T(8,128)S(1)} %get-tuple-element.30), custom_call_target="InvertDiagBlocksLowerTriangular" | custom-call | tf_op jit(solution)/shard_map/jit(_solve_triangular)/triangular_solve | solution.py:115
  361.5 11.7 %cholesky.248 = f32[128,128]{1,0:T(8,128)S(1)} custom-call(f32[128,128]{1,0:T(8,128)S(1)} %cholesky.349), custom_call_target="Cholesky" | custom-call | tf_op jit(solution)/shard_map/jit(cholesky)/cholesky | solution.py:117
  373.3 9.8 custom-call.19
  385.3 11.7 %cholesky.265 = f32[128,128]{1,0:T(8,128)S(1)} custom-call(f32[128,128]{1,0:T(8,128)S(1)} %convolution_subtract_fusion.15), custom_call_target="Cholesky" | custom-call | tf_op jit(solution)/shard_map/jit(cholesky)/cholesky | solution.py:117
  399.7 3.9 while.9
  403.6 19.8 %custom-call.20 = f32[2,128,128]{1,2,0:T(8,128)S(1)} custom-call(f32[2,128,128]{2,1,0:T(8,128)S(1)} %get-tuple-element.31), custom_call_target="InvertDiagBlocksLowerTriangular" | custom-call | tf_op jit(solution)/shard_map/jit(_solve_triangular)/triangular_solve | solution.py:118
  428.1 2.3 convolution_add_fusion.3
  430.5 3.1 broadcast_select_fusion
  435.7 21.4 %fusion.98 = f32[256,1152]{1,0:T(8,128)S(1)} fusion(f32[2304,256]{1,0:T(8,128)S(1)} %convolution_add_fusion.1, f32[1152,2304]{1,0:T(8,128)} %param.4), kind=kOutput, calls=%fused_computation.208 | convolution fusion | flops 8153726976 | bytes 14155776 | tf_op jit(solution)/shard_map/dot_general | solution.py:18
  457.1 3.9 fusion.18
  463.5 2.7 copy.16
  466.3 24.4 %shard_map.34 = f32[8,208,256]{2,1,0:T(8,128)} custom-call(f32[8,208,256]{2,1,0:T(8,128)} %bitcast.226), custom_call_target="tpu_custom_call" | custom-call | tf_op jit(solution)/shard_map/pallas_call | solution.py:64
  490.7 2.3 reduce_sum.55
  492.9 2.3 broadcast_in_dim.105.x_ref
  495.2 22.7 %shard_map.35 = f32[8,208,256]{2,1,0:T(8,128)} custom-call(f32[8,208,256]{2,1,0:T(8,128)} %broadcast_in_dim.105.x_ref), custom_call_target="tpu_custom_call" | custom-call | tf_op jit(solution)/shard_map/pallas_call | solution.py:64
  517.9 2.5 slice.139
  520.4 2.5 collective-permute-start.2
  522.9 2.5 collective-permute-start.3
  527.3 2.2 fusion.90
  529.5 97.0 %shard_map.36 = f32[16,16,256]{2,1,0:T(8,128)} custom-call(f32[16,16,256]{2,1,0:T(8,128)} %bitcast.237), custom_call_target="tpu_custom_call" | custom-call | tf_op jit(solution)/shard_map/pallas_call | solution.py:64
  628.2 12.0 %shard_map.37 = f32[16,16,256]{2,1,0:T(8,128)} custom-call(f32[16,16,256]{2,1,0:T(8,128)} %broadcast_in_dim.106.x_ref), custom_call_target="tpu_custom_call" | custom-call | tf_op jit(solution)/shard_map/pallas_call | solution.py:64
  654.0 2.3 convolution_subtract_fusion.6
  658.5 19.4 %convolution_subtract_fusion.3 = f32[1152,2304]{1,0:T(8,128)} fusion(f32[1152,2304]{1,0:T(8,128)S(1)} %bitcast.210, f32[1152,256]{0,1:T(8,128)S(1)} %convolution_add_fusion.3, f32[2304,256]{1,0:T(8,128)S(1)} %convolution_subtract_fusion.6), kind=kOutput, calls=%fused_computation.11 | convolution fusion | flops 8156381184 | bytes 24772608 | tf_op jit(solution)/shard_map/dot_general | solution.py:26
  677.9 2.2 fusion.1
  680.2 4.0 fusion.105
  685.1 11.5 %shard_map.38 = f32[8,64,256]{2,1,0:T(8,128)} custom-call(f32[8,64,256]{2,1,0:T(8,128)} %bitcast.231), custom_call_target="tpu_custom_call" | custom-call | tf_op jit(solution)/shard_map/pallas_call | solution.py:64
  699.9 10.0 shard_map.39
  716.1 13.2 %cholesky.282 = f32[128,128]{1,0:T(8,128)} custom-call(f32[128,128]{1,0:T(8,128)} %cholesky.352), custom_call_target="Cholesky" | custom-call | tf_op jit(solution)/shard_map/jit(cholesky)/cholesky | solution.py:114
  732.3 11.7 %custom-call.21 = f32[1,128,128]{1,2,0:T(8,128)} custom-call(f32[1,128,128]{2,1,0:T(8,128)} %get-tuple-element.95), custom_call_target="InvertDiagBlocksLowerTriangular" | custom-call | tf_op jit(solution)/shard_map/jit(cholesky)/cholesky | solution.py:114
  747.4 13.2 %cholesky.299 = f32[128,128]{1,0:T(8,128)} custom-call(f32[128,128]{1,0:T(8,128)} %convolution_subtract_fusion.14), custom_call_target="Cholesky" | custom-call | tf_op jit(solution)/shard_map/jit(cholesky)/cholesky | solution.py:114
  767.0 7.0 while.10
  767.7 2.9 bitcast_dynamic-update-slice_fusion.10
  771.2 2.8 bitcast_dynamic-update-slice_fusion.10
  774.1 21.1 %custom-call.22 = f32[2,128,128]{1,2,0:T(8,128)} custom-call(f32[2,128,128]{2,1,0:T(8,128)} %get-tuple-element.32), custom_call_target="InvertDiagBlocksLowerTriangular" | custom-call | tf_op jit(solution)/shard_map/jit(_solve_triangular)/triangular_solve | solution.py:115
  798.9 13.2 %convolution_subtract_fusion.2 = f32[1152,2304]{1,0:T(8,128)S(1)} fusion(f32[1152,2304]{1,0:T(8,128)} %convolution_subtract_fusion.3, f32[1152,256]{1,0:T(8,128)} %copy-done.15, f32[2304,256]{1,0:T(8,128)S(1)} %convolution_add_fusion.1), kind=kOutput, calls=%fused_computation.10 | convolution fusion | flops 8156381184 | bytes 24772608 | tf_op jit(solution)/shard_map/dot_general | solution.py:26
  814.2 8.7 fusion.106
  828.1 19.9 %shard_map.40 = f32[8,176,256]{2,1,0:T(8,128)} custom-call(f32[8,176,256]{2,1,0:T(8,128)} %bitcast.227), custom_call_target="tpu_custom_call" | custom-call | tf_op jit(solution)/shard_map/pallas_call | solution.py:64
  852.3 19.9 %shard_map.41 = f32[8,176,256]{2,1,0:T(8,128)} custom-call(f32[8,176,256]{2,1,0:T(8,128)} %broadcast_in_dim.110.x_ref), custom_call_target="tpu_custom_call" | custom-call | tf_op jit(solution)/shard_map/pallas_call | solution.py:64
  873.9 2.4 slice.144
  877.8 3.3 collective-permute-start.5
  884.4 11.7 %cholesky.316 = f32[128,128]{1,0:T(8,128)S(1)} custom-call(f32[128,128]{1,0:T(8,128)S(1)} %cholesky.355), custom_call_target="Cholesky" | custom-call | tf_op jit(solution)/shard_map/jit(cholesky)/cholesky | solution.py:117
  896.2 9.8 custom-call.23
  908.2 11.7 %cholesky.333 = f32[128,128]{1,0:T(8,128)S(1)} custom-call(f32[128,128]{1,0:T(8,128)S(1)} %convolution_subtract_fusion.13), custom_call_target="Cholesky" | custom-call | tf_op jit(solution)/shard_map/jit(cholesky)/cholesky | solution.py:117
  922.6 4.1 while.11
  926.7 19.7 %custom-call.24 = f32[2,128,128]{1,2,0:T(8,128)S(1)} custom-call(f32[2,128,128]{2,1,0:T(8,128)S(1)} %get-tuple-element.33), custom_call_target="InvertDiagBlocksLowerTriangular" | custom-call | tf_op jit(solution)/shard_map/jit(_solve_triangular)/triangular_solve | solution.py:118
  950.0 32.9 %shard_map.42 = f32[16,16,256]{2,1,0:T(8,128)} custom-call(f32[16,16,256]{2,1,0:T(8,128)} %bitcast.235), custom_call_target="tpu_custom_call" | custom-call | tf_op jit(solution)/shard_map/pallas_call | solution.py:64
  984.6 10.2 shard_map.43
  994.8 3.1 copy.20
  998.7 2.6 fusion.88
  1001.3 3.1 fusion.2
  1010.7 18.1 %convolution_subtract_fusion.1 = f32[1152,2304]{1,0:T(8,128)S(1)} fusion(f32[1152,2304]{1,0:T(8,128)S(1)} %bitcast.208, f32[1152,256]{0,1:T(8,128)S(1)} %copy-done.9, f32[2304,256]{1,0:T(8,128)S(1)} %convolution_subtract_fusion.4), kind=kOutput, calls=%fused_computation.9 | convolution fusion | flops 8156381184 | bytes 24772608 | tf_op jit(solution)/shard_map/dot_general | solution.py:26
  1028.9 11.5 %convolution_subtract_fusion = f32[1152,2304]{1,0:T(8,128)} fusion(f32[1152,2304]{1,0:T(8,128)S(1)} %convolution_subtract_fusion.1, f32[1152,256]{1,0:T(8,128)S(1)} %copy-done.20, f32[2304,256]{1,0:T(8,128)S(1)} %convolution_add_fusion), kind=kOutput, calls=%fused_computation.8 | convolution fusion | flops 8156381184 | bytes 24772608 | tf_op jit(solution)/shard_map/dot_general | solution.py:26
  (250 shorter events, 118.3 us)
Async XLA Ops:
  68.1 362.4 %collective-permute-start = (f32[1152,512]{1,0:T(8,128)}, f32[1152,512]{1,0:T(8,128)}, u32[]{:S(2)}, u32[]{:S(2)}) collective-permute-start(f32[1152,512]{1,0:T(8,128)} %bitcast.211), channel_id=1, source_target_pairs={{0,8},{1,24},{2,40},{3,56},{4,72},{5,88},{6,104},{7,120},{8,0},{9,... | collective-permute-start | bytes 7077896 | tf_op jit(solution)/shard_map/ppermute | solution.py:105
  70.9 359.6 %collective-permute-start.1 = (f32[1152,512]{1,0:T(8,128)}, f32[1152,512]{1,0:T(8,128)}, u32[]{:S(2)}, u32[]{:S(2)}) collective-permute-start(f32[1152,512]{1,0:T(8,128)} %bitcast.212), channel_id=1, source_target_pairs={{0,0},{1,16},{2,32},{3,48},{4,64},{5,80},{6,96},{7,112},{8,8},{9,2... | collective-permute-start | bytes 7077896 | tf_op jit(solution)/shard_map/ppermute | solution.py:104
  73.8 351.8 %copy-start.18 = (f32[256,256]{1,0:T(8,128)}, f32[256,256]{1,0:T(8,128)S(1)}, u32[]{:S(2)}) copy-start(f32[256,256]{1,0:T(8,128)S(1)} %fusion.37) | copy-start | bytes 786436
  358.5 26.8 %copy-start.23 = (f32[128,256]{1,0:T(8,128)}, f32[128,256]{1,0:T(8,128)S(1)}, u32[]{:S(2)}) copy-start(f32[128,256]{1,0:T(8,128)S(1)} %fusion.44) | copy-start | bytes 393220
  359.1 0.7 copy-start.27
  360.2 66.6 %copy-start.12 = (f32[256,256]{1,0:T(8,128)}, f32[256,256]{1,0:T(8,128)S(1)}, u32[]{:S(2)}) copy-start(f32[256,256]{1,0:T(8,128)S(1)} %convolution_add_fusion.5) | copy-start | bytes 786436
  360.8 0.7 copy-start.34
  373.3 54.9 %copy-start.10 = (f32[8,144,512]{2,1,0:T(8,128)S(1)}, f32[8,144,512]{2,1,0:T(8,128)}, u32[]{:S(2)}) copy-start(f32[8,144,512]{2,1,0:T(8,128)} %shard_map.31) | copy-start | bytes 7077892
  403.6 26.9 %copy-start.42 = (s32[2,2]{1,0:T(2,128)}, s32[2,2]{1,0:T(2,128)S(1)}, u32[]{:S(2)}) copy-start(s32[2,2]{1,0:T(2,128)S(1)} %get-tuple-element.301) | copy-start | bytes 52
  423.5 4.6 copy-start.24
  430.5 3.2 copy-start.28
  433.6 23.5 %copy-start.3 = (f32[1152,512]{1,0:T(8,128)}, f32[1152,512]{1,0:T(8,128)S(1)}, u32[]{:S(2)}) copy-start(f32[1152,512]{1,0:T(8,128)S(1)} %get-tuple-element.78) | copy-start | bytes 7077892
  433.6 23.5 %copy-start.5 = (f32[1152,512]{1,0:T(8,128)}, f32[1152,512]{1,0:T(8,128)S(1)}, u32[]{:S(2)}) copy-start(f32[1152,512]{1,0:T(8,128)S(1)} %get-tuple-element.79) | copy-start | bytes 7077892
  517.9 7.5 copy-start.14
  517.9 8.3 copy-start.16
  520.4 131.6 %collective-permute-start.2 = (f32[1152,256]{1,0:T(8,128)}, f32[1152,256]{1,0:T(8,128)}, u32[]{:S(2)}, u32[]{:S(2)}) collective-permute-start(f32[1152,256]{1,0:T(8,128)} %slice.139), channel_id=1, source_target_pairs={{0,8},{1,24},{2,40},{3,56},{4,72},{5,88},{6,104},{7,120},{8,0},{9,... | collective-permute-start | bytes 3538952 | tf_op jit(solution)/shard_map/ppermute | solution.py:105
  522.9 129.1 %collective-permute-start.3 = (f32[1152,256]{1,0:T(8,128)}, f32[1152,256]{1,0:T(8,128)}, u32[]{:S(2)}, u32[]{:S(2)}) collective-permute-start(f32[1152,256]{1,0:T(8,128)} %slice.139), channel_id=1, source_target_pairs={{0,0},{1,16},{2,32},{3,48},{4,64},{5,80},{6,96},{7,112},{8,8},{9,2... | collective-permute-start | bytes 3538952 | tf_op jit(solution)/shard_map/ppermute | solution.py:104
  640.2 3.0 copy-start.22
  641.7 3.5 copy-start.13
  641.7 3.5 copy-start.33
  643.2 2.5 copy-start.11
  645.2 2.4 copy-start.15
  645.2 2.4 copy-start.41
  649.8 8.6 slice-start.3
  651.9 2.0 copy-start.17
  652.0 6.5 slice-start.4
  653.9 4.5 slice-start.5
  658.5 19.4 %copy-start.4 = (f32[1152,512]{1,0:T(8,128)S(1)}, f32[1152,512]{1,0:T(8,128)}, u32[]{:S(2)}) copy-start(f32[1152,512]{1,0:T(8,128)} %copy-done.3) | copy-start | bytes 7077892
  658.5 19.4 %copy-start.6 = (f32[1152,512]{1,0:T(8,128)S(1)}, f32[1152,512]{1,0:T(8,128)}, u32[]{:S(2)}) copy-start(f32[1152,512]{1,0:T(8,128)} %copy-done.5) | copy-start | bytes 7077892
  658.5 19.4 %copy-start.40 = (pred[2304]{0:T(1024)(128)(4,1)S(1)}, pred[2304]{0:T(1024)(128)(4,1)}, u32[]{:S(2)}) copy-start(pred[2304]{0:T(1024)(128)(4,1)} %get-tuple-element.116) | copy-start | bytes 6916
  680.1 4.1 copy-start.1
  710.0 57.0 %copy-start.43 = (s32[2,2]{1,0:T(2,128)S(1)}, s32[2,2]{1,0:T(2,128)}, u32[]{:S(2)}) copy-start(s32[2,2]{1,0:T(2,128)} %copy-done.42) | copy-start | bytes 52
  714.7 0.7 copy-start.35
  796.4 26.5 %copy-start.25 = (f32[128,256]{1,0:T(8,128)}, f32[128,256]{1,0:T(8,128)S(1)}, u32[]{:S(2)}) copy-start(f32[128,256]{1,0:T(8,128)S(1)} %fusion.40) | copy-start | bytes 393220
  798.8 24.1 %copy-start.29 = (f32[128,256]{1,0:T(8,128)}, f32[128,256]{1,0:T(8,128)S(1)}, u32[]{:S(2)}) copy-start(f32[128,256]{1,0:T(8,128)S(1)} %fusion.51) | copy-start | bytes 393220
  798.8 13.3 %copy-start.2 = (f32[2304,256]{1,0:T(8,128)S(1)}, f32[2304,256]{1,0:T(8,128)}, u32[]{:S(2)}) copy-start(f32[2304,256]{1,0:T(8,128)} %copy-done.1) | copy-start | bytes 7077892
  798.9 13.3 %copy-start.38 = (s32[2304]{0:T(1024)S(1)}, s32[2304]{0:T(1024)}, u32[]{:S(2)}) copy-start(s32[2304]{0:T(1024)} %fusion.66) | copy-start | bytes 27652
  812.1 10.8 %copy-start = (f32[1152,2304]{1,0:T(8,128)}, f32[1152,2304]{1,0:T(8,128)S(1)}, u32[]{:S(2)}) copy-start(f32[1152,2304]{1,0:T(8,128)S(1)} %convolution_subtract_fusion.2) | copy-start | bytes 31850500
  814.2 8.8 copy-start.21
  814.2 8.8 copy-start.39
  824.7 1.0 copy-start.7
  872.2 8.9 copy-start.8
  876.4 6.3 copy-start.26
  876.4 6.3 copy-start.30
  876.4 6.3 copy-start.32
  876.4 130.2 %collective-permute-start.4 = (f32[1152,256]{1,0:T(8,128)}, f32[1152,256]{1,0:T(8,128)}, u32[]{:S(2)}, u32[]{:S(2)}) collective-permute-start(f32[1152,256]{1,0:T(8,128)} %slice.144), channel_id=1, source_target_pairs={{0,8},{1,24},{2,40},{3,56},{4,72},{5,88},{6,104},{7,120},{8,0},{9,... | collective-permute-start | bytes 3538952 | tf_op jit(solution)/shard_map/ppermute | solution.py:105
  877.8 128.8 %collective-permute-start.5 = (f32[1152,256]{1,0:T(8,128)}, f32[1152,256]{1,0:T(8,128)}, u32[]{:S(2)}, u32[]{:S(2)}) collective-permute-start(f32[1152,256]{1,0:T(8,128)} %slice.144), channel_id=1, source_target_pairs={{0,0},{1,16},{2,32},{3,48},{4,64},{5,80},{6,96},{7,112},{8,8},{9,2... | collective-permute-start | bytes 3538952 | tf_op jit(solution)/shard_map/ppermute | solution.py:104
  883.1 64.0 %copy-start.19 = (f32[256,256]{1,0:T(8,128)S(1)}, f32[256,256]{1,0:T(8,128)}, u32[]{:S(2)}) copy-start(f32[256,256]{1,0:T(8,128)} %copy-done.18) | copy-start | bytes 786436
  883.7 0.7 copy-start.36
  946.4 0.7 copy-start.37
  994.8 3.1 copy-start.31
  997.9 3.4 copy-start.9
  998.7 11.9 %slice-start = ((s8[10616832]{0:T(1024)(128)(4,1)}), s8[4194304]{0:T(1024)(128)(4,1)S(1)}, s32[]{:S(2)}) async-start(s8[10616832]{0:T(1024)(128)(4,1)} %bitcast.207), calls=%async_computation | async-start | bytes 8388608
  1004.5 6.2 slice-start.1
  1006.6 4.1 slice-start.2
  1010.7 18.1 %copy-start.20 = (f32[1152,256]{1,0:T(8,128)S(1)}, f32[1152,256]{1,0:T(8,128)}, u32[]{:S(2)}) copy-start(f32[1152,256]{1,0:T(8,128)} %fusion.2) | copy-start | bytes 3538948

commit v3 on v2

--- a/solution.py
+++ b/solution.py
@@ -11,19 +11,20 @@
 BAND = 256
 PANELS = 2
 HIGH = lax.Precision.HIGHEST
+FAST = lax.Precision.HIGH
 MESH_ID = pl.DeviceIdType.MESH
 
 
-def mm(a, b):
-    return jnp.dot(a, b, precision=HIGH)
+def mm(a, b, precision=HIGH):
+    return jnp.dot(a, b, precision=precision)
 
 
-def mm_tn(a, b):
-    return lax.dot_general(a, b, (((0,), (0,)), ((), ())), precision=HIGH)
+def mm_tn(a, b, precision=HIGH):
+    return lax.dot_general(a, b, (((0,), (0,)), ((), ())), precision=precision)
 
 
-def mm_nt(a, b):
-    return lax.dot_general(a, b, (((1,), (1,)), ((), ())), precision=HIGH)
+def mm_nt(a, b, precision=HIGH):
+    return lax.dot_general(a, b, (((1,), (1,)), ((), ())), precision=precision)
 
 
 def _a2a_kernel(axis, groups, x_ref, o_ref, local_sem, send_sems, recv_sems):
@@ -165,19 +166,21 @@
         y_c = mm_nt(pc, low_inv) + unit_c
         stored.append(y_r)
 
-        xp = mm(current, y_c)
-        parts = [xp, mm_tn(y_r, xp)]
+        xp = mm(current, y_c, FAST)
+        xq = mm_tn(current, y_r, FAST)
+        summed_c = comm.psum(jnp.concatenate([xq, mm_tn(y_r, xp)], axis=0), "row", rows)
+        x_c = summed_c[:col_count]
+        parts = [xp, summed_c[col_count:]]
         if k + 1 < PANELS:
             nlo = (k + 1) * BAND
             parts.append(mm_tn(strip_t[:, nlo:nlo + BAND], y_c))
         summed = comm.psum(jnp.concatenate(parts, axis=0), "col", cols)
         x_r = summed[:row_count]
-        curv = comm.psum(summed[row_count:row_count + BAND], "row", rows)
-        x_c = transpose_exchange(x_r, rows, cols)
+        curv = summed[row_count:row_count + BAND]
         middle = mm_nt(mm(transform, curv), transform)
         w_r = mm_nt(x_r, transform) - 0.5 * mm(y_r, middle)
         w_c = mm_nt(x_c, transform) - 0.5 * mm(y_c, middle)
-        current = current - mm_nt(y_r, w_c) - mm_nt(w_r, y_c)
+        current = current - mm_nt(y_r, w_c, FAST) - mm_nt(w_r, y_c, FAST)
         if k + 1 < PANELS:
             x_e = summed[row_count + BAND:]
             y_e = mm_nt(top, low_inv) + jnp.eye(BAND, dtype=jnp.float32)

time: 1060 us -> 1100 us (1.038)
  Pallas kernels: 536 us -> 586 us
  matrix products: 167 us -> 149 us
  other arithmetic: 255 us -> 269 us
    pallas_call x14, Pallas kernels: 536 us -> 586 us  [a2a(): pl.pallas_call(functools.partial(_a2a_kernel, axis, groups), out_shape=ja...]
    dot_general x41 -> x43, matrix products: 152 us -> 135 us  [the longest x23 73 us: mm_nt(): return lax.dot_general(a, b, (((1,), (1,)), ((), ())), precision=precision)]
  transfers between devices with their start and end apart: 6 -> 2, of which waited for: 0 -> 0; matrix products, arithmetic and copies ran while one was open for 23% -> 14% of each run, Pallas kernels for 35% -> 20%
where the time goes in v3:
time: 1100 us; the launch traced here: 1080 us
  Pallas kernels  586 us (53%)
  other arithmetic  269 us (24%)
  matrix products  149 us (14%)
  local copies, waits for them, and re-layouts  66 us (6%)
    pallas_call x14, Pallas kernels, a2a(): pl.pallas_call(functools.partial(_a2a_kernel, axis, groups), out_shape=ja...  586 us
    another operation x14, other arithmetic, small_factors(): low = jnp.linalg.cholesky(gram)  87.8 us
    dot_general x23, matrix products, mm_nt(): return lax.dot_general(a, b, (((1,), (1,)), ((), ())), precision=precision)  73 us
    another operation x14, other arithmetic, small_factors(): second = jnp.linalg.cholesky(mm_nt(shifted, shifted))  69.4 us
    another operation x5, other arithmetic, small_factors(): low_inv = jax.scipy.linalg.solve_triangular(low, identity, lower=True)  42.5 us
    another operation x4, other arithmetic, small_factors(): second_inv = jax.scipy.linalg.solve_triangular(second, identity, lower=True)  40 us
    dot_general x11, matrix products, mm_tn(): return lax.dot_general(a, b, (((0,), (0,)), ((), ())), precision=precision)  35.5 us
    dot_general x9, matrix products, mm(): return jnp.dot(a, b, precision=precision)  26.2 us
  transfers between devices with their start and end apart: 2, of which 0 were waited for; matrix products, arithmetic and copies ran while one was open for 14% of the time, Pallas kernels for 20%

profile of v3, /device:TPU:1, one launch (start us, length us, event | category | flops | bytes accessed | tf_op | source)
XLA Modules:
  0.0 1083.9 jit_solution(17616001592319415242)
XLA Ops:
  0.6 3.3 slice.109
  3.9 31.8 %shard_map.30 = f32[8,144,512]{2,1,0:T(8,128)} custom-call(f32[8,144,512]{2,1,0:T(8,128)} %bitcast.230), custom_call_target="tpu_custom_call" | custom-call | tf_op jit(solution)/shard_map/pallas_call | solution.py:65
  38.4 29.7 %shard_map.31 = f32[8,144,512]{2,1,0:T(8,128)} custom-call(f32[8,144,512]{2,1,0:T(8,128)} %broadcast_in_dim.99.x_ref), custom_call_target="tpu_custom_call" | custom-call | tf_op jit(solution)/shard_map/pallas_call | solution.py:65
  68.1 2.8 collective-permute-start
  70.9 2.9 collective-permute-start.1
  75.5 4.0 fusion.21
  80.4 199.9 %shard_map.32 = f32[16,32,256]{2,1,0:T(8,128)} custom-call(f32[16,32,256]{2,1,0:T(8,128)} %bitcast.240), custom_call_target="tpu_custom_call" | custom-call | tf_op jit(solution)/shard_map/pallas_call | solution.py:65
  282.2 14.0 %shard_map.33 = f32[16,32,256]{2,1,0:T(8,128)} custom-call(f32[16,32,256]{2,1,0:T(8,128)} %broadcast_in_dim.102.x_ref), custom_call_target="tpu_custom_call" | custom-call | tf_op jit(solution)/shard_map/pallas_call | solution.py:65
  297.5 11.7 %cholesky.214 = f32[128,128]{1,0:T(8,128)S(1)} custom-call(f32[128,128]{1,0:T(8,128)S(1)} %cholesky.346), custom_call_target="Cholesky" | custom-call | tf_op jit(solution)/shard_map/jit(cholesky)/cholesky | solution.py:115
  309.2 9.8 custom-call.17
  319.6 22.9 %cholesky.231 = f32[128,128]{1,0:T(8,128)S(1)} custom-call(f32[128,128]{1,0:T(8,128)S(1)} %convolution_subtract_fusion.14), custom_call_target="Cholesky" | custom-call | tf_op jit(solution)/shard_map/jit(cholesky)/cholesky | solution.py:115
  345.2 4.0 while.8
  349.1 19.7 %custom-call.18 = f32[2,128,128]{1,2,0:T(8,128)S(1)} custom-call(f32[2,128,128]{2,1,0:T(8,128)S(1)} %get-tuple-element.30), custom_call_target="InvertDiagBlocksLowerTriangular" | custom-call | tf_op jit(solution)/shard_map/jit(_solve_triangular)/triangular_solve | solution.py:116
  372.1 11.7 %cholesky.248 = f32[128,128]{1,0:T(8,128)S(1)} custom-call(f32[128,128]{1,0:T(8,128)S(1)} %cholesky.349), custom_call_target="Cholesky" | custom-call | tf_op jit(solution)/shard_map/jit(cholesky)/cholesky | solution.py:118
  383.9 9.8 custom-call.19
  395.9 11.7 %cholesky.265 = f32[128,128]{1,0:T(8,128)S(1)} custom-call(f32[128,128]{1,0:T(8,128)S(1)} %convolution_subtract_fusion.13), custom_call_target="Cholesky" | custom-call | tf_op jit(solution)/shard_map/jit(cholesky)/cholesky | solution.py:118
  410.3 4.0 while.9
  414.9 19.9 %custom-call.20 = f32[2,128,128]{1,2,0:T(8,128)S(1)} custom-call(f32[2,128,128]{2,1,0:T(8,128)S(1)} %get-tuple-element.31), custom_call_target="InvertDiagBlocksLowerTriangular" | custom-call | tf_op jit(solution)/shard_map/jit(_solve_triangular)/triangular_solve | solution.py:119
  438.3 2.3 convolution_add_fusion.3
  440.6 8.2 convolution_bitcast_fusion
  449.0 3.3 broadcast_select_fusion
  454.6 4.6 fusion.22
  459.2 9.9 fusion.100
  473.1 3.3 copy.17
  476.4 38.6 %shard_map.34 = f32[16,160,256]{2,1,0:T(8,128)} custom-call(f32[16,160,256]{2,1,0:T(8,128)} %bitcast.229), custom_call_target="tpu_custom_call" | custom-call | tf_op jit(solution)/shard_map/pallas_call | solution.py:65
  515.0 2.6 reduce_sum.55
  517.6 2.7 broadcast_in_dim.105.x_ref
  520.3 45.9 %shard_map.35 = f32[16,160,256]{2,1,0:T(8,128)} custom-call(f32[16,160,256]{2,1,0:T(8,128)} %broadcast_in_dim.105.x_ref), custom_call_target="tpu_custom_call" | custom-call | tf_op jit(solution)/shard_map/pallas_call | solution.py:65
  569.6 2.7 pad_maximum_fusion.4
  572.4 2.9 copy.21
  575.3 30.8 %shard_map.36 = f32[8,208,256]{2,1,0:T(8,128)} custom-call(f32[8,208,256]{2,1,0:T(8,128)} %bitcast.234), custom_call_target="tpu_custom_call" | custom-call | tf_op jit(solution)/shard_map/pallas_call | solution.py:65
  606.1 2.3 reduce_sum.56
  610.6 22.7 %shard_map.37 = f32[8,208,256]{2,1,0:T(8,128)} custom-call(f32[8,208,256]{2,1,0:T(8,128)} %broadcast_in_dim.106.x_ref), custom_call_target="tpu_custom_call" | custom-call | tf_op jit(solution)/shard_map/pallas_call | solution.py:65
  636.3 3.9 fusion.12
  647.3 12.8 %convolution_subtract_fusion.3 = f32[1152,2304]{1,0:T(8,128)} fusion(f32[1152,2304]{1,0:T(8,128)S(1)} %bitcast.216, f32[1152,256]{0,1:T(8,128)S(1)} %convolution_add_fusion.3, f32[2304,256]{1,0:T(8,128)S(1)} %fusion.3), kind=kOutput, calls=%fused_computation.11 | convolution fusion | flops 4079517696 | bytes 24772608 | tf_op jit(solution)/shard_map/dot_general | solution.py:27
  660.6 3.1 convolution_subtract_fusion.6
  665.9 4.0 fusion.106
  670.8 10.0 shard_map.38
  684.2 10.0 shard_map.39
  700.3 13.3 %cholesky.282 = f32[128,128]{1,0:T(8,128)} custom-call(f32[128,128]{1,0:T(8,128)} %cholesky.352), custom_call_target="Cholesky" | custom-call | tf_op jit(solution)/shard_map/jit(cholesky)/cholesky | solution.py:115
  716.7 11.3 %custom-call.21 = f32[1,128,128]{1,2,0:T(8,128)} custom-call(f32[1,128,128]{2,1,0:T(8,128)} %get-tuple-element.91), custom_call_target="InvertDiagBlocksLowerTriangular" | custom-call | tf_op jit(solution)/shard_map/jit(cholesky)/cholesky | solution.py:115
  731.5 13.2 %cholesky.299 = f32[128,128]{1,0:T(8,128)} custom-call(f32[128,128]{1,0:T(8,128)} %convolution_subtract_fusion.12), custom_call_target="Cholesky" | custom-call | tf_op jit(solution)/shard_map/jit(cholesky)/cholesky | solution.py:115
  751.1 8.5 while.10
  752.4 2.9 bitcast_dynamic-update-slice_fusion.10
  756.7 2.9 bitcast_dynamic-update-slice_fusion.10
  759.6 21.1 %custom-call.22 = f32[2,128,128]{1,2,0:T(8,128)} custom-call(f32[2,128,128]{2,1,0:T(8,128)} %get-tuple-element.32), custom_call_target="InvertDiagBlocksLowerTriangular" | custom-call | tf_op jit(solution)/shard_map/jit(_solve_triangular)/triangular_solve | solution.py:116
  784.4 3.4 fusion.6
  787.9 8.2 convolution_subtract_fusion.2
  803.1 9.1 fusion.107
  812.2 4.4 fusion.108
  819.4 57.7 %shard_map.40 = f32[16,160,256]{2,1,0:T(8,128)} custom-call(f32[16,160,256]{2,1,0:T(8,128)} %bitcast.228), custom_call_target="tpu_custom_call" | custom-call | tf_op jit(solution)/shard_map/pallas_call | solution.py:65
  877.1 2.6 reduce_sum.58
  879.7 2.7 broadcast_in_dim.110.x_ref
  882.4 51.0 %shard_map.41 = f32[16,160,256]{2,1,0:T(8,128)} custom-call(f32[16,160,256]{2,1,0:T(8,128)} %broadcast_in_dim.110.x_ref), custom_call_target="tpu_custom_call" | custom-call | tf_op jit(solution)/shard_map/pallas_call | solution.py:65
  935.6 23.9 %shard_map.42 = f32[8,176,256]{2,1,0:T(8,128)} custom-call(f32[8,176,256]{2,1,0:T(8,128)} %bitcast.237), custom_call_target="tpu_custom_call" | custom-call | tf_op jit(solution)/shard_map/pallas_call | solution.py:65
  962.2 19.9 %shard_map.43 = f32[8,176,256]{2,1,0:T(8,128)} custom-call(f32[8,176,256]{2,1,0:T(8,128)} %broadcast_in_dim.111.x_ref), custom_call_target="tpu_custom_call" | custom-call | tf_op jit(solution)/shard_map/pallas_call | solution.py:65
  983.9 11.9 %cholesky.316 = f32[128,128]{1,0:T(8,128)S(1)} custom-call(f32[128,128]{1,0:T(8,128)S(1)} %cholesky.355), custom_call_target="Cholesky" | custom-call | tf_op jit(solution)/shard_map/jit(cholesky)/cholesky | solution.py:118
  995.9 9.8 custom-call.23
  1007.8 11.7 %cholesky.333 = f32[128,128]{1,0:T(8,128)S(1)} custom-call(f32[128,128]{1,0:T(8,128)S(1)} %convolution_subtract_fusion.11), custom_call_target="Cholesky" | custom-call | tf_op jit(solution)/shard_map/jit(cholesky)/cholesky | solution.py:118
  1022.2 4.0 while.11
  1026.2 20.1 %custom-call.24 = f32[2,128,128]{1,2,0:T(8,128)S(1)} custom-call(f32[2,128,128]{2,1,0:T(8,128)S(1)} %get-tuple-element.33), custom_call_target="InvertDiagBlocksLowerTriangular" | custom-call | tf_op jit(solution)/shard_map/jit(_solve_triangular)/triangular_solve | solution.py:119
  1058.5 12.6 %convolution_subtract_fusion.1 = f32[1152,2304]{1,0:T(8,128)} fusion(f32[1152,2304]{1,0:T(8,128)S(1)} %bitcast.212, f32[1152,256]{0,1:T(8,128)S(1)} %convolution_add_fusion.2, f32[2304,256]{1,0:T(8,128)S(1)} %fusion), kind=kOutput, calls=%fused_computation.9 | convolution fusion | flops 4079517696 | bytes 24772608 | tf_op jit(solution)/shard_map/dot_general | solution.py:27
  1071.0 3.2 copy.24
  1074.2 9.5 convolution_subtract_fusion
  (247 shorter events, 117.8 us)
Async XLA Ops:
  68.1 380.8 %collective-permute-start = (f32[1152,512]{1,0:T(8,128)}, f32[1152,512]{1,0:T(8,128)}, u32[]{:S(2)}, u32[]{:S(2)}) collective-permute-start(f32[1152,512]{1,0:T(8,128)} %bitcast.217), channel_id=1, source_target_pairs={{0,8},{1,24},{2,40},{3,56},{4,72},{5,88},{6,104},{7,120},{8,0},{9,... | collective-permute-start | bytes 7077896 | tf_op jit(solution)/shard_map/ppermute | solution.py:106
  70.9 378.0 %collective-permute-start.1 = (f32[1152,512]{1,0:T(8,128)}, f32[1152,512]{1,0:T(8,128)}, u32[]{:S(2)}, u32[]{:S(2)}) collective-permute-start(f32[1152,512]{1,0:T(8,128)} %bitcast.218), channel_id=1, source_target_pairs={{0,0},{1,16},{2,32},{3,48},{4,64},{5,80},{6,96},{7,112},{8,8},{9,2... | collective-permute-start | bytes 7077896 | tf_op jit(solution)/shard_map/ppermute | solution.py:105
  73.8 361.9 %copy-start.19 = (f32[256,256]{1,0:T(8,128)}, f32[256,256]{1,0:T(8,128)S(1)}, u32[]{:S(2)}) copy-start(f32[256,256]{1,0:T(8,128)S(1)} %fusion.45) | copy-start | bytes 786436
  369.1 26.7 %copy-start.24 = (f32[128,256]{1,0:T(8,128)}, f32[128,256]{1,0:T(8,128)S(1)}, u32[]{:S(2)}) copy-start(f32[128,256]{1,0:T(8,128)S(1)} %fusion.52) | copy-start | bytes 393220
  369.7 0.7 copy-start.28
  370.8 66.1 %copy-start.12 = (f32[256,256]{1,0:T(8,128)}, f32[256,256]{1,0:T(8,128)S(1)}, u32[]{:S(2)}) copy-start(f32[256,256]{1,0:T(8,128)S(1)} %convolution_add_fusion.5) | copy-start | bytes 786436
  371.4 0.7 copy-start.33
  383.9 54.4 %copy-start.10 = (f32[8,144,512]{2,1,0:T(8,128)S(1)}, f32[8,144,512]{2,1,0:T(8,128)}, u32[]{:S(2)}) copy-start(f32[8,144,512]{2,1,0:T(8,128)} %shard_map.31) | copy-start | bytes 7077892
  414.3 20.5 %copy-start.40 = (s32[2,2]{1,0:T(2,128)}, s32[2,2]{1,0:T(2,128)S(1)}, u32[]{:S(2)}) copy-start(s32[2,2]{1,0:T(2,128)S(1)} %get-tuple-element.297) | copy-start | bytes 52
  434.8 3.5 copy-start.25
  448.9 3.4 copy-start.29
  448.9 3.4 copy-start.37
  448.9 10.3 slice-start.3
  448.9 10.3 slice-start.4
  452.2 2.1 copy-start.6
  452.2 2.4 copy-start.8
  452.3 6.9 slice-start.5
  469.1 1.0 copy-start.15
  633.3 7.0 copy-start.18
  636.3 4.0 copy-start.17
  636.3 10.9 %slice-start.6 = ((s8[10616832]{0:T(1024)(128)(4,1)}), s8[4194304]{0:T(1024)(128)(4,1)S(1)}, s32[]{:S(2)}) async-start(s8[10616832]{0:T(1024)(128)(4,1)} %bitcast.215), calls=%async_computation.6 | async-start | bytes 8388608
  640.3 7.0 slice-start.7
  642.9 17.2 %copy-start.23 = (f32[256,256]{1,0:T(8,128)}, f32[256,256]{1,0:T(8,128)S(1)}, u32[]{:S(2)}) copy-start(f32[256,256]{1,0:T(8,128)S(1)} %fusion.104) | copy-start | bytes 786436
  642.9 2.2 copy-start.13
  642.9 4.3 slice-start.8
  647.3 13.3 %copy-start.11 = (f32[8,144,512]{2,1,0:T(8,128)S(1)}, f32[8,144,512]{2,1,0:T(8,128)}, u32[]{:S(2)}) copy-start(f32[8,144,512]{2,1,0:T(8,128)} %shard_map.31) | copy-start | bytes 7077892
  660.1 3.5 copy-start.7
  660.2 3.5 copy-start.9
  660.2 3.5 copy-start.38
  665.9 4.1 copy-start.1
  699.0 0.7 copy-start.34
  782.0 19.7 %copy-start.26 = (f32[128,256]{1,0:T(8,128)}, f32[128,256]{1,0:T(8,128)S(1)}, u32[]{:S(2)}) copy-start(f32[128,256]{1,0:T(8,128)S(1)} %fusion.48) | copy-start | bytes 393220
  784.4 17.3 %copy-start.30 = (f32[128,256]{1,0:T(8,128)}, f32[128,256]{1,0:T(8,128)S(1)}, u32[]{:S(2)}) copy-start(f32[128,256]{1,0:T(8,128)S(1)} %fusion.59) | copy-start | bytes 393220
  787.9 8.3 copy-start.14
  787.9 8.3 copy-start.22
  787.9 8.3 copy-start.39
  796.1 16.0 %copy-start = (f32[1152,2304]{1,0:T(8,128)}, f32[1152,2304]{1,0:T(8,128)S(1)}, u32[]{:S(2)}) copy-start(f32[1152,2304]{1,0:T(8,128)S(1)} %convolution_subtract_fusion.2) | copy-start | bytes 31850500
  796.1 3.4 copy-start.2
  799.6 2.2 copy-start.36
  801.7 10.5 copy-start.3
  961.0 21.1 %copy-start.27 = (f32[128,256]{1,0:T(8,128)S(1)}, f32[128,256]{1,0:T(8,128)}, u32[]{:S(2)}) copy-start(f32[128,256]{1,0:T(8,128)} %copy-done.26) | copy-start | bytes 393220
  961.0 21.1 %copy-start.31 = (f32[128,256]{1,0:T(8,128)S(1)}, f32[128,256]{1,0:T(8,128)}, u32[]{:S(2)}) copy-start(f32[128,256]{1,0:T(8,128)} %copy-done.30) | copy-start | bytes 393220
  961.0 21.1 %copy-start.32 = (f32[4,64,256]{2,1,0:T(8,128)S(1)}, f32[4,64,256]{2,1,0:T(8,128)}, u32[]{:S(2)}) copy-start(f32[4,64,256]{2,1,0:T(8,128)} %get-tuple-element.80) | copy-start | bytes 786436
  982.1 40.1 %copy-start.41 = (s32[2,2]{1,0:T(2,128)S(1)}, s32[2,2]{1,0:T(2,128)}, u32[]{:S(2)}) copy-start(s32[2,2]{1,0:T(2,128)} %get-tuple-element.298) | copy-start | bytes 52
  982.6 63.7 %copy-start.20 = (f32[256,256]{1,0:T(8,128)S(1)}, f32[256,256]{1,0:T(8,128)}, u32[]{:S(2)}) copy-start(f32[256,256]{1,0:T(8,128)} %copy-done.19) | copy-start | bytes 786436
  983.2 0.7 copy-start.35
  1046.3 2.1 copy-start.21
  1047.2 2.8 copy-start.16
  1049.6 8.8 slice-start
  1052.2 6.3 slice-start.1
  1053.8 2.5 copy-start.4
  1054.2 4.2 slice-start.2
  1071.0 3.2 copy-start.5

commit v4 on v3

--- a/solution.py
+++ b/solution.py
@@ -1,18 +1,12 @@
-import functools
-import itertools
-
 import jax
 import jax.numpy as jnp
 from jax import lax
-from jax.experimental import pallas as pl
-from jax.experimental.pallas import tpu as pltpu
 from jax.sharding import PartitionSpec as P
 
 BAND = 256
 PANELS = 2
 HIGH = lax.Precision.HIGHEST
 FAST = lax.Precision.HIGH
-MESH_ID = pl.DeviceIdType.MESH
 
 
 def mm(a, b, precision=HIGH):
@@ -27,55 +21,9 @@
     return lax.dot_general(a, b, (((1,), (1,)), ((), ())), precision=precision)
 
 
-def _a2a_kernel(axis, groups, x_ref, o_ref, local_sem, send_sems, recv_sems):
-    me = lax.axis_index(axis)
-    barrier = pltpu.get_barrier_semaphore()
-    for k in range(1, groups):
-        peer = (me + k) % groups
-        pl.semaphore_signal(barrier, 1, device_id={axis: peer}, device_id_type=MESH_ID)
-    pl.semaphore_wait(barrier, groups - 1)
-    local = pltpu.make_async_copy(x_ref.at[me], o_ref.at[me], local_sem)
-    local.start()
-    copies = []
-    for k in range(1, groups):
-        peer = (me + k) % groups
-        copy = pltpu.make_async_remote_copy(
-            src_ref=x_ref.at[peer],
-            dst_ref=o_ref.at[me],
-            send_sem=send_sems.at[k],
-            recv_sem=recv_sems.at[k],
-            device_id={axis: peer},
-            device_id_type=MESH_ID,
-        )
-        copy.start()
-        copies.append(copy)
-    for copy in copies:
-        copy.wait_send()
-    for copy in copies:
-        copy.wait_recv()
-    local.wait()
-
-
 class Comm:
-    def __init__(self):
-        self.ids = itertools.count()
-
     def a2a(self, x, axis):
-        groups = x.shape[0]
-        return pl.pallas_call(
-            functools.partial(_a2a_kernel, axis, groups),
-            out_shape=jax.ShapeDtypeStruct(x.shape, x.dtype),
-            in_specs=[pl.BlockSpec(memory_space=pl.ANY)],
-            out_specs=pl.BlockSpec(memory_space=pl.ANY),
-            scratch_shapes=[
-                pltpu.SemaphoreType.DMA,
-                pltpu.SemaphoreType.DMA((groups,)),
-                pltpu.SemaphoreType.DMA((groups,)),
-            ],
-            compiler_params=pltpu.CompilerParams(
-                collective_id=next(self.ids), has_side_effects=True
-            ),
-        )(x)
+        return lax.all_to_all(x, axis, 0, 0, tiled=False)
 
     def reduce_scatter(self, x, axis, groups):
         parts = self.a2a(x.reshape(groups, x.shape[0] // groups, *x.shape[1:]), axis)
@@ -139,7 +87,9 @@
     top_part = jnp.where(r == 0, colb[lo:lo + BAND, :BAND], 0.0)
     summed = comm.psum(jnp.concatenate([mm_tn(p0, p0), top_part], axis=0), "row", rows)
     gram0, top0 = summed[:BAND], summed[BAND:]
-    strip_t = transpose_exchange(colb, rows, cols)
+    colb_late, summed = lax.optimization_barrier((colb, summed))
+    gram0, top0 = summed[:BAND], summed[BAND:]
+    strip_t = transpose_exchange(colb_late, rows, cols)
 
     stored = []
     current = a

time: 1100 us -> 890 us (0.81)
  Pallas kernels: 586 us -> 0 us
  blocking collectives: 0 us -> 223 us
  waiting for transfers between devices: 0.01 us -> 71.8 us
  starting transfers between devices: 5.68 us -> 73.4 us
  matrix products: 149 us -> 173 us
    pallas_call x14 -> x0, Pallas kernels: 586 us -> none  [a2a(): pl.pallas_call(functools.partial(_a2a_kernel, axis, groups), out_shape=ja...]
    all_to_all x0 -> x3, blocking collectives: none -> 223 us  [a2a(): return lax.all_to_all(x, axis, 0, 0, tiled=False)]
    all_to_all x0 -> x11, waiting for transfers between devices: none -> 71.7 us  [a2a(): return lax.all_to_all(x, axis, 0, 0, tiled=False)]
    all_to_all x0 -> x11, starting transfers between devices: none -> 66.9 us  [a2a(): return lax.all_to_all(x, axis, 0, 0, tiled=False)]
  transfers between devices with their start and end apart: 2 -> 13, of which waited for: 0 -> 6; matrix products, arithmetic and copies ran while one was open for 14% -> 31% of each run, Pallas kernels for 20% -> 0%
where the time goes in v4:
time: 890 us; the launch traced here: 883 us
  other arithmetic  264 us (30%)
  blocking collectives  223 us (25%)
  matrix products  173 us (19%)
  starting transfers between devices  73.4 us (8%)
  waiting for transfers between devices  71.8 us (8%)
  local copies, waits for them, and re-layouts  70.9 us (8%)
    all_to_all x3, blocking collectives, a2a(): return lax.all_to_all(x, axis, 0, 0, tiled=False)  223 us
    dot_general x23, matrix products, mm_nt(): return lax.dot_general(a, b, (((1,), (1,)), ((), ())), precision=precision)  82.5 us
    another operation x14, other arithmetic, small_factors(): low = jnp.linalg.cholesky(gram)  77.9 us
    another operation x14, other arithmetic, small_factors(): second = jnp.linalg.cholesky(mm_nt(shifted, shifted))  76.6 us
    all_to_all x11, waiting for transfers between devices, a2a(): return lax.all_to_all(x, axis, 0, 0, tiled=False)  71.7 us
    all_to_all x11, starting transfers between devices, a2a(): return lax.all_to_all(x, axis, 0, 0, tiled=False)  66.9 us
    another operation x5, other arithmetic, small_factors(): low_inv = jax.scipy.linalg.solve_triangular(low, identity, lower=True)  44 us
    dot_general x11, matrix products, mm_tn(): return lax.dot_general(a, b, (((0,), (0,)), ((), ())), precision=precision)  40.5 us
  transfers between devices with their start and end apart: 13, of which 6 were waited for; matrix products, arithmetic and copies ran while one was open for 31% of the time, Pallas kernels for 0%

profile of v4, /device:TPU:1, one launch (start us, length us, event | category | flops | bytes accessed | tf_op | source)
XLA Modules:
  0.0 883.3 jit_solution(6583890197674926853)
XLA Ops:
  2.3 34.9 %all_to_all.70 = f32[8,144,512]{2,1,0:T(8,128)S(1)} all-to-all(f32[8,144,512]{2,1,0:T(8,128)S(1)} %bitcast.214), channel_id=1, replica_groups=mesh['row'=16,'col'=8] {'col'}, dimensions={0} | all-to-all | bytes 4718592 | tf_op jit(solution)/shard_map/all_to_all | solution.py:26
  38.9 4.6 all-to-all-start.1
  44.1 28.6 %all-to-all-done.1 = f32[8,144,512]{2,1,0:T(8,128)S(1)} async-done(((f32[8,144,512]{2,1,0:T(8,128)}), f32[8,144,512]{2,1,0:T(8,128)S(1)}, u32[]{:S(2)}, u32[]{:S(2)}) %all-to-all-start.1) | async-done | bytes 2359328 | tf_op jit(solution)/shard_map/all_to_all | solution.py:26
  75.9 7.8 all-to-all-start.2
  83.7 10.2 %all-to-all-done.2 = f32[16,32,256]{2,1,0:T(8,128)S(1)} async-done(((f32[16,32,256]{2,1,0:T(8,128)}), f32[16,32,256]{2,1,0:T(8,128)S(1)}, u32[]{:S(2)}, u32[]{:S(2)}) %all-to-all-start.2) | async-done | bytes 524320 | tf_op jit(solution)/shard_map/all_to_all | solution.py:26
  94.7 3.6 all-to-all-start.3
  100.1 7.4 all-to-all-done.3
  107.4 3.4 collective-permute-start
  110.8 3.0 collective-permute-start.1
  119.3 11.7 %cholesky.214 = f32[128,128]{1,0:T(8,128)S(1)} custom-call(f32[128,128]{1,0:T(8,128)S(1)} %cholesky.346), custom_call_target="Cholesky" | custom-call | tf_op jit(solution)/shard_map/jit(cholesky)/cholesky | solution.py:63
  131.6 9.8 %custom-call.17 = f32[1,128,128]{1,2,0:T(8,128)S(1)} custom-call(f32[1,128,128]{2,1,0:T(8,128)S(1)} %get-tuple-element.101), custom_call_target="InvertDiagBlocksLowerTriangular" | custom-call | tf_op jit(solution)/shard_map/jit(cholesky)/cholesky | solution.py:63
  143.6 11.7 %cholesky.231 = f32[128,128]{1,0:T(8,128)S(1)} custom-call(f32[128,128]{1,0:T(8,128)S(1)} %convolution_subtract_fusion.14), custom_call_target="Cholesky" | custom-call | tf_op jit(solution)/shard_map/jit(cholesky)/cholesky | solution.py:63
  160.8 5.5 while.8
  166.3 19.7 %custom-call.18 = f32[2,128,128]{1,2,0:T(8,128)S(1)} custom-call(f32[2,128,128]{2,1,0:T(8,128)S(1)} %get-tuple-element.34), custom_call_target="InvertDiagBlocksLowerTriangular" | custom-call | tf_op jit(solution)/shard_map/jit(_solve_triangular)/triangular_solve | solution.py:64
  189.2 8.4 convolution_bitcast_fusion
  197.6 3.2 broadcast_select_fusion
  205.2 9.7 %fusion.100 = f32[256,1152]{1,0:T(8,128)S(1)} fusion(f32[2304,256]{1,0:T(8,128)S(1)} %convolution_add_fusion.1, f32[1152,2304]{1,0:T(8,128)S(1)} %bitcast.211), kind=kOutput, calls=%fused_computation.207 | convolution fusion | flops 4076863488 | bytes 14155776 | tf_op jit(solution)/shard_map/dot_general | solution.py:13
  219.4 3.3 copy.13
  222.7 149.9 %all_to_all.71 = f32[16,160,256]{2,1,0:T(8,128)} all-to-all(f32[16,160,256]{2,1,0:T(8,128)} %bitcast.223), channel_id=1, replica_groups=mesh['row'=16,'col'=8] {'row'}, dimensions={0} | all-to-all | bytes 5242880 | tf_op jit(solution)/shard_map/all_to_all | solution.py:26
  375.1 2.7 broadcast_in_dim.105
  377.8 4.5 all-to-all-start.5
  387.9 6.2 fusion.22
  394.1 16.5 %all-to-all-done.5 = f32[16,160,256]{2,1,0:T(8,128)} async-done(((f32[16,160,256]{2,1,0:T(8,128)}), f32[16,160,256]{2,1,0:T(8,128)}, u32[]{:S(2)}, u32[]{:S(2)}) %all-to-all-start.5) | async-done | bytes 2621472 | tf_op jit(solution)/shard_map/all_to_all | solution.py:26
  414.9 14.5 %all-to-all-start.6 = ((f32[8,208,256]{2,1,0:T(8,128)}), f32[8,208,256]{2,1,0:T(8,128)S(1)}, u32[]{:S(2)}, u32[]{:S(2)}) async-start(f32[8,208,256]{2,1,0:T(8,128)} %bitcast.224), calls=%async_computation.6 | async-start | bytes 3407872 | tf_op jit(solution)/shard_map/all_to_all | solution.py:26
  430.1 11.7 %cholesky.248 = f32[128,128]{1,0:T(8,128)S(1)} custom-call(f32[128,128]{1,0:T(8,128)S(1)} %cholesky.349), custom_call_target="Cholesky" | custom-call | tf_op jit(solution)/shard_map/jit(cholesky)/cholesky | solution.py:66
  441.9 9.8 %custom-call.19 = f32[1,128,128]{1,2,0:T(8,128)S(1)} custom-call(f32[1,128,128]{2,1,0:T(8,128)S(1)} %get-tuple-element.97), custom_call_target="InvertDiagBlocksLowerTriangular" | custom-call | tf_op jit(solution)/shard_map/jit(cholesky)/cholesky | solution.py:66
  453.9 11.7 %cholesky.265 = f32[128,128]{1,0:T(8,128)S(1)} custom-call(f32[128,128]{1,0:T(8,128)S(1)} %convolution_subtract_fusion.13), custom_call_target="Cholesky" | custom-call | tf_op jit(solution)/shard_map/jit(cholesky)/cholesky | solution.py:66
  469.8 5.4 all-to-all-start.7
  475.2 4.0 while.9
  479.2 19.7 %custom-call.20 = f32[2,128,128]{1,2,0:T(8,128)S(1)} custom-call(f32[2,128,128]{2,1,0:T(8,128)S(1)} %get-tuple-element.35), custom_call_target="InvertDiagBlocksLowerTriangular" | custom-call | tf_op jit(solution)/shard_map/jit(_solve_triangular)/triangular_solve | solution.py:67
  501.7 5.3 fusion.12
  510.0 3.6 fusion.16
  514.1 3.9 fusion.3
  520.2 12.4 %convolution_subtract_fusion.3 = f32[1152,2304]{1,0:T(8,128)} fusion(f32[1152,2304]{1,0:T(8,128)S(1)} %bitcast.213, f32[1152,256]{0,1:T(8,128)S(1)} %convolution_add_fusion.3, f32[2304,256]{1,0:T(8,128)S(1)} %fusion.3), kind=kOutput, calls=%fused_computation.11 | convolution fusion | flops 4079517696 | bytes 24772608 | tf_op jit(solution)/shard_map/dot_general | solution.py:21
  535.3 4.0 fusion.106
  540.2 4.9 all-to-all-start.8
  545.2 3.4 fusion.6
  549.6 9.5 %convolution_subtract_fusion.2 = f32[1152,2304]{1,0:T(8,128)} fusion(f32[1152,2304]{1,0:T(8,128)} %convolution_subtract_fusion.3, f32[1152,256]{1,0:T(8,128)S(1)} %fusion.6, f32[2304,256]{1,0:T(8,128)S(1)} %copy-done.2), kind=kOutput, calls=%fused_computation.10 | convolution fusion | flops 4079517696 | bytes 24772608 | tf_op jit(solution)/shard_map/dot_general | solution.py:21
  561.2 5.3 all-to-all-start.9
  566.5 3.3 convolution_subtract_fusion.6
  572.0 3.6 all-to-all-done.9
  580.5 13.2 %cholesky.282 = f32[128,128]{1,0:T(8,128)} custom-call(f32[128,128]{1,0:T(8,128)} %cholesky.352), custom_call_target="Cholesky" | custom-call | tf_op jit(solution)/shard_map/jit(cholesky)/cholesky | solution.py:63
  596.7 11.3 %custom-call.21 = f32[1,128,128]{1,2,0:T(8,128)} custom-call(f32[1,128,128]{2,1,0:T(8,128)} %get-tuple-element.93), custom_call_target="InvertDiagBlocksLowerTriangular" | custom-call | tf_op jit(solution)/shard_map/jit(cholesky)/cholesky | solution.py:63
  611.4 13.3 %cholesky.299 = f32[128,128]{1,0:T(8,128)} custom-call(f32[128,128]{1,0:T(8,128)} %convolution_subtract_fusion.12), custom_call_target="Cholesky" | custom-call | tf_op jit(solution)/shard_map/jit(cholesky)/cholesky | solution.py:63
  631.1 8.5 while.10
  632.5 2.9 bitcast_dynamic-update-slice_fusion.10
  636.8 2.9 bitcast_dynamic-update-slice_fusion.10
  639.6 21.1 %custom-call.22 = f32[2,128,128]{1,2,0:T(8,128)} custom-call(f32[2,128,128]{2,1,0:T(8,128)} %get-tuple-element.36), custom_call_target="InvertDiagBlocksLowerTriangular" | custom-call | tf_op jit(solution)/shard_map/jit(_solve_triangular)/triangular_solve | solution.py:64
  668.0 12.3 %fusion.107 = f32[2304,256]{1,0:T(8,128)S(1)} fusion(f32[1152,2304]{1,0:T(8,128)} %convolution_subtract_fusion.2, f32[1152,256]{0,1:T(8,128)S(1)} %convolution_add_fusion.2), kind=kOutput, calls=%fused_computation.214 | convolution fusion | flops 4076863488 | bytes 14155776 | tf_op jit(solution)/shard_map/dot_general | solution.py:17
  680.4 4.4 fusion.108
  686.1 38.2 %all_to_all.72 = f32[16,160,256]{2,1,0:T(8,128)} all-to-all(f32[16,160,256]{2,1,0:T(8,128)S(1)} %bitcast.222), channel_id=1, replica_groups=mesh['row'=16,'col'=8] {'row'}, dimensions={0} | all-to-all | bytes 5242880 | tf_op jit(solution)/shard_map/all_to_all | solution.py:26
  726.9 2.7 broadcast_in_dim.110
  729.6 4.9 all-to-all-start.11
  742.0 13.2 %cholesky.316 = f32[128,128]{1,0:T(8,128)} custom-call(f32[128,128]{1,0:T(8,128)} %cholesky.355), custom_call_target="Cholesky" | custom-call | tf_op jit(solution)/shard_map/jit(cholesky)/cholesky | solution.py:66
  758.2 11.3 %custom-call.23 = f32[1,128,128]{1,2,0:T(8,128)} custom-call(f32[1,128,128]{2,1,0:T(8,128)} %get-tuple-element.89), custom_call_target="InvertDiagBlocksLowerTriangular" | custom-call | tf_op jit(solution)/shard_map/jit(cholesky)/cholesky | solution.py:66
  772.9 13.2 %cholesky.333 = f32[128,128]{1,0:T(8,128)} custom-call(f32[128,128]{1,0:T(8,128)} %convolution_subtract_fusion.11), custom_call_target="Cholesky" | custom-call | tf_op jit(solution)/shard_map/jit(cholesky)/cholesky | solution.py:66
  790.6 6.8 all-to-all-start.12
  799.4 4.1 while.11
  803.6 20.3 %custom-call.24 = f32[2,128,128]{1,2,0:T(8,128)} custom-call(f32[2,128,128]{2,1,0:T(8,128)S(1)} %get-tuple-element.37), custom_call_target="InvertDiagBlocksLowerTriangular" | custom-call | tf_op jit(solution)/shard_map/jit(_solve_triangular)/triangular_solve | solution.py:67
  829.9 4.8 all-to-all-start.13
  844.9 3.7 fusion.10
  848.6 5.5 all-to-all-done.13
  862.6 12.8 %convolution_subtract_fusion.1 = f32[1152,2304]{1,0:T(8,128)S(1)} fusion(f32[1152,2304]{1,0:T(8,128)} %convolution_subtract_fusion.2, f32[1152,256]{0,1:T(8,128)S(1)} %convolution_add_fusion.2, f32[2304,256]{1,0:T(8,128)S(1)} %fusion), kind=kOutput, calls=%fused_computation.9 | convolution fusion | flops 4079517696 | bytes 24772608 | tf_op jit(solution)/shard_map/dot_general | solution.py:21
  875.4 7.6 convolution_subtract_fusion
  (280 shorter events, 156.7 us)
Async XLA Ops:
  0.6 1.7 slice-start.9
  38.9 33.7 %all-to-all-start.1 = ((f32[8,144,512]{2,1,0:T(8,128)}), f32[8,144,512]{2,1,0:T(8,128)S(1)}, u32[]{:S(2)}, u32[]{:S(2)}) async-start(f32[8,144,512]{2,1,0:T(8,128)} %broadcast_in_dim.99), calls=%async_computation.1 | async-start | bytes 4718592 | tf_op jit(solution)/shard_map/all_to_all | solution.py:26
  72.7 114.3 %copy-start.11 = (f32[8,144,512]{2,1,0:T(8,128)}, f32[8,144,512]{2,1,0:T(8,128)S(1)}, u32[]{:S(2)}) copy-start(f32[8,144,512]{2,1,0:T(8,128)S(1)} %all-to-all-done.1) | copy-start | bytes 7077892
  75.9 17.9 %all-to-all-start.2 = ((f32[16,32,256]{2,1,0:T(8,128)}), f32[16,32,256]{2,1,0:T(8,128)S(1)}, u32[]{:S(2)}, u32[]{:S(2)}) async-start(f32[16,32,256]{2,1,0:T(8,128)} %bitcast.3), calls=%async_computation.2 | async-start | bytes 1048576 | tf_op jit(solution)/shard_map/all_to_all | solution.py:26
  94.7 12.7 %all-to-all-start.3 = ((f32[16,32,256]{2,1,0:T(8,128)}), f32[16,32,256]{2,1,0:T(8,128)S(1)}, u32[]{:S(2)}, u32[]{:S(2)}) async-start(f32[16,32,256]{2,1,0:T(8,128)} %broadcast_in_dim.102), calls=%async_computation.3 | async-start | bytes 1048576 | tf_op jit(solution)/shard_map/all_to_all | solution.py:26
  100.1 86.3 %copy-start.24 = (f32[256,256]{1,0:T(8,128)}, f32[256,256]{1,0:T(8,128)S(1)}, u32[]{:S(2)}) copy-start(f32[256,256]{1,0:T(8,128)S(1)} %fusion.46) | copy-start | bytes 786436
  107.4 53.4 %copy-start.30 = (f32[16,32,256]{2,1,0:T(8,128)}, f32[16,32,256]{2,1,0:T(8,128)S(1)}, u32[]{:S(2)}) copy-start(f32[16,32,256]{2,1,0:T(8,128)S(1)} %all-to-all-done.3) | copy-start | bytes 1572868
  107.4 90.2 %collective-permute-start = (f32[1152,512]{1,0:T(8,128)S(1)}, f32[1152,512]{1,0:T(8,128)}, u32[]{:S(2)}, u32[]{:S(2)}) collective-permute-start(f32[1152,512]{1,0:T(8,128)S(1)} %bitcast.217), channel_id=1, source_target_pairs={{0,8},{1,24},{2,40},{3,56},{4,72},{5,88},{6,104},{7,120},{8,0},{9,... | collective-permute-start | bytes 7077896 | tf_op jit(solution)/shard_map/ppermute | solution.py:54
  110.8 86.8 %collective-permute-start.1 = (f32[1152,512]{1,0:T(8,128)S(1)}, f32[1152,512]{1,0:T(8,128)}, u32[]{:S(2)}, u32[]{:S(2)}) collective-permute-start(f32[1152,512]{1,0:T(8,128)S(1)} %bitcast.218), channel_id=1, source_target_pairs={{0,0},{1,16},{2,32},{3,48},{4,64},{5,80},{6,96},{7,112},{8,8},{9,2... | collective-permute-start | bytes 7077896 | tf_op jit(solution)/shard_map/ppermute | solution.py:53
  155.3 3.2 copy-start.41
  186.3 14.6 %copy-start.29 = (f32[128,256]{1,0:T(8,128)}, f32[128,256]{1,0:T(8,128)S(1)}, u32[]{:S(2)}) copy-start(f32[128,256]{1,0:T(8,128)S(1)} %fusion.53) | copy-start | bytes 393220
  186.9 14.0 %copy-start.36 = (f32[128,256]{1,0:T(8,128)}, f32[128,256]{1,0:T(8,128)S(1)}, u32[]{:S(2)}) copy-start(f32[128,256]{1,0:T(8,128)S(1)} %fusion.68) | copy-start | bytes 393220
  189.1 16.1 %slice-start.3 = ((s8[10616832]{0:T(1024)(128)(4,1)}), s8[4194304]{0:T(1024)(128)(4,1)S(1)}, s32[]{:S(2)}) async-start(s8[10616832]{0:T(1024)(128)(4,1)} %bitcast.210), calls=%async_computation.17 | async-start | bytes 8388608
  189.1 16.1 %slice-start.4 = ((s8[10616832]{0:T(1024)(128)(4,1)}), s8[4194304]{0:T(1024)(128)(4,1)S(1)}, s32[]{:S(2)}) async-start(s8[10616832]{0:T(1024)(128)(4,1)} %bitcast.210), calls=%async_computation.18 | async-start | bytes 8388608
  197.6 5.5 copy-start.47
  197.6 7.6 slice-start.5
  200.9 1.4 copy-start.7
  200.9 2.2 copy-start.9
  205.2 182.7 %copy-start = (f32[2304,256]{1,0:T(8,128)}, f32[2304,256]{1,0:T(8,128)S(1)}, u32[]{:S(2)}) copy-start(f32[2304,256]{1,0:T(8,128)S(1)} %convolution_add_fusion.1) | copy-start | bytes 7077892
  377.8 32.9 %all-to-all-start.5 = ((f32[16,160,256]{2,1,0:T(8,128)}), f32[16,160,256]{2,1,0:T(8,128)}, u32[]{:S(2)}, u32[]{:S(2)}) async-start(f32[16,160,256]{2,1,0:T(8,128)} %broadcast_in_dim.105), calls=%async_computation.5 | async-start | bytes 5242880 | tf_op jit(solution)/shard_map/all_to_all | solution.py:26
  414.9 14.5 %copy-start.32 = (f32[256,256]{1,0:T(8,128)S(1)}, f32[256,256]{1,0:T(8,128)}, u32[]{:S(2)}) copy-start(f32[256,256]{1,0:T(8,128)} %fusion.102) | copy-start | bytes 786436
  414.9 14.5 %copy-start.39 = (f32[256,256]{0,1:T(8,128)S(1)}, f32[256,256]{0,1:T(8,128)}, u32[]{:S(2)}) copy-start(f32[256,256]{0,1:T(8,128)} %copy.14) | copy-start | bytes 786436
  414.9 53.4 %all-to-all-start.6 = ((f32[8,208,256]{2,1,0:T(8,128)}), f32[8,208,256]{2,1,0:T(8,128)S(1)}, u32[]{:S(2)}, u32[]{:S(2)}) async-start(f32[8,208,256]{2,1,0:T(8,128)} %bitcast.224), calls=%async_computation.6 | async-start | bytes 3407872 | tf_op jit(solution)/shard_map/all_to_all | solution.py:26
  468.4 6.8 copy-start.49
  469.8 29.1 %copy-start.25 = (f32[256,256]{1,0:T(8,128)S(1)}, f32[256,256]{1,0:T(8,128)}, u32[]{:S(2)}) copy-start(f32[256,256]{1,0:T(8,128)} %copy-done.24) | copy-start | bytes 786436
  469.8 30.6 %copy-start.13 = (f32[256,256]{1,0:T(8,128)S(1)}, f32[256,256]{1,0:T(8,128)}, u32[]{:S(2)}) copy-start(f32[256,256]{1,0:T(8,128)} %copy-done.12) | copy-start | bytes 786436
  469.8 37.2 %all-to-all-start.7 = ((f32[8,208,256]{2,1,0:T(8,128)}), f32[8,208,256]{2,1,0:T(8,128)}, u32[]{:S(2)}, u32[]{:S(2)}) async-start(f32[8,208,256]{2,1,0:T(8,128)} %broadcast_in_dim.106), calls=%async_computation.7 | async-start | bytes 3407872 | tf_op jit(solution)/shard_map/all_to_all | solution.py:26
  501.7 18.5 %slice-start.6 = ((s8[10616832]{0:T(1024)(128)(4,1)}), s8[2228224]{0:T(1024)(128)(4,1)S(1)}, s32[]{:S(2)}) async-start(s8[10616832]{0:T(1024)(128)(4,1)} %bitcast.212), calls=%async_computation.20 | async-start | bytes 4456448
  506.9 6.7 copy-start.20
  506.9 7.1 copy-start.1
  510.0 10.2 %slice-start.7 = ((s8[10616832]{0:T(1024)(128)(4,1)}), s8[4194304]{0:T(1024)(128)(4,1)S(1)}, s32[]{:S(2)}) async-start(s8[10616832]{0:T(1024)(128)(4,1)} %bitcast.212), calls=%async_computation.21 | async-start | bytes 8388608
  514.0 18.6 %copy-start.28 = (f32[256,256]{1,0:T(8,128)}, f32[256,256]{1,0:T(8,128)S(1)}, u32[]{:S(2)}) copy-start(f32[256,256]{1,0:T(8,128)S(1)} %fusion.104) | copy-start | bytes 786436
  514.0 4.0 copy-start.14
  514.1 6.1 slice-start.8
  520.2 12.8 %copy-start.8 = (f32[1152,512]{1,0:T(8,128)S(1)}, f32[1152,512]{1,0:T(8,128)}, u32[]{:S(2)}) copy-start(f32[1152,512]{1,0:T(8,128)} %copy-done.7) | copy-start | bytes 7077892
  520.2 12.8 %copy-start.10 = (f32[1152,512]{1,0:T(8,128)S(1)}, f32[1152,512]{1,0:T(8,128)}, u32[]{:S(2)}) copy-start(f32[1152,512]{1,0:T(8,128)} %copy-done.9) | copy-start | bytes 7077892
  533.0 2.2 copy-start.34
  535.3 4.1 copy-start.3
  540.2 9.4 %copy-start.2 = (f32[2304,256]{1,0:T(8,128)S(1)}, f32[2304,256]{1,0:T(8,128)}, u32[]{:S(2)}) copy-start(f32[2304,256]{1,0:T(8,128)} %copy-done) | copy-start | bytes 7077892
  540.2 19.0 %all-to-all-start.8 = ((f32[8,64,256]{2,1,0:T(8,128)}), f32[8,64,256]{2,1,0:T(8,128)}, u32[]{:S(2)}, u32[]{:S(2)}) async-start(f32[8,64,256]{2,1,0:T(8,128)} %bitcast.229), calls=%async_computation.8 | async-start | bytes 1048576 | tf_op jit(solution)/shard_map/all_to_all | solution.py:26
  548.6 1.1 copy-start.17
  559.2 7.3 copy-start.35
  561.1 8.6 copy-start.15
  561.1 8.6 copy-start.18
  561.2 8.6 copy-start.48
  561.2 14.4 %all-to-all-start.9 = ((f32[8,64,256]{2,1,0:T(8,128)}), f32[8,64,256]{2,1,0:T(8,128)S(1)}, u32[]{:S(2)}, u32[]{:S(2)}) async-start(f32[8,64,256]{2,1,0:T(8,128)} %broadcast_in_dim.109), calls=%async_computation.9 | async-start | bytes 1048576 | tf_op jit(solution)/shard_map/all_to_all | solution.py:26
  577.9 86.5 %copy-start.4 = (f32[2304,256]{1,0:T(8,128)S(1)}, f32[2304,256]{1,0:T(8,128)}, u32[]{:S(2)}) copy-start(f32[2304,256]{1,0:T(8,128)} %copy-done.3) | copy-start | bytes 7077892
  662.0 4.6 copy-start.31
  664.4 2.2 copy-start.37
  664.4 2.2 copy-start.26
  664.5 2.2 copy-start.46
  666.6 13.7 %copy-start.5 = (f32[2304,256]{1,0:T(8,128)}, f32[2304,256]{1,0:T(8,128)S(1)}, u32[]{:S(2)}) copy-start(f32[2304,256]{1,0:T(8,128)S(1)} %convolution_add_fusion) | copy-start | bytes 7077892
  666.6 13.7 %slice-start = ((s8[10616832]{0:T(1024)(128)(4,1)}), s8[4194304]{0:T(1024)(128)(4,1)S(1)}, s32[]{:S(2)}) async-start(s8[10616832]{0:T(1024)(128)(4,1)} %bitcast.208), calls=%async_computation.14 | async-start | bytes 8388608
  668.0 12.4 %slice-start.1 = ((s8[10616832]{0:T(1024)(128)(4,1)}), s8[4194304]{0:T(1024)(128)(4,1)S(1)}, s32[]{:S(2)}) async-start(s8[10616832]{0:T(1024)(128)(4,1)} %bitcast.208), calls=%async_computation.15 | async-start | bytes 8388608
  668.0 12.4 %slice-start.2 = ((s8[10616832]{0:T(1024)(128)(4,1)}), s8[2228224]{0:T(1024)(128)(4,1)S(1)}, s32[]{:S(2)}) async-start(s8[10616832]{0:T(1024)(128)(4,1)} %bitcast.208), calls=%async_computation.16 | async-start | bytes 4456448
  729.6 58.7 %all-to-all-start.11 = ((f32[16,160,256]{2,1,0:T(8,128)}), f32[16,160,256]{2,1,0:T(8,128)}, u32[]{:S(2)}, u32[]{:S(2)}) async-start(f32[16,160,256]{2,1,0:T(8,128)} %broadcast_in_dim.110), calls=%async_computation.11 | async-start | bytes 5242880 | tf_op jit(solution)/shard_map/all_to_all | solution.py:26
  790.6 8.8 copy-start.40
  790.6 8.8 %copy-start.50 = (s32[2,2]{1,0:T(2,128)S(1)}, s32[2,2]{1,0:T(2,128)}, u32[]{:S(2)}) copy-start(s32[2,2]{1,0:T(2,128)} %get-tuple-element.319) | copy-start | bytes 52
  790.6 34.8 %all-to-all-start.12 = ((f32[8,176,256]{2,1,0:T(8,128)}), f32[8,176,256]{2,1,0:T(8,128)}, u32[]{:S(2)}, u32[]{:S(2)}) async-start(f32[8,176,256]{2,1,0:T(8,128)} %bitcast.225), calls=%async_computation.12 | async-start | bytes 2883584 | tf_op jit(solution)/shard_map/all_to_all | solution.py:26
  803.5 21.9 %copy-start.38 = (f32[256,256]{1,0:T(8,128)}, f32[256,256]{1,0:T(8,128)S(1)}, u32[]{:S(2)}) copy-start(f32[256,256]{1,0:T(8,128)S(1)} %get-tuple-element.313) | copy-start | bytes 786436
  827.5 9.1 %copy-start.21 = (f32[1152,512]{0,1:T(8,128)S(1)}, f32[1152,512]{0,1:T(8,128)}, u32[]{:S(2)}) copy-start(f32[1152,512]{0,1:T(8,128)} %pad_maximum_fusion.3) | copy-start | bytes 7077892
  829.9 24.2 %all-to-all-start.13 = ((f32[8,176,256]{2,1,0:T(8,128)}), f32[8,176,256]{2,1,0:T(8,128)}, u32[]{:S(2)}, u32[]{:S(2)}) async-start(f32[8,176,256]{2,1,0:T(8,128)} %broadcast_in_dim.111), calls=%async_computation.13 | async-start | bytes 2883584 | tf_op jit(solution)/shard_map/all_to_all | solution.py:26
  854.2 2.5 copy-start.23
  858.0 2.5 copy-start.6
  (10 other events, 7.4 us)

commit v5 on v4

--- a/solution.py
+++ b/solution.py
@@ -81,15 +81,14 @@
     band_idx = jnp.arange(BAND, dtype=jnp.int32)
     width = PANELS * BAND
 
+    strip = lax.psum(jnp.where(r == 0, a[:width, :], 0.0), "row")
     colb = comm.broadcast(a[:, :width], "col", cols, 0)
     lo = BAND
     p0 = jnp.where(row_pos[:, None] >= lo, colb[:, :BAND], 0.0)
     top_part = jnp.where(r == 0, colb[lo:lo + BAND, :BAND], 0.0)
     summed = comm.psum(jnp.concatenate([mm_tn(p0, p0), top_part], axis=0), "row", rows)
     gram0, top0 = summed[:BAND], summed[BAND:]
-    colb_late, summed = lax.optimization_barrier((colb, summed))
-    gram0, top0 = summed[:BAND], summed[BAND:]
-    strip_t = transpose_exchange(colb_late, rows, cols)
+    strip_t = strip.T
 
     stored = []
     current = a

time: 890 us -> 810 us (0.910)
  blocking collectives: 223 us -> 110 us
  between operations: 7.3 us -> 20.5 us
  other arithmetic: 264 us -> 277 us
  local copies, waits for them, and re-layouts: 70.9 us -> 83.6 us
  starting transfers between devices: 73.4 us -> 63.6 us
    all_to_all x3, blocking collectives: 223 us -> 110 us  [a2a(): return lax.all_to_all(x, axis, 0, 0, tiled=False)]
  transfers between devices with their start and end apart: 13 -> 12, of which waited for: 6 -> 7; matrix products, arithmetic and copies ran while one was open for 31% -> 37% of each run, Pallas kernels for 0% -> 0%
where the time goes in v5:
time: 810 us; the launch traced here: 801 us
  other arithmetic  277 us (34%)
  matrix products  180 us (22%)
  blocking collectives  110 us (14%)
  local copies, waits for them, and re-layouts  83.6 us (10%)
  waiting for transfers between devices  66.1 us (8%)
  starting transfers between devices  63.6 us (8%)
  between operations  20.5 us (3%)
    all_to_all x3, blocking collectives, a2a(): return lax.all_to_all(x, axis, 0, 0, tiled=False)  110 us
    dot_general x23, matrix products, mm_nt(): return lax.dot_general(a, b, (((1,), (1,)), ((), ())), precision=precision)  88.5 us
    another operation x14, other arithmetic, small_factors(): second = jnp.linalg.cholesky(mm_nt(shifted, shifted))  85 us
    another operation x14, other arithmetic, small_factors(): low = jnp.linalg.cholesky(gram)  76.7 us
    all_to_all x11, waiting for transfers between devices, a2a(): return lax.all_to_all(x, axis, 0, 0, tiled=False)  64.5 us
    all_to_all x11, starting transfers between devices, a2a(): return lax.all_to_all(x, axis, 0, 0, tiled=False)  63.6 us
    another operation x4, other arithmetic, small_factors(): second_inv = jax.scipy.linalg.solve_triangular(second, identity, lower=True)  43.1 us
    another operation x5, other arithmetic, small_factors(): low_inv = jax.scipy.linalg.solve_triangular(low, identity, lower=True)  43 us
  transfers between devices with their start and end apart: 12, of which 7 were waited for; matrix products, arithmetic and copies ran while one was open for 37% of the time, Pallas kernels for 0%

profile of v5, /device:TPU:1, one launch (start us, length us, event | category | flops | bytes accessed | tf_op | source)
XLA Modules:
  0.0 801.4 jit_solution(16823833681085017727)
XLA Ops:
  8.8 34.9 %all_to_all.70 = f32[8,144,512]{2,1,0:T(8,128)S(1)} all-to-all(f32[8,144,512]{2,1,0:T(8,128)S(1)} %bitcast.217), channel_id=1, replica_groups=mesh['row'=16,'col'=8] {'col'}, dimensions={0} | all-to-all | bytes 4718592 | tf_op jit(solution)/shard_map/all_to_all | solution.py:26
  45.5 4.6 all-to-all-start.1
  50.0 4.8 slice.118
  54.9 6.1 copy.24
  60.9 5.1 select_bitcast_fusion
  66.6 12.6 %all-to-all-done.1 = f32[8,144,512]{2,1,0:T(8,128)S(1)} async-done(((f32[8,144,512]{2,1,0:T(8,128)}), f32[8,144,512]{2,1,0:T(8,128)S(1)}, u32[]{:S(2)}, u32[]{:S(2)}) %all-to-all-start.1) | async-done | bytes 2359328 | tf_op jit(solution)/shard_map/all_to_all | solution.py:26
  82.4 7.8 all-to-all-start.2
  90.2 12.8 %all-to-all-done.2 = f32[16,32,256]{2,1,0:T(8,128)S(1)} async-done(((f32[16,32,256]{2,1,0:T(8,128)}), f32[16,32,256]{2,1,0:T(8,128)S(1)}, u32[]{:S(2)}, u32[]{:S(2)}) %all-to-all-start.2) | async-done | bytes 524320 | tf_op jit(solution)/shard_map/all_to_all | solution.py:26
  103.9 4.6 all-to-all-start.3
  108.7 10.8 %all-to-all-done.3 = f32[16,32,256]{2,1,0:T(8,128)S(1)} async-done(((f32[16,32,256]{2,1,0:T(8,128)}), f32[16,32,256]{2,1,0:T(8,128)S(1)}, u32[]{:S(2)}, u32[]{:S(2)}) %all-to-all-start.3) | async-done | bytes 524320 | tf_op jit(solution)/shard_map/all_to_all | solution.py:26
  120.4 11.7 %cholesky.214 = f32[128,128]{1,0:T(8,128)S(1)} custom-call(f32[128,128]{1,0:T(8,128)S(1)} %cholesky.346), custom_call_target="Cholesky" | custom-call | tf_op jit(solution)/shard_map/jit(cholesky)/cholesky | solution.py:63
  132.2 9.8 %custom-call.17 = f32[1,128,128]{1,2,0:T(8,128)S(1)} custom-call(f32[1,128,128]{2,1,0:T(8,128)S(1)} %get-tuple-element.97), custom_call_target="InvertDiagBlocksLowerTriangular" | custom-call | tf_op jit(solution)/shard_map/jit(cholesky)/cholesky | solution.py:63
  142.5 11.7 %cholesky.231 = f32[128,128]{1,0:T(8,128)S(1)} custom-call(f32[128,128]{1,0:T(8,128)S(1)} %convolution_subtract_fusion.15), custom_call_target="Cholesky" | custom-call | tf_op jit(solution)/shard_map/jit(cholesky)/cholesky | solution.py:63
  156.9 3.9 while.8
  160.8 20.2 %custom-call.18 = f32[2,128,128]{1,2,0:T(8,128)S(1)} custom-call(f32[2,128,128]{2,1,0:T(8,128)S(1)} %get-tuple-element.30), custom_call_target="InvertDiagBlocksLowerTriangular" | custom-call | tf_op jit(solution)/shard_map/jit(_solve_triangular)/triangular_solve | solution.py:64
  183.5 4.5 convolution_add_fusion.1
  188.1 12.3 %fusion.96 = f32[256,1152]{1,0:T(8,128)S(1)} fusion(f32[2304,256]{1,0:T(8,128)S(1)} %convolution_add_fusion.1, f32[1152,2304]{1,0:T(8,128)} %param.4), kind=kOutput, calls=%fused_computation.202 | convolution fusion | flops 4076863488 | bytes 14155776 | tf_op jit(solution)/shard_map/dot_general | solution.py:13
  203.1 6.0 convolution_bitcast_fusion
  212.1 3.2 copy.14
  215.3 38.5 %all_to_all.71 = f32[16,160,256]{2,1,0:T(8,128)} all-to-all(f32[16,160,256]{2,1,0:T(8,128)} %bitcast.226), channel_id=1, replica_groups=mesh['row'=16,'col'=8] {'row'}, dimensions={0} | all-to-all | bytes 5242880 | tf_op jit(solution)/shard_map/all_to_all | solution.py:26
  259.0 4.7 all-to-all-start.5
  269.4 6.2 fusion.10
  275.6 18.9 %all-to-all-done.5 = f32[16,160,256]{2,1,0:T(8,128)} async-done(((f32[16,160,256]{2,1,0:T(8,128)}), f32[16,160,256]{2,1,0:T(8,128)}, u32[]{:S(2)}, u32[]{:S(2)}) %all-to-all-start.5) | async-done | bytes 2621472 | tf_op jit(solution)/shard_map/all_to_all | solution.py:26
  303.4 10.7 %all-to-all-start.6 = ((f32[8,208,256]{2,1,0:T(8,128)}), f32[8,208,256]{2,1,0:T(8,128)}, u32[]{:S(2)}, u32[]{:S(2)}) async-start(f32[8,208,256]{2,1,0:T(8,128)} %bitcast.227), calls=%async_computation.6 | async-start | bytes 3407872 | tf_op jit(solution)/shard_map/all_to_all | solution.py:26
  316.5 13.2 %cholesky.248 = f32[128,128]{1,0:T(8,128)} custom-call(f32[128,128]{1,0:T(8,128)} %cholesky.349), custom_call_target="Cholesky" | custom-call | tf_op jit(solution)/shard_map/jit(cholesky)/cholesky | solution.py:66
  333.3 11.3 %custom-call.19 = f32[1,128,128]{1,2,0:T(8,128)} custom-call(f32[1,128,128]{2,1,0:T(8,128)} %get-tuple-element.93), custom_call_target="InvertDiagBlocksLowerTriangular" | custom-call | tf_op jit(solution)/shard_map/jit(cholesky)/cholesky | solution.py:66
  348.0 13.2 %cholesky.265 = f32[128,128]{1,0:T(8,128)} custom-call(f32[128,128]{1,0:T(8,128)} %convolution_subtract_fusion.14), custom_call_target="Cholesky" | custom-call | tf_op jit(solution)/shard_map/jit(cholesky)/cholesky | solution.py:66
  372.0 5.0 all-to-all-start.7
  377.7 8.4 %while.9 = (s32[]{:T(128)}, f32[256,256]{1,0:T(8,128)}, s32[2,2]{1,0:T(2,128)}, f32[2,128,128]{2,1,0:T(8,128)}, s32[]{:T(128)}) while((s32[]{:T(128)}, f32[256,256]{1,0:T(8,128)}, s32[2,2]{1,0:T(2,128)}, f32[2,128,128]{2,1,0:T(8,128)}, s32[]{:T(128)}) %tuple.99), condition=%wide.while_cond.clone, body=%wide.while_body.clone.sunk | while | flops 2 | bytes 132705 | solution.py:67
  379.1 2.9 bitcast_dynamic-update-slice_fusion.9
  383.3 2.9 bitcast_dynamic-update-slice_fusion.9
  386.2 21.1 %custom-call.20 = f32[2,128,128]{1,2,0:T(8,128)} custom-call(f32[2,128,128]{2,1,0:T(8,128)} %get-tuple-element.31), custom_call_target="InvertDiagBlocksLowerTriangular" | custom-call | tf_op jit(solution)/shard_map/jit(_solve_triangular)/triangular_solve | solution.py:67
  413.7 5.1 fusion.8
  421.8 3.6 fusion.14
  428.8 14.8 %convolution_subtract_fusion.3 = f32[1152,2304]{1,0:T(8,128)} fusion(f32[1152,2304]{1,0:T(8,128)} %param.4, f32[1152,256]{0,1:T(8,128)S(1)} %convolution_add_fusion.3, f32[2304,256]{1,0:T(8,128)S(1)} %fusion.2), kind=kOutput, calls=%fused_computation.11 | convolution fusion | flops 4079517696 | bytes 24772608 | tf_op jit(solution)/shard_map/dot_general | solution.py:21
  445.7 3.1 fusion.1
  448.8 4.1 fusion.101
  453.8 4.8 all-to-all-start.8
  458.6 3.4 fusion.5
  463.1 9.5 %convolution_subtract_fusion.2 = f32[1152,2304]{1,0:T(8,128)} fusion(f32[1152,2304]{1,0:T(8,128)} %convolution_subtract_fusion.3, f32[1152,256]{1,0:T(8,128)S(1)} %fusion.5, f32[2304,256]{1,0:T(8,128)S(1)} %convolution_add_fusion.1), kind=kOutput, calls=%fused_computation.10 | convolution fusion | flops 4079517696 | bytes 24772608 | tf_op jit(solution)/shard_map/dot_general | solution.py:21
  474.6 5.1 all-to-all-start.9
  479.7 3.3 convolution_subtract_fusion.7
  485.2 3.9 all-to-all-done.9
  493.9 13.2 %cholesky.282 = f32[128,128]{1,0:T(8,128)} custom-call(f32[128,128]{1,0:T(8,128)} %cholesky.352), custom_call_target="Cholesky" | custom-call | tf_op jit(solution)/shard_map/jit(cholesky)/cholesky | solution.py:63
  510.1 11.3 %custom-call.21 = f32[1,128,128]{1,2,0:T(8,128)} custom-call(f32[1,128,128]{2,1,0:T(8,128)} %get-tuple-element.89), custom_call_target="InvertDiagBlocksLowerTriangular" | custom-call | tf_op jit(solution)/shard_map/jit(cholesky)/cholesky | solution.py:63
  524.8 13.4 %cholesky.299 = f32[128,128]{1,0:T(8,128)} custom-call(f32[128,128]{1,0:T(8,128)} %convolution_subtract_fusion.13), custom_call_target="Cholesky" | custom-call | tf_op jit(solution)/shard_map/jit(cholesky)/cholesky | solution.py:63
  544.4 8.2 %while.10 = (s32[]{:T(128)}, f32[256,256]{1,0:T(8,128)}, s32[2,2]{1,0:T(2,128)}, f32[2,128,128]{2,1,0:T(8,128)}, s32[]{:T(128)}) while((s32[]{:T(128)}, f32[256,256]{1,0:T(8,128)}, s32[2,2]{1,0:T(2,128)}, f32[2,128,128]{2,1,0:T(8,128)}, s32[]{:T(128)}) %tuple.100), condition=%wide.while_cond.clone.1, body=%wide.while_body.clone.1.sunk | while | flops 2 | bytes 132705 | solution.py:64
  545.7 2.8 bitcast_dynamic-update-slice_fusion.10
  552.6 21.1 %custom-call.22 = f32[2,128,128]{1,2,0:T(8,128)} custom-call(f32[2,128,128]{2,1,0:T(8,128)} %get-tuple-element.32), custom_call_target="InvertDiagBlocksLowerTriangular" | custom-call | tf_op jit(solution)/shard_map/jit(_solve_triangular)/triangular_solve | solution.py:64
  581.0 12.5 %fusion.102 = f32[2304,256]{1,0:T(8,128)S(1)} fusion(f32[1152,2304]{1,0:T(8,128)} %convolution_subtract_fusion.2, f32[1152,256]{0,1:T(8,128)S(1)} %convolution_add_fusion.2), kind=kOutput, calls=%fused_computation.208 | convolution fusion | flops 4076863488 | bytes 14155776 | tf_op jit(solution)/shard_map/dot_general | solution.py:17
  593.5 4.4 fusion.103
  599.3 36.5 %all_to_all.72 = f32[16,160,256]{2,1,0:T(8,128)} all-to-all(f32[16,160,256]{2,1,0:T(8,128)S(1)} %bitcast.225), channel_id=1, replica_groups=mesh['row'=16,'col'=8] {'row'}, dimensions={0} | all-to-all | bytes 5242880 | tf_op jit(solution)/shard_map/all_to_all | solution.py:26
  641.0 4.6 all-to-all-start.11
  653.1 13.2 %cholesky.316 = f32[128,128]{1,0:T(8,128)} custom-call(f32[128,128]{1,0:T(8,128)} %cholesky.355), custom_call_target="Cholesky" | custom-call | tf_op jit(solution)/shard_map/jit(cholesky)/cholesky | solution.py:66
  669.4 11.3 %custom-call.23 = f32[1,128,128]{1,2,0:T(8,128)} custom-call(f32[1,128,128]{2,1,0:T(8,128)} %get-tuple-element.85), custom_call_target="InvertDiagBlocksLowerTriangular" | custom-call | tf_op jit(solution)/shard_map/jit(cholesky)/cholesky | solution.py:66
  684.1 13.2 %cholesky.333 = f32[128,128]{1,0:T(8,128)} custom-call(f32[128,128]{1,0:T(8,128)} %convolution_subtract_fusion.12), custom_call_target="Cholesky" | custom-call | tf_op jit(solution)/shard_map/jit(cholesky)/cholesky | solution.py:66
  701.7 6.8 all-to-all-start.12
  710.5 4.0 while.11
  714.5 20.3 %custom-call.24 = f32[2,128,128]{1,2,0:T(8,128)} custom-call(f32[2,128,128]{2,1,0:T(8,128)S(1)} %get-tuple-element.33), custom_call_target="InvertDiagBlocksLowerTriangular" | custom-call | tf_op jit(solution)/shard_map/jit(_solve_triangular)/triangular_solve | solution.py:67
  740.9 4.8 all-to-all-start.13
  755.8 3.7 fusion.6
  759.5 5.6 all-to-all-done.13
  773.6 12.9 %convolution_subtract_fusion.1 = f32[1152,2304]{1,0:T(8,128)S(1)} fusion(f32[1152,2304]{1,0:T(8,128)} %convolution_subtract_fusion.2, f32[1152,256]{0,1:T(8,128)S(1)} %convolution_add_fusion.2, f32[2304,256]{1,0:T(8,128)S(1)} %fusion), kind=kOutput, calls=%fused_computation.9 | convolution fusion | flops 4079517696 | bytes 24772608 | tf_op jit(solution)/shard_map/dot_general | solution.py:21
  786.4 7.6 convolution_subtract_fusion
  (252 shorter events, 169.1 us)
Async XLA Ops:
  7.2 1.7 slice-start.6
  45.5 33.7 %all-to-all-start.1 = ((f32[8,144,512]{2,1,0:T(8,128)}), f32[8,144,512]{2,1,0:T(8,128)S(1)}, u32[]{:S(2)}, u32[]{:S(2)}) async-start(f32[8,144,512]{2,1,0:T(8,128)} %broadcast_in_dim.103), calls=%async_computation.1 | async-start | bytes 4718592 | tf_op jit(solution)/shard_map/all_to_all | solution.py:26
  50.0 133.5 %all-reduce.3.cloned.1.call-start = ((), (), s32[]{:S(2)}) async-start(), calls=%async_computation.14 | async-start | bytes 9437184 | tf_op jit(solution)/shard_map/psum | solution.py:84
  79.2 24.7 %copy-start.4 = (f32[8,144,512]{2,1,0:T(8,128)}, f32[8,144,512]{2,1,0:T(8,128)S(1)}, u32[]{:S(2)}) copy-start(f32[8,144,512]{2,1,0:T(8,128)S(1)} %all-to-all-done.1) | copy-start | bytes 7077892
  82.4 20.6 %all-to-all-start.2 = ((f32[16,32,256]{2,1,0:T(8,128)}), f32[16,32,256]{2,1,0:T(8,128)S(1)}, u32[]{:S(2)}, u32[]{:S(2)}) async-start(f32[16,32,256]{2,1,0:T(8,128)} %bitcast.3), calls=%async_computation.2 | async-start | bytes 1048576 | tf_op jit(solution)/shard_map/all_to_all | solution.py:26
  103.9 15.6 %all-to-all-start.3 = ((f32[16,32,256]{2,1,0:T(8,128)}), f32[16,32,256]{2,1,0:T(8,128)S(1)}, u32[]{:S(2)}, u32[]{:S(2)}) async-start(f32[16,32,256]{2,1,0:T(8,128)} %broadcast_in_dim.106), calls=%async_computation.3 | async-start | bytes 1048576 | tf_op jit(solution)/shard_map/all_to_all | solution.py:26
  108.7 72.7 %copy-start.18 = (f32[256,256]{1,0:T(8,128)}, f32[256,256]{1,0:T(8,128)S(1)}, u32[]{:S(2)}) copy-start(f32[256,256]{1,0:T(8,128)S(1)} %fusion.42) | copy-start | bytes 786436
  160.8 27.2 %copy-start.36 = (s32[2,2]{1,0:T(2,128)}, s32[2,2]{1,0:T(2,128)S(1)}, u32[]{:S(2)}) copy-start(s32[2,2]{1,0:T(2,128)S(1)} %get-tuple-element.314) | copy-start | bytes 52
  181.4 6.7 copy-start.22
  181.9 6.1 copy-start.27
  183.5 19.6 %slice-start.3 = ((s8[10616832]{0:T(1024)(128)(4,1)}), s8[4194304]{0:T(1024)(128)(4,1)S(1)}, s32[]{:S(2)}) async-start(s8[10616832]{0:T(1024)(128)(4,1)} %bitcast.215), calls=%async_computation.18 | async-start | bytes 8388608
  188.0 12.3 %copy-start.5 = (f32[8,144,512]{2,1,0:T(8,128)S(1)}, f32[8,144,512]{2,1,0:T(8,128)}, u32[]{:S(2)}) copy-start(f32[8,144,512]{2,1,0:T(8,128)} %copy-done.4) | copy-start | bytes 7077892
  188.0 15.0 %slice-start.4 = ((s8[10616832]{0:T(1024)(128)(4,1)}), s8[4194304]{0:T(1024)(128)(4,1)S(1)}, s32[]{:S(2)}) async-start(s8[10616832]{0:T(1024)(128)(4,1)} %bitcast.215), calls=%async_computation.19 | async-start | bytes 8388608
  188.1 15.0 %slice-start.5 = ((s8[10616832]{0:T(1024)(128)(4,1)}), s8[2228224]{0:T(1024)(128)(4,1)S(1)}, s32[]{:S(2)}) async-start(s8[10616832]{0:T(1024)(128)(4,1)} %bitcast.215), calls=%async_computation.20 | async-start | bytes 4456448
  200.3 8.7 %copy-start.9 = (f32[256,1152]{1,0:T(8,128)}, f32[256,1152]{1,0:T(8,128)S(1)}, u32[]{:S(2)}) copy-start(f32[256,1152]{1,0:T(8,128)S(1)} %fusion.96) | copy-start | bytes 3538948
  259.0 35.5 %all-to-all-start.5 = ((f32[16,160,256]{2,1,0:T(8,128)}), f32[16,160,256]{2,1,0:T(8,128)}, u32[]{:S(2)}, u32[]{:S(2)}) async-start(f32[16,160,256]{2,1,0:T(8,128)} %broadcast_in_dim.110), calls=%async_computation.5 | async-start | bytes 5242880 | tf_op jit(solution)/shard_map/all_to_all | solution.py:26
  265.8 0.7 copy-start.6
  303.4 64.1 %all-to-all-start.6 = ((f32[8,208,256]{2,1,0:T(8,128)}), f32[8,208,256]{2,1,0:T(8,128)}, u32[]{:S(2)}, u32[]{:S(2)}) async-start(f32[8,208,256]{2,1,0:T(8,128)} %bitcast.227), calls=%async_computation.6 | async-start | bytes 3407872 | tf_op jit(solution)/shard_map/all_to_all | solution.py:26
  315.2 0.7 copy-start.31
  372.0 46.8 %all-to-all-start.7 = ((f32[8,208,256]{2,1,0:T(8,128)}), f32[8,208,256]{2,1,0:T(8,128)}, u32[]{:S(2)}, u32[]{:S(2)}) async-start(f32[8,208,256]{2,1,0:T(8,128)} %broadcast_in_dim.111), calls=%async_computation.7 | async-start | bytes 3407872 | tf_op jit(solution)/shard_map/all_to_all | solution.py:26
  413.1 0.7 copy-start.12
  418.9 6.6 copy-start.13
  418.9 7.0 copy-start.7
  421.8 4.8 copy-start.14
  425.8 0.7 copy-start.21
  426.6 17.0 %copy-start.25 = (f32[256,256]{1,0:T(8,128)}, f32[256,256]{1,0:T(8,128)S(1)}, u32[]{:S(2)}) copy-start(f32[256,256]{1,0:T(8,128)S(1)} %fusion.18) | copy-start | bytes 786436
  426.6 17.0 %slice-start.7 = ((s8[4718592]{0:T(1024)(128)(4,1)}), s8[4194304]{0:T(1024)(128)(4,1)S(1)}, s32[]{:S(2)}) async-start(s8[4718592]{0:T(1024)(128)(4,1)} %bitcast.223), calls=%async_computation.22 | async-start | bytes 8388608
  428.7 14.8 %slice-start.8 = ((s8[4718592]{0:T(1024)(128)(4,1)}), s8[524288]{0:T(1024)(128)(4,1)S(1)}, s32[]{:S(2)}) async-start(s8[4718592]{0:T(1024)(128)(4,1)} %bitcast.223), calls=%async_computation.23 | async-start | bytes 1048576
  448.8 4.1 copy-start
  453.8 18.8 %all-to-all-start.8 = ((f32[8,64,256]{2,1,0:T(8,128)}), f32[8,64,256]{2,1,0:T(8,128)}, u32[]{:S(2)}, u32[]{:S(2)}) async-start(f32[8,64,256]{2,1,0:T(8,128)} %bitcast.231), calls=%async_computation.8 | async-start | bytes 1048576 | tf_op jit(solution)/shard_map/all_to_all | solution.py:26
  462.0 1.1 copy-start.10
  472.6 7.1 copy-start.26
  474.6 8.4 %copy-start.8 = (f32[256,256]{1,0:T(8,128)S(1)}, f32[256,256]{1,0:T(8,128)}, u32[]{:S(2)}) copy-start(f32[256,256]{1,0:T(8,128)} %copy-done.6) | copy-start | bytes 786436
  474.6 8.4 %copy-start.11 = (f32[1152,256]{1,0:T(8,128)S(1)}, f32[1152,256]{1,0:T(8,128)}, u32[]{:S(2)}) copy-start(f32[1152,256]{1,0:T(8,128)} %copy-done.10) | copy-start | bytes 3538948
  474.6 8.4 %copy-start.35 = (pred[1152]{0:T(1024)(128)(4,1)S(1)}, pred[1152]{0:T(1024)(128)(4,1)}, u32[]{:S(2)}) copy-start(pred[1152]{0:T(1024)(128)(4,1)} %get-tuple-element.106) | copy-start | bytes 3460
  474.6 14.4 %all-to-all-start.9 = ((f32[8,64,256]{2,1,0:T(8,128)}), f32[8,64,256]{2,1,0:T(8,128)S(1)}, u32[]{:S(2)}, u32[]{:S(2)}) async-start(f32[8,64,256]{2,1,0:T(8,128)} %broadcast_in_dim.114), calls=%async_computation.9 | async-start | bytes 1048576 | tf_op jit(solution)/shard_map/all_to_all | solution.py:26
  489.8 0.7 copy-start.24
  491.3 86.1 %copy-start.1 = (f32[2304,256]{1,0:T(8,128)S(1)}, f32[2304,256]{1,0:T(8,128)}, u32[]{:S(2)}) copy-start(f32[2304,256]{1,0:T(8,128)} %copy-done) | copy-start | bytes 7077892
  492.5 0.7 copy-start.32
  574.9 4.6 copy-start.23
  577.4 2.2 copy-start.28
  577.4 2.2 copy-start.19
  577.4 2.2 copy-start.34
  579.6 13.9 %copy-start.2 = (f32[2304,256]{1,0:T(8,128)}, f32[2304,256]{1,0:T(8,128)S(1)}, u32[]{:S(2)}) copy-start(f32[2304,256]{1,0:T(8,128)S(1)} %convolution_add_fusion) | copy-start | bytes 7077892
  579.6 13.9 %slice-start = ((s8[10616832]{0:T(1024)(128)(4,1)}), s8[4194304]{0:T(1024)(128)(4,1)S(1)}, s32[]{:S(2)}) async-start(s8[10616832]{0:T(1024)(128)(4,1)} %bitcast.213), calls=%async_computation.15 | async-start | bytes 8388608
  580.9 12.5 %slice-start.1 = ((s8[10616832]{0:T(1024)(128)(4,1)}), s8[4194304]{0:T(1024)(128)(4,1)S(1)}, s32[]{:S(2)}) async-start(s8[10616832]{0:T(1024)(128)(4,1)} %bitcast.213), calls=%async_computation.16 | async-start | bytes 8388608
  580.9 12.5 %slice-start.2 = ((s8[10616832]{0:T(1024)(128)(4,1)}), s8[2228224]{0:T(1024)(128)(4,1)S(1)}, s32[]{:S(2)}) async-start(s8[10616832]{0:T(1024)(128)(4,1)} %bitcast.213), calls=%async_computation.17 | async-start | bytes 4456448
  641.0 58.4 %all-to-all-start.11 = ((f32[16,160,256]{2,1,0:T(8,128)}), f32[16,160,256]{2,1,0:T(8,128)}, u32[]{:S(2)}, u32[]{:S(2)}) async-start(f32[16,160,256]{2,1,0:T(8,128)} %broadcast_in_dim.115), calls=%async_computation.11 | async-start | bytes 5242880 | tf_op jit(solution)/shard_map/all_to_all | solution.py:26
  647.1 0.7 copy-start.20
  651.8 0.7 copy-start.33
  701.7 8.7 %copy-start.30 = (f32[256,256]{1,0:T(8,128)S(1)}, f32[256,256]{1,0:T(8,128)}, u32[]{:S(2)}) copy-start(f32[256,256]{1,0:T(8,128)} %get-tuple-element.83) | copy-start | bytes 786436
  701.7 8.8 %copy-start.37 = (s32[2,2]{1,0:T(2,128)S(1)}, s32[2,2]{1,0:T(2,128)}, u32[]{:S(2)}) copy-start(s32[2,2]{1,0:T(2,128)} %get-tuple-element.316) | copy-start | bytes 52
  701.7 34.6 %all-to-all-start.12 = ((f32[8,176,256]{2,1,0:T(8,128)}), f32[8,176,256]{2,1,0:T(8,128)}, u32[]{:S(2)}, u32[]{:S(2)}) async-start(f32[8,176,256]{2,1,0:T(8,128)} %bitcast.228), calls=%async_computation.12 | async-start | bytes 2883584 | tf_op jit(solution)/shard_map/all_to_all | solution.py:26
  714.5 21.9 %copy-start.29 = (f32[256,256]{1,0:T(8,128)}, f32[256,256]{1,0:T(8,128)S(1)}, u32[]{:S(2)}) copy-start(f32[256,256]{1,0:T(8,128)S(1)} %get-tuple-element.310) | copy-start | bytes 786436
  738.5 9.1 %copy-start.15 = (f32[1152,512]{0,1:T(8,128)S(1)}, f32[1152,512]{0,1:T(8,128)}, u32[]{:S(2)}) copy-start(f32[1152,512]{0,1:T(8,128)} %pad_maximum_fusion.2) | copy-start | bytes 7077892
  740.9 24.2 %all-to-all-start.13 = ((f32[8,176,256]{2,1,0:T(8,128)}), f32[8,176,256]{2,1,0:T(8,128)}, u32[]{:S(2)}, u32[]{:S(2)}) async-start(f32[8,176,256]{2,1,0:T(8,128)} %broadcast_in_dim.116), calls=%async_computation.13 | async-start | bytes 2883584 | tf_op jit(solution)/shard_map/all_to_all | solution.py:26
  755.1 0.7 copy-start.16
  765.1 2.5 copy-start.17
  769.0 2.5 copy-start.3
Sparse Core Ops, SparseCore 0:
  66.1 117.2 all-reduce.2

commit v6 on v5

--- a/solution.py
+++ b/solution.py
@@ -58,13 +58,34 @@
     return jnp.concatenate([even, odd], axis=0)
 
 
+def tri_inv(low, leaf=32):
+    n = low.shape[0]
+    count = n // leaf
+    blocks = low.reshape(count, leaf, count, leaf).transpose(0, 2, 1, 3)
+    diag = blocks[jnp.arange(count), jnp.arange(count)]
+    eye = jnp.broadcast_to(jnp.eye(leaf, dtype=low.dtype), diag.shape)
+    inv = lax.linalg.triangular_solve(diag, eye, left_side=True, lower=True)
+    size = leaf
+    while size < n:
+        count = n // size
+        blocks = low.reshape(count, size, count, size).transpose(0, 2, 1, 3)
+        even = jnp.arange(0, count, 2)
+        below = blocks[even + 1, even]
+        first, last = inv[0::2], inv[1::2]
+        corner = -jnp.matmul(jnp.matmul(last, below, precision=HIGH), first, precision=HIGH)
+        zeros = jnp.zeros_like(first)
+        top_half = jnp.concatenate([first, zeros], axis=2)
+        bottom_half = jnp.concatenate([corner, last], axis=2)
+        inv = jnp.concatenate([top_half, bottom_half], axis=1)
+        size *= 2
+    return inv[0]
+
+
 def small_factors(gram, top):
     identity = jnp.eye(BAND, dtype=jnp.float32)
-    low = jnp.linalg.cholesky(gram)
-    low_inv = jax.scipy.linalg.solve_triangular(low, identity, lower=True)
+    low_inv = tri_inv(jnp.linalg.cholesky(gram))
     shifted = identity + mm_nt(top, low_inv)
-    second = jnp.linalg.cholesky(mm_nt(shifted, shifted))
-    second_inv = jax.scipy.linalg.solve_triangular(second, identity, lower=True)
+    second_inv = tri_inv(jnp.linalg.cholesky(mm_nt(shifted, shifted)))
     transform = mm_tn(shifted, mm_tn(second_inv, second_inv))
     return low_inv, transform
 

time: 810 us -> 887 us (1.095)
  waiting for transfers between devices: 66.1 us -> 178 us
  blocking collectives: 110 us -> 34.9 us
  local copies, waits for them, and re-layouts: 83.6 us -> 105 us
  other arithmetic: 277 us -> 290 us
  starting transfers between devices: 63.6 us -> 72.6 us
    all_to_all x11 -> x13, waiting for transfers between devices: 64.5 us -> 160 us  [a2a(): return lax.all_to_all(x, axis, 0, 0, tiled=False)]
    all_to_all x3 -> x1, blocking collectives: 110 us -> 34.9 us  [a2a(): return lax.all_to_all(x, axis, 0, 0, tiled=False)]
    reshape x0 -> x20, local copies, waits for them, and re-layouts: none -> 25.8 us  [the longest x12 15.7 us: tri_inv(): blocks = low.reshape(count, size, count, size).transpose(0, 2, 1, 3)]
    another operation x37 -> x12, local copies, waits for them, and re-layouts: 32.2 us -> 7.98 us  [the longest x4 4.41 us: small_factors(): second_inv = tri_inv(jnp.linalg.cholesky(mm_nt(shifted, shifted)))]
    gather x0 -> x12, local copies, waits for them, and re-layouts: none -> 20.4 us  [the longest x8 13.7 us: tri_inv(): below = blocks[even + 1, even]]
    psum x1, waiting for transfers between devices: 1.53 us -> 18.6 us  [body(): strip = lax.psum(jnp.where(r == 0, a[:width, :], 0.0), 'row')]
    another operation x20 -> x12, matrix products: 23.2 us -> 11.2 us  [the longest x4 6.86 us: small_factors(): second_inv = tri_inv(jnp.linalg.cholesky(mm_nt(shifted, shifted)))]
    dot_general x0 -> x24, matrix products: none -> 10.8 us  [the longest x12 6.3 us: tri_inv(): jnp.matmul(last, below, precision=HIGH)]
  transfers between devices with their start and end apart: 12 -> 14, of which waited for: 7 -> 11; matrix products, arithmetic and copies ran while one was open for 37% -> 38% of each run, Pallas kernels for 0% -> 0%
where the time goes in v6:
time: 887 us; the launch traced here: 879 us
  other arithmetic  290 us (33%)
  waiting for transfers between devices  178 us (20%)
  matrix products  177 us (20%)
  local copies, waits for them, and re-layouts  105 us (12%)
  starting transfers between devices  72.6 us (8%)
  blocking collectives  34.9 us (4%)
  between operations  20.8 us (2%)
    all_to_all x13, waiting for transfers between devices, a2a(): return lax.all_to_all(x, axis, 0, 0, tiled=False)  160 us
    another operation x9, other arithmetic, tri_inv(): inv = lax.linalg.triangular_solve(diag, eye, left_side=True, lower=True)  98.4 us
    dot_general x23, matrix products, mm_nt(): return lax.dot_general(a, b, (((1,), (1,)), ((), ())), precision=precision)  89 us
    another operation x14, other arithmetic, small_factors(): second_inv = tri_inv(jnp.linalg.cholesky(mm_nt(shifted, shifted)))  86.3 us
    all_to_all x13, starting transfers between devices, a2a(): return lax.all_to_all(x, axis, 0, 0, tiled=False)  72.5 us
    another operation x14, other arithmetic, small_factors(): low_inv = tri_inv(jnp.linalg.cholesky(gram))  69.4 us
    dot_general x11, matrix products, mm_tn(): return lax.dot_general(a, b, (((0,), (0,)), ((), ())), precision=precision)  36.7 us
    all_to_all x1, blocking collectives, a2a(): return lax.all_to_all(x, axis, 0, 0, tiled=False)  34.9 us
  transfers between devices with their start and end apart: 14, of which 11 were waited for; matrix products, arithmetic and copies ran while one was open for 38% of the time, Pallas kernels for 0%

profile of v6, /device:TPU:1, one launch (start us, length us, event | category | flops | bytes accessed | tf_op | source)
XLA Modules:
  0.0 878.8 jit_solution(3027601035072505307)
XLA Ops:
  8.8 34.9 %all_to_all.70 = f32[8,144,512]{2,1,0:T(8,128)S(1)} all-to-all(f32[8,144,512]{2,1,0:T(8,128)S(1)} %bitcast.275), channel_id=1, replica_groups=mesh['row'=16,'col'=8] {'col'}, dimensions={0} | all-to-all | bytes 4718592 | tf_op jit(solution)/shard_map/all_to_all | solution.py:26
  45.5 4.6 all-to-all-start.1
  50.0 4.8 slice.196
  54.9 6.1 copy.56
  61.5 17.7 %all-to-all-done.1 = f32[8,144,512]{2,1,0:T(8,128)S(1)} async-done(((f32[8,144,512]{2,1,0:T(8,128)}), f32[8,144,512]{2,1,0:T(8,128)S(1)}, u32[]{:S(2)}, u32[]{:S(2)}) %all-to-all-start.1) | async-done | bytes 2359328 | tf_op jit(solution)/shard_map/all_to_all | solution.py:26
  82.5 7.8 all-to-all-start.2
  90.3 5.1 select_bitcast_fusion
  95.5 4.9 all-to-all-done.2
  101.3 4.0 all-to-all-start.3
  106.0 13.1 %all-to-all-done.3 = f32[16,32,256]{2,1,0:T(8,128)S(1)} async-done(((f32[16,32,256]{2,1,0:T(8,128)}), f32[16,32,256]{2,1,0:T(8,128)S(1)}, u32[]{:S(2)}, u32[]{:S(2)}) %all-to-all-start.3) | async-done | bytes 524320 | tf_op jit(solution)/shard_map/all_to_all | solution.py:26
  120.0 11.7 %cholesky.214 = f32[128,128]{1,0:T(8,128)S(1)} custom-call(f32[128,128]{1,0:T(8,128)S(1)} %cholesky.346), custom_call_target="Cholesky" | custom-call | tf_op jit(solution)/shard_map/jit(cholesky)/cholesky | solution.py:86
  131.8 9.8 %custom-call.41 = f32[1,128,128]{1,2,0:T(8,128)S(1)} custom-call(f32[1,128,128]{2,1,0:T(8,128)S(1)} %get-tuple-element.131), custom_call_target="InvertDiagBlocksLowerTriangular" | custom-call | tf_op jit(solution)/shard_map/jit(cholesky)/cholesky | solution.py:86
  142.0 11.7 %cholesky.231 = f32[128,128]{1,0:T(8,128)S(1)} custom-call(f32[128,128]{1,0:T(8,128)S(1)} %convolution_subtract_fusion.11), custom_call_target="Cholesky" | custom-call | tf_op jit(solution)/shard_map/jit(cholesky)/cholesky | solution.py:86
  157.8 30.3 %custom-call.42 = f32[8,1,32,32]{2,3,1,0:T(8,128)S(1)} custom-call(f32[8,1,32,32]{3,2,1,0:T(8,128)S(1)} %select_bitcast_fusion.4), custom_call_target="InvertDiagBlocksLowerTriangular" | custom-call | tf_op jit(solution)/shard_map/triangular_solve/custom-call.0 | solution.py:67
  191.3 18.6 %all-reduce.15.cloned.1.call-done = f32[2304,512]{1,0:T(8,128)} async-done(((f32[2304,512]{1,0:T(8,128)}), f32[2304,512]{1,0:T(8,128)}) %all-reduce.15.cloned.1.call-update) | async-done | bytes 4718608 | tf_op jit(solution)/shard_map/psum | solution.py:105
  209.9 4.5 convolution_add_fusion.1
  214.5 12.1 %fusion.190 = f32[256,1152]{1,0:T(8,128)S(1)} fusion(f32[2304,256]{1,0:T(8,128)S(1)} %convolution_add_fusion.1, f32[1152,2304]{1,0:T(8,128)} %param.4), kind=kOutput, calls=%fused_computation.323 | convolution fusion | flops 4076863488 | bytes 14155776 | tf_op jit(solution)/shard_map/dot_general | solution.py:13
  229.2 6.0 convolution_bitcast_fusion
  238.3 3.3 copy.26
  241.5 5.1 all-to-all-start.4
  248.5 33.1 %all-to-all-done.4 = f32[16,160,256]{2,1,0:T(8,128)} async-done(((f32[16,160,256]{2,1,0:T(8,128)}), f32[16,160,256]{2,1,0:T(8,128)}, u32[]{:S(2)}, u32[]{:S(2)}) %all-to-all-start.4) | async-done | bytes 2621472 | tf_op jit(solution)/shard_map/all_to_all | solution.py:26
  286.8 5.3 all-to-all-start.5
  299.6 13.2 %cholesky.248 = f32[128,128]{1,0:T(8,128)} custom-call(f32[128,128]{1,0:T(8,128)} %cholesky.349), custom_call_target="Cholesky" | custom-call | tf_op jit(solution)/shard_map/jit(cholesky)/cholesky | solution.py:88
  316.4 11.3 %custom-call.43 = f32[1,128,128]{1,2,0:T(8,128)} custom-call(f32[1,128,128]{2,1,0:T(8,128)} %get-tuple-element.127), custom_call_target="InvertDiagBlocksLowerTriangular" | custom-call | tf_op jit(solution)/shard_map/jit(cholesky)/cholesky | solution.py:88
  331.1 13.2 %cholesky.265 = f32[128,128]{1,0:T(8,128)} custom-call(f32[128,128]{1,0:T(8,128)} %convolution_subtract_fusion.10), custom_call_target="Cholesky" | custom-call | tf_op jit(solution)/shard_map/jit(cholesky)/cholesky | solution.py:88
  363.7 21.2 %custom-call.44 = f32[8,1,32,32]{2,3,1,0:T(8,128)} custom-call(f32[8,1,32,32]{3,2,1,0:T(8,128)} %select_bitcast_fusion.3), custom_call_target="InvertDiagBlocksLowerTriangular" | custom-call | tf_op jit(solution)/shard_map/triangular_solve/custom-call.0 | solution.py:67
  389.0 6.2 fusion.10
  404.2 7.0 all-to-all-start.6
  416.2 17.2 %all-to-all-done.6 = f32[8,208,256]{2,1,0:T(8,128)} async-done(((f32[8,208,256]{2,1,0:T(8,128)}), f32[8,208,256]{2,1,0:T(8,128)}, u32[]{:S(2)}, u32[]{:S(2)}) %all-to-all-start.6) | async-done | bytes 1703968 | tf_op jit(solution)/shard_map/all_to_all | solution.py:26
  438.0 5.1 all-to-all-start.7
  451.7 5.1 fusion.8
  456.8 8.5 all-to-all-done.7
  468.2 3.6 fusion.14
  475.2 14.8 %convolution_subtract_fusion.3 = f32[1152,2304]{1,0:T(8,128)} fusion(f32[1152,2304]{1,0:T(8,128)} %param.4, f32[1152,256]{0,1:T(8,128)S(1)} %convolution_add_fusion.3, f32[2304,256]{1,0:T(8,128)S(1)} %fusion.2), kind=kOutput, calls=%fused_computation.15 | convolution fusion | flops 4079517696 | bytes 24772608 | tf_op jit(solution)/shard_map/dot_general | solution.py:21
  492.2 3.1 fusion.1
  495.3 4.1 fusion.195
  500.2 4.9 all-to-all-start.8
  505.1 3.4 fusion.5
  509.6 9.5 %convolution_subtract_fusion.2 = f32[1152,2304]{1,0:T(8,128)} fusion(f32[1152,2304]{1,0:T(8,128)} %convolution_subtract_fusion.3, f32[1152,256]{1,0:T(8,128)S(1)} %fusion.5, f32[2304,256]{1,0:T(8,128)S(1)} %convolution_add_fusion.1), kind=kOutput, calls=%fused_computation.14 | convolution fusion | flops 4079517696 | bytes 24772608 | tf_op jit(solution)/shard_map/dot_general | solution.py:21
  521.1 5.1 all-to-all-start.9
  526.2 3.3 convolution_subtract_fusion.7
  531.7 3.8 all-to-all-done.9
  536.5 11.7 %cholesky.282 = f32[128,128]{1,0:T(8,128)S(1)} custom-call(f32[128,128]{1,0:T(8,128)S(1)} %cholesky.352), custom_call_target="Cholesky" | custom-call | tf_op jit(solution)/shard_map/jit(cholesky)/cholesky | solution.py:86
  548.3 9.8 %custom-call.45 = f32[1,128,128]{1,2,0:T(8,128)S(1)} custom-call(f32[1,128,128]{2,1,0:T(8,128)S(1)} %get-tuple-element.123), custom_call_target="InvertDiagBlocksLowerTriangular" | custom-call | tf_op jit(solution)/shard_map/jit(cholesky)/cholesky | solution.py:86
  558.6 11.9 %cholesky.299 = f32[128,128]{1,0:T(8,128)S(1)} custom-call(f32[128,128]{1,0:T(8,128)S(1)} %convolution_subtract_fusion.9), custom_call_target="Cholesky" | custom-call | tf_op jit(solution)/shard_map/jit(cholesky)/cholesky | solution.py:86
  579.4 21.0 %custom-call.46 = f32[8,1,32,32]{2,3,1,0:T(8,128)} custom-call(f32[8,1,32,32]{3,2,1,0:T(8,128)} %select_bitcast_fusion.2), custom_call_target="InvertDiagBlocksLowerTriangular" | custom-call | tf_op jit(solution)/shard_map/triangular_solve/custom-call.0 | solution.py:67
  612.1 2.9 convolution_add_fusion
  616.5 12.5 %fusion.196 = f32[2304,256]{1,0:T(8,128)S(1)} fusion(f32[1152,2304]{1,0:T(8,128)} %convolution_subtract_fusion.2, f32[1152,256]{0,1:T(8,128)S(1)} %convolution_add_fusion.2), kind=kOutput, calls=%fused_computation.329 | convolution fusion | flops 4076863488 | bytes 14155776 | tf_op jit(solution)/shard_map/dot_general | solution.py:17
  629.0 4.4 fusion.197
  636.3 7.0 all-to-all-start.10
  648.4 29.5 %all-to-all-done.10 = f32[16,160,256]{2,1,0:T(8,128)} async-done(((f32[16,160,256]{2,1,0:T(8,128)}), f32[16,160,256]{2,1,0:T(8,128)}, u32[]{:S(2)}, u32[]{:S(2)}) %all-to-all-start.10) | async-done | bytes 2621472 | tf_op jit(solution)/shard_map/all_to_all | solution.py:26
  683.1 4.6 all-to-all-start.11
  690.2 13.2 %cholesky.316 = f32[128,128]{1,0:T(8,128)} custom-call(f32[128,128]{1,0:T(8,128)} %cholesky.355), custom_call_target="Cholesky" | custom-call | tf_op jit(solution)/shard_map/jit(cholesky)/cholesky | solution.py:88
  707.0 11.3 %custom-call.47 = f32[1,128,128]{1,2,0:T(8,128)} custom-call(f32[1,128,128]{2,1,0:T(8,128)} %get-tuple-element.119), custom_call_target="InvertDiagBlocksLowerTriangular" | custom-call | tf_op jit(solution)/shard_map/jit(cholesky)/cholesky | solution.py:88
  721.7 13.2 %cholesky.333 = f32[128,128]{1,0:T(8,128)} custom-call(f32[128,128]{1,0:T(8,128)} %convolution_subtract_fusion.8), custom_call_target="Cholesky" | custom-call | tf_op jit(solution)/shard_map/jit(cholesky)/cholesky | solution.py:88
  756.1 21.0 %custom-call.48 = f32[8,1,32,32]{2,3,1,0:T(8,128)} custom-call(f32[8,1,32,32]{3,2,1,0:T(8,128)} %select_bitcast_fusion.1), custom_call_target="InvertDiagBlocksLowerTriangular" | custom-call | tf_op jit(solution)/shard_map/triangular_solve/custom-call.0 | solution.py:67
  784.5 3.3 copy.45
  790.4 6.9 all-to-all-start.12
  798.3 18.3 %all-to-all-done.12 = f32[8,176,256]{2,1,0:T(8,128)S(1)} async-done(((f32[8,176,256]{2,1,0:T(8,128)}), f32[8,176,256]{2,1,0:T(8,128)S(1)}, u32[]{:S(2)}, u32[]{:S(2)}) %all-to-all-start.12) | async-done | bytes 1441824 | tf_op jit(solution)/shard_map/all_to_all | solution.py:26
  818.1 5.2 all-to-all-start.13
  825.5 3.7 fusion.6
  829.2 13.5 %all-to-all-done.13 = f32[8,176,256]{2,1,0:T(8,128)} async-done(((f32[8,176,256]{2,1,0:T(8,128)}), f32[8,176,256]{2,1,0:T(8,128)}, u32[]{:S(2)}, u32[]{:S(2)}) %all-to-all-start.13) | async-done | bytes 1441824 | tf_op jit(solution)/shard_map/all_to_all | solution.py:26
  851.2 12.9 %convolution_subtract_fusion.1 = f32[1152,2304]{1,0:T(8,128)S(1)} fusion(f32[1152,2304]{1,0:T(8,128)} %convolution_subtract_fusion.2, f32[1152,256]{0,1:T(8,128)S(1)} %convolution_add_fusion.2, f32[2304,256]{1,0:T(8,128)S(1)} %fusion), kind=kOutput, calls=%fused_computation.13 | convolution fusion | flops 4079517696 | bytes 24772608 | tf_op jit(solution)/shard_map/dot_general | solution.py:21
  864.0 7.6 convolution_subtract_fusion
  (312 shorter events, 194.6 us)
Async XLA Ops:
  7.2 1.7 slice-start.6
  45.5 33.7 %all-to-all-start.1 = ((f32[8,144,512]{2,1,0:T(8,128)}), f32[8,144,512]{2,1,0:T(8,128)S(1)}, u32[]{:S(2)}, u32[]{:S(2)}) async-start(f32[8,144,512]{2,1,0:T(8,128)} %broadcast_in_dim.72), calls=%async_computation.1 | async-start | bytes 4718592 | tf_op jit(solution)/shard_map/all_to_all | solution.py:26
  61.5 21.0 %copy-start.40 = (pred[1152]{0:T(1024)(128)(4,1)}, pred[1152]{0:T(1024)(128)(4,1)S(1)}, u32[]{:S(2)}) copy-start(pred[1152]{0:T(1024)(128)(4,1)S(1)} %get-tuple-element.141) | copy-start | bytes 3460
  79.2 16.2 %copy-start.4 = (f32[8,144,512]{2,1,0:T(8,128)}, f32[8,144,512]{2,1,0:T(8,128)S(1)}, u32[]{:S(2)}) copy-start(f32[8,144,512]{2,1,0:T(8,128)S(1)} %all-to-all-done.1) | copy-start | bytes 7077892
  82.5 17.9 %all-to-all-start.2 = ((f32[16,32,256]{2,1,0:T(8,128)}), f32[16,32,256]{2,1,0:T(8,128)S(1)}, u32[]{:S(2)}, u32[]{:S(2)}) async-start(f32[16,32,256]{2,1,0:T(8,128)} %bitcast.3), calls=%async_computation.2 | async-start | bytes 1048576 | tf_op jit(solution)/shard_map/all_to_all | solution.py:26
  90.3 119.7 %all-reduce.15.cloned.1.call-start = ((), (), s32[]{:S(2)}) async-start(), calls=%async_computation.14 | async-start | bytes 9437184 | tf_op jit(solution)/shard_map/psum | solution.py:105
  101.3 17.7 %all-to-all-start.3 = ((f32[16,32,256]{2,1,0:T(8,128)}), f32[16,32,256]{2,1,0:T(8,128)S(1)}, u32[]{:S(2)}, u32[]{:S(2)}) async-start(f32[16,32,256]{2,1,0:T(8,128)} %broadcast_in_dim.75), calls=%async_computation.3 | async-start | bytes 1048576 | tf_op jit(solution)/shard_map/all_to_all | solution.py:26
  106.0 83.4 %copy-start.32 = (f32[32,32]{1,0:T(8,128)}, f32[32,32]{1,0:T(8,128)S(1)}, u32[]{:S(2)}) copy-start(f32[32,32]{1,0:T(8,128)S(1)} %fusion.100) | copy-start | bytes 12292
  191.2 23.2 %copy-start.24 = (f32[1,128,128]{2,1,0:T(8,128)}, f32[1,128,128]{2,1,0:T(8,128)S(1)}, u32[]{:S(2)}) copy-start(f32[1,128,128]{2,1,0:T(8,128)S(1)} %fusion.22) | copy-start | bytes 196612
  191.2 23.2 %copy-start.26 = (f32[1,128,128]{2,1,0:T(8,128)}, f32[1,128,128]{2,1,0:T(8,128)S(1)}, u32[]{:S(2)}) copy-start(f32[1,128,128]{2,1,0:T(8,128)S(1)} %get-tuple-element.110) | copy-start | bytes 196612
  191.3 23.2 %copy-start.27 = (f32[1,128,128]{2,1,0:T(8,128)}, f32[1,128,128]{2,1,0:T(8,128)S(1)}, u32[]{:S(2)}) copy-start(f32[1,128,128]{2,1,0:T(8,128)S(1)} %get-tuple-element.111) | copy-start | bytes 196612
  209.9 19.3 %slice-start.3 = ((s8[10616832]{0:T(1024)(128)(4,1)}), s8[4194304]{0:T(1024)(128)(4,1)S(1)}, s32[]{:S(2)}) async-start(s8[10616832]{0:T(1024)(128)(4,1)} %bitcast.273), calls=%async_computation.18 | async-start | bytes 8388608
  214.5 12.1 %copy-start.5 = (f32[8,144,512]{2,1,0:T(8,128)S(1)}, f32[8,144,512]{2,1,0:T(8,128)}, u32[]{:S(2)}) copy-start(f32[8,144,512]{2,1,0:T(8,128)} %copy-done.4) | copy-start | bytes 7077892
  214.5 12.1 %copy-start.39 = (s32[1152]{0:T(1024)S(1)}, s32[1152]{0:T(1024)}, u32[]{:S(2)}) copy-start(s32[1152]{0:T(1024)} %fusion.107) | copy-start | bytes 13828
  214.5 12.1 %copy-start.41 = (pred[1152]{0:T(1024)(128)(4,1)S(1)}, pred[1152]{0:T(1024)(128)(4,1)}, u32[]{:S(2)}) copy-start(pred[1152]{0:T(1024)(128)(4,1)} %copy-done.40) | copy-start | bytes 3460
  214.5 14.7 %slice-start.4 = ((s8[10616832]{0:T(1024)(128)(4,1)}), s8[4194304]{0:T(1024)(128)(4,1)S(1)}, s32[]{:S(2)}) async-start(s8[10616832]{0:T(1024)(128)(4,1)} %bitcast.273), calls=%async_computation.19 | async-start | bytes 8388608
  214.5 14.7 %slice-start.5 = ((s8[10616832]{0:T(1024)(128)(4,1)}), s8[2228224]{0:T(1024)(128)(4,1)S(1)}, s32[]{:S(2)}) async-start(s8[10616832]{0:T(1024)(128)(4,1)} %bitcast.273), calls=%async_computation.20 | async-start | bytes 4456448
  226.6 8.6 copy-start.9
  241.5 40.0 %all-to-all-start.4 = ((f32[16,160,256]{2,1,0:T(8,128)}), f32[16,160,256]{2,1,0:T(8,128)}, u32[]{:S(2)}, u32[]{:S(2)}) async-start(f32[16,160,256]{2,1,0:T(8,128)} %bitcast.284), calls=%async_computation.4 | async-start | bytes 5242880 | tf_op jit(solution)/shard_map/all_to_all | solution.py:26
  286.8 108.5 %all-to-all-start.5 = ((f32[16,160,256]{2,1,0:T(8,128)}), f32[16,160,256]{2,1,0:T(8,128)}, u32[]{:S(2)}, u32[]{:S(2)}) async-start(f32[16,160,256]{2,1,0:T(8,128)} %broadcast_in_dim.80), calls=%async_computation.5 | async-start | bytes 5242880 | tf_op jit(solution)/shard_map/all_to_all | solution.py:26
  298.2 0.7 copy-start.30
  404.2 29.2 %all-to-all-start.6 = ((f32[8,208,256]{2,1,0:T(8,128)}), f32[8,208,256]{2,1,0:T(8,128)}, u32[]{:S(2)}, u32[]{:S(2)}) async-start(f32[8,208,256]{2,1,0:T(8,128)} %bitcast.285), calls=%async_computation.6 | async-start | bytes 3407872 | tf_op jit(solution)/shard_map/all_to_all | solution.py:26
  438.0 27.3 %all-to-all-start.7 = ((f32[8,208,256]{2,1,0:T(8,128)}), f32[8,208,256]{2,1,0:T(8,128)}, u32[]{:S(2)}, u32[]{:S(2)}) async-start(f32[8,208,256]{2,1,0:T(8,128)} %broadcast_in_dim.81), calls=%async_computation.7 | async-start | bytes 3407872 | tf_op jit(solution)/shard_map/all_to_all | solution.py:26
  465.3 6.6 copy-start.13
  465.3 7.0 copy-start.7
  468.2 4.8 copy-start.14
  472.3 0.7 copy-start.20
  473.0 17.0 %copy-start.21 = (f32[256,256]{1,0:T(8,128)}, f32[256,256]{1,0:T(8,128)S(1)}, u32[]{:S(2)}) copy-start(f32[256,256]{1,0:T(8,128)S(1)} %fusion.18) | copy-start | bytes 786436
  473.0 17.0 %slice-start.7 = ((s8[4718592]{0:T(1024)(128)(4,1)}), s8[4194304]{0:T(1024)(128)(4,1)S(1)}, s32[]{:S(2)}) async-start(s8[4718592]{0:T(1024)(128)(4,1)} %bitcast.281), calls=%async_computation.22 | async-start | bytes 8388608
  475.2 14.8 %slice-start.8 = ((s8[4718592]{0:T(1024)(128)(4,1)}), s8[524288]{0:T(1024)(128)(4,1)S(1)}, s32[]{:S(2)}) async-start(s8[4718592]{0:T(1024)(128)(4,1)} %bitcast.281), calls=%async_computation.23 | async-start | bytes 1048576
  490.0 2.2 copy-start.42
  495.3 4.1 copy-start
  500.2 18.9 %all-to-all-start.8 = ((f32[8,64,256]{2,1,0:T(8,128)}), f32[8,64,256]{2,1,0:T(8,128)}, u32[]{:S(2)}, u32[]{:S(2)}) async-start(f32[8,64,256]{2,1,0:T(8,128)} %bitcast.289), calls=%async_computation.8 | async-start | bytes 1048576 | tf_op jit(solution)/shard_map/all_to_all | solution.py:26
  508.5 1.0 copy-start.10
  519.1 7.1 copy-start.22
  521.1 8.4 copy-start.8
  521.1 8.4 copy-start.11
  521.1 8.4 copy-start.43
  521.1 14.4 %all-to-all-start.9 = ((f32[8,64,256]{2,1,0:T(8,128)}), f32[8,64,256]{2,1,0:T(8,128)S(1)}, u32[]{:S(2)}, u32[]{:S(2)}) async-start(f32[8,64,256]{2,1,0:T(8,128)} %broadcast_in_dim.84), calls=%async_computation.9 | async-start | bytes 1048576 | tf_op jit(solution)/shard_map/all_to_all | solution.py:26
  577.7 34.4 %copy-start.1 = (f32[2304,256]{1,0:T(8,128)S(1)}, f32[2304,256]{1,0:T(8,128)}, u32[]{:S(2)}) copy-start(f32[2304,256]{1,0:T(8,128)} %copy-done) | copy-start | bytes 7077892
  611.6 3.4 copy-start.28
  611.6 3.4 copy-start.29
  612.1 3.0 copy-start.25
  612.1 3.0 copy-start.17
  612.1 3.0 copy-start.38
  615.1 13.9 %copy-start.2 = (f32[2304,256]{1,0:T(8,128)}, f32[2304,256]{1,0:T(8,128)S(1)}, u32[]{:S(2)}) copy-start(f32[2304,256]{1,0:T(8,128)S(1)} %convolution_add_fusion) | copy-start | bytes 7077892
  615.1 13.9 %slice-start = ((s8[10616832]{0:T(1024)(128)(4,1)}), s8[4194304]{0:T(1024)(128)(4,1)S(1)}, s32[]{:S(2)}) async-start(s8[10616832]{0:T(1024)(128)(4,1)} %bitcast.271), calls=%async_computation.15 | async-start | bytes 8388608
  616.5 12.6 %slice-start.1 = ((s8[10616832]{0:T(1024)(128)(4,1)}), s8[4194304]{0:T(1024)(128)(4,1)S(1)}, s32[]{:S(2)}) async-start(s8[10616832]{0:T(1024)(128)(4,1)} %bitcast.271), calls=%async_computation.16 | async-start | bytes 8388608
  616.5 12.6 %slice-start.2 = ((s8[10616832]{0:T(1024)(128)(4,1)}), s8[2228224]{0:T(1024)(128)(4,1)S(1)}, s32[]{:S(2)}) async-start(s8[10616832]{0:T(1024)(128)(4,1)} %bitcast.271), calls=%async_computation.17 | async-start | bytes 4456448
  636.3 41.5 %all-to-all-start.10 = ((f32[16,160,256]{2,1,0:T(8,128)}), f32[16,160,256]{2,1,0:T(8,128)}, u32[]{:S(2)}, u32[]{:S(2)}) async-start(f32[16,160,256]{2,1,0:T(8,128)} %bitcast.283), calls=%async_computation.10 | async-start | bytes 5242880 | tf_op jit(solution)/shard_map/all_to_all | solution.py:26
  644.8 0.7 copy-start.18
  683.1 105.1 %all-to-all-start.11 = ((f32[16,160,256]{2,1,0:T(8,128)}), f32[16,160,256]{2,1,0:T(8,128)}, u32[]{:S(2)}, u32[]{:S(2)}) async-start(f32[16,160,256]{2,1,0:T(8,128)} %broadcast_in_dim.85), calls=%async_computation.11 | async-start | bytes 5242880 | tf_op jit(solution)/shard_map/all_to_all | solution.py:26
  688.8 0.7 copy-start.31
  784.5 3.3 copy-start.33
  784.5 3.3 copy-start.37
  789.2 8.2 copy-start.35
  790.4 7.4 copy-start.36
  790.4 26.3 %all-to-all-start.12 = ((f32[8,176,256]{2,1,0:T(8,128)}), f32[8,176,256]{2,1,0:T(8,128)S(1)}, u32[]{:S(2)}, u32[]{:S(2)}) async-start(f32[8,176,256]{2,1,0:T(8,128)} %bitcast.286), calls=%async_computation.12 | async-start | bytes 2883584 | tf_op jit(solution)/shard_map/all_to_all | solution.py:26
  816.7 6.5 copy-start.34
  818.1 6.1 copy-start.19
  818.1 24.6 %all-to-all-start.13 = ((f32[8,176,256]{2,1,0:T(8,128)}), f32[8,176,256]{2,1,0:T(8,128)}, u32[]{:S(2)}, u32[]{:S(2)}) async-start(f32[8,176,256]{2,1,0:T(8,128)} %broadcast_in_dim.86), calls=%async_computation.13 | async-start | bytes 2883584 | tf_op jit(solution)/shard_map/all_to_all | solution.py:26
  824.8 0.7 copy-start.15
  842.7 2.5 copy-start.16
  846.5 2.5 copy-start.3
  (3 other events, 2.1 us)
Sparse Core Ops, SparseCore 0:
  95.5 114.3 all-reduce.14

commit v7 on v5

--- a/solution.py
+++ b/solution.py
@@ -82,12 +82,15 @@
     width = PANELS * BAND
 
     strip = lax.psum(jnp.where(r == 0, a[:width, :], 0.0), "row")
+    lo = BAND
+    p0_own = jnp.where(row_pos[:, None] >= lo, a[:, :BAND], 0.0)
+    own = jnp.concatenate([mm_tn(p0_own, p0_own), jnp.where(r == 0, a[lo:lo + BAND, :BAND], 0.0)], axis=0)
+    own = jnp.where(c == 0, own, 0.0)
+    summed = comm.psum(own.reshape(rows * cols, -1, 128), ("row", "col"), rows * cols)
+    summed = summed.reshape(2 * BAND, BAND)
+    gram0, top0 = summed[:BAND], summed[BAND:]
     colb = comm.broadcast(a[:, :width], "col", cols, 0)
-    lo = BAND
     p0 = jnp.where(row_pos[:, None] >= lo, colb[:, :BAND], 0.0)
-    top_part = jnp.where(r == 0, colb[lo:lo + BAND, :BAND], 0.0)
-    summed = comm.psum(jnp.concatenate([mm_tn(p0, p0), top_part], axis=0), "row", rows)
-    gram0, top0 = summed[:BAND], summed[BAND:]
     strip_t = strip.T
 
     stored = []

time: 810 us -> 793 us (0.979)
  blocking collectives: 110 us -> 74 us
  starting transfers between devices: 63.6 us -> 73.1 us
    all_to_all x3 -> x2, blocking collectives: 110 us -> 74 us  [a2a(): return lax.all_to_all(x, axis, 0, 0, tiled=False)]
    psum x1, waiting for transfers between devices: 1.53 us -> 23.7 us  [body(): strip = lax.psum(jnp.where(r == 0, a[:width, :], 0.0), 'row')]
    all_to_all x11 -> x12, waiting for transfers between devices: 64.5 us -> 44.2 us  [a2a(): return lax.all_to_all(x, axis, 0, 0, tiled=False)]
    all_to_all x11 -> x12, starting transfers between devices: 63.6 us -> 72.9 us  [a2a(): return lax.all_to_all(x, axis, 0, 0, tiled=False)]
    unnamed x95 -> x91, local copies, waits for them, and re-layouts: 16.8 us -> 18.8 us
  transfers between devices with their start and end apart: 12 -> 13, of which waited for: 7 -> 6; matrix products, arithmetic and copies ran while one was open for 37% -> 39% of each run, Pallas kernels for 0% -> 0%
where the time goes in v7:
time: 793 us; the launch traced here: 785 us
  other arithmetic  277 us (35%)
  matrix products  183 us (23%)
  local copies, waits for them, and re-layouts  88.6 us (11%)
  blocking collectives  74 us (9%)
  starting transfers between devices  73.1 us (9%)
  waiting for transfers between devices  67.9 us (9%)
  between operations  20.3 us (3%)
    dot_general x23, matrix products, mm_nt(): return lax.dot_general(a, b, (((1,), (1,)), ((), ())), precision=precision)  89.8 us
    another operation x14, other arithmetic, small_factors(): second = jnp.linalg.cholesky(mm_nt(shifted, shifted))  84.9 us
    another operation x14, other arithmetic, small_factors(): low = jnp.linalg.cholesky(gram)  76.7 us
    all_to_all x2, blocking collectives, a2a(): return lax.all_to_all(x, axis, 0, 0, tiled=False)  74 us
    all_to_all x12, starting transfers between devices, a2a(): return lax.all_to_all(x, axis, 0, 0, tiled=False)  72.9 us
    all_to_all x12, waiting for transfers between devices, a2a(): return lax.all_to_all(x, axis, 0, 0, tiled=False)  44.2 us
    dot_general x11, matrix products, mm_tn(): return lax.dot_general(a, b, (((0,), (0,)), ((), ())), precision=precision)  43.2 us
    another operation x5, other arithmetic, small_factors(): low_inv = jax.scipy.linalg.solve_triangular(low, identity, lower=True)  43 us
  transfers between devices with their start and end apart: 13, of which 6 were waited for; matrix products, arithmetic and copies ran while one was open for 39% of the time, Pallas kernels for 0%

profile of v7, /device:TPU:1, one launch (start us, length us, event | category | flops | bytes accessed | tf_op | source)
XLA Modules:
  0.0 784.7 jit_solution(6258173664984068765)
XLA Ops:
  8.7 4.2 fusion.17
  13.9 11.5 %all-to-all-start.2 = ((f32[128,1,8,128]{3,2,1,0:T(8,128)}), f32[128,1,8,128]{3,2,1,0:T(8,128)S(1)}, u32[]{:S(2)}, u32[]{:S(2)}) async-start(f32[128,1,8,128]{3,2,1,0:T(8,128)} %bitcast.3), calls=%async_computation.2 | async-start | bytes 1048576 | tf_op jit(solution)/shard_map/all_to_all | solution.py:26
  25.4 13.7 %all-to-all-done.2 = f32[128,1,8,128]{3,2,1,0:T(8,128)S(1)} async-done(((f32[128,1,8,128]{3,2,1,0:T(8,128)}), f32[128,1,8,128]{3,2,1,0:T(8,128)S(1)}, u32[]{:S(2)}, u32[]{:S(2)}) %all-to-all-start.2) | async-done | bytes 524320 | tf_op jit(solution)/shard_map/all_to_all | solution.py:26
  40.1 4.5 all-to-all-start.3
  44.6 4.8 slice.122
  49.4 3.3 slice.115
  52.7 6.1 copy.36
  58.8 4.8 all-to-all-start
  63.7 5.1 select_bitcast_fusion
  71.7 11.7 %cholesky.214 = f32[128,128]{1,0:T(8,128)S(1)} custom-call(f32[128,128]{1,0:T(8,128)S(1)} %cholesky.346), custom_call_target="Cholesky" | custom-call | tf_op jit(solution)/shard_map/jit(cholesky)/cholesky | solution.py:63
  83.5 9.8 %custom-call.17 = f32[1,128,128]{1,2,0:T(8,128)S(1)} custom-call(f32[1,128,128]{2,1,0:T(8,128)S(1)} %get-tuple-element.99), custom_call_target="InvertDiagBlocksLowerTriangular" | custom-call | tf_op jit(solution)/shard_map/jit(cholesky)/cholesky | solution.py:63
  93.8 11.7 %cholesky.231 = f32[128,128]{1,0:T(8,128)S(1)} custom-call(f32[128,128]{1,0:T(8,128)S(1)} %convolution_subtract_fusion.15), custom_call_target="Cholesky" | custom-call | tf_op jit(solution)/shard_map/jit(cholesky)/cholesky | solution.py:63
  107.2 5.2 all-to-all-start.1
  115.3 4.1 while.8
  119.4 19.7 %custom-call.18 = f32[2,128,128]{1,2,0:T(8,128)S(1)} custom-call(f32[2,128,128]{2,1,0:T(8,128)S(1)} %get-tuple-element.30), custom_call_target="InvertDiagBlocksLowerTriangular" | custom-call | tf_op jit(solution)/shard_map/jit(_solve_triangular)/triangular_solve | solution.py:64
  144.2 10.7 %convolution_bitcast_fusion = f32[2304,256]{0,1:T(8,128)} fusion(f32[1152,256]{0,1:T(8,128)S(1)} %convolution_add_fusion.3, f32[1152,2304]{1,0:T(8,128)} %param.4), kind=kOutput, calls=%fused_computation.22 | convolution fusion | flops 4076863488 | bytes 14155776 | tf_op jit(solution)/shard_map/dot_general | solution.py:17
  154.9 23.7 %all-reduce.3.cloned.1.call-done = f32[2304,512]{1,0:T(8,128)} async-done(((f32[2304,512]{1,0:T(8,128)}), f32[2304,512]{1,0:T(8,128)}) %all-reduce.3.cloned.1.call-update) | async-done | bytes 4718608 | tf_op jit(solution)/shard_map/psum | solution.py:84
  178.6 4.4 convolution_add_fusion.1
  183.0 12.3 %fusion.98 = f32[256,1152]{1,0:T(8,128)S(1)} fusion(f32[2304,256]{1,0:T(8,128)S(1)} %convolution_add_fusion.1, f32[1152,2304]{1,0:T(8,128)} %param.4), kind=kOutput, calls=%fused_computation.204 | convolution fusion | flops 4076863488 | bytes 14155776 | tf_op jit(solution)/shard_map/dot_general | solution.py:13
  199.9 3.2 copy.26
  203.1 37.4 %all_to_all.70 = f32[16,160,256]{2,1,0:T(8,128)} all-to-all(f32[16,160,256]{2,1,0:T(8,128)} %bitcast.220), channel_id=1, replica_groups=mesh['row'=16,'col'=8] {'row'}, dimensions={0} | all-to-all | bytes 5242880 | tf_op jit(solution)/shard_map/all_to_all | solution.py:26
  245.8 4.4 all-to-all-start.5
  257.6 6.2 fusion.10
  263.8 17.0 %all-to-all-done.5 = f32[16,160,256]{2,1,0:T(8,128)} async-done(((f32[16,160,256]{2,1,0:T(8,128)}), f32[16,160,256]{2,1,0:T(8,128)}, u32[]{:S(2)}, u32[]{:S(2)}) %all-to-all-start.5) | async-done | bytes 2621472 | tf_op jit(solution)/shard_map/all_to_all | solution.py:26
  289.6 10.6 %all-to-all-start.6 = ((f32[8,208,256]{2,1,0:T(8,128)}), f32[8,208,256]{2,1,0:T(8,128)}, u32[]{:S(2)}, u32[]{:S(2)}) async-start(f32[8,208,256]{2,1,0:T(8,128)} %bitcast.223), calls=%async_computation.6 | async-start | bytes 3407872 | tf_op jit(solution)/shard_map/all_to_all | solution.py:26
  302.7 13.2 %cholesky.248 = f32[128,128]{1,0:T(8,128)} custom-call(f32[128,128]{1,0:T(8,128)} %cholesky.349), custom_call_target="Cholesky" | custom-call | tf_op jit(solution)/shard_map/jit(cholesky)/cholesky | solution.py:66
  319.4 11.3 %custom-call.19 = f32[1,128,128]{1,2,0:T(8,128)} custom-call(f32[1,128,128]{2,1,0:T(8,128)} %get-tuple-element.95), custom_call_target="InvertDiagBlocksLowerTriangular" | custom-call | tf_op jit(solution)/shard_map/jit(cholesky)/cholesky | solution.py:66
  334.1 13.2 %cholesky.265 = f32[128,128]{1,0:T(8,128)} custom-call(f32[128,128]{1,0:T(8,128)} %convolution_subtract_fusion.14), custom_call_target="Cholesky" | custom-call | tf_op jit(solution)/shard_map/jit(cholesky)/cholesky | solution.py:66
  358.0 5.3 all-to-all-start.7
  364.0 8.0 %while.9 = (s32[]{:T(128)}, f32[256,256]{1,0:T(8,128)}, s32[2,2]{1,0:T(2,128)}, f32[2,128,128]{2,1,0:T(8,128)}, s32[]{:T(128)}) while((s32[]{:T(128)}, f32[256,256]{1,0:T(8,128)}, s32[2,2]{1,0:T(2,128)}, f32[2,128,128]{2,1,0:T(8,128)}, s32[]{:T(128)}) %tuple.100), condition=%wide.while_cond.clone, body=%wide.while_body.clone.sunk | while | flops 2 | bytes 132705 | solution.py:67
  371.9 21.1 %custom-call.20 = f32[2,128,128]{1,2,0:T(8,128)} custom-call(f32[2,128,128]{2,1,0:T(8,128)} %get-tuple-element.31), custom_call_target="InvertDiagBlocksLowerTriangular" | custom-call | tf_op jit(solution)/shard_map/jit(_solve_triangular)/triangular_solve | solution.py:67
  399.5 5.1 fusion.8
  411.9 4.0 convolution_subtract_fusion.5
  418.8 4.0 fusion.103
  422.9 3.4 fusion.14
  426.4 12.4 %convolution_subtract_fusion.3 = f32[1152,2304]{1,0:T(8,128)} fusion(f32[1152,2304]{1,0:T(8,128)S(1)} %bitcast.217, f32[1152,256]{0,1:T(8,128)S(1)} %convolution_add_fusion.3, f32[2304,256]{1,0:T(8,128)S(1)} %fusion.2), kind=kOutput, calls=%fused_computation.11 | convolution fusion | flops 4079517696 | bytes 24772608 | tf_op jit(solution)/shard_map/dot_general | solution.py:21
  439.6 4.8 all-to-all-start.8
  444.4 3.4 fusion.5
  448.8 9.5 %convolution_subtract_fusion.2 = f32[1152,2304]{1,0:T(8,128)} fusion(f32[1152,2304]{1,0:T(8,128)} %convolution_subtract_fusion.3, f32[1152,256]{1,0:T(8,128)S(1)} %fusion.5, f32[2304,256]{1,0:T(8,128)S(1)} %convolution_add_fusion.1), kind=kOutput, calls=%fused_computation.10 | convolution fusion | flops 4079517696 | bytes 24772608 | tf_op jit(solution)/shard_map/dot_general | solution.py:21
  460.3 5.3 all-to-all-start.9
  465.7 3.3 convolution_subtract_fusion.7
  471.1 3.6 all-to-all-done.9
  479.6 13.2 %cholesky.282 = f32[128,128]{1,0:T(8,128)} custom-call(f32[128,128]{1,0:T(8,128)} %cholesky.352), custom_call_target="Cholesky" | custom-call | tf_op jit(solution)/shard_map/jit(cholesky)/cholesky | solution.py:63
  495.8 11.3 %custom-call.21 = f32[1,128,128]{1,2,0:T(8,128)} custom-call(f32[1,128,128]{2,1,0:T(8,128)} %get-tuple-element.91), custom_call_target="InvertDiagBlocksLowerTriangular" | custom-call | tf_op jit(solution)/shard_map/jit(cholesky)/cholesky | solution.py:63
  510.5 13.3 %cholesky.299 = f32[128,128]{1,0:T(8,128)} custom-call(f32[128,128]{1,0:T(8,128)} %convolution_subtract_fusion.13), custom_call_target="Cholesky" | custom-call | tf_op jit(solution)/shard_map/jit(cholesky)/cholesky | solution.py:63
  530.1 8.3 %while.10 = (s32[]{:T(128)}, f32[256,256]{1,0:T(8,128)}, s32[2,2]{1,0:T(2,128)}, f32[2,128,128]{2,1,0:T(8,128)}, s32[]{:T(128)}) while((s32[]{:T(128)}, f32[256,256]{1,0:T(8,128)}, s32[2,2]{1,0:T(2,128)}, f32[2,128,128]{2,1,0:T(8,128)}, s32[]{:T(128)}) %tuple.101), condition=%wide.while_cond.clone.1, body=%wide.while_body.clone.1.sunk | while | flops 2 | bytes 132705 | solution.py:64
  531.4 2.9 bitcast_dynamic-update-slice_fusion.10
  538.4 21.1 %custom-call.22 = f32[2,128,128]{1,2,0:T(8,128)} custom-call(f32[2,128,128]{2,1,0:T(8,128)} %get-tuple-element.32), custom_call_target="InvertDiagBlocksLowerTriangular" | custom-call | tf_op jit(solution)/shard_map/jit(_solve_triangular)/triangular_solve | solution.py:64
  566.8 12.3 %fusion.104 = f32[2304,256]{1,0:T(8,128)S(1)} fusion(f32[1152,2304]{1,0:T(8,128)} %convolution_subtract_fusion.2, f32[1152,256]{0,1:T(8,128)S(1)} %convolution_add_fusion.2), kind=kOutput, calls=%fused_computation.210 | convolution fusion | flops 4076863488 | bytes 14155776 | tf_op jit(solution)/shard_map/dot_general | solution.py:17
  579.1 4.4 fusion.105
  584.9 36.5 %all_to_all.71 = f32[16,160,256]{2,1,0:T(8,128)} all-to-all(f32[16,160,256]{2,1,0:T(8,128)S(1)} %bitcast.219), channel_id=1, replica_groups=mesh['row'=16,'col'=8] {'row'}, dimensions={0} | all-to-all | bytes 5242880 | tf_op jit(solution)/shard_map/all_to_all | solution.py:26
  626.7 4.9 all-to-all-start.11
  639.1 13.2 %cholesky.316 = f32[128,128]{1,0:T(8,128)} custom-call(f32[128,128]{1,0:T(8,128)} %cholesky.355), custom_call_target="Cholesky" | custom-call | tf_op jit(solution)/shard_map/jit(cholesky)/cholesky | solution.py:66
  655.3 11.3 %custom-call.23 = f32[1,128,128]{1,2,0:T(8,128)} custom-call(f32[1,128,128]{2,1,0:T(8,128)} %get-tuple-element.87), custom_call_target="InvertDiagBlocksLowerTriangular" | custom-call | tf_op jit(solution)/shard_map/jit(cholesky)/cholesky | solution.py:66
  670.0 13.2 %cholesky.333 = f32[128,128]{1,0:T(8,128)} custom-call(f32[128,128]{1,0:T(8,128)} %convolution_subtract_fusion.12), custom_call_target="Cholesky" | custom-call | tf_op jit(solution)/shard_map/jit(cholesky)/cholesky | solution.py:66
  687.5 6.8 all-to-all-start.12
  696.3 4.0 while.11
  700.3 19.7 %custom-call.24 = f32[2,128,128]{1,2,0:T(8,128)S(1)} custom-call(f32[2,128,128]{2,1,0:T(8,128)S(1)} %get-tuple-element.33), custom_call_target="InvertDiagBlocksLowerTriangular" | custom-call | tf_op jit(solution)/shard_map/jit(_solve_triangular)/triangular_solve | solution.py:67
  724.4 4.8 all-to-all-start.13
  729.5 3.1 copy.33
  734.4 5.1 fusion.6
  739.5 9.1 %all-to-all-done.13 = f32[8,176,256]{2,1,0:T(8,128)} async-done(((f32[8,176,256]{2,1,0:T(8,128)}), f32[8,176,256]{2,1,0:T(8,128)}, u32[]{:S(2)}, u32[]{:S(2)}) %all-to-all-start.13) | async-done | bytes 1441824 | tf_op jit(solution)/shard_map/all_to_all | solution.py:26
  757.2 12.8 %convolution_subtract_fusion.1 = f32[1152,2304]{1,0:T(8,128)S(1)} fusion(f32[1152,2304]{1,0:T(8,128)} %convolution_subtract_fusion.2, f32[1152,256]{0,1:T(8,128)S(1)} %convolution_add_fusion.2, f32[2304,256]{1,0:T(8,128)S(1)} %fusion), kind=kOutput, calls=%fused_computation.9 | convolution fusion | flops 4079517696 | bytes 24772608 | tf_op jit(solution)/shard_map/dot_general | solution.py:21
  770.0 7.6 convolution_subtract_fusion
  (250 shorter events, 168.8 us)
Async XLA Ops:
  13.9 25.2 %all-to-all-start.2 = ((f32[128,1,8,128]{3,2,1,0:T(8,128)}), f32[128,1,8,128]{3,2,1,0:T(8,128)S(1)}, u32[]{:S(2)}, u32[]{:S(2)}) async-start(f32[128,1,8,128]{3,2,1,0:T(8,128)} %bitcast.3), calls=%async_computation.2 | async-start | bytes 1048576 | tf_op jit(solution)/shard_map/all_to_all | solution.py:26
  40.1 18.7 %all-to-all-start.3 = ((f32[128,1,8,128]{3,2,1,0:T(8,128)}), f32[128,1,8,128]{3,2,1,0:T(8,128)S(1)}, u32[]{:S(2)}, u32[]{:S(2)}) async-start(f32[128,1,8,128]{3,2,1,0:T(8,128)} %broadcast_in_dim.116), calls=%async_computation.3 | async-start | bytes 1048576 | tf_op jit(solution)/shard_map/all_to_all | solution.py:26
  58.8 46.7 %all-to-all-start = ((f32[8,144,512]{2,1,0:T(8,128)}), f32[8,144,512]{2,1,0:T(8,128)S(1)}, u32[]{:S(2)}, u32[]{:S(2)}) async-start(f32[8,144,512]{2,1,0:T(8,128)} %bitcast), calls=%async_computation | async-start | bytes 4718592 | tf_op jit(solution)/shard_map/all_to_all | solution.py:26
  63.6 115.0 %all-reduce.3.cloned.1.call-start = ((), (), s32[]{:S(2)}) async-start(), calls=%async_computation.14 | async-start | bytes 9437184 | tf_op jit(solution)/shard_map/psum | solution.py:84
  70.6 68.8 %copy-start.16 = (f32[256,256]{1,0:T(8,128)}, f32[256,256]{1,0:T(8,128)S(1)}, u32[]{:S(2)}) copy-start(f32[256,256]{1,0:T(8,128)S(1)} %fusion.44) | copy-start | bytes 786436
  107.2 7.9 %copy-start.37 = (s32[2]{0:T(128)S(1)}, s32[2]{0:T(128)}, u32[]{:S(2)}) copy-start(s32[2]{0:T(128)} %iota_multiply_fusion) | copy-start | bytes 28
  107.2 34.3 %all-to-all-start.1 = ((f32[8,144,512]{2,1,0:T(8,128)}), f32[8,144,512]{2,1,0:T(8,128)S(1)}, u32[]{:S(2)}, u32[]{:S(2)}) async-start(f32[8,144,512]{2,1,0:T(8,128)} %broadcast_in_dim.112), calls=%async_computation.1 | async-start | bytes 4718592 | tf_op jit(solution)/shard_map/all_to_all | solution.py:26
  119.4 19.7 %copy-start.35 = (s32[2,2]{1,0:T(2,128)}, s32[2,2]{1,0:T(2,128)S(1)}, u32[]{:S(2)}) copy-start(s32[2,2]{1,0:T(2,128)S(1)} %get-tuple-element.317) | copy-start | bytes 52
  139.4 2.1 copy-start.22
  141.5 13.4 %copy-start.15 = (f32[8,144,512]{2,1,0:T(8,128)}, f32[8,144,512]{2,1,0:T(8,128)S(1)}, u32[]{:S(2)}) copy-start(f32[8,144,512]{2,1,0:T(8,128)S(1)} %all-to-all-done.1) | copy-start | bytes 7077892
  144.2 34.3 %copy-start.33 = (pred[2304]{0:T(1024)(128)(4,1)S(1)}, pred[2304]{0:T(1024)(128)(4,1)}, u32[]{:S(2)}) copy-start(pred[2304]{0:T(1024)(128)(4,1)} %fusion.76) | copy-start | bytes 6916
  195.3 1.1 copy-start.7
  196.4 1.7 copy-start.14
  245.8 35.0 %all-to-all-start.5 = ((f32[16,160,256]{2,1,0:T(8,128)}), f32[16,160,256]{2,1,0:T(8,128)}, u32[]{:S(2)}, u32[]{:S(2)}) async-start(f32[16,160,256]{2,1,0:T(8,128)} %broadcast_in_dim.120), calls=%async_computation.5 | async-start | bytes 5242880 | tf_op jit(solution)/shard_map/all_to_all | solution.py:26
  254.0 0.7 copy-start.4
  289.6 63.9 %all-to-all-start.6 = ((f32[8,208,256]{2,1,0:T(8,128)}), f32[8,208,256]{2,1,0:T(8,128)}, u32[]{:S(2)}, u32[]{:S(2)}) async-start(f32[8,208,256]{2,1,0:T(8,128)} %bitcast.223), calls=%async_computation.6 | async-start | bytes 3407872 | tf_op jit(solution)/shard_map/all_to_all | solution.py:26
  301.3 0.7 copy-start.29
  358.0 46.6 %all-to-all-start.7 = ((f32[8,208,256]{2,1,0:T(8,128)}), f32[8,208,256]{2,1,0:T(8,128)}, u32[]{:S(2)}, u32[]{:S(2)}) async-start(f32[8,208,256]{2,1,0:T(8,128)} %broadcast_in_dim.121), calls=%async_computation.7 | async-start | bytes 3407872 | tf_op jit(solution)/shard_map/all_to_all | solution.py:26
  398.8 0.7 copy-start.10
  404.6 4.4 copy-start.5
  404.6 5.1 copy-start.13
  409.0 0.7 copy-start.21
  409.7 2.2 copy-start.25
  411.9 14.5 %slice-start.3 = ((s8[10616832]{0:T(1024)(128)(4,1)}), s8[4194304]{0:T(1024)(128)(4,1)S(1)}, s32[]{:S(2)}) async-start(s8[10616832]{0:T(1024)(128)(4,1)} %bitcast.216), calls=%async_computation.18 | async-start | bytes 8388608
  415.9 10.5 %slice-start.4 = ((s8[10616832]{0:T(1024)(128)(4,1)}), s8[4194304]{0:T(1024)(128)(4,1)S(1)}, s32[]{:S(2)}) async-start(s8[10616832]{0:T(1024)(128)(4,1)} %bitcast.216), calls=%async_computation.19 | async-start | bytes 8388608
  418.8 4.1 copy-start
  418.8 4.1 copy-start.11
  418.8 7.5 slice-start.5
  439.6 18.8 %all-to-all-start.8 = ((f32[8,64,256]{2,1,0:T(8,128)}), f32[8,64,256]{2,1,0:T(8,128)}, u32[]{:S(2)}, u32[]{:S(2)}) async-start(f32[8,64,256]{2,1,0:T(8,128)} %bitcast.226), calls=%async_computation.8 | async-start | bytes 1048576 | tf_op jit(solution)/shard_map/all_to_all | solution.py:26
  447.8 1.0 copy-start.8
  458.4 7.3 copy-start.26
  460.3 8.6 %copy-start.6 = (f32[256,256]{1,0:T(8,128)S(1)}, f32[256,256]{1,0:T(8,128)}, u32[]{:S(2)}) copy-start(f32[256,256]{1,0:T(8,128)} %copy-done.4) | copy-start | bytes 786436
  460.3 8.6 %copy-start.9 = (f32[1152,256]{1,0:T(8,128)S(1)}, f32[1152,256]{1,0:T(8,128)}, u32[]{:S(2)}) copy-start(f32[1152,256]{1,0:T(8,128)} %copy-done.8) | copy-start | bytes 3538948
  460.3 8.7 %copy-start.34 = (pred[1152]{0:T(1024)(128)(4,1)S(1)}, pred[1152]{0:T(1024)(128)(4,1)}, u32[]{:S(2)}) copy-start(pred[1152]{0:T(1024)(128)(4,1)} %get-tuple-element.108) | copy-start | bytes 3460
  460.3 14.4 %all-to-all-start.9 = ((f32[8,64,256]{2,1,0:T(8,128)}), f32[8,64,256]{2,1,0:T(8,128)S(1)}, u32[]{:S(2)}, u32[]{:S(2)}) async-start(f32[8,64,256]{2,1,0:T(8,128)} %broadcast_in_dim.124), calls=%async_computation.9 | async-start | bytes 1048576 | tf_op jit(solution)/shard_map/all_to_all | solution.py:26
  475.5 0.7 copy-start.24
  477.1 86.1 %copy-start.1 = (f32[2304,256]{1,0:T(8,128)S(1)}, f32[2304,256]{1,0:T(8,128)}, u32[]{:S(2)}) copy-start(f32[2304,256]{1,0:T(8,128)} %copy-done) | copy-start | bytes 7077892
  478.3 0.7 copy-start.30
  560.8 4.6 copy-start.23
  563.2 2.2 copy-start.27
  563.2 2.2 copy-start.18
  563.2 2.2 copy-start.32
  565.4 13.7 %copy-start.2 = (f32[2304,256]{1,0:T(8,128)}, f32[2304,256]{1,0:T(8,128)S(1)}, u32[]{:S(2)}) copy-start(f32[2304,256]{1,0:T(8,128)S(1)} %convolution_add_fusion) | copy-start | bytes 7077892
  565.4 13.7 %slice-start = ((s8[10616832]{0:T(1024)(128)(4,1)}), s8[4194304]{0:T(1024)(128)(4,1)S(1)}, s32[]{:S(2)}) async-start(s8[10616832]{0:T(1024)(128)(4,1)} %bitcast.214), calls=%async_computation.15 | async-start | bytes 8388608
  566.7 12.4 %slice-start.1 = ((s8[10616832]{0:T(1024)(128)(4,1)}), s8[4194304]{0:T(1024)(128)(4,1)S(1)}, s32[]{:S(2)}) async-start(s8[10616832]{0:T(1024)(128)(4,1)} %bitcast.214), calls=%async_computation.16 | async-start | bytes 8388608
  566.8 12.4 %slice-start.2 = ((s8[10616832]{0:T(1024)(128)(4,1)}), s8[2228224]{0:T(1024)(128)(4,1)S(1)}, s32[]{:S(2)}) async-start(s8[10616832]{0:T(1024)(128)(4,1)} %bitcast.214), calls=%async_computation.17 | async-start | bytes 4456448
  626.7 58.5 %all-to-all-start.11 = ((f32[16,160,256]{2,1,0:T(8,128)}), f32[16,160,256]{2,1,0:T(8,128)}, u32[]{:S(2)}, u32[]{:S(2)}) async-start(f32[16,160,256]{2,1,0:T(8,128)} %broadcast_in_dim.125), calls=%async_computation.11 | async-start | bytes 5242880 | tf_op jit(solution)/shard_map/all_to_all | solution.py:26
  633.1 0.7 copy-start.19
  637.8 0.7 copy-start.31
  687.5 8.8 %copy-start.28 = (f32[256,256]{1,0:T(8,128)S(1)}, f32[256,256]{1,0:T(8,128)}, u32[]{:S(2)}) copy-start(f32[256,256]{1,0:T(8,128)} %get-tuple-element.85) | copy-start | bytes 786436
  687.5 8.9 %copy-start.36 = (s32[2,2]{1,0:T(2,128)S(1)}, s32[2,2]{1,0:T(2,128)}, u32[]{:S(2)}) copy-start(s32[2,2]{1,0:T(2,128)} %get-tuple-element.319) | copy-start | bytes 52
  687.5 34.2 %all-to-all-start.12 = ((f32[8,176,256]{2,1,0:T(8,128)}), f32[8,176,256]{2,1,0:T(8,128)}, u32[]{:S(2)}, u32[]{:S(2)}) async-start(f32[8,176,256]{2,1,0:T(8,128)} %bitcast.224), calls=%async_computation.12 | async-start | bytes 2883584 | tf_op jit(solution)/shard_map/all_to_all | solution.py:26
  723.1 6.1 copy-start.17
  724.4 24.2 %all-to-all-start.13 = ((f32[8,176,256]{2,1,0:T(8,128)}), f32[8,176,256]{2,1,0:T(8,128)}, u32[]{:S(2)}, u32[]{:S(2)}) async-start(f32[8,176,256]{2,1,0:T(8,128)} %broadcast_in_dim.126), calls=%async_computation.13 | async-start | bytes 2883584 | tf_op jit(solution)/shard_map/all_to_all | solution.py:26
  729.5 4.3 copy-start.20
  751.0 4.0 copy-start.12
  752.5 2.5 copy-start.3
Sparse Core Ops, SparseCore 0:
  69.0 109.5 all-reduce.2

commit v8 on v7

--- a/solution.py
+++ b/solution.py
@@ -81,7 +81,12 @@
     band_idx = jnp.arange(BAND, dtype=jnp.int32)
     width = PANELS * BAND
 
-    strip = lax.psum(jnp.where(r == 0, a[:width, :], 0.0), "row")
+    strip_parts = []
+    for k in range(PANELS):
+        rows_k = jnp.where(r == 0, a[k * BAND:(k + 1) * BAND, :], 0.0)
+        if strip_parts:
+            rows_k, _ = lax.optimization_barrier((rows_k, strip_parts[-1]))
+        strip_parts.append(lax.psum(rows_k, "row"))
     lo = BAND
     p0_own = jnp.where(row_pos[:, None] >= lo, a[:, :BAND], 0.0)
     own = jnp.concatenate([mm_tn(p0_own, p0_own), jnp.where(r == 0, a[lo:lo + BAND, :BAND], 0.0)], axis=0)
@@ -91,7 +96,7 @@
     gram0, top0 = summed[:BAND], summed[BAND:]
     colb = comm.broadcast(a[:, :width], "col", cols, 0)
     p0 = jnp.where(row_pos[:, None] >= lo, colb[:, :BAND], 0.0)
-    strip_t = strip.T
+    strip_t = [part.T for part in strip_parts]
 
     stored = []
     current = a
@@ -101,11 +106,11 @@
         if k == 0:
             gram, top = gram0, top0
             pr = p0
-            pc = jnp.where(col_pos[:, None] >= lo, strip_t[:, :BAND], 0.0)
+            pc = jnp.where(col_pos[:, None] >= lo, strip_t[0], 0.0)
         else:
             y_r0, w_r0, y_c0, w_c0, y_e0, w_e0 = prev
             pr = colb[:, k * BAND:(k + 1) * BAND] - mm_nt(y_r0, w_e0) - mm_nt(w_r0, y_e0)
-            pc = strip_t[:, k * BAND:(k + 1) * BAND] - mm_nt(y_c0, w_e0) - mm_nt(w_c0, y_e0)
+            pc = strip_t[k] - mm_nt(y_c0, w_e0) - mm_nt(w_c0, y_e0)
             pr = jnp.where(row_pos[:, None] >= lo, pr, 0.0)
             pc = jnp.where(col_pos[:, None] >= lo, pc, 0.0)
             top_part = jnp.where(c == 0, pc[lo:lo + BAND], 0.0)
@@ -125,7 +130,7 @@
         parts = [xp, summed_c[col_count:]]
         if k + 1 < PANELS:
             nlo = (k + 1) * BAND
-            parts.append(mm_tn(strip_t[:, nlo:nlo + BAND], y_c))
+            parts.append(mm_tn(strip_t[k + 1], y_c))
         summed = comm.psum(jnp.concatenate(parts, axis=0), "col", cols)
         x_r = summed[:row_count]
         curv = summed[row_count:row_count + BAND]

time: 793 us -> 826 us (1.042)
  waiting for transfers between devices: 67.9 us -> 142 us
  blocking collectives: 74 us -> 36.9 us
    psum x1 -> x2, waiting for transfers between devices: 23.7 us -> 87.2 us  [body(): strip_parts.append(lax.psum(rows_k, 'row'))]
    all_to_all x2 -> x1, blocking collectives: 74 us -> 36.9 us  [a2a(): return lax.all_to_all(x, axis, 0, 0, tiled=False)]
    all_to_all x12 -> x13, waiting for transfers between devices: 44.2 us -> 55.1 us  [a2a(): return lax.all_to_all(x, axis, 0, 0, tiled=False)]
    all_to_all x12 -> x13, starting transfers between devices: 72.9 us -> 75.9 us  [a2a(): return lax.all_to_all(x, axis, 0, 0, tiled=False)]
    unnamed x91 -> x92, local copies, waits for them, and re-layouts: 18.8 us -> 16.4 us
  transfers between devices with their start and end apart: 13 -> 15, of which waited for: 6 -> 7; matrix products, arithmetic and copies ran while one was open for 39% -> 39% of each run, Pallas kernels for 0% -> 0%
where the time goes in v8:
time: 826 us; the launch traced here: 818 us
  other arithmetic  277 us (34%)
  matrix products  178 us (22%)
  waiting for transfers between devices  142 us (17%)
  local copies, waits for them, and re-layouts  86.9 us (11%)
  starting transfers between devices  76 us (9%)
  blocking collectives  36.9 us (4%)
  between operations  20.6 us (2%)
    dot_general x23, matrix products, mm_nt(): return lax.dot_general(a, b, (((1,), (1,)), ((), ())), precision=precision)  87.9 us
    psum x2, waiting for transfers between devices, body(): strip_parts.append(lax.psum(rows_k, 'row'))  87.2 us
    another operation x14, other arithmetic, small_factors(): second = jnp.linalg.cholesky(mm_nt(shifted, shifted))  85 us
    another operation x14, other arithmetic, small_factors(): low = jnp.linalg.cholesky(gram)  76.7 us
    all_to_all x13, starting transfers between devices, a2a(): return lax.all_to_all(x, axis, 0, 0, tiled=False)  75.9 us
    all_to_all x13, waiting for transfers between devices, a2a(): return lax.all_to_all(x, axis, 0, 0, tiled=False)  55.1 us
    another operation x5, other arithmetic, small_factors(): low_inv = jax.scipy.linalg.solve_triangular(low, identity, lower=True)  42.5 us
    another operation x4, other arithmetic, small_factors(): second_inv = jax.scipy.linalg.solve_triangular(second, identity, lower=True)  42.5 us
  transfers between devices with their start and end apart: 15, of which 7 were waited for; matrix products, arithmetic and copies ran while one was open for 39% of the time, Pallas kernels for 0%

profile of v8, /device:TPU:1, one launch (start us, length us, event | category | flops | bytes accessed | tf_op | source)
XLA Modules:
  0.0 818.0 jit_solution(10016340551703590228)
XLA Ops:
  8.7 4.2 fusion.16
  13.7 11.5 %all-to-all-start.2 = ((f32[128,1,8,128]{3,2,1,0:T(8,128)}), f32[128,1,8,128]{3,2,1,0:T(8,128)S(1)}, u32[]{:S(2)}, u32[]{:S(2)}) async-start(f32[128,1,8,128]{3,2,1,0:T(8,128)} %bitcast.3), calls=%async_computation.2 | async-start | bytes 1048576 | tf_op jit(solution)/shard_map/all_to_all | solution.py:26
  25.2 4.9 fusion.95
  32.2 6.8 all-to-all-done.2
  40.0 4.5 all-to-all-start.3
  46.1 3.3 slice.111
  50.6 7.6 all-to-all-done.3
  58.2 4.6 all-to-all-start
  63.9 11.7 %cholesky.214 = f32[128,128]{1,0:T(8,128)S(1)} custom-call(f32[128,128]{1,0:T(8,128)S(1)} %cholesky.346), custom_call_target="Cholesky" | custom-call | tf_op jit(solution)/shard_map/jit(cholesky)/cholesky | solution.py:63
  75.7 9.8 %custom-call.17 = f32[1,128,128]{1,2,0:T(8,128)S(1)} custom-call(f32[1,128,128]{2,1,0:T(8,128)S(1)} %get-tuple-element.103), custom_call_target="InvertDiagBlocksLowerTriangular" | custom-call | tf_op jit(solution)/shard_map/jit(cholesky)/cholesky | solution.py:63
  86.0 11.7 %cholesky.231 = f32[128,128]{1,0:T(8,128)S(1)} custom-call(f32[128,128]{1,0:T(8,128)S(1)} %convolution_subtract_fusion.15), custom_call_target="Cholesky" | custom-call | tf_op jit(solution)/shard_map/jit(cholesky)/cholesky | solution.py:63
  102.3 5.2 all-to-all-start.1
  107.6 4.3 while.8
  112.0 19.7 %custom-call.18 = f32[2,128,128]{1,2,0:T(8,128)S(1)} custom-call(f32[2,128,128]{2,1,0:T(8,128)S(1)} %get-tuple-element.32), custom_call_target="InvertDiagBlocksLowerTriangular" | custom-call | tf_op jit(solution)/shard_map/jit(_solve_triangular)/triangular_solve | solution.py:64
  132.6 9.5 %all-reduce.4.cloned.1.call-done = f32[256,2304]{0,1:T(8,128)} async-done(((f32[256,2304]{0,1:T(8,128)}), f32[256,2304]{0,1:T(8,128)}) %all-reduce.4.cloned.1.call-update) | async-done | bytes 2359312 | tf_op jit(solution)/shard_map/psum | solution.py:89
  142.1 4.3 convolution_add_fusion.1
  146.5 12.8 %fusion.98 = f32[256,1152]{1,0:T(8,128)} fusion(f32[2304,256]{1,0:T(8,128)S(1)} %convolution_add_fusion.1, f32[1152,2304]{1,0:T(8,128)} %param.4), kind=kOutput, calls=%fused_computation.204 | convolution fusion | flops 4076863488 | bytes 14155776 | tf_op jit(solution)/shard_map/dot_general | solution.py:13
  162.0 7.9 convolution_bitcast_fusion
  173.0 3.6 copy.28
  176.6 4.5 all-to-all-start.4
  181.1 3.0 copy.41
  184.2 3.2 broadcast_select_fusion
  187.4 28.0 %all-to-all-done.4 = f32[16,160,256]{2,1,0:T(8,128)} async-done(((f32[16,160,256]{2,1,0:T(8,128)}), f32[16,160,256]{2,1,0:T(8,128)}, u32[]{:S(2)}, u32[]{:S(2)}) %all-to-all-start.4) | async-done | bytes 2621472 | tf_op jit(solution)/shard_map/all_to_all | solution.py:26
  220.7 7.7 all-to-all-start.5
  235.9 77.7 %all-reduce.6.cloned.1.call-done = f32[256,2304]{0,1:T(8,128)} async-done(((f32[256,2304]{0,1:T(8,128)}), f32[256,2304]{0,1:T(8,128)}) %all-reduce.6.cloned.1.call-update) | async-done | bytes 2359312 | tf_op jit(solution)/shard_map/psum | solution.py:89
  313.5 6.2 fusion.102
  328.6 6.1 all-to-all-start.6
  337.1 13.2 %cholesky.248 = f32[128,128]{1,0:T(8,128)} custom-call(f32[128,128]{1,0:T(8,128)} %cholesky.349), custom_call_target="Cholesky" | custom-call | tf_op jit(solution)/shard_map/jit(cholesky)/cholesky | solution.py:66
  353.9 11.3 %custom-call.19 = f32[1,128,128]{1,2,0:T(8,128)} custom-call(f32[1,128,128]{2,1,0:T(8,128)} %get-tuple-element.99), custom_call_target="InvertDiagBlocksLowerTriangular" | custom-call | tf_op jit(solution)/shard_map/jit(cholesky)/cholesky | solution.py:66
  368.6 13.2 %cholesky.265 = f32[128,128]{1,0:T(8,128)} custom-call(f32[128,128]{1,0:T(8,128)} %convolution_subtract_fusion.14), custom_call_target="Cholesky" | custom-call | tf_op jit(solution)/shard_map/jit(cholesky)/cholesky | solution.py:66
  392.8 5.3 all-to-all-start.7
  398.7 8.1 while.9
  406.8 21.1 %custom-call.20 = f32[2,128,128]{1,2,0:T(8,128)} custom-call(f32[2,128,128]{2,1,0:T(8,128)} %get-tuple-element.33), custom_call_target="InvertDiagBlocksLowerTriangular" | custom-call | tf_op jit(solution)/shard_map/jit(_solve_triangular)/triangular_solve | solution.py:67
  434.4 5.1 fusion.8
  451.8 4.0 fusion.104
  455.9 3.4 fusion.13
  459.4 12.4 %convolution_subtract_fusion.3 = f32[1152,2304]{1,0:T(8,128)} fusion(f32[1152,2304]{1,0:T(8,128)S(1)} %bitcast.218, f32[1152,256]{0,1:T(8,128)S(1)} %convolution_add_fusion.3, f32[2304,256]{1,0:T(8,128)S(1)} %fusion.2), kind=kOutput, calls=%fused_computation.11 | convolution fusion | flops 4079517696 | bytes 24772608 | tf_op jit(solution)/shard_map/dot_general | solution.py:21
  472.6 4.8 all-to-all-start.8
  477.4 3.4 fusion.5
  481.9 9.5 %convolution_subtract_fusion.2 = f32[1152,2304]{1,0:T(8,128)} fusion(f32[1152,2304]{1,0:T(8,128)} %convolution_subtract_fusion.3, f32[1152,256]{1,0:T(8,128)S(1)} %fusion.5, f32[2304,256]{1,0:T(8,128)S(1)} %convolution_add_fusion.1), kind=kOutput, calls=%fused_computation.10 | convolution fusion | flops 4079517696 | bytes 24772608 | tf_op jit(solution)/shard_map/dot_general | solution.py:21
  493.4 5.3 all-to-all-start.9
  498.7 3.3 convolution_subtract_fusion.7
  504.2 3.6 all-to-all-done.9
  512.7 13.2 %cholesky.282 = f32[128,128]{1,0:T(8,128)} custom-call(f32[128,128]{1,0:T(8,128)} %cholesky.352), custom_call_target="Cholesky" | custom-call | tf_op jit(solution)/shard_map/jit(cholesky)/cholesky | solution.py:63
  528.9 11.3 %custom-call.21 = f32[1,128,128]{1,2,0:T(8,128)} custom-call(f32[1,128,128]{2,1,0:T(8,128)} %get-tuple-element.95), custom_call_target="InvertDiagBlocksLowerTriangular" | custom-call | tf_op jit(solution)/shard_map/jit(cholesky)/cholesky | solution.py:63
  543.7 13.3 %cholesky.299 = f32[128,128]{1,0:T(8,128)} custom-call(f32[128,128]{1,0:T(8,128)} %convolution_subtract_fusion.13), custom_call_target="Cholesky" | custom-call | tf_op jit(solution)/shard_map/jit(cholesky)/cholesky | solution.py:63
  563.3 8.2 %while.10 = (s32[]{:T(128)}, f32[256,256]{1,0:T(8,128)}, s32[2,2]{1,0:T(2,128)}, f32[2,128,128]{2,1,0:T(8,128)}, s32[]{:T(128)}) while((s32[]{:T(128)}, f32[256,256]{1,0:T(8,128)}, s32[2,2]{1,0:T(2,128)}, f32[2,128,128]{2,1,0:T(8,128)}, s32[]{:T(128)}) %tuple.106), condition=%wide.while_cond.clone.1, body=%wide.while_body.clone.1.sunk | while | flops 2 | bytes 132705 | solution.py:64
  571.5 21.1 %custom-call.22 = f32[2,128,128]{1,2,0:T(8,128)} custom-call(f32[2,128,128]{2,1,0:T(8,128)} %get-tuple-element.34), custom_call_target="InvertDiagBlocksLowerTriangular" | custom-call | tf_op jit(solution)/shard_map/jit(_solve_triangular)/triangular_solve | solution.py:64
  599.9 12.3 %fusion.105 = f32[2304,256]{1,0:T(8,128)S(1)} fusion(f32[1152,2304]{1,0:T(8,128)} %convolution_subtract_fusion.2, f32[1152,256]{0,1:T(8,128)S(1)} %convolution_add_fusion.2), kind=kOutput, calls=%fused_computation.211 | convolution fusion | flops 4076863488 | bytes 14155776 | tf_op jit(solution)/shard_map/dot_general | solution.py:17
  612.2 4.4 fusion.106
  618.0 36.9 %all_to_all.70 = f32[16,160,256]{2,1,0:T(8,128)} all-to-all(f32[16,160,256]{2,1,0:T(8,128)S(1)} %bitcast.221), channel_id=1, replica_groups=mesh['row'=16,'col'=8] {'row'}, dimensions={0} | all-to-all | bytes 5242880 | tf_op jit(solution)/shard_map/all_to_all | solution.py:26
  660.3 4.9 all-to-all-start.11
  672.6 13.2 %cholesky.316 = f32[128,128]{1,0:T(8,128)} custom-call(f32[128,128]{1,0:T(8,128)} %cholesky.355), custom_call_target="Cholesky" | custom-call | tf_op jit(solution)/shard_map/jit(cholesky)/cholesky | solution.py:66
  688.8 11.3 %custom-call.23 = f32[1,128,128]{1,2,0:T(8,128)} custom-call(f32[1,128,128]{2,1,0:T(8,128)} %get-tuple-element.91), custom_call_target="InvertDiagBlocksLowerTriangular" | custom-call | tf_op jit(solution)/shard_map/jit(cholesky)/cholesky | solution.py:66
  703.5 13.2 %cholesky.333 = f32[128,128]{1,0:T(8,128)} custom-call(f32[128,128]{1,0:T(8,128)} %convolution_subtract_fusion.12), custom_call_target="Cholesky" | custom-call | tf_op jit(solution)/shard_map/jit(cholesky)/cholesky | solution.py:66
  721.1 6.8 all-to-all-start.12
  729.8 3.8 while.11
  733.6 19.7 %custom-call.24 = f32[2,128,128]{1,2,0:T(8,128)S(1)} custom-call(f32[2,128,128]{2,1,0:T(8,128)S(1)} %get-tuple-element.35), custom_call_target="InvertDiagBlocksLowerTriangular" | custom-call | tf_op jit(solution)/shard_map/jit(_solve_triangular)/triangular_solve | solution.py:67
  757.7 4.8 all-to-all-start.13
  762.8 3.1 copy.36
  767.7 5.2 fusion.6
  772.9 9.0 %all-to-all-done.13 = f32[8,176,256]{2,1,0:T(8,128)} async-done(((f32[8,176,256]{2,1,0:T(8,128)}), f32[8,176,256]{2,1,0:T(8,128)}, u32[]{:S(2)}, u32[]{:S(2)}) %all-to-all-start.13) | async-done | bytes 1441824 | tf_op jit(solution)/shard_map/all_to_all | solution.py:26
  790.5 12.8 %convolution_subtract_fusion.1 = f32[1152,2304]{1,0:T(8,128)S(1)} fusion(f32[1152,2304]{1,0:T(8,128)} %convolution_subtract_fusion.2, f32[1152,256]{0,1:T(8,128)S(1)} %convolution_add_fusion.2, f32[2304,256]{1,0:T(8,128)S(1)} %fusion), kind=kOutput, calls=%fused_computation.9 | convolution fusion | flops 4079517696 | bytes 24772608 | tf_op jit(solution)/shard_map/dot_general | solution.py:21
  803.3 7.6 convolution_subtract_fusion
  (256 shorter events, 174.2 us)
Async XLA Ops:
  13.7 25.2 %all-to-all-start.2 = ((f32[128,1,8,128]{3,2,1,0:T(8,128)}), f32[128,1,8,128]{3,2,1,0:T(8,128)S(1)}, u32[]{:S(2)}, u32[]{:S(2)}) async-start(f32[128,1,8,128]{3,2,1,0:T(8,128)} %bitcast.3), calls=%async_computation.2 | async-start | bytes 1048576 | tf_op jit(solution)/shard_map/all_to_all | solution.py:26
  40.0 18.2 %all-to-all-start.3 = ((f32[128,1,8,128]{3,2,1,0:T(8,128)}), f32[128,1,8,128]{3,2,1,0:T(8,128)S(1)}, u32[]{:S(2)}, u32[]{:S(2)}) async-start(f32[128,1,8,128]{3,2,1,0:T(8,128)} %broadcast_in_dim.117), calls=%async_computation.3 | async-start | bytes 1048576 | tf_op jit(solution)/shard_map/all_to_all | solution.py:26
  44.5 97.6 %all-reduce.4.cloned.1.call-start = ((), (), s32[]{:S(2)}) async-start(), calls=%async_computation.14 | async-start | bytes 4718592 | tf_op jit(solution)/shard_map/psum | solution.py:89
  58.2 42.4 %all-to-all-start = ((f32[8,144,512]{2,1,0:T(8,128)}), f32[8,144,512]{2,1,0:T(8,128)S(1)}, u32[]{:S(2)}, u32[]{:S(2)}) async-start(f32[8,144,512]{2,1,0:T(8,128)} %bitcast), calls=%async_computation | async-start | bytes 4718592 | tf_op jit(solution)/shard_map/all_to_all | solution.py:26
  62.8 69.1 %copy-start.15 = (f32[256,256]{1,0:T(8,128)}, f32[256,256]{1,0:T(8,128)S(1)}, u32[]{:S(2)}) copy-start(f32[256,256]{1,0:T(8,128)S(1)} %fusion.43) | copy-start | bytes 786436
  102.3 39.8 %copy-start.34 = (pred[2304]{0:T(1024)(128)(4,1)S(1)}, pred[2304]{0:T(1024)(128)(4,1)}, u32[]{:S(2)}) copy-start(pred[2304]{0:T(1024)(128)(4,1)} %fusion.75) | copy-start | bytes 6916
  102.3 56.9 %all-to-all-start.1 = ((f32[8,144,512]{2,1,0:T(8,128)}), f32[8,144,512]{2,1,0:T(8,128)}, u32[]{:S(2)}, u32[]{:S(2)}) async-start(f32[8,144,512]{2,1,0:T(8,128)} %broadcast_in_dim.113), calls=%async_computation.1 | async-start | bytes 4718592 | tf_op jit(solution)/shard_map/all_to_all | solution.py:26
  112.0 19.7 %copy-start.36 = (s32[2,2]{1,0:T(2,128)}, s32[2,2]{1,0:T(2,128)S(1)}, u32[]{:S(2)}) copy-start(s32[2,2]{1,0:T(2,128)S(1)} %get-tuple-element.326) | copy-start | bytes 52
  132.0 14.5 %copy-start.21 = (f32[128,256]{1,0:T(8,128)}, f32[128,256]{1,0:T(8,128)S(1)}, u32[]{:S(2)}) copy-start(f32[128,256]{1,0:T(8,128)S(1)} %fusion.50) | copy-start | bytes 393220
  132.6 13.9 %copy-start.26 = (f32[128,256]{1,0:T(8,128)}, f32[128,256]{1,0:T(8,128)S(1)}, u32[]{:S(2)}) copy-start(f32[128,256]{1,0:T(8,128)S(1)} %fusion.65) | copy-start | bytes 393220
  146.5 12.8 %copy-start.33 = (s32[1152]{0:T(1024)S(1)}, s32[1152]{0:T(1024)}, u32[]{:S(2)}) copy-start(s32[1152]{0:T(1024)} %fusion.78) | copy-start | bytes 13828
  162.0 8.0 copy-start.7
  176.6 38.8 %all-to-all-start.4 = ((f32[16,160,256]{2,1,0:T(8,128)}), f32[16,160,256]{2,1,0:T(8,128)}, u32[]{:S(2)}, u32[]{:S(2)}) async-start(f32[16,160,256]{2,1,0:T(8,128)} %bitcast.220), calls=%async_computation.4 | async-start | bytes 5242880 | tf_op jit(solution)/shard_map/all_to_all | solution.py:26
  181.1 132.4 %all-reduce.6.cloned.1.call-start = ((), (), s32[]{:S(2)}) async-start(), calls=%async_computation.15 | async-start | bytes 4718592 | tf_op jit(solution)/shard_map/psum | solution.py:89
  220.7 99.0 %all-to-all-start.5 = ((f32[16,160,256]{2,1,0:T(8,128)}), f32[16,160,256]{2,1,0:T(8,128)}, u32[]{:S(2)}, u32[]{:S(2)}) async-start(f32[16,160,256]{2,1,0:T(8,128)} %broadcast_in_dim.120), calls=%async_computation.5 | async-start | bytes 5242880 | tf_op jit(solution)/shard_map/all_to_all | solution.py:26
  232.2 0.7 copy-start.4
  328.6 59.6 %all-to-all-start.6 = ((f32[8,208,256]{2,1,0:T(8,128)}), f32[8,208,256]{2,1,0:T(8,128)}, u32[]{:S(2)}, u32[]{:S(2)}) async-start(f32[8,208,256]{2,1,0:T(8,128)} %bitcast.222), calls=%async_computation.6 | async-start | bytes 3407872 | tf_op jit(solution)/shard_map/all_to_all | solution.py:26
  335.8 0.7 copy-start.29
  392.8 46.7 %all-to-all-start.7 = ((f32[8,208,256]{2,1,0:T(8,128)}), f32[8,208,256]{2,1,0:T(8,128)}, u32[]{:S(2)}, u32[]{:S(2)}) async-start(f32[8,208,256]{2,1,0:T(8,128)} %broadcast_in_dim.121), calls=%async_computation.7 | async-start | bytes 3407872 | tf_op jit(solution)/shard_map/all_to_all | solution.py:26
  433.7 0.7 copy-start.10
  439.5 4.4 copy-start.5
  439.5 5.1 copy-start.14
  443.9 0.7 copy-start.20
  444.6 2.1 copy-start.24
  444.6 2.2 copy-start.12
  446.8 12.6 %slice-start.3 = ((s8[10616832]{0:T(1024)(128)(4,1)}), s8[4194304]{0:T(1024)(128)(4,1)S(1)}, s32[]{:S(2)}) async-start(s8[10616832]{0:T(1024)(128)(4,1)} %bitcast.217), calls=%async_computation.19 | async-start | bytes 8388608
  448.9 10.5 %slice-start.4 = ((s8[10616832]{0:T(1024)(128)(4,1)}), s8[4194304]{0:T(1024)(128)(4,1)S(1)}, s32[]{:S(2)}) async-start(s8[10616832]{0:T(1024)(128)(4,1)} %bitcast.217), calls=%async_computation.20 | async-start | bytes 8388608
  451.8 4.1 copy-start
  451.8 4.1 copy-start.11
  451.8 7.5 slice-start.5
  472.6 18.8 %all-to-all-start.8 = ((f32[8,64,256]{2,1,0:T(8,128)}), f32[8,64,256]{2,1,0:T(8,128)}, u32[]{:S(2)}, u32[]{:S(2)}) async-start(f32[8,64,256]{2,1,0:T(8,128)} %bitcast.225), calls=%async_computation.8 | async-start | bytes 1048576 | tf_op jit(solution)/shard_map/all_to_all | solution.py:26
  480.8 1.0 copy-start.8
  491.4 7.3 copy-start.25
  493.4 8.6 %copy-start.6 = (f32[256,256]{1,0:T(8,128)S(1)}, f32[256,256]{1,0:T(8,128)}, u32[]{:S(2)}) copy-start(f32[256,256]{1,0:T(8,128)} %copy-done.4) | copy-start | bytes 786436
  493.4 8.6 %copy-start.9 = (f32[1152,256]{1,0:T(8,128)S(1)}, f32[1152,256]{1,0:T(8,128)}, u32[]{:S(2)}) copy-start(f32[1152,256]{1,0:T(8,128)} %copy-done.8) | copy-start | bytes 3538948
  493.4 8.6 %copy-start.35 = (pred[1152]{0:T(1024)(128)(4,1)S(1)}, pred[1152]{0:T(1024)(128)(4,1)}, u32[]{:S(2)}) copy-start(pred[1152]{0:T(1024)(128)(4,1)} %get-tuple-element.112) | copy-start | bytes 3460
  493.4 14.4 %all-to-all-start.9 = ((f32[8,64,256]{2,1,0:T(8,128)}), f32[8,64,256]{2,1,0:T(8,128)S(1)}, u32[]{:S(2)}, u32[]{:S(2)}) async-start(f32[8,64,256]{2,1,0:T(8,128)} %broadcast_in_dim.125), calls=%async_computation.9 | async-start | bytes 1048576 | tf_op jit(solution)/shard_map/all_to_all | solution.py:26
  508.6 0.7 copy-start.23
  510.1 86.2 %copy-start.1 = (f32[2304,256]{1,0:T(8,128)S(1)}, f32[2304,256]{1,0:T(8,128)}, u32[]{:S(2)}) copy-start(f32[2304,256]{1,0:T(8,128)} %copy-done) | copy-start | bytes 7077892
  511.4 0.7 copy-start.30
  593.9 4.6 copy-start.22
  596.3 2.2 copy-start.27
  596.3 2.2 copy-start.17
  596.3 2.2 copy-start.32
  598.5 13.7 %copy-start.2 = (f32[2304,256]{1,0:T(8,128)}, f32[2304,256]{1,0:T(8,128)S(1)}, u32[]{:S(2)}) copy-start(f32[2304,256]{1,0:T(8,128)S(1)} %convolution_add_fusion) | copy-start | bytes 7077892
  598.5 13.7 %slice-start = ((s8[10616832]{0:T(1024)(128)(4,1)}), s8[4194304]{0:T(1024)(128)(4,1)S(1)}, s32[]{:S(2)}) async-start(s8[10616832]{0:T(1024)(128)(4,1)} %bitcast.215), calls=%async_computation.16 | async-start | bytes 8388608
  599.9 12.4 %slice-start.1 = ((s8[10616832]{0:T(1024)(128)(4,1)}), s8[4194304]{0:T(1024)(128)(4,1)S(1)}, s32[]{:S(2)}) async-start(s8[10616832]{0:T(1024)(128)(4,1)} %bitcast.215), calls=%async_computation.17 | async-start | bytes 8388608
  599.9 12.3 %slice-start.2 = ((s8[10616832]{0:T(1024)(128)(4,1)}), s8[2228224]{0:T(1024)(128)(4,1)S(1)}, s32[]{:S(2)}) async-start(s8[10616832]{0:T(1024)(128)(4,1)} %bitcast.215), calls=%async_computation.18 | async-start | bytes 4456448
  660.3 58.6 %all-to-all-start.11 = ((f32[16,160,256]{2,1,0:T(8,128)}), f32[16,160,256]{2,1,0:T(8,128)}, u32[]{:S(2)}, u32[]{:S(2)}) async-start(f32[16,160,256]{2,1,0:T(8,128)} %broadcast_in_dim.126), calls=%async_computation.11 | async-start | bytes 5242880 | tf_op jit(solution)/shard_map/all_to_all | solution.py:26
  666.6 0.7 copy-start.18
  671.3 0.7 copy-start.31
  721.1 8.7 %copy-start.28 = (f32[256,256]{1,0:T(8,128)S(1)}, f32[256,256]{1,0:T(8,128)}, u32[]{:S(2)}) copy-start(f32[256,256]{1,0:T(8,128)} %get-tuple-element.89) | copy-start | bytes 786436
  721.1 8.8 %copy-start.37 = (s32[2,2]{1,0:T(2,128)S(1)}, s32[2,2]{1,0:T(2,128)}, u32[]{:S(2)}) copy-start(s32[2,2]{1,0:T(2,128)} %get-tuple-element.328) | copy-start | bytes 52
  721.1 33.9 %all-to-all-start.12 = ((f32[8,176,256]{2,1,0:T(8,128)}), f32[8,176,256]{2,1,0:T(8,128)}, u32[]{:S(2)}, u32[]{:S(2)}) async-start(f32[8,176,256]{2,1,0:T(8,128)} %bitcast.223), calls=%async_computation.12 | async-start | bytes 2883584 | tf_op jit(solution)/shard_map/all_to_all | solution.py:26
  756.4 6.1 copy-start.16
  757.7 24.2 %all-to-all-start.13 = ((f32[8,176,256]{2,1,0:T(8,128)}), f32[8,176,256]{2,1,0:T(8,128)}, u32[]{:S(2)}, u32[]{:S(2)}) async-start(f32[8,176,256]{2,1,0:T(8,128)} %broadcast_in_dim.127), calls=%async_computation.13 | async-start | bytes 2883584 | tf_op jit(solution)/shard_map/all_to_all | solution.py:26
  762.8 4.3 copy-start.19
  784.3 4.0 copy-start.13
  785.8 2.5 copy-start.3
Sparse Core Ops, SparseCore 0:
  49.3 92.7 all-reduce.3
  187.6 125.9 all-reduce.5

commit v9 on v7

--- a/solution.py
+++ b/solution.py
@@ -58,13 +58,25 @@
     return jnp.concatenate([even, odd], axis=0)
 
 
+def cholesky_inverse(spd):
+    half = spd.shape[0] // 2
+    identity = jnp.eye(half, dtype=spd.dtype)
+    low11 = jnp.linalg.cholesky(spd[:half, :half])
+    inv11 = jax.scipy.linalg.solve_triangular(low11, identity, lower=True)
+    low21 = mm_nt(spd[half:, :half], inv11)
+    low22 = jnp.linalg.cholesky(spd[half:, half:] - mm_nt(low21, low21))
+    inv22 = jax.scipy.linalg.solve_triangular(low22, identity, lower=True)
+    inv21 = -mm(mm(inv22, low21), inv11)
+    upper = jnp.concatenate([inv11, jnp.zeros_like(inv11)], axis=1)
+    lower = jnp.concatenate([inv21, inv22], axis=1)
+    return jnp.concatenate([upper, lower], axis=0)
+
+
 def small_factors(gram, top):
     identity = jnp.eye(BAND, dtype=jnp.float32)
-    low = jnp.linalg.cholesky(gram)
-    low_inv = jax.scipy.linalg.solve_triangular(low, identity, lower=True)
+    low_inv = cholesky_inverse(gram)
     shifted = identity + mm_nt(top, low_inv)
-    second = jnp.linalg.cholesky(mm_nt(shifted, shifted))
-    second_inv = jax.scipy.linalg.solve_triangular(second, identity, lower=True)
+    second_inv = cholesky_inverse(mm_nt(shifted, shifted))
     transform = mm_tn(shifted, mm_tn(second_inv, second_inv))
     return low_inv, transform
 

time: 793 us -> 742 us (0.936)
  other arithmetic: 277 us -> 244 us
  blocking collectives: 74 us -> 99.1 us
  local copies, waits for them, and re-layouts: 88.6 us -> 70.9 us
  waiting for transfers between devices: 67.9 us -> 54 us
  starting transfers between devices: 73.1 us -> 60.9 us
    another operation x37 -> x40, other arithmetic: 247 us -> 209 us  [the longest x12 56.5 us: cholesky_inverse(): low11 = jnp.linalg.cholesky(spd[:half, :half])]
    another operation x37 -> x4, local copies, waits for them, and re-layouts: 32.2 us -> 3.91 us  [cholesky_inverse(): inv22 = jax.scipy.linalg.solve_triangular(low22, identity, lower=True)]
    all_to_all x2 -> x3, blocking collectives: 74 us -> 99.1 us  [a2a(): return lax.all_to_all(x, axis, 0, 0, tiled=False)]
    all_to_all x12 -> x11, waiting for transfers between devices: 44.2 us -> 24.4 us  [a2a(): return lax.all_to_all(x, axis, 0, 0, tiled=False)]
    another operation x20 -> x8, matrix products: 20.4 us -> 7.64 us  [the longest x4 4.28 us: cholesky_inverse(): inv11 = jax.scipy.linalg.solve_triangular(low11, identity, lower=True)]
    all_to_all x12 -> x11, starting transfers between devices: 72.9 us -> 60.8 us  [a2a(): return lax.all_to_all(x, axis, 0, 0, tiled=False)]
    unnamed x91 -> x99, local copies, waits for them, and re-layouts: 18.8 us -> 28.6 us
    dot_general x23 -> x31, matrix products: 89.8 us -> 97.6 us  [mm_nt(): return lax.dot_general(a, b, (((1,), (1,)), ((), ())), precision=precision)]
  transfers between devices with their start and end apart: 13 -> 12, of which waited for: 6 -> 5; matrix products, arithmetic and copies ran while one was open for 39% -> 37% of each run, Pallas kernels for 0% -> 0%
where the time goes in v9:
time: 742 us; the launch traced here: 730 us
  other arithmetic  244 us (33%)
  matrix products  186 us (25%)
  blocking collectives  99.1 us (13%)
  local copies, waits for them, and re-layouts  70.9 us (10%)
  starting transfers between devices  60.9 us (8%)
  waiting for transfers between devices  54 us (7%)
  between operations  15.7 us (2%)
    all_to_all x3, blocking collectives, a2a(): return lax.all_to_all(x, axis, 0, 0, tiled=False)  99.1 us
    dot_general x31, matrix products, mm_nt(): return lax.dot_general(a, b, (((1,), (1,)), ((), ())), precision=precision)  97.6 us
    all_to_all x11, starting transfers between devices, a2a(): return lax.all_to_all(x, axis, 0, 0, tiled=False)  60.8 us
    another operation x12, other arithmetic, cholesky_inverse(): low11 = jnp.linalg.cholesky(spd[:half, :half])  56.5 us
    another operation x12, other arithmetic, cholesky_inverse(): low22 = jnp.linalg.cholesky(spd[half:, half:] - mm_nt(low21, low21))  54.5 us
    another operation x8, other arithmetic, cholesky_inverse(): inv11 = jax.scipy.linalg.solve_triangular(low11, identity, lower=True)  50.6 us
    another operation x8, other arithmetic, cholesky_inverse(): inv22 = jax.scipy.linalg.solve_triangular(low22, identity, lower=True)  47.6 us
    dot_general x11, matrix products, mm_tn(): return lax.dot_general(a, b, (((0,), (0,)), ((), ())), precision=precision)  44.4 us
  transfers between devices with their start and end apart: 12, of which 5 were waited for; matrix products, arithmetic and copies ran while one was open for 37% of the time, Pallas kernels for 0%

profile of v9, /device:TPU:1, one launch (start us, length us, event | category | flops | bytes accessed | tf_op | source)
XLA Modules:
  0.0 730.1 jit_solution(10430769238416043153)
XLA Ops:
  7.7 4.2 fusion.17
  13.0 25.0 %all_to_all.70 = f32[128,1,8,128]{3,2,1,0:T(8,128)S(1)} all-to-all(f32[128,1,8,128]{3,2,1,0:T(8,128)S(1)} %bitcast.201), channel_id=1, replica_groups=mesh['row'=16,'col'=8] {'row','col'}, dimensions={0} | all-to-all | bytes 1048576 | tf_op jit(solution)/shard_map/all_to_all | solution.py:26
  39.0 4.5 all-to-all-start.3
  43.5 4.8 slice.136
  48.3 3.3 slice.126
  51.6 6.1 copy.110
  57.7 4.8 all-to-all-start
  62.5 5.1 select_bitcast_fusion
  69.7 11.7 %cholesky.134 = f32[128,128]{1,0:T(8,128)S(1)} custom-call(f32[128,128]{1,0:T(8,128)S(1)} %get-tuple-element.21), custom_call_target="Cholesky" | custom-call | tf_op jit(solution)/shard_map/jit(cholesky)/cholesky | solution.py:64
  82.1 9.5 %all-to-all-done = f32[8,144,512]{2,1,0:T(8,128)S(1)} async-done(((f32[8,144,512]{2,1,0:T(8,128)}), f32[8,144,512]{2,1,0:T(8,128)S(1)}, u32[]{:S(2)}, u32[]{:S(2)}) %all-to-all-start) | async-done | bytes 2359328 | tf_op jit(solution)/shard_map/all_to_all | solution.py:26
  93.4 4.5 all-to-all-start.1
  98.5 9.8 %custom-call.12 = f32[1,128,128]{1,2,0:T(8,128)S(1)} custom-call(f32[1,128,128]{2,1,0:T(8,128)S(1)} %fusion.62), custom_call_target="InvertDiagBlocksLowerTriangular" | custom-call | tf_op jit(solution)/shard_map/jit(_solve_triangular)/triangular_solve | solution.py:65
  109.4 11.7 %cholesky.145 = f32[128,128]{1,0:T(8,128)S(1)} custom-call(f32[128,128]{1,0:T(8,128)S(1)} %fusion.91), custom_call_target="Cholesky" | custom-call | tf_op jit(solution)/shard_map/jit(cholesky)/cholesky | solution.py:67
  122.3 9.8 %custom-call.13 = f32[1,128,128]{1,2,0:T(8,128)S(1)} custom-call(f32[1,128,128]{2,1,0:T(8,128)S(1)} %fusion.63), custom_call_target="InvertDiagBlocksLowerTriangular" | custom-call | tf_op jit(solution)/shard_map/jit(_solve_triangular)/triangular_solve | solution.py:68
  136.8 11.0 %convolution_bitcast_fusion = f32[2304,256]{0,1:T(8,128)} fusion(f32[1152,256]{0,1:T(8,128)S(1)} %convolution_add_fusion.3, f32[1152,2304]{1,0:T(8,128)} %param.4), kind=kOutput, calls=%fused_computation.14 | convolution fusion | flops 4076863488 | bytes 14155776 | tf_op jit(solution)/shard_map/dot_general | solution.py:17
  147.8 29.6 %all-reduce.6.cloned.1.call-done = f32[2304,512]{1,0:T(8,128)} async-done(((f32[2304,512]{1,0:T(8,128)}), f32[2304,512]{1,0:T(8,128)}) %all-reduce.6.cloned.1.call-update) | async-done | bytes 4718608 | tf_op jit(solution)/shard_map/psum | solution.py:96
  177.4 4.4 convolution_add_fusion.1
  181.7 11.9 %fusion.134 = f32[256,1152]{1,0:T(8,128)S(1)} fusion(f32[2304,256]{1,0:T(8,128)S(1)} %convolution_add_fusion.1, f32[1152,2304]{1,0:T(8,128)} %param.4), kind=kOutput, calls=%fused_computation.221 | convolution fusion | flops 4076863488 | bytes 14155776 | tf_op jit(solution)/shard_map/dot_general | solution.py:13
  198.2 3.2 copy.72
  201.5 37.4 %all_to_all.71 = f32[16,160,256]{2,1,0:T(8,128)} all-to-all(f32[16,160,256]{2,1,0:T(8,128)} %bitcast.195), channel_id=1, replica_groups=mesh['row'=16,'col'=8] {'row'}, dimensions={0} | all-to-all | bytes 5242880 | tf_op jit(solution)/shard_map/all_to_all | solution.py:26
  241.5 2.7 broadcast_in_dim.120
  244.1 4.9 all-to-all-start.5
  258.3 13.2 %cholesky.156 = f32[128,128]{1,0:T(8,128)} custom-call(f32[128,128]{1,0:T(8,128)} %get-tuple-element.19), custom_call_target="Cholesky" | custom-call | tf_op jit(solution)/shard_map/jit(cholesky)/cholesky | solution.py:64
  271.5 6.2 fusion.10
  283.0 2.7 pad_maximum_fusion.3
  285.8 2.7 copy.82
  288.4 10.6 %all-to-all-start.6 = ((f32[8,208,256]{2,1,0:T(8,128)}), f32[8,208,256]{2,1,0:T(8,128)}, u32[]{:S(2)}, u32[]{:S(2)}) async-start(f32[8,208,256]{2,1,0:T(8,128)} %bitcast.198), calls=%async_computation.6 | async-start | bytes 3407872 | tf_op jit(solution)/shard_map/all_to_all | solution.py:26
  302.7 11.3 %custom-call.14 = f32[1,128,128]{1,2,0:T(8,128)} custom-call(f32[1,128,128]{2,1,0:T(8,128)} %fusion.64), custom_call_target="InvertDiagBlocksLowerTriangular" | custom-call | tf_op jit(solution)/shard_map/jit(_solve_triangular)/triangular_solve | solution.py:65
  323.8 13.2 %cholesky.167 = f32[128,128]{1,0:T(8,128)} custom-call(f32[128,128]{1,0:T(8,128)} %fusion.87), custom_call_target="Cholesky" | custom-call | tf_op jit(solution)/shard_map/jit(cholesky)/cholesky | solution.py:67
  343.0 5.1 all-to-all-start.7
  350.2 11.3 %custom-call.15 = f32[1,128,128]{1,2,0:T(8,128)} custom-call(f32[1,128,128]{2,1,0:T(8,128)} %fusion.65), custom_call_target="InvertDiagBlocksLowerTriangular" | custom-call | tf_op jit(solution)/shard_map/jit(_solve_triangular)/triangular_solve | solution.py:68
  370.7 5.1 fusion.8
  383.1 4.0 convolution_subtract_fusion.5
  387.1 3.2 fusion.1
  390.3 4.0 fusion.140
  394.4 3.4 fusion.14
  397.8 12.4 %convolution_subtract_fusion.3 = f32[1152,2304]{1,0:T(8,128)} fusion(f32[1152,2304]{1,0:T(8,128)S(1)} %bitcast.192, f32[1152,256]{0,1:T(8,128)S(1)} %convolution_add_fusion.3, f32[2304,256]{1,0:T(8,128)S(1)} %fusion.2), kind=kOutput, calls=%fused_computation.3 | convolution fusion | flops 4079517696 | bytes 24772608 | tf_op jit(solution)/shard_map/dot_general | solution.py:21
  411.1 4.8 all-to-all-start.8
  415.9 3.4 fusion.5
  420.3 9.5 %convolution_subtract_fusion.2 = f32[1152,2304]{1,0:T(8,128)} fusion(f32[1152,2304]{1,0:T(8,128)} %convolution_subtract_fusion.3, f32[1152,256]{1,0:T(8,128)S(1)} %fusion.5, f32[2304,256]{1,0:T(8,128)S(1)} %convolution_add_fusion.1), kind=kOutput, calls=%fused_computation.2 | convolution fusion | flops 4079517696 | bytes 24772608 | tf_op jit(solution)/shard_map/dot_general | solution.py:21
  431.8 5.1 all-to-all-start.9
  436.9 3.3 convolution_subtract_fusion.7
  442.4 3.9 all-to-all-done.9
  452.6 13.2 %cholesky.178 = f32[128,128]{1,0:T(8,128)} custom-call(f32[128,128]{1,0:T(8,128)} %get-tuple-element.17), custom_call_target="Cholesky" | custom-call | tf_op jit(solution)/shard_map/jit(cholesky)/cholesky | solution.py:64
  469.5 11.3 %custom-call.16 = f32[1,128,128]{1,2,0:T(8,128)} custom-call(f32[1,128,128]{2,1,0:T(8,128)} %fusion.66), custom_call_target="InvertDiagBlocksLowerTriangular" | custom-call | tf_op jit(solution)/shard_map/jit(_solve_triangular)/triangular_solve | solution.py:65
  490.7 13.4 %cholesky.189 = f32[128,128]{1,0:T(8,128)} custom-call(f32[128,128]{1,0:T(8,128)} %fusion.83), custom_call_target="Cholesky" | custom-call | tf_op jit(solution)/shard_map/jit(cholesky)/cholesky | solution.py:67
  507.7 11.3 %custom-call.17 = f32[1,128,128]{1,2,0:T(8,128)} custom-call(f32[1,128,128]{2,1,0:T(8,128)} %fusion.67), custom_call_target="InvertDiagBlocksLowerTriangular" | custom-call | tf_op jit(solution)/shard_map/jit(_solve_triangular)/triangular_solve | solution.py:68
  525.1 3.1 convolution_add_fusion
  529.6 12.5 %fusion.142 = f32[2304,256]{1,0:T(8,128)S(1)} fusion(f32[1152,2304]{1,0:T(8,128)} %convolution_subtract_fusion.2, f32[1152,256]{0,1:T(8,128)S(1)} %convolution_add_fusion.2), kind=kOutput, calls=%fused_computation.229 | convolution fusion | flops 4076863488 | bytes 14155776 | tf_op jit(solution)/shard_map/dot_general | solution.py:17
  542.1 4.4 fusion.143
  547.9 36.6 %all_to_all.72 = f32[16,160,256]{2,1,0:T(8,128)} all-to-all(f32[16,160,256]{2,1,0:T(8,128)S(1)} %bitcast.194), channel_id=1, replica_groups=mesh['row'=16,'col'=8] {'row'}, dimensions={0} | all-to-all | bytes 5242880 | tf_op jit(solution)/shard_map/all_to_all | solution.py:26
  587.1 2.7 broadcast_in_dim.125
  589.8 4.6 all-to-all-start.11
  601.5 13.2 %cholesky.200 = f32[128,128]{1,0:T(8,128)} custom-call(f32[128,128]{1,0:T(8,128)} %get-tuple-element.15), custom_call_target="Cholesky" | custom-call | tf_op jit(solution)/shard_map/jit(cholesky)/cholesky | solution.py:64
  618.3 11.3 %custom-call.18 = f32[1,128,128]{1,2,0:T(8,128)} custom-call(f32[1,128,128]{2,1,0:T(8,128)} %fusion.68), custom_call_target="InvertDiagBlocksLowerTriangular" | custom-call | tf_op jit(solution)/shard_map/jit(_solve_triangular)/triangular_solve | solution.py:65
  633.5 6.8 all-to-all-start.12
  641.9 11.7 %cholesky.211 = f32[128,128]{1,0:T(8,128)S(1)} custom-call(f32[128,128]{1,0:T(8,128)S(1)} %fusion.79), custom_call_target="Cholesky" | custom-call | tf_op jit(solution)/shard_map/jit(cholesky)/cholesky | solution.py:67
  655.1 9.8 %custom-call.19 = f32[1,128,128]{1,2,0:T(8,128)S(1)} custom-call(f32[1,128,128]{2,1,0:T(8,128)S(1)} %fusion.69), custom_call_target="InvertDiagBlocksLowerTriangular" | custom-call | tf_op jit(solution)/shard_map/jit(_solve_triangular)/triangular_solve | solution.py:68
  669.2 5.1 all-to-all-start.13
  674.7 3.1 copy.97
  679.4 5.2 fusion.6
  684.5 9.1 %all-to-all-done.13 = f32[8,176,256]{2,1,0:T(8,128)} async-done(((f32[8,176,256]{2,1,0:T(8,128)}), f32[8,176,256]{2,1,0:T(8,128)}, u32[]{:S(2)}, u32[]{:S(2)}) %all-to-all-start.13) | async-done | bytes 1441824 | tf_op jit(solution)/shard_map/all_to_all | solution.py:26
  702.2 12.9 %convolution_subtract_fusion.1 = f32[1152,2304]{1,0:T(8,128)S(1)} fusion(f32[1152,2304]{1,0:T(8,128)} %convolution_subtract_fusion.2, f32[1152,256]{0,1:T(8,128)S(1)} %convolution_add_fusion.2, f32[2304,256]{1,0:T(8,128)S(1)} %fusion), kind=kOutput, calls=%fused_computation.1 | convolution fusion | flops 4079517696 | bytes 24772608 | tf_op jit(solution)/shard_map/dot_general | solution.py:21
  715.1 7.6 %convolution_subtract_fusion = f32[1152,2304]{1,0:T(8,128)} fusion(f32[1152,2304]{1,0:T(8,128)S(1)} %convolution_subtract_fusion.1, f32[1152,256]{1,0:T(8,128)S(1)} %fusion.3, f32[2304,256]{1,0:T(8,128)S(1)} %copy-done.3), kind=kOutput, calls=%fused_computation | convolution fusion | flops 4079517696 | bytes 24772608 | tf_op jit(solution)/shard_map/dot_general | solution.py:21
  (234 shorter events, 147.4 us)
Async XLA Ops:
  39.0 18.7 %all-to-all-start.3 = ((f32[128,1,8,128]{3,2,1,0:T(8,128)}), f32[128,1,8,128]{3,2,1,0:T(8,128)S(1)}, u32[]{:S(2)}, u32[]{:S(2)}) async-start(f32[128,1,8,128]{3,2,1,0:T(8,128)} %broadcast_in_dim.116), calls=%async_computation.3 | async-start | bytes 1048576 | tf_op jit(solution)/shard_map/all_to_all | solution.py:26
  57.7 33.9 %all-to-all-start = ((f32[8,144,512]{2,1,0:T(8,128)}), f32[8,144,512]{2,1,0:T(8,128)S(1)}, u32[]{:S(2)}, u32[]{:S(2)}) async-start(f32[8,144,512]{2,1,0:T(8,128)} %bitcast), calls=%async_computation | async-start | bytes 4718592 | tf_op jit(solution)/shard_map/all_to_all | solution.py:26
  62.5 114.9 %all-reduce.6.cloned.1.call-start = ((), (), s32[]{:S(2)}) async-start(), calls=%async_computation.14 | async-start | bytes 9437184 | tf_op jit(solution)/shard_map/psum | solution.py:96
  93.4 40.9 %all-to-all-start.1 = ((f32[8,144,512]{2,1,0:T(8,128)}), f32[8,144,512]{2,1,0:T(8,128)S(1)}, u32[]{:S(2)}, u32[]{:S(2)}) async-start(f32[8,144,512]{2,1,0:T(8,128)} %broadcast_in_dim.112), calls=%async_computation.1 | async-start | bytes 4718592 | tf_op jit(solution)/shard_map/all_to_all | solution.py:26
  108.7 25.6 %copy-start.20 = (f32[128,128]{1,0:T(8,128)}, f32[128,128]{1,0:T(8,128)S(1)}, u32[]{:S(2)}) copy-start(f32[128,128]{1,0:T(8,128)S(1)} %fusion.56) | copy-start | bytes 196612
  134.3 13.5 %copy-start.15 = (f32[8,144,512]{2,1,0:T(8,128)}, f32[8,144,512]{2,1,0:T(8,128)S(1)}, u32[]{:S(2)}) copy-start(f32[8,144,512]{2,1,0:T(8,128)S(1)} %all-to-all-done.1) | copy-start | bytes 7077892
  136.8 40.6 %copy-start.36 = (pred[2304]{0:T(1024)(128)(4,1)S(1)}, pred[2304]{0:T(1024)(128)(4,1)}, u32[]{:S(2)}) copy-start(pred[2304]{0:T(1024)(128)(4,1)} %fusion.97) | copy-start | bytes 6916
  193.7 1.1 copy-start.7
  194.8 1.7 copy-start.14
  244.1 35.4 %all-to-all-start.5 = ((f32[16,160,256]{2,1,0:T(8,128)}), f32[16,160,256]{2,1,0:T(8,128)}, u32[]{:S(2)}, u32[]{:S(2)}) async-start(f32[16,160,256]{2,1,0:T(8,128)} %broadcast_in_dim.120), calls=%async_computation.5 | async-start | bytes 5242880 | tf_op jit(solution)/shard_map/all_to_all | solution.py:26
  252.8 0.7 copy-start.4
  253.9 0.7 copy-start.27
  288.4 50.1 %all-to-all-start.6 = ((f32[8,208,256]{2,1,0:T(8,128)}), f32[8,208,256]{2,1,0:T(8,128)}, u32[]{:S(2)}, u32[]{:S(2)}) async-start(f32[8,208,256]{2,1,0:T(8,128)} %bitcast.198), calls=%async_computation.6 | async-start | bytes 3407872 | tf_op jit(solution)/shard_map/all_to_all | solution.py:26
  316.6 0.6 copy-start.32
  318.4 0.6 copy-start.29
  343.0 32.8 %all-to-all-start.7 = ((f32[8,208,256]{2,1,0:T(8,128)}), f32[8,208,256]{2,1,0:T(8,128)}, u32[]{:S(2)}, u32[]{:S(2)}) async-start(f32[8,208,256]{2,1,0:T(8,128)} %broadcast_in_dim.121), calls=%async_computation.7 | async-start | bytes 3407872 | tf_op jit(solution)/shard_map/all_to_all | solution.py:26
  370.0 0.7 copy-start.10
  375.8 4.4 copy-start.5
  375.8 5.1 copy-start.13
  380.2 0.7 copy-start.19
  380.9 2.2 copy-start.23
  383.1 14.7 %slice-start.3 = ((s8[10616832]{0:T(1024)(128)(4,1)}), s8[4194304]{0:T(1024)(128)(4,1)S(1)}, s32[]{:S(2)}) async-start(s8[10616832]{0:T(1024)(128)(4,1)} %bitcast.191), calls=%async_computation.18 | async-start | bytes 8388608
  387.1 10.7 %slice-start.4 = ((s8[10616832]{0:T(1024)(128)(4,1)}), s8[4194304]{0:T(1024)(128)(4,1)S(1)}, s32[]{:S(2)}) async-start(s8[10616832]{0:T(1024)(128)(4,1)} %bitcast.191), calls=%async_computation.19 | async-start | bytes 8388608
  390.3 4.1 copy-start
  390.3 4.1 copy-start.11
  390.3 7.5 %slice-start.5 = ((s8[10616832]{0:T(1024)(128)(4,1)}), s8[2228224]{0:T(1024)(128)(4,1)S(1)}, s32[]{:S(2)}) async-start(s8[10616832]{0:T(1024)(128)(4,1)} %bitcast.191), calls=%async_computation.20 | async-start | bytes 4456448
  411.1 18.8 %all-to-all-start.8 = ((f32[8,64,256]{2,1,0:T(8,128)}), f32[8,64,256]{2,1,0:T(8,128)}, u32[]{:S(2)}, u32[]{:S(2)}) async-start(f32[8,64,256]{2,1,0:T(8,128)} %bitcast.200), calls=%async_computation.8 | async-start | bytes 1048576 | tf_op jit(solution)/shard_map/all_to_all | solution.py:26
  419.3 1.0 copy-start.8
  429.9 7.1 copy-start.24
  431.8 8.4 %copy-start.6 = (f32[256,256]{1,0:T(8,128)S(1)}, f32[256,256]{1,0:T(8,128)}, u32[]{:S(2)}) copy-start(f32[256,256]{1,0:T(8,128)} %copy-done.4) | copy-start | bytes 786436
  431.8 8.4 %copy-start.9 = (f32[1152,256]{1,0:T(8,128)S(1)}, f32[1152,256]{1,0:T(8,128)}, u32[]{:S(2)}) copy-start(f32[1152,256]{1,0:T(8,128)} %copy-done.8) | copy-start | bytes 3538948
  431.8 8.4 %copy-start.37 = (pred[1152]{0:T(1024)(128)(4,1)S(1)}, pred[1152]{0:T(1024)(128)(4,1)}, u32[]{:S(2)}) copy-start(pred[1152]{0:T(1024)(128)(4,1)} %get-tuple-element.22) | copy-start | bytes 3460
  431.8 14.5 %all-to-all-start.9 = ((f32[8,64,256]{2,1,0:T(8,128)}), f32[8,64,256]{2,1,0:T(8,128)}, u32[]{:S(2)}, u32[]{:S(2)}) async-start(f32[8,64,256]{2,1,0:T(8,128)} %broadcast_in_dim.124), calls=%async_computation.9 | async-start | bytes 1048576 | tf_op jit(solution)/shard_map/all_to_all | solution.py:26
  442.4 82.6 %copy-start.1 = (f32[2304,256]{1,0:T(8,128)S(1)}, f32[2304,256]{1,0:T(8,128)}, u32[]{:S(2)}) copy-start(f32[2304,256]{1,0:T(8,128)} %copy-done) | copy-start | bytes 7077892
  448.1 0.7 copy-start.30
  481.9 0.6 copy-start.21
  520.0 0.6 copy-start.33
  525.0 3.1 copy-start.25
  525.1 3.1 copy-start.16
  525.1 3.1 copy-start.22
  525.1 3.1 copy-start.26
  525.1 3.1 copy-start.35
  528.2 13.9 %copy-start.2 = (f32[2304,256]{1,0:T(8,128)}, f32[2304,256]{1,0:T(8,128)S(1)}, u32[]{:S(2)}) copy-start(f32[2304,256]{1,0:T(8,128)S(1)} %convolution_add_fusion) | copy-start | bytes 7077892
  528.3 13.9 %slice-start = ((s8[10616832]{0:T(1024)(128)(4,1)}), s8[4194304]{0:T(1024)(128)(4,1)S(1)}, s32[]{:S(2)}) async-start(s8[10616832]{0:T(1024)(128)(4,1)} %bitcast.189), calls=%async_computation.15 | async-start | bytes 8388608
  529.6 12.5 %slice-start.1 = ((s8[10616832]{0:T(1024)(128)(4,1)}), s8[4194304]{0:T(1024)(128)(4,1)S(1)}, s32[]{:S(2)}) async-start(s8[10616832]{0:T(1024)(128)(4,1)} %bitcast.189), calls=%async_computation.16 | async-start | bytes 8388608
  529.6 12.5 %slice-start.2 = ((s8[10616832]{0:T(1024)(128)(4,1)}), s8[2228224]{0:T(1024)(128)(4,1)S(1)}, s32[]{:S(2)}) async-start(s8[10616832]{0:T(1024)(128)(4,1)} %bitcast.189), calls=%async_computation.17 | async-start | bytes 4456448
  589.8 41.5 %all-to-all-start.11 = ((f32[16,160,256]{2,1,0:T(8,128)}), f32[16,160,256]{2,1,0:T(8,128)}, u32[]{:S(2)}, u32[]{:S(2)}) async-start(f32[16,160,256]{2,1,0:T(8,128)} %broadcast_in_dim.125), calls=%async_computation.11 | async-start | bytes 5242880 | tf_op jit(solution)/shard_map/all_to_all | solution.py:26
  595.9 0.7 copy-start.17
  597.0 0.7 copy-start.28
  633.5 6.8 copy-start.31
  633.5 7.9 %copy-start.34 = (f32[128,128]{1,0:T(8,128)S(1)}, f32[128,128]{1,0:T(8,128)}, u32[]{:S(2)}) copy-start(f32[128,128]{1,0:T(8,128)} %get-tuple-element.14) | copy-start | bytes 196612
  633.5 33.0 %all-to-all-start.12 = ((f32[8,176,256]{2,1,0:T(8,128)}), f32[8,176,256]{2,1,0:T(8,128)}, u32[]{:S(2)}, u32[]{:S(2)}) async-start(f32[8,176,256]{2,1,0:T(8,128)} %bitcast.199), calls=%async_computation.12 | async-start | bytes 2883584 | tf_op jit(solution)/shard_map/all_to_all | solution.py:26
  669.2 24.5 %all-to-all-start.13 = ((f32[8,176,256]{2,1,0:T(8,128)}), f32[8,176,256]{2,1,0:T(8,128)}, u32[]{:S(2)}, u32[]{:S(2)}) async-start(f32[8,176,256]{2,1,0:T(8,128)} %broadcast_in_dim.126), calls=%async_computation.13 | async-start | bytes 2883584 | tf_op jit(solution)/shard_map/all_to_all | solution.py:26
  674.7 4.1 copy-start.18
  696.1 4.0 copy-start.12
  697.6 2.5 copy-start.3
Sparse Core Ops, SparseCore 0:
  67.7 109.5 all-reduce.5

commit v10 on v9

--- a/solution.py
+++ b/solution.py
@@ -93,7 +93,12 @@
     band_idx = jnp.arange(BAND, dtype=jnp.int32)
     width = PANELS * BAND
 
-    strip = lax.psum(jnp.where(r == 0, a[:width, :], 0.0), "row")
+    strip_parts = []
+    for k in range(PANELS):
+        rows_k = jnp.where(r == 0, a[k * BAND:(k + 1) * BAND, :], 0.0)
+        if strip_parts:
+            rows_k, _ = lax.optimization_barrier((rows_k, strip_parts[-1]))
+        strip_parts.append(lax.psum(rows_k, "row"))
     lo = BAND
     p0_own = jnp.where(row_pos[:, None] >= lo, a[:, :BAND], 0.0)
     own = jnp.concatenate([mm_tn(p0_own, p0_own), jnp.where(r == 0, a[lo:lo + BAND, :BAND], 0.0)], axis=0)
@@ -103,7 +108,7 @@
     gram0, top0 = summed[:BAND], summed[BAND:]
     colb = comm.broadcast(a[:, :width], "col", cols, 0)
     p0 = jnp.where(row_pos[:, None] >= lo, colb[:, :BAND], 0.0)
-    strip_t = strip.T
+    strip_t = [part.T for part in strip_parts]
 
     stored = []
     current = a
@@ -113,11 +118,11 @@
         if k == 0:
             gram, top = gram0, top0
             pr = p0
-            pc = jnp.where(col_pos[:, None] >= lo, strip_t[:, :BAND], 0.0)
+            pc = jnp.where(col_pos[:, None] >= lo, strip_t[0], 0.0)
         else:
             y_r0, w_r0, y_c0, w_c0, y_e0, w_e0 = prev
             pr = colb[:, k * BAND:(k + 1) * BAND] - mm_nt(y_r0, w_e0) - mm_nt(w_r0, y_e0)
-            pc = strip_t[:, k * BAND:(k + 1) * BAND] - mm_nt(y_c0, w_e0) - mm_nt(w_c0, y_e0)
+            pc = strip_t[k] - mm_nt(y_c0, w_e0) - mm_nt(w_c0, y_e0)
             pr = jnp.where(row_pos[:, None] >= lo, pr, 0.0)
             pc = jnp.where(col_pos[:, None] >= lo, pc, 0.0)
             top_part = jnp.where(c == 0, pc[lo:lo + BAND], 0.0)
@@ -132,13 +137,13 @@
 
         xp = mm(current, y_c, FAST)
         xq = mm_tn(current, y_r, FAST)
-        summed_c = comm.psum(jnp.concatenate([xq, mm_tn(y_r, xp)], axis=0), "row", rows)
-        x_c = summed_c[:col_count]
-        parts = [xp, summed_c[col_count:]]
+        row_parts = [xq, mm_tn(y_r, xp)]
         if k + 1 < PANELS:
             nlo = (k + 1) * BAND
-            parts.append(mm_tn(strip_t[:, nlo:nlo + BAND], y_c))
-        summed = comm.psum(jnp.concatenate(parts, axis=0), "col", cols)
+            row_parts.append(mm_tn(colb[:, nlo:nlo + BAND], y_r))
+        summed_c = comm.psum(jnp.concatenate(row_parts, axis=0), "row", rows)
+        x_c = summed_c[:col_count]
+        summed = comm.psum(jnp.concatenate([xp, summed_c[col_count:col_count + BAND]], axis=0), "col", cols)
         x_r = summed[:row_count]
         curv = summed[row_count:row_count + BAND]
         middle = mm_nt(mm(transform, curv), transform)
@@ -146,7 +151,7 @@
         w_c = mm_nt(x_c, transform) - 0.5 * mm(y_c, middle)
         current = current - mm_nt(y_r, w_c, FAST) - mm_nt(w_r, y_c, FAST)
         if k + 1 < PANELS:
-            x_e = summed[row_count + BAND:]
+            x_e = summed_c[col_count + BAND:]
             y_e = mm_nt(top, low_inv) + jnp.eye(BAND, dtype=jnp.float32)
             w_e = mm_nt(x_e, transform) - 0.5 * mm(y_e, middle)
             prev = (y_r, w_r, y_c, w_c, y_e, w_e)

time: 742 us -> 775 us (1.044)
  waiting for transfers between devices: 54 us -> 109 us
  blocking collectives: 99.1 us -> 75.6 us
  starting transfers between devices: 60.9 us -> 71.6 us
    psum x1 -> x2, waiting for transfers between devices: 29.6 us -> 76 us  [body(): strip_parts.append(lax.psum(rows_k, 'row'))]
    all_to_all x3 -> x2, blocking collectives: 99.1 us -> 75.6 us  [a2a(): return lax.all_to_all(x, axis, 0, 0, tiled=False)]
    all_to_all x11 -> x12, starting transfers between devices: 60.8 us -> 71.3 us  [a2a(): return lax.all_to_all(x, axis, 0, 0, tiled=False)]
    all_to_all x11 -> x12, waiting for transfers between devices: 24.4 us -> 33.2 us  [a2a(): return lax.all_to_all(x, axis, 0, 0, tiled=False)]
    unnamed x99 -> x96, local copies, waits for them, and re-layouts: 28.6 us -> 24.7 us
  transfers between devices with their start and end apart: 12 -> 14, of which waited for: 5 -> 7; matrix products, arithmetic and copies ran while one was open for 37% -> 36% of each run, Pallas kernels for 0% -> 0%
where the time goes in v10:
time: 775 us; the launch traced here: 766 us
  other arithmetic  242 us (31%)
  matrix products  184 us (24%)
  waiting for transfers between devices  109 us (14%)
  blocking collectives  75.6 us (10%)
  starting transfers between devices  71.6 us (9%)
  local copies, waits for them, and re-layouts  67.6 us (9%)
  between operations  15.4 us (2%)
    dot_general x31, matrix products, mm_nt(): return lax.dot_general(a, b, (((1,), (1,)), ((), ())), precision=precision)  98.2 us
    psum x2, waiting for transfers between devices, body(): strip_parts.append(lax.psum(rows_k, 'row'))  76 us
    all_to_all x2, blocking collectives, a2a(): return lax.all_to_all(x, axis, 0, 0, tiled=False)  75.6 us
    all_to_all x12, starting transfers between devices, a2a(): return lax.all_to_all(x, axis, 0, 0, tiled=False)  71.3 us
    another operation x12, other arithmetic, cholesky_inverse(): low11 = jnp.linalg.cholesky(spd[:half, :half])  56.5 us
    another operation x12, other arithmetic, cholesky_inverse(): low22 = jnp.linalg.cholesky(spd[half:, half:] - mm_nt(low21, low21))  54.7 us
    another operation x8, other arithmetic, cholesky_inverse(): inv11 = jax.scipy.linalg.solve_triangular(low11, identity, lower=True)  50.5 us
    another operation x8, other arithmetic, cholesky_inverse(): inv22 = jax.scipy.linalg.solve_triangular(low22, identity, lower=True)  47.7 us
  transfers between devices with their start and end apart: 14, of which 7 were waited for; matrix products, arithmetic and copies ran while one was open for 36% of the time, Pallas kernels for 0%

profile of v10, /device:TPU:1, one launch (start us, length us, event | category | flops | bytes accessed | tf_op | source)
XLA Modules:
  0.0 766.1 jit_solution(9310200212677534395)
XLA Ops:
  7.8 4.2 fusion.16
  13.8 11.5 %all-to-all-start.2 = ((f32[128,1,8,128]{3,2,1,0:T(8,128)}), f32[128,1,8,128]{3,2,1,0:T(8,128)S(1)}, u32[]{:S(2)}, u32[]{:S(2)}) async-start(f32[128,1,8,128]{3,2,1,0:T(8,128)} %bitcast.3), calls=%async_computation.2 | async-start | bytes 1048576 | tf_op jit(solution)/shard_map/all_to_all | solution.py:26
  25.3 4.9 fusion.127
  32.2 6.8 all-to-all-done.2
  40.0 4.5 all-to-all-start.3
  46.2 3.3 slice.123
  49.5 8.8 %all-to-all-done.3 = f32[128,1,8,128]{3,2,1,0:T(8,128)S(1)} async-done(((f32[128,1,8,128]{3,2,1,0:T(8,128)}), f32[128,1,8,128]{3,2,1,0:T(8,128)S(1)}, u32[]{:S(2)}, u32[]{:S(2)}) %all-to-all-start.3) | async-done | bytes 524320 | tf_op jit(solution)/shard_map/all_to_all | solution.py:26
  58.3 4.7 all-to-all-start
  64.0 11.7 %cholesky.134 = f32[128,128]{1,0:T(8,128)S(1)} custom-call(f32[128,128]{1,0:T(8,128)S(1)} %get-tuple-element.25), custom_call_target="Cholesky" | custom-call | tf_op jit(solution)/shard_map/jit(cholesky)/cholesky | solution.py:64
  77.1 9.8 %custom-call.12 = f32[1,128,128]{1,2,0:T(8,128)S(1)} custom-call(f32[1,128,128]{2,1,0:T(8,128)S(1)} %fusion.62), custom_call_target="InvertDiagBlocksLowerTriangular" | custom-call | tf_op jit(solution)/shard_map/jit(_solve_triangular)/triangular_solve | solution.py:65
  87.9 11.7 %cholesky.145 = f32[128,128]{1,0:T(8,128)S(1)} custom-call(f32[128,128]{1,0:T(8,128)S(1)} %fusion.91), custom_call_target="Cholesky" | custom-call | tf_op jit(solution)/shard_map/jit(cholesky)/cholesky | solution.py:67
  101.4 5.4 all-to-all-start.1
  108.3 9.8 %custom-call.13 = f32[1,128,128]{1,2,0:T(8,128)S(1)} custom-call(f32[1,128,128]{2,1,0:T(8,128)S(1)} %fusion.63), custom_call_target="InvertDiagBlocksLowerTriangular" | custom-call | tf_op jit(solution)/shard_map/jit(_solve_triangular)/triangular_solve | solution.py:68
  119.0 22.9 %all-reduce.7.cloned.1.call-done = f32[256,2304]{0,1:T(8,128)} async-done(((f32[256,2304]{0,1:T(8,128)}), f32[256,2304]{0,1:T(8,128)}) %all-reduce.7.cloned.1.call-update) | async-done | bytes 2359312 | tf_op jit(solution)/shard_map/psum | solution.py:101
  141.9 4.3 convolution_add_fusion.1
  146.3 12.8 %fusion.135 = f32[256,1152]{1,0:T(8,128)} fusion(f32[2304,256]{1,0:T(8,128)S(1)} %convolution_add_fusion.1, f32[1152,2304]{1,0:T(8,128)} %param.4), kind=kOutput, calls=%fused_computation.223 | convolution fusion | flops 4076863488 | bytes 14155776 | tf_op jit(solution)/shard_map/dot_general | solution.py:13
  164.3 8.1 %convolution_bitcast_fusion = f32[2304,256]{0,1:T(8,128)S(1)} fusion(f32[1152,256]{0,1:T(8,128)S(1)} %convolution_add_fusion.3, f32[1152,2304]{1,0:T(8,128)} %param.4), kind=kOutput, calls=%fused_computation.13 | convolution fusion | flops 4076863488 | bytes 14155776 | tf_op jit(solution)/shard_map/dot_general | solution.py:17
  175.4 3.4 copy.75
  178.8 38.7 %all_to_all.70 = f32[16,176,256]{2,1,0:T(8,128)} all-to-all(f32[16,176,256]{2,1,0:T(8,128)} %bitcast.194), channel_id=1, replica_groups=mesh['row'=16,'col'=8] {'row'}, dimensions={0} | all-to-all | bytes 5767168 | tf_op jit(solution)/shard_map/all_to_all | solution.py:26
  222.9 4.5 all-to-all-start.5
  227.4 3.0 copy.117
  231.1 3.3 broadcast_select_fusion
  243.1 13.2 %cholesky.156 = f32[128,128]{1,0:T(8,128)} custom-call(f32[128,128]{1,0:T(8,128)} %get-tuple-element.23), custom_call_target="Cholesky" | custom-call | tf_op jit(solution)/shard_map/jit(cholesky)/cholesky | solution.py:64
  259.8 11.3 %custom-call.14 = f32[1,128,128]{1,2,0:T(8,128)} custom-call(f32[1,128,128]{2,1,0:T(8,128)} %fusion.64), custom_call_target="InvertDiagBlocksLowerTriangular" | custom-call | tf_op jit(solution)/shard_map/jit(_solve_triangular)/triangular_solve | solution.py:65
  280.4 2.9 copy.84
  283.3 7.6 all-to-all-start.6
  297.7 13.2 %cholesky.167 = f32[128,128]{1,0:T(8,128)} custom-call(f32[128,128]{1,0:T(8,128)} %fusion.87), custom_call_target="Cholesky" | custom-call | tf_op jit(solution)/shard_map/jit(cholesky)/cholesky | solution.py:67
  314.4 11.3 %custom-call.15 = f32[1,128,128]{1,2,0:T(8,128)} custom-call(f32[1,128,128]{2,1,0:T(8,128)} %fusion.65), custom_call_target="InvertDiagBlocksLowerTriangular" | custom-call | tf_op jit(solution)/shard_map/jit(_solve_triangular)/triangular_solve | solution.py:68
  331.8 5.3 all-to-all-start.7
  346.7 5.1 fusion.8
  351.8 4.6 all-to-all-done.7
  361.6 3.4 fusion.2
  365.0 53.0 %all-reduce.9.cloned.1.call-done = f32[2304,256]{1,0:T(8,128)} async-done(((f32[2304,256]{1,0:T(8,128)}), f32[2304,256]{1,0:T(8,128)}) %all-reduce.9.cloned.1.call-update) | async-done | bytes 2359312 | tf_op jit(solution)/shard_map/psum | solution.py:101
  418.1 4.1 convolution_subtract_fusion.5
  422.2 2.9 fusion.1
  425.1 4.0 fusion.141
  429.2 3.5 fusion.13
  432.7 12.4 %convolution_subtract_fusion.3 = f32[1152,2304]{1,0:T(8,128)} fusion(f32[1152,2304]{1,0:T(8,128)S(1)} %bitcast.193, f32[1152,256]{0,1:T(8,128)S(1)} %convolution_add_fusion.3, f32[2304,256]{1,0:T(8,128)S(1)} %copy-done.4), kind=kOutput, calls=%fused_computation.3 | convolution fusion | flops 4079517696 | bytes 24772608 | tf_op jit(solution)/shard_map/dot_general | solution.py:21
  445.9 5.9 all-to-all-start.8
  451.8 3.4 fusion.5
  456.3 9.5 %convolution_subtract_fusion.2 = f32[1152,2304]{1,0:T(8,128)} fusion(f32[1152,2304]{1,0:T(8,128)} %convolution_subtract_fusion.3, f32[1152,256]{1,0:T(8,128)S(1)} %fusion.5, f32[2304,256]{1,0:T(8,128)S(1)} %convolution_add_fusion.1), kind=kOutput, calls=%fused_computation.2 | convolution fusion | flops 4079517696 | bytes 24772608 | tf_op jit(solution)/shard_map/dot_general | solution.py:21
  467.8 5.1 all-to-all-start.9
  472.9 3.3 convolution_subtract_fusion.7
  478.4 3.9 all-to-all-done.9
  488.5 13.2 %cholesky.178 = f32[128,128]{1,0:T(8,128)} custom-call(f32[128,128]{1,0:T(8,128)} %get-tuple-element.21), custom_call_target="Cholesky" | custom-call | tf_op jit(solution)/shard_map/jit(cholesky)/cholesky | solution.py:64
  505.4 11.3 %custom-call.16 = f32[1,128,128]{1,2,0:T(8,128)} custom-call(f32[1,128,128]{2,1,0:T(8,128)} %fusion.66), custom_call_target="InvertDiagBlocksLowerTriangular" | custom-call | tf_op jit(solution)/shard_map/jit(_solve_triangular)/triangular_solve | solution.py:65
  526.6 13.6 %cholesky.189 = f32[128,128]{1,0:T(8,128)} custom-call(f32[128,128]{1,0:T(8,128)} %fusion.83), custom_call_target="Cholesky" | custom-call | tf_op jit(solution)/shard_map/jit(cholesky)/cholesky | solution.py:67
  543.8 11.3 %custom-call.17 = f32[1,128,128]{1,2,0:T(8,128)} custom-call(f32[1,128,128]{2,1,0:T(8,128)} %fusion.67), custom_call_target="InvertDiagBlocksLowerTriangular" | custom-call | tf_op jit(solution)/shard_map/jit(_solve_triangular)/triangular_solve | solution.py:68
  561.3 3.1 convolution_add_fusion
  565.8 12.3 %fusion.143 = f32[2304,256]{1,0:T(8,128)S(1)} fusion(f32[1152,2304]{1,0:T(8,128)} %convolution_subtract_fusion.2, f32[1152,256]{0,1:T(8,128)S(1)} %convolution_add_fusion.2), kind=kOutput, calls=%fused_computation.231 | convolution fusion | flops 4076863488 | bytes 14155776 | tf_op jit(solution)/shard_map/dot_general | solution.py:17
  578.1 4.4 fusion.144
  583.9 36.9 %all_to_all.71 = f32[16,160,256]{2,1,0:T(8,128)} all-to-all(f32[16,160,256]{2,1,0:T(8,128)S(1)} %bitcast.196), channel_id=1, replica_groups=mesh['row'=16,'col'=8] {'row'}, dimensions={0} | all-to-all | bytes 5242880 | tf_op jit(solution)/shard_map/all_to_all | solution.py:26
  626.1 4.7 all-to-all-start.11
  637.8 13.2 %cholesky.200 = f32[128,128]{1,0:T(8,128)} custom-call(f32[128,128]{1,0:T(8,128)} %get-tuple-element.19), custom_call_target="Cholesky" | custom-call | tf_op jit(solution)/shard_map/jit(cholesky)/cholesky | solution.py:64
  654.6 11.3 %custom-call.18 = f32[1,128,128]{1,2,0:T(8,128)} custom-call(f32[1,128,128]{2,1,0:T(8,128)} %fusion.68), custom_call_target="InvertDiagBlocksLowerTriangular" | custom-call | tf_op jit(solution)/shard_map/jit(_solve_triangular)/triangular_solve | solution.py:65
  669.8 6.9 all-to-all-start.12
  678.3 11.7 %cholesky.211 = f32[128,128]{1,0:T(8,128)S(1)} custom-call(f32[128,128]{1,0:T(8,128)S(1)} %fusion.79), custom_call_target="Cholesky" | custom-call | tf_op jit(solution)/shard_map/jit(cholesky)/cholesky | solution.py:67
  691.3 9.8 %custom-call.19 = f32[1,128,128]{1,2,0:T(8,128)S(1)} custom-call(f32[1,128,128]{2,1,0:T(8,128)S(1)} %fusion.69), custom_call_target="InvertDiagBlocksLowerTriangular" | custom-call | tf_op jit(solution)/shard_map/jit(_solve_triangular)/triangular_solve | solution.py:68
  705.4 5.3 all-to-all-start.13
  711.2 3.1 copy.100
  715.9 5.2 fusion.6
  721.0 9.1 %all-to-all-done.13 = f32[8,176,256]{2,1,0:T(8,128)} async-done(((f32[8,176,256]{2,1,0:T(8,128)}), f32[8,176,256]{2,1,0:T(8,128)}, u32[]{:S(2)}, u32[]{:S(2)}) %all-to-all-start.13) | async-done | bytes 1441824 | tf_op jit(solution)/shard_map/all_to_all | solution.py:26
  738.7 12.8 %convolution_subtract_fusion.1 = f32[1152,2304]{1,0:T(8,128)S(1)} fusion(f32[1152,2304]{1,0:T(8,128)} %convolution_subtract_fusion.2, f32[1152,256]{0,1:T(8,128)S(1)} %convolution_add_fusion.2, f32[2304,256]{1,0:T(8,128)S(1)} %fusion), kind=kOutput, calls=%fused_computation.1 | convolution fusion | flops 4079517696 | bytes 24772608 | tf_op jit(solution)/shard_map/dot_general | solution.py:21
  751.5 7.6 convolution_subtract_fusion
  (236 shorter events, 157.2 us)
Async XLA Ops:
  13.8 25.2 %all-to-all-start.2 = ((f32[128,1,8,128]{3,2,1,0:T(8,128)}), f32[128,1,8,128]{3,2,1,0:T(8,128)S(1)}, u32[]{:S(2)}, u32[]{:S(2)}) async-start(f32[128,1,8,128]{3,2,1,0:T(8,128)} %bitcast.3), calls=%async_computation.2 | async-start | bytes 1048576 | tf_op jit(solution)/shard_map/all_to_all | solution.py:26
  40.0 18.2 %all-to-all-start.3 = ((f32[128,1,8,128]{3,2,1,0:T(8,128)}), f32[128,1,8,128]{3,2,1,0:T(8,128)S(1)}, u32[]{:S(2)}, u32[]{:S(2)}) async-start(f32[128,1,8,128]{3,2,1,0:T(8,128)} %broadcast_in_dim.117), calls=%async_computation.3 | async-start | bytes 1048576 | tf_op jit(solution)/shard_map/all_to_all | solution.py:26
  44.6 97.3 %all-reduce.7.cloned.1.call-start = ((), (), s32[]{:S(2)}) async-start(), calls=%async_computation.14 | async-start | bytes 4718592 | tf_op jit(solution)/shard_map/psum | solution.py:101
  58.3 41.4 %all-to-all-start = ((f32[8,144,512]{2,1,0:T(8,128)}), f32[8,144,512]{2,1,0:T(8,128)S(1)}, u32[]{:S(2)}, u32[]{:S(2)}) async-start(f32[8,144,512]{2,1,0:T(8,128)} %bitcast), calls=%async_computation | async-start | bytes 4718592 | tf_op jit(solution)/shard_map/all_to_all | solution.py:26
  87.3 54.6 %copy-start.19 = (f32[128,128]{1,0:T(8,128)}, f32[128,128]{1,0:T(8,128)S(1)}, u32[]{:S(2)}) copy-start(f32[128,128]{1,0:T(8,128)S(1)} %fusion.56) | copy-start | bytes 196612
  101.4 57.6 %all-to-all-start.1 = ((f32[8,144,512]{2,1,0:T(8,128)}), f32[8,144,512]{2,1,0:T(8,128)}, u32[]{:S(2)}, u32[]{:S(2)}) async-start(f32[8,144,512]{2,1,0:T(8,128)} %broadcast_in_dim.113), calls=%async_computation.1 | async-start | bytes 4718592 | tf_op jit(solution)/shard_map/all_to_all | solution.py:26
  118.5 27.8 %copy-start.25 = (f32[128,128]{1,0:T(8,128)}, f32[128,128]{1,0:T(8,128)S(1)}, u32[]{:S(2)}) copy-start(f32[128,128]{1,0:T(8,128)S(1)} %copy.71) | copy-start | bytes 196612
  119.0 27.3 %copy-start.23 = (f32[128,128]{1,0:T(8,128)}, f32[128,128]{1,0:T(8,128)S(1)}, u32[]{:S(2)}) copy-start(f32[128,128]{1,0:T(8,128)S(1)} %convolution_negate_fusion.3) | copy-start | bytes 196612
  164.2 8.1 %copy-start.8 = (f32[256,1152]{1,0:T(8,128)S(1)}, f32[256,1152]{1,0:T(8,128)}, u32[]{:S(2)}) copy-start(f32[256,1152]{1,0:T(8,128)} %fusion.135) | copy-start | bytes 3538948
  222.9 51.5 %all-to-all-start.5 = ((f32[16,176,256]{2,1,0:T(8,128)}), f32[16,176,256]{2,1,0:T(8,128)}, u32[]{:S(2)}, u32[]{:S(2)}) async-start(f32[16,176,256]{2,1,0:T(8,128)} %broadcast_in_dim.120), calls=%async_computation.5 | async-start | bytes 5767168 | tf_op jit(solution)/shard_map/all_to_all | solution.py:26
  237.4 0.7 copy-start.5
  238.6 0.7 copy-start.27
  283.3 44.2 %all-to-all-start.6 = ((f32[8,176,256]{2,1,0:T(8,128)}), f32[8,176,256]{2,1,0:T(8,128)}, u32[]{:S(2)}, u32[]{:S(2)}) async-start(f32[8,176,256]{2,1,0:T(8,128)} %bitcast.198), calls=%async_computation.6 | async-start | bytes 2883584 | tf_op jit(solution)/shard_map/all_to_all | solution.py:26
  290.9 127.2 %all-reduce.9.cloned.1.call-start = ((), (), s32[]{:S(2)}) async-start(), calls=%async_computation.15 | async-start | bytes 4718592 | tf_op jit(solution)/shard_map/psum | solution.py:101
  292.3 0.6 copy-start.29
  331.8 24.6 %all-to-all-start.7 = ((f32[8,176,256]{2,1,0:T(8,128)}), f32[8,176,256]{2,1,0:T(8,128)}, u32[]{:S(2)}, u32[]{:S(2)}) async-start(f32[8,176,256]{2,1,0:T(8,128)} %broadcast_in_dim.121), calls=%async_computation.7 | async-start | bytes 2883584 | tf_op jit(solution)/shard_map/all_to_all | solution.py:26
  344.5 2.2 copy-start.11
  356.4 5.2 copy-start.14
  359.3 2.2 copy-start.18
  418.1 4.1 copy-start.4
  418.1 4.1 copy-start.6
  418.1 14.6 %slice-start.3 = ((s8[10616832]{0:T(1024)(128)(4,1)}), s8[4194304]{0:T(1024)(128)(4,1)S(1)}, s32[]{:S(2)}) async-start(s8[10616832]{0:T(1024)(128)(4,1)} %bitcast.192), calls=%async_computation.19 | async-start | bytes 8388608
  422.1 10.5 %slice-start.4 = ((s8[10616832]{0:T(1024)(128)(4,1)}), s8[4194304]{0:T(1024)(128)(4,1)S(1)}, s32[]{:S(2)}) async-start(s8[10616832]{0:T(1024)(128)(4,1)} %bitcast.192), calls=%async_computation.20 | async-start | bytes 8388608
  425.0 4.1 copy-start
  425.1 4.1 copy-start.12
  425.1 7.6 slice-start.5
  445.9 19.9 %all-to-all-start.8 = ((f32[8,64,256]{2,1,0:T(8,128)}), f32[8,64,256]{2,1,0:T(8,128)}, u32[]{:S(2)}, u32[]{:S(2)}) async-start(f32[8,64,256]{2,1,0:T(8,128)} %bitcast.200), calls=%async_computation.8 | async-start | bytes 1048576 | tf_op jit(solution)/shard_map/all_to_all | solution.py:26
  455.2 1.0 copy-start.9
  465.8 7.1 copy-start.22
  467.8 8.4 %copy-start.7 = (f32[256,256]{1,0:T(8,128)S(1)}, f32[256,256]{1,0:T(8,128)}, u32[]{:S(2)}) copy-start(f32[256,256]{1,0:T(8,128)} %copy-done.5) | copy-start | bytes 786436
  467.8 8.5 %copy-start.10 = (f32[1152,256]{1,0:T(8,128)S(1)}, f32[1152,256]{1,0:T(8,128)}, u32[]{:S(2)}) copy-start(f32[1152,256]{1,0:T(8,128)} %copy-done.9) | copy-start | bytes 3538948
  467.8 8.5 %copy-start.35 = (pred[1152]{0:T(1024)(128)(4,1)S(1)}, pred[1152]{0:T(1024)(128)(4,1)}, u32[]{:S(2)}) copy-start(pred[1152]{0:T(1024)(128)(4,1)} %get-tuple-element.26) | copy-start | bytes 3460
  467.8 14.5 %all-to-all-start.9 = ((f32[8,64,256]{2,1,0:T(8,128)}), f32[8,64,256]{2,1,0:T(8,128)}, u32[]{:S(2)}, u32[]{:S(2)}) async-start(f32[8,64,256]{2,1,0:T(8,128)} %broadcast_in_dim.125), calls=%async_computation.9 | async-start | bytes 1048576 | tf_op jit(solution)/shard_map/all_to_all | solution.py:26
  478.4 82.8 %copy-start.1 = (f32[2304,256]{1,0:T(8,128)S(1)}, f32[2304,256]{1,0:T(8,128)}, u32[]{:S(2)}) copy-start(f32[2304,256]{1,0:T(8,128)} %copy-done) | copy-start | bytes 7077892
  484.1 0.7 copy-start.30
  517.8 0.6 copy-start.20
  556.2 0.6 copy-start.32
  561.3 3.1 copy-start.24
  561.3 3.1 copy-start.15
  561.3 3.1 copy-start.21
  561.3 3.1 copy-start.26
  561.3 3.1 copy-start.34
  564.5 13.6 %copy-start.2 = (f32[2304,256]{1,0:T(8,128)}, f32[2304,256]{1,0:T(8,128)S(1)}, u32[]{:S(2)}) copy-start(f32[2304,256]{1,0:T(8,128)S(1)} %convolution_add_fusion) | copy-start | bytes 7077892
  564.5 13.6 %slice-start = ((s8[10616832]{0:T(1024)(128)(4,1)}), s8[4194304]{0:T(1024)(128)(4,1)S(1)}, s32[]{:S(2)}) async-start(s8[10616832]{0:T(1024)(128)(4,1)} %bitcast.190), calls=%async_computation.16 | async-start | bytes 8388608
  565.8 12.3 %slice-start.1 = ((s8[10616832]{0:T(1024)(128)(4,1)}), s8[4194304]{0:T(1024)(128)(4,1)S(1)}, s32[]{:S(2)}) async-start(s8[10616832]{0:T(1024)(128)(4,1)} %bitcast.190), calls=%async_computation.17 | async-start | bytes 8388608
  565.8 12.3 %slice-start.2 = ((s8[10616832]{0:T(1024)(128)(4,1)}), s8[2228224]{0:T(1024)(128)(4,1)S(1)}, s32[]{:S(2)}) async-start(s8[10616832]{0:T(1024)(128)(4,1)} %bitcast.190), calls=%async_computation.18 | async-start | bytes 4456448
  626.1 41.5 %all-to-all-start.11 = ((f32[16,160,256]{2,1,0:T(8,128)}), f32[16,160,256]{2,1,0:T(8,128)}, u32[]{:S(2)}, u32[]{:S(2)}) async-start(f32[16,160,256]{2,1,0:T(8,128)} %broadcast_in_dim.126), calls=%async_computation.11 | async-start | bytes 5242880 | tf_op jit(solution)/shard_map/all_to_all | solution.py:26
  632.2 0.7 copy-start.16
  633.3 0.7 copy-start.28
  669.8 6.9 copy-start.31
  669.8 8.0 %copy-start.33 = (f32[128,128]{1,0:T(8,128)S(1)}, f32[128,128]{1,0:T(8,128)}, u32[]{:S(2)}) copy-start(f32[128,128]{1,0:T(8,128)} %get-tuple-element.18) | copy-start | bytes 196612
  669.8 33.0 %all-to-all-start.12 = ((f32[8,176,256]{2,1,0:T(8,128)}), f32[8,176,256]{2,1,0:T(8,128)}, u32[]{:S(2)}, u32[]{:S(2)}) async-start(f32[8,176,256]{2,1,0:T(8,128)} %bitcast.199), calls=%async_computation.12 | async-start | bytes 2883584 | tf_op jit(solution)/shard_map/all_to_all | solution.py:26
  705.4 24.7 %all-to-all-start.13 = ((f32[8,176,256]{2,1,0:T(8,128)}), f32[8,176,256]{2,1,0:T(8,128)}, u32[]{:S(2)}, u32[]{:S(2)}) async-start(f32[8,176,256]{2,1,0:T(8,128)} %broadcast_in_dim.127), calls=%async_computation.13 | async-start | bytes 2883584 | tf_op jit(solution)/shard_map/all_to_all | solution.py:26
  711.2 4.1 copy-start.17
  732.5 4.0 copy-start.13
  734.0 2.5 copy-start.3
Sparse Core Ops, SparseCore 0:
  49.4 92.5 all-reduce.6
  327.6 90.4 all-reduce.8

commit v11 on v9

--- a/solution.py
+++ b/solution.py
@@ -5,7 +5,7 @@
 
 BAND = 256
 PANELS = 2
-HIGH = lax.Precision.HIGHEST
+HIGH = lax.Precision.HIGH
 FAST = lax.Precision.HIGH
 
 

time: 742 us -> 727 us (0.980)
  matrix products: 186 us -> 165 us
    dot_general x31, matrix products: 97.6 us -> 87.9 us  [mm_nt(): return lax.dot_general(a, b, (((1,), (1,)), ((), ())), precision=precision)]
  transfers between devices with their start and end apart: 12 -> 12, of which waited for: 5 -> 5; matrix products, arithmetic and copies ran while one was open for 37% -> 36% of each run, Pallas kernels for 0% -> 0%
where the time goes in v11:
time: 727 us; the launch traced here: 716 us
  other arithmetic  244 us (34%)
  matrix products  165 us (23%)
  blocking collectives  99 us (14%)
  local copies, waits for them, and re-layouts  71.7 us (10%)
  starting transfers between devices  61.4 us (8%)
  waiting for transfers between devices  59.2 us (8%)
  between operations  15.4 us (2%)
    all_to_all x3, blocking collectives, a2a(): return lax.all_to_all(x, axis, 0, 0, tiled=False)  99 us
    dot_general x31, matrix products, mm_nt(): return lax.dot_general(a, b, (((1,), (1,)), ((), ())), precision=precision)  87.9 us
    all_to_all x11, starting transfers between devices, a2a(): return lax.all_to_all(x, axis, 0, 0, tiled=False)  61.4 us
    another operation x12, other arithmetic, cholesky_inverse(): low11 = jnp.linalg.cholesky(spd[:half, :half])  56.5 us
    another operation x12, other arithmetic, cholesky_inverse(): low22 = jnp.linalg.cholesky(spd[half:, half:] - mm_nt(low21, low21))  54.4 us
    another operation x8, other arithmetic, cholesky_inverse(): inv11 = jax.scipy.linalg.solve_triangular(low11, identity, lower=True)  50.6 us
    another operation x8, other arithmetic, cholesky_inverse(): inv22 = jax.scipy.linalg.solve_triangular(low22, identity, lower=True)  47.6 us
    dot_general x11, matrix products, mm_tn(): return lax.dot_general(a, b, (((0,), (0,)), ((), ())), precision=precision)  38.1 us
  transfers between devices with their start and end apart: 12, of which 5 were waited for; matrix products, arithmetic and copies ran while one was open for 36% of the time, Pallas kernels for 0%

profile of v11, /device:TPU:1, one launch (start us, length us, event | category | flops | bytes accessed | tf_op | source)
XLA Modules:
  0.0 715.8 jit_solution(14840188445179915886)
XLA Ops:
  7.7 3.2 fusion.17
  12.1 25.0 %all_to_all.70 = f32[128,1,8,128]{3,2,1,0:T(8,128)S(1)} all-to-all(f32[128,1,8,128]{3,2,1,0:T(8,128)S(1)} %bitcast.201), channel_id=1, replica_groups=mesh['row'=16,'col'=8] {'row','col'}, dimensions={0} | all-to-all | bytes 1048576 | tf_op jit(solution)/shard_map/all_to_all | solution.py:26
  38.1 4.5 all-to-all-start.3
  42.6 4.8 slice.136
  47.4 3.3 slice.126
  50.7 6.1 copy.110
  56.7 4.8 all-to-all-start
  61.5 5.1 select_bitcast_fusion
  68.8 11.7 %cholesky.134 = f32[128,128]{1,0:T(8,128)S(1)} custom-call(f32[128,128]{1,0:T(8,128)S(1)} %get-tuple-element.21), custom_call_target="Cholesky" | custom-call | tf_op jit(solution)/shard_map/jit(cholesky)/cholesky | solution.py:64
  81.2 9.5 %all-to-all-done = f32[8,144,512]{2,1,0:T(8,128)S(1)} async-done(((f32[8,144,512]{2,1,0:T(8,128)}), f32[8,144,512]{2,1,0:T(8,128)S(1)}, u32[]{:S(2)}, u32[]{:S(2)}) %all-to-all-start) | async-done | bytes 2359328 | tf_op jit(solution)/shard_map/all_to_all | solution.py:26
  92.4 4.5 all-to-all-start.1
  97.6 9.8 %custom-call.12 = f32[1,128,128]{1,2,0:T(8,128)S(1)} custom-call(f32[1,128,128]{2,1,0:T(8,128)S(1)} %fusion.62), custom_call_target="InvertDiagBlocksLowerTriangular" | custom-call | tf_op jit(solution)/shard_map/jit(_solve_triangular)/triangular_solve | solution.py:65
  108.3 11.7 %cholesky.145 = f32[128,128]{1,0:T(8,128)S(1)} custom-call(f32[128,128]{1,0:T(8,128)S(1)} %fusion.91), custom_call_target="Cholesky" | custom-call | tf_op jit(solution)/shard_map/jit(cholesky)/cholesky | solution.py:67
  121.3 9.8 %custom-call.13 = f32[1,128,128]{1,2,0:T(8,128)S(1)} custom-call(f32[1,128,128]{2,1,0:T(8,128)S(1)} %fusion.63), custom_call_target="InvertDiagBlocksLowerTriangular" | custom-call | tf_op jit(solution)/shard_map/jit(_solve_triangular)/triangular_solve | solution.py:68
  135.1 11.0 %convolution_bitcast_fusion = f32[2304,256]{0,1:T(8,128)} fusion(f32[1152,256]{0,1:T(8,128)S(1)} %convolution_add_fusion.3, f32[1152,2304]{1,0:T(8,128)} %param.4), kind=kOutput, calls=%fused_computation.14 | convolution fusion | flops 4076863488 | bytes 14155776 | tf_op jit(solution)/shard_map/dot_general | solution.py:17
  146.1 30.2 %all-reduce.6.cloned.1.call-done = f32[2304,512]{1,0:T(8,128)} async-done(((f32[2304,512]{1,0:T(8,128)}), f32[2304,512]{1,0:T(8,128)}) %all-reduce.6.cloned.1.call-update) | async-done | bytes 4718608 | tf_op jit(solution)/shard_map/psum | solution.py:96
  176.3 4.0 convolution_add_fusion.1
  180.3 11.9 %fusion.134 = f32[256,1152]{1,0:T(8,128)S(1)} fusion(f32[2304,256]{1,0:T(8,128)S(1)} %convolution_add_fusion.1, f32[1152,2304]{1,0:T(8,128)} %param.4), kind=kOutput, calls=%fused_computation.221 | convolution fusion | flops 4076863488 | bytes 14155776 | tf_op jit(solution)/shard_map/dot_general | solution.py:13
  196.8 3.2 copy.72
  200.0 37.4 %all_to_all.71 = f32[16,160,256]{2,1,0:T(8,128)} all-to-all(f32[16,160,256]{2,1,0:T(8,128)} %bitcast.195), channel_id=1, replica_groups=mesh['row'=16,'col'=8] {'row'}, dimensions={0} | all-to-all | bytes 5242880 | tf_op jit(solution)/shard_map/all_to_all | solution.py:26
  237.5 2.6 reduce_sum.55
  240.0 2.7 broadcast_in_dim.120
  242.7 4.7 all-to-all-start.5
  256.6 13.2 %cholesky.156 = f32[128,128]{1,0:T(8,128)} custom-call(f32[128,128]{1,0:T(8,128)} %get-tuple-element.19), custom_call_target="Cholesky" | custom-call | tf_op jit(solution)/shard_map/jit(cholesky)/cholesky | solution.py:64
  269.8 4.4 fusion.10
  274.2 3.9 all-to-all-done.5
  281.5 2.7 pad_maximum_fusion.3
  284.2 2.7 copy.82
  286.9 10.8 %all-to-all-start.6 = ((f32[8,208,256]{2,1,0:T(8,128)}), f32[8,208,256]{2,1,0:T(8,128)}, u32[]{:S(2)}, u32[]{:S(2)}) async-start(f32[8,208,256]{2,1,0:T(8,128)} %bitcast.198), calls=%async_computation.6 | async-start | bytes 3407872 | tf_op jit(solution)/shard_map/all_to_all | solution.py:26
  301.4 11.3 %custom-call.14 = f32[1,128,128]{1,2,0:T(8,128)} custom-call(f32[1,128,128]{2,1,0:T(8,128)} %fusion.64), custom_call_target="InvertDiagBlocksLowerTriangular" | custom-call | tf_op jit(solution)/shard_map/jit(_solve_triangular)/triangular_solve | solution.py:65
  322.4 13.2 %cholesky.167 = f32[128,128]{1,0:T(8,128)} custom-call(f32[128,128]{1,0:T(8,128)} %fusion.87), custom_call_target="Cholesky" | custom-call | tf_op jit(solution)/shard_map/jit(cholesky)/cholesky | solution.py:67
  341.6 5.0 all-to-all-start.7
  348.8 11.3 %custom-call.15 = f32[1,128,128]{1,2,0:T(8,128)} custom-call(f32[1,128,128]{2,1,0:T(8,128)} %fusion.65), custom_call_target="InvertDiagBlocksLowerTriangular" | custom-call | tf_op jit(solution)/shard_map/jit(_solve_triangular)/triangular_solve | solution.py:68
  368.8 4.2 fusion.8
  379.1 3.0 convolution_subtract_fusion.5
  386.1 3.0 fusion.14
  389.1 12.6 %convolution_subtract_fusion.3 = f32[1152,2304]{1,0:T(8,128)} fusion(f32[1152,2304]{1,0:T(8,128)S(1)} %bitcast.192, f32[1152,256]{0,1:T(8,128)S(1)} %convolution_add_fusion.3, f32[2304,256]{1,0:T(8,128)S(1)} %fusion.2), kind=kOutput, calls=%fused_computation.3 | convolution fusion | flops 4079517696 | bytes 24772608 | tf_op jit(solution)/shard_map/dot_general | solution.py:21
  402.6 4.8 all-to-all-start.8
  407.4 2.5 fusion.5
  410.9 9.5 %convolution_subtract_fusion.2 = f32[1152,2304]{1,0:T(8,128)} fusion(f32[1152,2304]{1,0:T(8,128)} %convolution_subtract_fusion.3, f32[1152,256]{1,0:T(8,128)S(1)} %fusion.5, f32[2304,256]{1,0:T(8,128)S(1)} %convolution_add_fusion.1), kind=kOutput, calls=%fused_computation.2 | convolution fusion | flops 4079517696 | bytes 24772608 | tf_op jit(solution)/shard_map/dot_general | solution.py:21
  422.4 5.3 all-to-all-start.9
  427.7 2.4 convolution_subtract_fusion.7
  431.9 5.1 all-to-all-done.9
  443.1 13.2 %cholesky.178 = f32[128,128]{1,0:T(8,128)} custom-call(f32[128,128]{1,0:T(8,128)} %get-tuple-element.17), custom_call_target="Cholesky" | custom-call | tf_op jit(solution)/shard_map/jit(cholesky)/cholesky | solution.py:64
  460.1 11.3 %custom-call.16 = f32[1,128,128]{1,2,0:T(8,128)} custom-call(f32[1,128,128]{2,1,0:T(8,128)} %fusion.66), custom_call_target="InvertDiagBlocksLowerTriangular" | custom-call | tf_op jit(solution)/shard_map/jit(_solve_triangular)/triangular_solve | solution.py:65
  481.1 13.3 %cholesky.189 = f32[128,128]{1,0:T(8,128)} custom-call(f32[128,128]{1,0:T(8,128)} %fusion.83), custom_call_target="Cholesky" | custom-call | tf_op jit(solution)/shard_map/jit(cholesky)/cholesky | solution.py:67
  498.1 11.3 %custom-call.17 = f32[1,128,128]{1,2,0:T(8,128)} custom-call(f32[1,128,128]{2,1,0:T(8,128)} %fusion.67), custom_call_target="InvertDiagBlocksLowerTriangular" | custom-call | tf_op jit(solution)/shard_map/jit(_solve_triangular)/triangular_solve | solution.py:68
  518.4 12.6 %fusion.142 = f32[2304,256]{1,0:T(8,128)S(1)} fusion(f32[1152,2304]{1,0:T(8,128)} %convolution_subtract_fusion.2, f32[1152,256]{0,1:T(8,128)S(1)} %convolution_add_fusion.2), kind=kOutput, calls=%fused_computation.229 | convolution fusion | flops 4076863488 | bytes 14155776 | tf_op jit(solution)/shard_map/dot_general | solution.py:17
  531.1 4.4 fusion.143
  536.3 36.6 %all_to_all.72 = f32[16,160,256]{2,1,0:T(8,128)} all-to-all(f32[16,160,256]{2,1,0:T(8,128)S(1)} %bitcast.194), channel_id=1, replica_groups=mesh['row'=16,'col'=8] {'row'}, dimensions={0} | all-to-all | bytes 5242880 | tf_op jit(solution)/shard_map/all_to_all | solution.py:26
  572.9 2.6 reduce_sum.58
  575.5 2.7 broadcast_in_dim.125
  578.2 4.7 all-to-all-start.11
  589.8 13.2 %cholesky.200 = f32[128,128]{1,0:T(8,128)} custom-call(f32[128,128]{1,0:T(8,128)} %get-tuple-element.15), custom_call_target="Cholesky" | custom-call | tf_op jit(solution)/shard_map/jit(cholesky)/cholesky | solution.py:64
  606.6 11.3 %custom-call.18 = f32[1,128,128]{1,2,0:T(8,128)} custom-call(f32[1,128,128]{2,1,0:T(8,128)} %fusion.68), custom_call_target="InvertDiagBlocksLowerTriangular" | custom-call | tf_op jit(solution)/shard_map/jit(_solve_triangular)/triangular_solve | solution.py:65
  621.8 7.1 all-to-all-start.12
  630.4 11.7 %cholesky.211 = f32[128,128]{1,0:T(8,128)S(1)} custom-call(f32[128,128]{1,0:T(8,128)S(1)} %fusion.79), custom_call_target="Cholesky" | custom-call | tf_op jit(solution)/shard_map/jit(cholesky)/cholesky | solution.py:67
  643.5 9.8 %custom-call.19 = f32[1,128,128]{1,2,0:T(8,128)S(1)} custom-call(f32[1,128,128]{2,1,0:T(8,128)S(1)} %fusion.69), custom_call_target="InvertDiagBlocksLowerTriangular" | custom-call | tf_op jit(solution)/shard_map/jit(_solve_triangular)/triangular_solve | solution.py:68
  657.6 5.0 all-to-all-start.13
  663.1 3.1 copy.97
  667.4 4.2 fusion.6
  671.6 10.4 %all-to-all-done.13 = f32[8,176,256]{2,1,0:T(8,128)} async-done(((f32[8,176,256]{2,1,0:T(8,128)}), f32[8,176,256]{2,1,0:T(8,128)}, u32[]{:S(2)}, u32[]{:S(2)}) %all-to-all-start.13) | async-done | bytes 1441824 | tf_op jit(solution)/shard_map/all_to_all | solution.py:26
  688.3 12.6 %convolution_subtract_fusion.1 = f32[1152,2304]{1,0:T(8,128)S(1)} fusion(f32[1152,2304]{1,0:T(8,128)} %convolution_subtract_fusion.2, f32[1152,256]{0,1:T(8,128)S(1)} %convolution_add_fusion.2, f32[2304,256]{1,0:T(8,128)S(1)} %fusion), kind=kOutput, calls=%fused_computation.1 | convolution fusion | flops 4079517696 | bytes 24772608 | tf_op jit(solution)/shard_map/dot_general | solution.py:21
  700.9 7.8 %convolution_subtract_fusion = f32[1152,2304]{1,0:T(8,128)} fusion(f32[1152,2304]{1,0:T(8,128)S(1)} %convolution_subtract_fusion.1, f32[1152,256]{1,0:T(8,128)S(1)} %fusion.3, f32[2304,256]{1,0:T(8,128)S(1)} %copy-done.3), kind=kOutput, calls=%fused_computation | convolution fusion | flops 4079517696 | bytes 24772608 | tf_op jit(solution)/shard_map/dot_general | solution.py:21
  (234 shorter events, 139.2 us)
Async XLA Ops:
  38.1 18.7 %all-to-all-start.3 = ((f32[128,1,8,128]{3,2,1,0:T(8,128)}), f32[128,1,8,128]{3,2,1,0:T(8,128)S(1)}, u32[]{:S(2)}, u32[]{:S(2)}) async-start(f32[128,1,8,128]{3,2,1,0:T(8,128)} %broadcast_in_dim.116), calls=%async_computation.3 | async-start | bytes 1048576 | tf_op jit(solution)/shard_map/all_to_all | solution.py:26
  56.7 33.9 %all-to-all-start = ((f32[8,144,512]{2,1,0:T(8,128)}), f32[8,144,512]{2,1,0:T(8,128)S(1)}, u32[]{:S(2)}, u32[]{:S(2)}) async-start(f32[8,144,512]{2,1,0:T(8,128)} %bitcast), calls=%async_computation | async-start | bytes 4718592 | tf_op jit(solution)/shard_map/all_to_all | solution.py:26
  61.5 114.8 %all-reduce.6.cloned.1.call-start = ((), (), s32[]{:S(2)}) async-start(), calls=%async_computation.14 | async-start | bytes 9437184 | tf_op jit(solution)/shard_map/psum | solution.py:96
  92.4 40.7 %all-to-all-start.1 = ((f32[8,144,512]{2,1,0:T(8,128)}), f32[8,144,512]{2,1,0:T(8,128)S(1)}, u32[]{:S(2)}, u32[]{:S(2)}) async-start(f32[8,144,512]{2,1,0:T(8,128)} %broadcast_in_dim.112), calls=%async_computation.1 | async-start | bytes 4718592 | tf_op jit(solution)/shard_map/all_to_all | solution.py:26
  107.8 25.4 %copy-start.20 = (f32[128,128]{1,0:T(8,128)}, f32[128,128]{1,0:T(8,128)S(1)}, u32[]{:S(2)}) copy-start(f32[128,128]{1,0:T(8,128)S(1)} %fusion.56) | copy-start | bytes 196612
  133.2 12.9 %copy-start.15 = (f32[8,144,512]{2,1,0:T(8,128)}, f32[8,144,512]{2,1,0:T(8,128)S(1)}, u32[]{:S(2)}) copy-start(f32[8,144,512]{2,1,0:T(8,128)S(1)} %all-to-all-done.1) | copy-start | bytes 7077892
  135.1 41.2 %copy-start.36 = (pred[2304]{0:T(1024)(128)(4,1)S(1)}, pred[2304]{0:T(1024)(128)(4,1)}, u32[]{:S(2)}) copy-start(pred[2304]{0:T(1024)(128)(4,1)} %fusion.97) | copy-start | bytes 6916
  192.2 1.1 copy-start.7
  193.3 1.7 copy-start.14
  242.7 35.3 %all-to-all-start.5 = ((f32[16,160,256]{2,1,0:T(8,128)}), f32[16,160,256]{2,1,0:T(8,128)}, u32[]{:S(2)}, u32[]{:S(2)}) async-start(f32[16,160,256]{2,1,0:T(8,128)} %broadcast_in_dim.120), calls=%async_computation.5 | async-start | bytes 5242880 | tf_op jit(solution)/shard_map/all_to_all | solution.py:26
  251.1 0.7 copy-start.4
  252.2 0.7 copy-start.27
  286.9 50.2 %all-to-all-start.6 = ((f32[8,208,256]{2,1,0:T(8,128)}), f32[8,208,256]{2,1,0:T(8,128)}, u32[]{:S(2)}, u32[]{:S(2)}) async-start(f32[8,208,256]{2,1,0:T(8,128)} %bitcast.198), calls=%async_computation.6 | async-start | bytes 3407872 | tf_op jit(solution)/shard_map/all_to_all | solution.py:26
  315.3 0.6 copy-start.32
  317.0 0.6 copy-start.29
  341.6 31.4 %all-to-all-start.7 = ((f32[8,208,256]{2,1,0:T(8,128)}), f32[8,208,256]{2,1,0:T(8,128)}, u32[]{:S(2)}, u32[]{:S(2)}) async-start(f32[8,208,256]{2,1,0:T(8,128)} %broadcast_in_dim.121), calls=%async_computation.7 | async-start | bytes 3407872 | tf_op jit(solution)/shard_map/all_to_all | solution.py:26
  368.1 0.7 copy-start.10
  373.0 4.2 copy-start.5
  373.0 4.9 copy-start.13
  377.2 0.7 copy-start.19
  377.9 1.2 copy-start.23
  379.0 10.0 %slice-start.3 = ((s8[10616832]{0:T(1024)(128)(4,1)}), s8[4194304]{0:T(1024)(128)(4,1)S(1)}, s32[]{:S(2)}) async-start(s8[10616832]{0:T(1024)(128)(4,1)} %bitcast.191), calls=%async_computation.18 | async-start | bytes 8388608
  382.0 7.1 slice-start.4
  383.9 2.1 copy-start
  383.9 2.2 copy-start.11
  383.9 5.2 slice-start.5
  402.6 17.9 %all-to-all-start.8 = ((f32[8,64,256]{2,1,0:T(8,128)}), f32[8,64,256]{2,1,0:T(8,128)}, u32[]{:S(2)}, u32[]{:S(2)}) async-start(f32[8,64,256]{2,1,0:T(8,128)} %bitcast.200), calls=%async_computation.8 | async-start | bytes 1048576 | tf_op jit(solution)/shard_map/all_to_all | solution.py:26
  409.8 1.0 copy-start.8
  420.4 7.3 %copy-start.24 = (f32[256,256]{1,0:T(8,128)S(1)}, f32[256,256]{1,0:T(8,128)}, u32[]{:S(2)}) copy-start(f32[256,256]{1,0:T(8,128)} %copy-done.23) | copy-start | bytes 786436
  422.4 7.7 %copy-start.6 = (f32[256,256]{1,0:T(8,128)S(1)}, f32[256,256]{1,0:T(8,128)}, u32[]{:S(2)}) copy-start(f32[256,256]{1,0:T(8,128)} %copy-done.4) | copy-start | bytes 786436
  422.4 7.7 %copy-start.9 = (f32[1152,256]{1,0:T(8,128)S(1)}, f32[1152,256]{1,0:T(8,128)}, u32[]{:S(2)}) copy-start(f32[1152,256]{1,0:T(8,128)} %copy-done.8) | copy-start | bytes 3538948
  422.4 7.7 %copy-start.37 = (pred[1152]{0:T(1024)(128)(4,1)S(1)}, pred[1152]{0:T(1024)(128)(4,1)}, u32[]{:S(2)}) copy-start(pred[1152]{0:T(1024)(128)(4,1)} %get-tuple-element.22) | copy-start | bytes 3460
  422.4 14.5 %all-to-all-start.9 = ((f32[8,64,256]{2,1,0:T(8,128)}), f32[8,64,256]{2,1,0:T(8,128)}, u32[]{:S(2)}, u32[]{:S(2)}) async-start(f32[8,64,256]{2,1,0:T(8,128)} %broadcast_in_dim.124), calls=%async_computation.9 | async-start | bytes 1048576 | tf_op jit(solution)/shard_map/all_to_all | solution.py:26
  431.9 83.5 %copy-start.1 = (f32[2304,256]{1,0:T(8,128)S(1)}, f32[2304,256]{1,0:T(8,128)}, u32[]{:S(2)}) copy-start(f32[2304,256]{1,0:T(8,128)} %copy-done) | copy-start | bytes 7077892
  438.7 0.7 copy-start.30
  472.5 0.6 copy-start.21
  510.4 0.6 copy-start.33
  515.4 2.2 copy-start.25
  515.4 2.2 copy-start.16
  515.4 2.2 copy-start.22
  515.4 2.2 copy-start.26
  515.4 2.2 copy-start.35
  517.6 13.4 %copy-start.2 = (f32[2304,256]{1,0:T(8,128)}, f32[2304,256]{1,0:T(8,128)S(1)}, u32[]{:S(2)}) copy-start(f32[2304,256]{1,0:T(8,128)S(1)} %convolution_add_fusion) | copy-start | bytes 7077892
  517.6 13.4 %slice-start = ((s8[10616832]{0:T(1024)(128)(4,1)}), s8[4194304]{0:T(1024)(128)(4,1)S(1)}, s32[]{:S(2)}) async-start(s8[10616832]{0:T(1024)(128)(4,1)} %bitcast.189), calls=%async_computation.15 | async-start | bytes 8388608
  518.4 12.7 %slice-start.1 = ((s8[10616832]{0:T(1024)(128)(4,1)}), s8[4194304]{0:T(1024)(128)(4,1)S(1)}, s32[]{:S(2)}) async-start(s8[10616832]{0:T(1024)(128)(4,1)} %bitcast.189), calls=%async_computation.16 | async-start | bytes 8388608
  518.4 12.7 %slice-start.2 = ((s8[10616832]{0:T(1024)(128)(4,1)}), s8[2228224]{0:T(1024)(128)(4,1)S(1)}, s32[]{:S(2)}) async-start(s8[10616832]{0:T(1024)(128)(4,1)} %bitcast.189), calls=%async_computation.17 | async-start | bytes 4456448
  578.2 41.4 %all-to-all-start.11 = ((f32[16,160,256]{2,1,0:T(8,128)}), f32[16,160,256]{2,1,0:T(8,128)}, u32[]{:S(2)}, u32[]{:S(2)}) async-start(f32[16,160,256]{2,1,0:T(8,128)} %broadcast_in_dim.125), calls=%async_computation.11 | async-start | bytes 5242880 | tf_op jit(solution)/shard_map/all_to_all | solution.py:26
  584.2 0.7 copy-start.17
  585.3 0.7 copy-start.28
  621.8 7.1 copy-start.31
  621.8 8.2 %copy-start.34 = (f32[128,128]{1,0:T(8,128)S(1)}, f32[128,128]{1,0:T(8,128)}, u32[]{:S(2)}) copy-start(f32[128,128]{1,0:T(8,128)} %get-tuple-element.14) | copy-start | bytes 196612
  621.8 33.2 %all-to-all-start.12 = ((f32[8,176,256]{2,1,0:T(8,128)}), f32[8,176,256]{2,1,0:T(8,128)}, u32[]{:S(2)}, u32[]{:S(2)}) async-start(f32[8,176,256]{2,1,0:T(8,128)} %bitcast.199), calls=%async_computation.12 | async-start | bytes 2883584 | tf_op jit(solution)/shard_map/all_to_all | solution.py:26
  657.6 24.4 %all-to-all-start.13 = ((f32[8,176,256]{2,1,0:T(8,128)}), f32[8,176,256]{2,1,0:T(8,128)}, u32[]{:S(2)}, u32[]{:S(2)}) async-start(f32[8,176,256]{2,1,0:T(8,128)} %broadcast_in_dim.126), calls=%async_computation.13 | async-start | bytes 2883584 | tf_op jit(solution)/shard_map/all_to_all | solution.py:26
  663.1 3.9 copy-start.18
  684.0 2.9 copy-start.12
  685.4 1.8 copy-start.3
Sparse Core Ops, SparseCore 0:
  66.8 109.4 all-reduce.5

commit v12 on v11

--- a/solution.py
+++ b/solution.py
@@ -124,6 +124,8 @@
             summed = comm.psum(jnp.concatenate([mm_tn(pc, pc), top_part], axis=0), "col", cols)
             gram, top = summed[:BAND], summed[BAND:]
         low_inv, transform = small_factors(gram, top)
+        if k == 0:
+            low_inv, transform = lax.optimization_barrier((low_inv, transform))
         unit_r = (row_pos[:, None] - lo == band_idx[None, :]).astype(jnp.float32)
         unit_c = (col_pos[:, None] - lo == band_idx[None, :]).astype(jnp.float32)
         y_r = mm_nt(pr, low_inv) + unit_r

time: 727 us -> 711 us (0.978)
  other arithmetic: 244 us -> 231 us
  local copies, waits for them, and re-layouts: 71.7 us -> 62.1 us
  waiting for transfers between devices: 59.2 us -> 66.6 us
    all_to_all x11, waiting for transfers between devices: 28.9 us -> 66.6 us  [a2a(): return lax.all_to_all(x, axis, 0, 0, tiled=False)]
    psum x1, waiting for transfers between devices: 30.2 us -> 0.01 us  [body(): strip = lax.psum(jnp.where(r == 0, a[:width, :], 0.0), 'row')]
    unnamed x99 -> x113, local copies, waits for them, and re-layouts: 29.4 us -> 25.5 us
    dot_general x31 -> x32, matrix products: 87.9 us -> 86.2 us  [mm_nt(): return lax.dot_general(a, b, (((1,), (1,)), ((), ())), precision=precision)]
  transfers between devices with their start and end apart: 12 -> 12, of which waited for: 5 -> 7; matrix products, arithmetic and copies ran while one was open for 36% -> 33% of each run, Pallas kernels for 0% -> 0%
where the time goes in v12:
time: 711 us; the launch traced here: 704 us
  other arithmetic  231 us (32%)
  matrix products  158 us (22%)
  blocking collectives  106 us (15%)
  waiting for transfers between devices  66.6 us (9%)
  starting transfers between devices  64.9 us (9%)
  local copies, waits for them, and re-layouts  62.1 us (9%)
  between operations  15.6 us (2%)
    all_to_all x3, blocking collectives, a2a(): return lax.all_to_all(x, axis, 0, 0, tiled=False)  106 us
    dot_general x32, matrix products, mm_nt(): return lax.dot_general(a, b, (((1,), (1,)), ((), ())), precision=precision)  86.2 us
    all_to_all x11, waiting for transfers between devices, a2a(): return lax.all_to_all(x, axis, 0, 0, tiled=False)  66.6 us
    all_to_all x11, starting transfers between devices, a2a(): return lax.all_to_all(x, axis, 0, 0, tiled=False)  64.9 us
    another operation x12, other arithmetic, cholesky_inverse(): low11 = jnp.linalg.cholesky(spd[:half, :half])  54.1 us
    another operation x12, other arithmetic, cholesky_inverse(): low22 = jnp.linalg.cholesky(spd[half:, half:] - mm_nt(low21, low21))  52.2 us
    another operation x8, other arithmetic, cholesky_inverse(): inv11 = jax.scipy.linalg.solve_triangular(low11, identity, lower=True)  47.4 us
    another operation x8, other arithmetic, cholesky_inverse(): inv22 = jax.scipy.linalg.solve_triangular(low22, identity, lower=True)  44.8 us
  transfers between devices with their start and end apart: 12, of which 7 were waited for; matrix products, arithmetic and copies ran while one was open for 33% of the time, Pallas kernels for 0%

profile of v12, /device:TPU:1, one launch (start us, length us, event | category | flops | bytes accessed | tf_op | source)
XLA Modules:
  0.0 704.0 jit_solution(3058407657003359525)
XLA Ops:
  7.7 3.2 fusion.17
  12.8 11.5 %all-to-all-start.2 = ((f32[128,1,8,128]{3,2,1,0:T(8,128)}), f32[128,1,8,128]{3,2,1,0:T(8,128)S(1)}, u32[]{:S(2)}, u32[]{:S(2)}) async-start(f32[128,1,8,128]{3,2,1,0:T(8,128)} %bitcast.3), calls=%async_computation.2 | async-start | bytes 1048576 | tf_op jit(solution)/shard_map/all_to_all | solution.py:26
  24.3 4.8 slice.141
  29.1 6.1 copy.112
  35.2 2.8 all-to-all-done.2
  39.0 6.9 all-to-all-start.3
  46.0 5.1 select_bitcast_fusion
  51.1 3.3 slice.126
  55.6 4.1 all-to-all-done.3
  59.7 4.5 all-to-all-start
  64.5 11.7 %cholesky.134 = f32[128,128]{1,0:T(8,128)S(1)} custom-call(f32[128,128]{1,0:T(8,128)S(1)} %get-tuple-element.25), custom_call_target="Cholesky" | custom-call | tf_op jit(solution)/shard_map/jit(cholesky)/cholesky | solution.py:64
  77.4 9.8 %custom-call.12 = f32[1,128,128]{1,2,0:T(8,128)S(1)} custom-call(f32[1,128,128]{2,1,0:T(8,128)S(1)} %fusion.62), custom_call_target="InvertDiagBlocksLowerTriangular" | custom-call | tf_op jit(solution)/shard_map/jit(_solve_triangular)/triangular_solve | solution.py:65
  88.2 11.7 %cholesky.145 = f32[128,128]{1,0:T(8,128)S(1)} custom-call(f32[128,128]{1,0:T(8,128)S(1)} %fusion.91), custom_call_target="Cholesky" | custom-call | tf_op jit(solution)/shard_map/jit(cholesky)/cholesky | solution.py:67
  101.1 10.0 %custom-call.13 = f32[1,128,128]{1,2,0:T(8,128)S(1)} custom-call(f32[1,128,128]{2,1,0:T(8,128)S(1)} %fusion.63), custom_call_target="InvertDiagBlocksLowerTriangular" | custom-call | tf_op jit(solution)/shard_map/jit(_solve_triangular)/triangular_solve | solution.py:68
  113.5 11.7 %cholesky.156 = f32[128,128]{1,0:T(8,128)S(1)} custom-call(f32[128,128]{1,0:T(8,128)S(1)} %get-tuple-element.23), custom_call_target="Cholesky" | custom-call | tf_op jit(solution)/shard_map/jit(cholesky)/cholesky | solution.py:64
  126.5 9.8 %custom-call.14 = f32[1,128,128]{1,2,0:T(8,128)S(1)} custom-call(f32[1,128,128]{2,1,0:T(8,128)S(1)} %fusion.64), custom_call_target="InvertDiagBlocksLowerTriangular" | custom-call | tf_op jit(solution)/shard_map/jit(_solve_triangular)/triangular_solve | solution.py:65
  140.5 5.3 all-to-all-start.1
  146.3 11.7 %cholesky.167 = f32[128,128]{1,0:T(8,128)S(1)} custom-call(f32[128,128]{1,0:T(8,128)S(1)} %fusion.87), custom_call_target="Cholesky" | custom-call | tf_op jit(solution)/shard_map/jit(cholesky)/cholesky | solution.py:67
  159.3 9.8 %custom-call.15 = f32[1,128,128]{1,2,0:T(8,128)S(1)} custom-call(f32[1,128,128]{2,1,0:T(8,128)S(1)} %fusion.65), custom_call_target="InvertDiagBlocksLowerTriangular" | custom-call | tf_op jit(solution)/shard_map/jit(_solve_triangular)/triangular_solve | solution.py:68
  172.2 2.5 all-to-all-done.1
  176.6 10.8 %convolution_bitcast_fusion = f32[2304,256]{0,1:T(8,128)} fusion(f32[1152,256]{0,1:T(8,128)S(1)} %convolution_add_fusion.3, f32[1152,2304]{1,0:T(8,128)} %param.4), kind=kOutput, calls=%fused_computation.14 | convolution fusion | flops 4076863488 | bytes 14155776 | tf_op jit(solution)/shard_map/dot_general | solution.py:17
  187.5 4.3 convolution_add_fusion.1
  191.8 11.9 %fusion.130 = f32[256,1152]{1,0:T(8,128)S(1)} fusion(f32[2304,256]{1,0:T(8,128)S(1)} %convolution_add_fusion.1, f32[1152,2304]{1,0:T(8,128)} %param.4), kind=kOutput, calls=%fused_computation.218 | convolution fusion | flops 4076863488 | bytes 14155776 | tf_op jit(solution)/shard_map/dot_general | solution.py:13
  208.3 3.3 copy.79
  211.5 36.8 %all_to_all.70 = f32[16,160,256]{2,1,0:T(8,128)} all-to-all(f32[16,160,256]{2,1,0:T(8,128)} %bitcast.201), channel_id=1, replica_groups=mesh['row'=16,'col'=8] {'row'}, dimensions={0} | all-to-all | bytes 5242880 | tf_op jit(solution)/shard_map/all_to_all | solution.py:26
  248.3 2.6 reduce_sum.55
  250.9 2.7 broadcast_in_dim.120
  253.5 4.5 all-to-all-start.5
  258.0 4.4 fusion.10
  262.4 26.1 %all-to-all-done.5 = f32[16,160,256]{2,1,0:T(8,128)} async-done(((f32[16,160,256]{2,1,0:T(8,128)}), f32[16,160,256]{2,1,0:T(8,128)}, u32[]{:S(2)}, u32[]{:S(2)}) %all-to-all-start.5) | async-done | bytes 2621472 | tf_op jit(solution)/shard_map/all_to_all | solution.py:26
  292.0 2.7 pad_maximum_fusion.3
  294.7 2.7 copy.82
  297.4 32.8 %all_to_all.71 = f32[8,208,256]{2,1,0:T(8,128)} all-to-all(f32[8,208,256]{2,1,0:T(8,128)} %bitcast.204), channel_id=1, replica_groups=mesh['row'=16,'col'=8] {'col'}, dimensions={0} | all-to-all | bytes 3407872 | tf_op jit(solution)/shard_map/all_to_all | solution.py:26
  334.7 5.3 all-to-all-start.7
  342.7 4.2 fusion.8
  346.9 15.3 %all-to-all-done.7 = f32[8,208,256]{2,1,0:T(8,128)} async-done(((f32[8,208,256]{2,1,0:T(8,128)}), f32[8,208,256]{2,1,0:T(8,128)}, u32[]{:S(2)}, u32[]{:S(2)}) %all-to-all-start.7) | async-done | bytes 1703968 | tf_op jit(solution)/shard_map/all_to_all | solution.py:26
  374.0 3.0 fusion.14
  377.0 12.8 %convolution_subtract_fusion.3 = f32[1152,2304]{1,0:T(8,128)} fusion(f32[1152,2304]{1,0:T(8,128)S(1)} %bitcast.196, f32[1152,256]{0,1:T(8,128)S(1)} %convolution_add_fusion.3, f32[2304,256]{1,0:T(8,128)S(1)} %fusion.2), kind=kOutput, calls=%fused_computation.3 | convolution fusion | flops 4079517696 | bytes 24772608 | tf_op jit(solution)/shard_map/dot_general | solution.py:21
  390.7 4.9 all-to-all-start.8
  395.6 2.5 fusion.5
  399.1 9.5 %convolution_subtract_fusion.2 = f32[1152,2304]{1,0:T(8,128)} fusion(f32[1152,2304]{1,0:T(8,128)} %convolution_subtract_fusion.3, f32[1152,256]{1,0:T(8,128)S(1)} %fusion.5, f32[2304,256]{1,0:T(8,128)S(1)} %convolution_add_fusion.1), kind=kOutput, calls=%fused_computation.2 | convolution fusion | flops 4079517696 | bytes 24772608 | tf_op jit(solution)/shard_map/dot_general | solution.py:21
  410.6 5.1 all-to-all-start.9
  419.8 5.3 all-to-all-done.9
  431.4 13.2 %cholesky.178 = f32[128,128]{1,0:T(8,128)} custom-call(f32[128,128]{1,0:T(8,128)} %get-tuple-element.21), custom_call_target="Cholesky" | custom-call | tf_op jit(solution)/shard_map/jit(cholesky)/cholesky | solution.py:64
  448.1 11.3 %custom-call.16 = f32[1,128,128]{1,2,0:T(8,128)} custom-call(f32[1,128,128]{2,1,0:T(8,128)} %fusion.66), custom_call_target="InvertDiagBlocksLowerTriangular" | custom-call | tf_op jit(solution)/shard_map/jit(_solve_triangular)/triangular_solve | solution.py:65
  469.2 13.4 %cholesky.189 = f32[128,128]{1,0:T(8,128)} custom-call(f32[128,128]{1,0:T(8,128)} %fusion.83), custom_call_target="Cholesky" | custom-call | tf_op jit(solution)/shard_map/jit(cholesky)/cholesky | solution.py:67
  486.2 11.3 %custom-call.17 = f32[1,128,128]{1,2,0:T(8,128)} custom-call(f32[1,128,128]{2,1,0:T(8,128)} %fusion.67), custom_call_target="InvertDiagBlocksLowerTriangular" | custom-call | tf_op jit(solution)/shard_map/jit(_solve_triangular)/triangular_solve | solution.py:68
  506.6 12.6 %fusion.135 = f32[2304,256]{1,0:T(8,128)S(1)} fusion(f32[1152,2304]{1,0:T(8,128)} %convolution_subtract_fusion.2, f32[1152,256]{0,1:T(8,128)S(1)} %convolution_add_fusion.2), kind=kOutput, calls=%fused_computation.223 | convolution fusion | flops 4076863488 | bytes 14155776 | tf_op jit(solution)/shard_map/dot_general | solution.py:17
  519.3 4.4 fusion.136
  524.6 36.5 %all_to_all.72 = f32[16,160,256]{2,1,0:T(8,128)} all-to-all(f32[16,160,256]{2,1,0:T(8,128)S(1)} %bitcast.200), channel_id=1, replica_groups=mesh['row'=16,'col'=8] {'row'}, dimensions={0} | all-to-all | bytes 5242880 | tf_op jit(solution)/shard_map/all_to_all | solution.py:26
  561.1 2.6 reduce_sum.58
  563.7 2.7 broadcast_in_dim.125
  566.4 4.9 all-to-all-start.11
  578.2 13.2 %cholesky.200 = f32[128,128]{1,0:T(8,128)} custom-call(f32[128,128]{1,0:T(8,128)} %get-tuple-element.19), custom_call_target="Cholesky" | custom-call | tf_op jit(solution)/shard_map/jit(cholesky)/cholesky | solution.py:64
  595.0 11.3 %custom-call.18 = f32[1,128,128]{1,2,0:T(8,128)} custom-call(f32[1,128,128]{2,1,0:T(8,128)} %fusion.68), custom_call_target="InvertDiagBlocksLowerTriangular" | custom-call | tf_op jit(solution)/shard_map/jit(_solve_triangular)/triangular_solve | solution.py:65
  610.2 6.8 all-to-all-start.12
  618.5 11.7 %cholesky.211 = f32[128,128]{1,0:T(8,128)S(1)} custom-call(f32[128,128]{1,0:T(8,128)S(1)} %fusion.79), custom_call_target="Cholesky" | custom-call | tf_op jit(solution)/shard_map/jit(cholesky)/cholesky | solution.py:67
  631.6 9.8 %custom-call.19 = f32[1,128,128]{1,2,0:T(8,128)S(1)} custom-call(f32[1,128,128]{2,1,0:T(8,128)S(1)} %fusion.69), custom_call_target="InvertDiagBlocksLowerTriangular" | custom-call | tf_op jit(solution)/shard_map/jit(_solve_triangular)/triangular_solve | solution.py:68
  645.7 5.1 all-to-all-start.13
  651.1 3.1 copy.97
  655.4 4.2 fusion.6
  659.7 10.5 %all-to-all-done.13 = f32[8,176,256]{2,1,0:T(8,128)} async-done(((f32[8,176,256]{2,1,0:T(8,128)}), f32[8,176,256]{2,1,0:T(8,128)}, u32[]{:S(2)}, u32[]{:S(2)}) %all-to-all-start.13) | async-done | bytes 1441824 | tf_op jit(solution)/shard_map/all_to_all | solution.py:26
  676.4 12.6 %convolution_subtract_fusion.1 = f32[1152,2304]{1,0:T(8,128)S(1)} fusion(f32[1152,2304]{1,0:T(8,128)} %convolution_subtract_fusion.2, f32[1152,256]{0,1:T(8,128)S(1)} %convolution_add_fusion.2, f32[2304,256]{1,0:T(8,128)S(1)} %fusion), kind=kOutput, calls=%fused_computation.1 | convolution fusion | flops 4079517696 | bytes 24772608 | tf_op jit(solution)/shard_map/dot_general | solution.py:21
  689.0 7.9 %convolution_subtract_fusion = f32[1152,2304]{1,0:T(8,128)} fusion(f32[1152,2304]{1,0:T(8,128)S(1)} %convolution_subtract_fusion.1, f32[1152,256]{1,0:T(8,128)S(1)} %fusion.3, f32[2304,256]{1,0:T(8,128)S(1)} %copy-done.3), kind=kOutput, calls=%fused_computation | convolution fusion | flops 4079517696 | bytes 24772608 | tf_op jit(solution)/shard_map/dot_general | solution.py:21
  (251 shorter events, 119.5 us)
Async XLA Ops:
  12.8 25.2 %all-to-all-start.2 = ((f32[128,1,8,128]{3,2,1,0:T(8,128)}), f32[128,1,8,128]{3,2,1,0:T(8,128)S(1)}, u32[]{:S(2)}, u32[]{:S(2)}) async-start(f32[128,1,8,128]{3,2,1,0:T(8,128)} %bitcast.3), calls=%async_computation.2 | async-start | bytes 1048576 | tf_op jit(solution)/shard_map/all_to_all | solution.py:26
  39.0 20.7 %all-to-all-start.3 = ((f32[128,1,8,128]{3,2,1,0:T(8,128)}), f32[128,1,8,128]{3,2,1,0:T(8,128)S(1)}, u32[]{:S(2)}, u32[]{:S(2)}) async-start(f32[128,1,8,128]{3,2,1,0:T(8,128)} %broadcast_in_dim.116), calls=%async_computation.3 | async-start | bytes 1048576 | tf_op jit(solution)/shard_map/all_to_all | solution.py:26
  45.9 141.5 %all-reduce.6.cloned.1.call-start = ((), (), s32[]{:S(2)}) async-start(), calls=%async_computation.14 | async-start | bytes 9437184 | tf_op jit(solution)/shard_map/psum | solution.py:96
  59.7 79.1 %all-to-all-start = ((f32[8,144,512]{2,1,0:T(8,128)}), f32[8,144,512]{2,1,0:T(8,128)S(1)}, u32[]{:S(2)}, u32[]{:S(2)}) async-start(f32[8,144,512]{2,1,0:T(8,128)} %bitcast), calls=%async_computation | async-start | bytes 4718592 | tf_op jit(solution)/shard_map/all_to_all | solution.py:26
  87.5 49.5 %copy-start.23 = (f32[128,128]{1,0:T(8,128)}, f32[128,128]{1,0:T(8,128)S(1)}, u32[]{:S(2)}) copy-start(f32[128,128]{1,0:T(8,128)S(1)} %fusion.56) | copy-start | bytes 196612
  111.4 0.6 copy-start.36
  111.5 29.0 %copy-start.20 = (f32[256,256]{1,0:T(8,128)}, f32[256,256]{1,0:T(8,128)S(1)}, u32[]{:S(2)}) copy-start(f32[256,256]{1,0:T(8,128)S(1)} %slice.137) | copy-start | bytes 786436
  112.1 0.6 copy-start.34
  137.3 0.6 copy-start.31
  140.5 5.4 copy-start.28
  140.5 5.4 copy-start.39
  140.5 29.0 %copy-start.24 = (f32[128,128]{1,0:T(8,128)S(1)}, f32[128,128]{1,0:T(8,128)}, u32[]{:S(2)}) copy-start(f32[128,128]{1,0:T(8,128)} %copy-done.23) | copy-start | bytes 196612
  140.5 29.0 %copy-start.35 = (f32[128,128]{1,0:T(8,128)S(1)}, f32[128,128]{1,0:T(8,128)}, u32[]{:S(2)}) copy-start(f32[128,128]{1,0:T(8,128)} %copy-done.34) | copy-start | bytes 196612
  140.5 29.0 %copy-start.37 = (f32[128,128]{1,0:T(8,128)S(1)}, f32[128,128]{1,0:T(8,128)}, u32[]{:S(2)}) copy-start(f32[128,128]{1,0:T(8,128)} %copy-done.36) | copy-start | bytes 196612
  140.5 30.0 %copy-start.32 = (f32[128,128]{1,0:T(8,128)S(1)}, f32[128,128]{1,0:T(8,128)}, u32[]{:S(2)}) copy-start(f32[128,128]{1,0:T(8,128)} %copy-done.31) | copy-start | bytes 196612
  140.5 34.1 %all-to-all-start.1 = ((f32[8,144,512]{2,1,0:T(8,128)}), f32[8,144,512]{2,1,0:T(8,128)S(1)}, u32[]{:S(2)}, u32[]{:S(2)}) async-start(f32[8,144,512]{2,1,0:T(8,128)} %broadcast_in_dim.112), calls=%async_computation.1 | async-start | bytes 4718592 | tf_op jit(solution)/shard_map/all_to_all | solution.py:26
  174.7 12.8 %copy-start.11 = (f32[8,144,512]{2,1,0:T(8,128)}, f32[8,144,512]{2,1,0:T(8,128)S(1)}, u32[]{:S(2)}) copy-start(f32[8,144,512]{2,1,0:T(8,128)S(1)} %all-to-all-done.1) | copy-start | bytes 7077892
  176.6 10.9 %copy-start.41 = (pred[2304]{0:T(1024)(128)(4,1)S(1)}, pred[2304]{0:T(1024)(128)(4,1)}, u32[]{:S(2)}) copy-start(pred[2304]{0:T(1024)(128)(4,1)} %fusion.97) | copy-start | bytes 6916
  203.7 1.1 copy-start.4
  204.8 1.7 copy-start.10
  253.5 35.0 %all-to-all-start.5 = ((f32[16,160,256]{2,1,0:T(8,128)}), f32[16,160,256]{2,1,0:T(8,128)}, u32[]{:S(2)}, u32[]{:S(2)}) async-start(f32[16,160,256]{2,1,0:T(8,128)} %broadcast_in_dim.120), calls=%async_computation.5 | async-start | bytes 5242880 | tf_op jit(solution)/shard_map/all_to_all | solution.py:26
  334.7 27.5 %all-to-all-start.7 = ((f32[8,208,256]{2,1,0:T(8,128)}), f32[8,208,256]{2,1,0:T(8,128)}, u32[]{:S(2)}, u32[]{:S(2)}) async-start(f32[8,208,256]{2,1,0:T(8,128)} %broadcast_in_dim.121), calls=%async_computation.7 | async-start | bytes 3407872 | tf_op jit(solution)/shard_map/all_to_all | solution.py:26
  362.2 4.3 copy-start.9
  363.7 5.0 slice-start.6
  366.5 1.2 copy-start.17
  366.5 1.2 copy-start.13
  366.5 2.2 slice-start.7
  368.1 0.7 copy-start.21
  368.8 8.3 %slice-start.3 = ((s8[10616832]{0:T(1024)(128)(4,1)}), s8[4194304]{0:T(1024)(128)(4,1)S(1)}, s32[]{:S(2)}) async-start(s8[10616832]{0:T(1024)(128)(4,1)} %bitcast.195), calls=%async_computation.18 | async-start | bytes 8388608
  369.9 7.1 %slice-start.4 = ((s8[10616832]{0:T(1024)(128)(4,1)}), s8[4194304]{0:T(1024)(128)(4,1)S(1)}, s32[]{:S(2)}) async-start(s8[10616832]{0:T(1024)(128)(4,1)} %bitcast.195), calls=%async_computation.19 | async-start | bytes 8388608
  371.8 2.1 copy-start
  371.9 2.2 copy-start.7
  371.9 5.2 slice-start.5
  390.7 18.0 %all-to-all-start.8 = ((f32[8,64,256]{2,1,0:T(8,128)}), f32[8,64,256]{2,1,0:T(8,128)}, u32[]{:S(2)}, u32[]{:S(2)}) async-start(f32[8,64,256]{2,1,0:T(8,128)} %bitcast.206), calls=%async_computation.8 | async-start | bytes 1048576 | tf_op jit(solution)/shard_map/all_to_all | solution.py:26
  398.0 1.0 copy-start.5
  408.6 7.1 %copy-start.22 = (f32[256,256]{1,0:T(8,128)S(1)}, f32[256,256]{1,0:T(8,128)}, u32[]{:S(2)}) copy-start(f32[256,256]{1,0:T(8,128)} %copy-done.21) | copy-start | bytes 786436
  410.6 7.5 %copy-start.6 = (f32[1152,256]{1,0:T(8,128)S(1)}, f32[1152,256]{1,0:T(8,128)}, u32[]{:S(2)}) copy-start(f32[1152,256]{1,0:T(8,128)} %copy-done.5) | copy-start | bytes 3538948
  410.6 7.5 %copy-start.14 = (f32[256,256]{1,0:T(8,128)S(1)}, f32[256,256]{1,0:T(8,128)}, u32[]{:S(2)}) copy-start(f32[256,256]{1,0:T(8,128)} %convolution_add_fusion.5) | copy-start | bytes 786436
  410.6 7.5 %copy-start.42 = (pred[1152]{0:T(1024)(128)(4,1)S(1)}, pred[1152]{0:T(1024)(128)(4,1)}, u32[]{:S(2)}) copy-start(pred[1152]{0:T(1024)(128)(4,1)} %get-tuple-element.26) | copy-start | bytes 3460
  410.6 14.5 %all-to-all-start.9 = ((f32[8,64,256]{2,1,0:T(8,128)}), f32[8,64,256]{2,1,0:T(8,128)}, u32[]{:S(2)}, u32[]{:S(2)}) async-start(f32[8,64,256]{2,1,0:T(8,128)} %broadcast_in_dim.124), calls=%async_computation.9 | async-start | bytes 1048576 | tf_op jit(solution)/shard_map/all_to_all | solution.py:26
  419.8 83.7 %copy-start.1 = (f32[2304,256]{1,0:T(8,128)S(1)}, f32[2304,256]{1,0:T(8,128)}, u32[]{:S(2)}) copy-start(f32[2304,256]{1,0:T(8,128)} %copy-done) | copy-start | bytes 7077892
  426.9 0.7 copy-start.29
  460.5 0.6 copy-start.18
  498.6 0.6 copy-start.33
  503.6 2.2 copy-start.25
  503.6 2.2 copy-start.12
  503.6 2.2 copy-start.19
  503.6 2.2 copy-start.26
  503.6 2.2 copy-start.40
  505.8 13.5 %copy-start.2 = (f32[2304,256]{1,0:T(8,128)}, f32[2304,256]{1,0:T(8,128)S(1)}, u32[]{:S(2)}) copy-start(f32[2304,256]{1,0:T(8,128)S(1)} %convolution_add_fusion) | copy-start | bytes 7077892
  505.8 13.5 %slice-start = ((s8[10616832]{0:T(1024)(128)(4,1)}), s8[4194304]{0:T(1024)(128)(4,1)S(1)}, s32[]{:S(2)}) async-start(s8[10616832]{0:T(1024)(128)(4,1)} %bitcast.193), calls=%async_computation.15 | async-start | bytes 8388608
  506.6 12.7 %slice-start.1 = ((s8[10616832]{0:T(1024)(128)(4,1)}), s8[4194304]{0:T(1024)(128)(4,1)S(1)}, s32[]{:S(2)}) async-start(s8[10616832]{0:T(1024)(128)(4,1)} %bitcast.193), calls=%async_computation.16 | async-start | bytes 8388608
  506.6 12.7 %slice-start.2 = ((s8[10616832]{0:T(1024)(128)(4,1)}), s8[2228224]{0:T(1024)(128)(4,1)S(1)}, s32[]{:S(2)}) async-start(s8[10616832]{0:T(1024)(128)(4,1)} %bitcast.193), calls=%async_computation.17 | async-start | bytes 4456448
  566.4 41.6 %all-to-all-start.11 = ((f32[16,160,256]{2,1,0:T(8,128)}), f32[16,160,256]{2,1,0:T(8,128)}, u32[]{:S(2)}, u32[]{:S(2)}) async-start(f32[16,160,256]{2,1,0:T(8,128)} %broadcast_in_dim.125), calls=%async_computation.11 | async-start | bytes 5242880 | tf_op jit(solution)/shard_map/all_to_all | solution.py:26
  572.6 0.7 copy-start.15
  573.7 0.7 copy-start.27
  610.2 6.8 copy-start.30
  610.2 7.9 %copy-start.38 = (f32[128,128]{1,0:T(8,128)S(1)}, f32[128,128]{1,0:T(8,128)}, u32[]{:S(2)}) copy-start(f32[128,128]{1,0:T(8,128)} %get-tuple-element.18) | copy-start | bytes 196612
  610.2 32.8 %all-to-all-start.12 = ((f32[8,176,256]{2,1,0:T(8,128)}), f32[8,176,256]{2,1,0:T(8,128)}, u32[]{:S(2)}, u32[]{:S(2)}) async-start(f32[8,176,256]{2,1,0:T(8,128)} %bitcast.205), calls=%async_computation.12 | async-start | bytes 2883584 | tf_op jit(solution)/shard_map/all_to_all | solution.py:26
  645.7 24.4 %all-to-all-start.13 = ((f32[8,176,256]{2,1,0:T(8,128)}), f32[8,176,256]{2,1,0:T(8,128)}, u32[]{:S(2)}, u32[]{:S(2)}) async-start(f32[8,176,256]{2,1,0:T(8,128)} %broadcast_in_dim.126), calls=%async_computation.13 | async-start | bytes 2883584 | tf_op jit(solution)/shard_map/all_to_all | solution.py:26
  651.1 3.9 copy-start.16
  672.1 2.9 copy-start.8
  673.5 1.8 copy-start.3
Sparse Core Ops, SparseCore 0:
  51.2 109.8 all-reduce.5

commit v13 on v12

--- a/solution.py
+++ b/solution.py
@@ -134,21 +134,20 @@
 
         xp = mm(current, y_c, FAST)
         xq = mm_tn(current, y_r, FAST)
-        summed_c = comm.psum(jnp.concatenate([xq, mm_tn(y_r, xp)], axis=0), "row", rows)
-        x_c = summed_c[:col_count]
-        parts = [xp, summed_c[col_count:]]
+        x_c = comm.psum(xq, "row", rows)
+        parts = [xp]
         if k + 1 < PANELS:
             nlo = (k + 1) * BAND
             parts.append(mm_tn(strip_t[:, nlo:nlo + BAND], y_c))
         summed = comm.psum(jnp.concatenate(parts, axis=0), "col", cols)
         x_r = summed[:row_count]
-        curv = summed[row_count:row_count + BAND]
+        curv = comm.psum(mm_tn(y_c, x_c), "col", cols)
         middle = mm_nt(mm(transform, curv), transform)
         w_r = mm_nt(x_r, transform) - 0.5 * mm(y_r, middle)
         w_c = mm_nt(x_c, transform) - 0.5 * mm(y_c, middle)
         current = current - mm_nt(y_r, w_c, FAST) - mm_nt(w_r, y_c, FAST)
         if k + 1 < PANELS:
-            x_e = summed[row_count + BAND:]
+            x_e = summed[row_count:]
             y_e = mm_nt(top, low_inv) + jnp.eye(BAND, dtype=jnp.float32)
             w_e = mm_nt(x_e, transform) - 0.5 * mm(y_e, middle)
             prev = (y_r, w_r, y_c, w_c, y_e, w_e)

time: 711 us -> 693 us (0.975)
  blocking collectives: 106 us -> 0 us
  waiting for transfers between devices: 66.6 us -> 141 us
  starting transfers between devices: 64.9 us -> 101 us
  other arithmetic: 231 us -> 216 us
  local copies, waits for them, and re-layouts: 62.1 us -> 49.2 us
    all_to_all x3 -> x0, blocking collectives: 106 us -> none  [a2a(): return lax.all_to_all(x, axis, 0, 0, tiled=False)]
    all_to_all x11 -> x18, waiting for transfers between devices: 66.6 us -> 141 us  [a2a(): return lax.all_to_all(x, axis, 0, 0, tiled=False)]
    all_to_all x11 -> x18, starting transfers between devices: 64.9 us -> 101 us  [a2a(): return lax.all_to_all(x, axis, 0, 0, tiled=False)]
    unnamed x113 -> x98, local copies, waits for them, and re-layouts: 25.5 us -> 17.1 us
  transfers between devices with their start and end apart: 12 -> 19, of which waited for: 7 -> 15; matrix products, arithmetic and copies ran while one was open for 33% -> 41% of each run, Pallas kernels for 0% -> 0%
where the time goes in v13:
time: 693 us; the launch traced here: 686 us
  other arithmetic  216 us (31%)
  matrix products  163 us (24%)
  waiting for transfers between devices  141 us (20%)
  starting transfers between devices  101 us (15%)
  local copies, waits for them, and re-layouts  49.2 us (7%)
  between operations  15.8 us (2%)
    all_to_all x18, waiting for transfers between devices, a2a(): return lax.all_to_all(x, axis, 0, 0, tiled=False)  141 us
    all_to_all x18, starting transfers between devices, a2a(): return lax.all_to_all(x, axis, 0, 0, tiled=False)  101 us
    dot_general x32, matrix products, mm_nt(): return lax.dot_general(a, b, (((1,), (1,)), ((), ())), precision=precision)  86.2 us
    another operation x12, other arithmetic, cholesky_inverse(): low22 = jnp.linalg.cholesky(spd[half:, half:] - mm_nt(low21, low21))  52.3 us
    another operation x12, other arithmetic, cholesky_inverse(): low11 = jnp.linalg.cholesky(spd[:half, :half])  49.6 us
    another operation x8, other arithmetic, cholesky_inverse(): inv11 = jax.scipy.linalg.solve_triangular(low11, identity, lower=True)  46.1 us
    another operation x8, other arithmetic, cholesky_inverse(): inv22 = jax.scipy.linalg.solve_triangular(low22, identity, lower=True)  45.2 us
    dot_general x11, matrix products, mm_tn(): return lax.dot_general(a, b, (((0,), (0,)), ((), ())), precision=precision)  42.4 us
  transfers between devices with their start and end apart: 19, of which 15 were waited for; matrix products, arithmetic and copies ran while one was open for 41% of the time, Pallas kernels for 0%

profile of v13, /device:TPU:1, one launch (start us, length us, event | category | flops | bytes accessed | tf_op | source)
XLA Modules:
  0.0 685.6 jit_solution(11239556876107027072)
XLA Ops:
  12.9 11.5 %all-to-all-start.2 = ((f32[128,1,8,128]{3,2,1,0:T(8,128)}), f32[128,1,8,128]{3,2,1,0:T(8,128)S(1)}, u32[]{:S(2)}, u32[]{:S(2)}) async-start(f32[128,1,8,128]{3,2,1,0:T(8,128)} %bitcast.3), calls=%async_computation.2 | async-start | bytes 1048576 | tf_op jit(solution)/shard_map/all_to_all | solution.py:26
  24.4 4.8 slice.120
  29.2 6.1 copy.106
  39.1 6.9 %all-to-all-start.3 = ((f32[128,1,8,128]{3,2,1,0:T(8,128)}), f32[128,1,8,128]{3,2,1,0:T(8,128)S(1)}, u32[]{:S(2)}, u32[]{:S(2)}) async-start(f32[128,1,8,128]{3,2,1,0:T(8,128)} %broadcast_in_dim.128), calls=%async_computation.3 | async-start | bytes 1048576 | tf_op jit(solution)/shard_map/all_to_all | solution.py:26
  46.0 5.1 select_bitcast_fusion
  51.2 3.3 slice.105
  55.1 4.7 all-to-all-done.3
  59.7 4.6 all-to-all-start
  64.6 11.7 %cholesky.134 = f32[128,128]{1,0:T(8,128)S(1)} custom-call(f32[128,128]{1,0:T(8,128)S(1)} %get-tuple-element.25), custom_call_target="Cholesky" | custom-call | tf_op jit(solution)/shard_map/jit(cholesky)/cholesky | solution.py:64
  77.6 9.8 %custom-call.12 = f32[1,128,128]{1,2,0:T(8,128)S(1)} custom-call(f32[1,128,128]{2,1,0:T(8,128)S(1)} %fusion.63), custom_call_target="InvertDiagBlocksLowerTriangular" | custom-call | tf_op jit(solution)/shard_map/jit(_solve_triangular)/triangular_solve | solution.py:65
  88.4 11.7 %cholesky.145 = f32[128,128]{1,0:T(8,128)S(1)} custom-call(f32[128,128]{1,0:T(8,128)S(1)} %fusion.92), custom_call_target="Cholesky" | custom-call | tf_op jit(solution)/shard_map/jit(cholesky)/cholesky | solution.py:67
  101.5 10.2 %custom-call.13 = f32[1,128,128]{1,2,0:T(8,128)S(1)} custom-call(f32[1,128,128]{2,1,0:T(8,128)S(1)} %fusion.64), custom_call_target="InvertDiagBlocksLowerTriangular" | custom-call | tf_op jit(solution)/shard_map/jit(_solve_triangular)/triangular_solve | solution.py:68
  113.4 11.7 %cholesky.156 = f32[128,128]{1,0:T(8,128)S(1)} custom-call(f32[128,128]{1,0:T(8,128)S(1)} %get-tuple-element.23), custom_call_target="Cholesky" | custom-call | tf_op jit(solution)/shard_map/jit(cholesky)/cholesky | solution.py:64
  127.0 10.6 %custom-call.14 = f32[1,128,128]{1,2,0:T(8,128)S(1)} custom-call(f32[1,128,128]{2,1,0:T(8,128)} %fusion.65), custom_call_target="InvertDiagBlocksLowerTriangular" | custom-call | tf_op jit(solution)/shard_map/jit(_solve_triangular)/triangular_solve | solution.py:65
  140.1 11.7 %cholesky.167 = f32[128,128]{1,0:T(8,128)S(1)} custom-call(f32[128,128]{1,0:T(8,128)S(1)} %fusion.88), custom_call_target="Cholesky" | custom-call | tf_op jit(solution)/shard_map/jit(cholesky)/cholesky | solution.py:67
  153.1 9.9 %custom-call.15 = f32[1,128,128]{1,2,0:T(8,128)S(1)} custom-call(f32[1,128,128]{2,1,0:T(8,128)S(1)} %fusion.66), custom_call_target="InvertDiagBlocksLowerTriangular" | custom-call | tf_op jit(solution)/shard_map/jit(_solve_triangular)/triangular_solve | solution.py:68
  165.7 4.9 all-to-all-start.1
  172.1 4.7 bitcast_add_fusion.1
  178.2 7.8 %convolution_bitcast_fusion.1 = f32[1152,256]{0,1:T(8,128)S(1)} fusion(f32[1152,2304]{1,0:T(8,128)} %param.4, f32[2304,256]{0,1:T(8,128)S(1)} %get-tuple-element.27, s32[2304]{0:T(1024)S(1)} %fusion.97), kind=kOutput, calls=%fused_computation.22 | convolution fusion | flops 4078632960 | bytes 14164992 | tf_op jit(solution)/shard_map/dot_general | solution.py:13
  190.1 9.8 %all-to-all-done.1 = f32[8,144,512]{2,1,0:T(8,128)} async-done(((f32[8,144,512]{2,1,0:T(8,128)}), f32[8,144,512]{2,1,0:T(8,128)}, u32[]{:S(2)}, u32[]{:S(2)}) %all-to-all-start.1) | async-done | bytes 2359328 | tf_op jit(solution)/shard_map/all_to_all | solution.py:26
  199.9 5.3 all-to-all-start.8
  207.3 10.7 %convolution_bitcast_fusion = f32[2304,256]{0,1:T(8,128)} fusion(f32[1152,256]{0,1:T(8,128)S(1)} %convolution_add_fusion.1, f32[1152,2304]{1,0:T(8,128)} %param.4), kind=kOutput, calls=%fused_computation.12 | convolution fusion | flops 4076863488 | bytes 14155776 | tf_op jit(solution)/shard_map/dot_general | solution.py:17
  221.0 3.5 all-to-all-done.8
  224.6 4.5 all-to-all-start.4
  231.2 29.8 %all-to-all-done.4 = f32[16,144,256]{2,1,0:T(8,128)} async-done(((f32[16,144,256]{2,1,0:T(8,128)}), f32[16,144,256]{2,1,0:T(8,128)}, u32[]{:S(2)}, u32[]{:S(2)}) %all-to-all-start.4) | async-done | bytes 2359328 | tf_op jit(solution)/shard_map/all_to_all | solution.py:26
  263.1 7.0 %all-to-all-start.9 = ((f32[8,176,256]{2,1,0:T(8,128)}), f32[8,176,256]{2,1,0:T(8,128)}, u32[]{:S(2)}, u32[]{:S(2)}) async-start(f32[8,176,256]{2,1,0:T(8,128)} %broadcast_in_dim.134), calls=%async_computation.9 | async-start | bytes 2883584 | tf_op jit(solution)/shard_map/all_to_all | solution.py:26
  272.6 17.0 %all-to-all-done.9 = f32[8,176,256]{2,1,0:T(8,128)} async-done(((f32[8,176,256]{2,1,0:T(8,128)}), f32[8,176,256]{2,1,0:T(8,128)}, u32[]{:S(2)}, u32[]{:S(2)}) %all-to-all-start.9) | async-done | bytes 1441824 | tf_op jit(solution)/shard_map/all_to_all | solution.py:26
  292.1 4.5 all-to-all-start.5
  302.3 26.2 %all-to-all-done.5 = f32[16,144,256]{2,1,0:T(8,128)} async-done(((f32[16,144,256]{2,1,0:T(8,128)}), f32[16,144,256]{2,1,0:T(8,128)}, u32[]{:S(2)}, u32[]{:S(2)}) %all-to-all-start.5) | async-done | bytes 2359328 | tf_op jit(solution)/shard_map/all_to_all | solution.py:26
  328.5 4.2 fusion.132
  332.7 6.8 all-to-all-start.6
  341.6 4.6 all-to-all-done.6
  349.2 5.4 all-to-all-start.7
  354.6 4.2 fusion.131
  364.0 3.9 fusion.2
  374.5 12.6 %convolution_subtract_fusion.3 = f32[1152,2304]{1,0:T(8,128)} fusion(f32[1152,2304]{1,0:T(8,128)S(1)} %bitcast.204, f32[1152,256]{0,1:T(8,128)S(1)} %convolution_add_fusion.1, f32[2304,256]{1,0:T(8,128)S(1)} %fusion.2), kind=kOutput, calls=%fused_computation.3 | convolution fusion | flops 4079517696 | bytes 24772608 | tf_op jit(solution)/shard_map/dot_general | solution.py:21
  387.8 5.0 all-to-all-start.10
  396.4 9.6 %convolution_subtract_fusion.2 = f32[1152,2304]{1,0:T(8,128)} fusion(f32[1152,2304]{1,0:T(8,128)} %convolution_subtract_fusion.3, f32[1152,256]{1,0:T(8,128)S(1)} %fusion.5, f32[2304,256]{0,1:T(8,128)S(1)} %get-tuple-element.27, s32[2304]{0:T(1024)S(1)} %fusion.97), kind=kOutput, calls=%fused_computation.2 | convolution fusion | flops 4081287168 | bytes 24781824 | tf_op jit(solution)/shard_map/dot_general | solution.py:21
  408.0 5.1 all-to-all-start.11
  416.3 6.2 all-to-all-done.11
  424.4 11.7 %cholesky.178 = f32[128,128]{1,0:T(8,128)S(1)} custom-call(f32[128,128]{1,0:T(8,128)S(1)} %get-tuple-element.21), custom_call_target="Cholesky" | custom-call | tf_op jit(solution)/shard_map/jit(cholesky)/cholesky | solution.py:64
  437.5 9.8 %custom-call.16 = f32[1,128,128]{1,2,0:T(8,128)S(1)} custom-call(f32[1,128,128]{2,1,0:T(8,128)S(1)} %fusion.67), custom_call_target="InvertDiagBlocksLowerTriangular" | custom-call | tf_op jit(solution)/shard_map/jit(_solve_triangular)/triangular_solve | solution.py:65
  448.2 11.7 %cholesky.189 = f32[128,128]{1,0:T(8,128)S(1)} custom-call(f32[128,128]{1,0:T(8,128)S(1)} %fusion.84), custom_call_target="Cholesky" | custom-call | tf_op jit(solution)/shard_map/jit(cholesky)/cholesky | solution.py:67
  461.7 9.8 %custom-call.17 = f32[1,128,128]{1,2,0:T(8,128)S(1)} custom-call(f32[1,128,128]{2,1,0:T(8,128)S(1)} %fusion.68), custom_call_target="InvertDiagBlocksLowerTriangular" | custom-call | tf_op jit(solution)/shard_map/jit(_solve_triangular)/triangular_solve | solution.py:68
  473.1 14.4 %fusion.137 = f32[2304,256]{1,0:T(8,128)} fusion(f32[1152,2304]{1,0:T(8,128)} %convolution_subtract_fusion.2, f32[1152,256]{0,1:T(8,128)S(1)} %convolution_add_fusion), kind=kOutput, calls=%fused_computation.227 | convolution fusion | flops 4076863488 | bytes 14155776 | tf_op jit(solution)/shard_map/dot_general | solution.py:17
  487.5 4.8 all-to-all-start.12
  492.3 3.6 bitcast_add_fusion
  497.3 8.7 %fusion.9 = f32[1152,256]{1,0:T(8,128)} fusion(f32[1152,2304]{1,0:T(8,128)} %convolution_subtract_fusion.2, f32[2304,256]{0,1:T(8,128)S(1)} %get-tuple-element.29, s32[2304]{0:T(1024)S(1)} %fusion.95), kind=kOutput, calls=%fused_computation.36 | convolution fusion | flops 4078632960 | bytes 14164992 | tf_op jit(solution)/shard_map/dot_general | solution.py:13
  506.0 18.1 %all-to-all-done.12 = f32[16,144,256]{2,1,0:T(8,128)} async-done(((f32[16,144,256]{2,1,0:T(8,128)}), f32[16,144,256]{2,1,0:T(8,128)}, u32[]{:S(2)}, u32[]{:S(2)}) %all-to-all-start.12) | async-done | bytes 2359328 | tf_op jit(solution)/shard_map/all_to_all | solution.py:26
  524.2 6.3 all-to-all-start.16
  532.0 11.7 %cholesky.200 = f32[128,128]{1,0:T(8,128)S(1)} custom-call(f32[128,128]{1,0:T(8,128)S(1)} %get-tuple-element.19), custom_call_target="Cholesky" | custom-call | tf_op jit(solution)/shard_map/jit(cholesky)/cholesky | solution.py:64
  548.6 4.8 all-to-all-start.13
  556.1 11.3 %custom-call.18 = f32[1,128,128]{1,2,0:T(8,128)} custom-call(f32[1,128,128]{2,1,0:T(8,128)} %fusion.69), custom_call_target="InvertDiagBlocksLowerTriangular" | custom-call | tf_op jit(solution)/shard_map/jit(_solve_triangular)/triangular_solve | solution.py:65
  577.1 13.2 %cholesky.211 = f32[128,128]{1,0:T(8,128)} custom-call(f32[128,128]{1,0:T(8,128)} %fusion.80), custom_call_target="Cholesky" | custom-call | tf_op jit(solution)/shard_map/jit(cholesky)/cholesky | solution.py:67
  593.9 11.3 %custom-call.19 = f32[1,128,128]{1,2,0:T(8,128)} custom-call(f32[1,128,128]{2,1,0:T(8,128)} %fusion.70), custom_call_target="InvertDiagBlocksLowerTriangular" | custom-call | tf_op jit(solution)/shard_map/jit(_solve_triangular)/triangular_solve | solution.py:68
  609.7 4.3 all-to-all-start.17
  618.5 4.2 fusion.142
  622.7 7.8 %all-to-all-done.17 = f32[8,144,256]{2,1,0:T(8,128)S(1)} async-done(((f32[8,144,256]{2,1,0:T(8,128)}), f32[8,144,256]{2,1,0:T(8,128)S(1)}, u32[]{:S(2)}, u32[]{:S(2)}) %all-to-all-start.17) | async-done | bytes 1179680 | tf_op jit(solution)/shard_map/all_to_all | solution.py:26
  630.6 4.4 all-to-all-start.14
  636.8 4.8 all-to-all-done.14
  642.3 4.4 all-to-all-start.15
  646.6 4.3 fusion.141
  657.7 12.6 %convolution_subtract_fusion.1 = f32[1152,2304]{1,0:T(8,128)S(1)} fusion(f32[1152,2304]{1,0:T(8,128)} %convolution_subtract_fusion.2, f32[1152,256]{0,1:T(8,128)S(1)} %copy-done.5, f32[2304,256]{1,0:T(8,128)S(1)} %fusion), kind=kOutput, calls=%fused_computation.1 | convolution fusion | flops 4079517696 | bytes 24772608 | tf_op jit(solution)/shard_map/dot_general | solution.py:21
  670.3 7.9 %convolution_subtract_fusion = f32[1152,2304]{1,0:T(8,128)} fusion(f32[1152,2304]{1,0:T(8,128)S(1)} %convolution_subtract_fusion.1, f32[1152,256]{1,0:T(8,128)S(1)} %fusion.3, f32[2304,256]{0,1:T(8,128)S(1)} %copy-done.3, s32[2304]{0:T(1024)S(1)} %fusion.95), kind=kOutput, calls=%fused_computation | convolution fusion | flops 4081287168 | bytes 24781824 | tf_op jit(solution)/shard_map/dot_general | solution.py:21
  (244 shorter events, 126.2 us)
Async XLA Ops:
  12.9 25.2 %all-to-all-start.2 = ((f32[128,1,8,128]{3,2,1,0:T(8,128)}), f32[128,1,8,128]{3,2,1,0:T(8,128)S(1)}, u32[]{:S(2)}, u32[]{:S(2)}) async-start(f32[128,1,8,128]{3,2,1,0:T(8,128)} %bitcast.3), calls=%async_computation.2 | async-start | bytes 1048576 | tf_op jit(solution)/shard_map/all_to_all | solution.py:26
  39.1 20.7 %all-to-all-start.3 = ((f32[128,1,8,128]{3,2,1,0:T(8,128)}), f32[128,1,8,128]{3,2,1,0:T(8,128)S(1)}, u32[]{:S(2)}, u32[]{:S(2)}) async-start(f32[128,1,8,128]{3,2,1,0:T(8,128)} %broadcast_in_dim.128), calls=%async_computation.3 | async-start | bytes 1048576 | tf_op jit(solution)/shard_map/all_to_all | solution.py:26
  46.0 126.1 %all-reduce.6.cloned.1.call-start = ((), (), s32[]{:S(2)}) async-start(), calls=%async_computation.18 | async-start | bytes 9437184 | tf_op jit(solution)/shard_map/psum | solution.py:96
  59.7 104.2 %all-to-all-start = ((f32[8,144,512]{2,1,0:T(8,128)}), f32[8,144,512]{2,1,0:T(8,128)S(1)}, u32[]{:S(2)}, u32[]{:S(2)}) async-start(f32[8,144,512]{2,1,0:T(8,128)} %bitcast), calls=%async_computation | async-start | bytes 4718592 | tf_op jit(solution)/shard_map/all_to_all | solution.py:26
  112.1 51.2 %copy-start.19 = (f32[256,256]{1,0:T(8,128)}, f32[256,256]{1,0:T(8,128)S(1)}, u32[]{:S(2)}) copy-start(f32[256,256]{1,0:T(8,128)S(1)} %slice.116) | copy-start | bytes 786436
  163.5 8.6 %copy-start.11 = (f32[256,256]{1,0:T(8,128)}, f32[256,256]{1,0:T(8,128)S(1)}, u32[]{:S(2)}) copy-start(f32[256,256]{1,0:T(8,128)S(1)} %select_maximum_fusion.5) | copy-start | bytes 786436
  165.7 6.4 copy-start.36
  165.7 34.2 %all-to-all-start.1 = ((f32[8,144,512]{2,1,0:T(8,128)}), f32[8,144,512]{2,1,0:T(8,128)}, u32[]{:S(2)}, u32[]{:S(2)}) async-start(f32[8,144,512]{2,1,0:T(8,128)} %broadcast_in_dim.124), calls=%async_computation.1 | async-start | bytes 4718592 | tf_op jit(solution)/shard_map/all_to_all | solution.py:26
  172.1 4.7 copy-start.8
  199.9 24.7 %all-to-all-start.8 = ((f32[8,176,256]{2,1,0:T(8,128)}), f32[8,176,256]{2,1,0:T(8,128)}, u32[]{:S(2)}, u32[]{:S(2)}) async-start(f32[8,176,256]{2,1,0:T(8,128)} %bitcast.211), calls=%async_computation.8 | async-start | bytes 2883584 | tf_op jit(solution)/shard_map/all_to_all | solution.py:26
  224.6 36.4 %all-to-all-start.4 = ((f32[16,144,256]{2,1,0:T(8,128)}), f32[16,144,256]{2,1,0:T(8,128)}, u32[]{:S(2)}, u32[]{:S(2)}) async-start(f32[16,144,256]{2,1,0:T(8,128)} %bitcast.209), calls=%async_computation.4 | async-start | bytes 4718592 | tf_op jit(solution)/shard_map/all_to_all | solution.py:26
  263.1 26.4 %all-to-all-start.9 = ((f32[8,176,256]{2,1,0:T(8,128)}), f32[8,176,256]{2,1,0:T(8,128)}, u32[]{:S(2)}, u32[]{:S(2)}) async-start(f32[8,176,256]{2,1,0:T(8,128)} %broadcast_in_dim.134), calls=%async_computation.9 | async-start | bytes 2883584 | tf_op jit(solution)/shard_map/all_to_all | solution.py:26
  292.1 36.4 %all-to-all-start.5 = ((f32[16,144,256]{2,1,0:T(8,128)}), f32[16,144,256]{2,1,0:T(8,128)}, u32[]{:S(2)}, u32[]{:S(2)}) async-start(f32[16,144,256]{2,1,0:T(8,128)} %broadcast_in_dim.129), calls=%async_computation.5 | async-start | bytes 4718592 | tf_op jit(solution)/shard_map/all_to_all | solution.py:26
  332.7 13.4 %all-to-all-start.6 = ((f32[8,32,256]{2,1,0:T(8,128)}), f32[8,32,256]{2,1,0:T(8,128)}, u32[]{:S(2)}, u32[]{:S(2)}) async-start(f32[8,32,256]{2,1,0:T(8,128)} %fusion.132), calls=%async_computation.6 | async-start | bytes 524288 | tf_op jit(solution)/shard_map/all_to_all | solution.py:26
  349.2 12.0 %all-to-all-start.7 = ((f32[8,32,256]{2,1,0:T(8,128)}), f32[8,32,256]{2,1,0:T(8,128)}, u32[]{:S(2)}, u32[]{:S(2)}) async-start(f32[8,32,256]{2,1,0:T(8,128)} %broadcast_in_dim.133), calls=%async_computation.7 | async-start | bytes 524288 | tf_op jit(solution)/shard_map/all_to_all | solution.py:26
  361.2 7.0 %slice-start.3 = ((s8[4718592]{0:T(1024)(128)(4,1)}), s8[4194304]{0:T(1024)(128)(4,1)S(1)}, s32[]{:S(2)}) async-start(s8[4718592]{0:T(1024)(128)(4,1)} %bitcast.206), calls=%async_computation.22 | async-start | bytes 8388608
  363.9 3.9 copy-start.16
  363.9 3.9 copy-start.12
  364.0 3.9 copy-start.29
  364.0 4.2 slice-start.4
  364.0 6.4 copy-start.37
  368.2 2.1 copy-start.20
  368.2 6.2 slice-start
  368.2 6.2 slice-start.1
  370.4 4.1 slice-start.2
  372.3 2.1 copy-start
  387.8 18.2 %all-to-all-start.10 = ((f32[8,64,256]{2,1,0:T(8,128)}), f32[8,64,256]{2,1,0:T(8,128)}, u32[]{:S(2)}, u32[]{:S(2)}) async-start(f32[8,64,256]{2,1,0:T(8,128)} %bitcast.213), calls=%async_computation.10 | async-start | bytes 1048576 | tf_op jit(solution)/shard_map/all_to_all | solution.py:26
  395.4 1.0 copy-start.6
  406.0 7.1 %copy-start.21 = (f32[256,256]{1,0:T(8,128)S(1)}, f32[256,256]{1,0:T(8,128)}, u32[]{:S(2)}) copy-start(f32[256,256]{1,0:T(8,128)} %copy-done.20) | copy-start | bytes 786436
  407.9 7.6 %copy-start.7 = (f32[1152,256]{1,0:T(8,128)S(1)}, f32[1152,256]{1,0:T(8,128)}, u32[]{:S(2)}) copy-start(f32[1152,256]{1,0:T(8,128)} %copy-done.6) | copy-start | bytes 3538948
  408.0 7.6 %copy-start.38 = (pred[1152]{0:T(1024)(128)(4,1)S(1)}, pred[1152]{0:T(1024)(128)(4,1)}, u32[]{:S(2)}) copy-start(pred[1152]{0:T(1024)(128)(4,1)} %get-tuple-element.30) | copy-start | bytes 3460
  408.0 14.5 %all-to-all-start.11 = ((f32[8,64,256]{2,1,0:T(8,128)}), f32[8,64,256]{2,1,0:T(8,128)}, u32[]{:S(2)}, u32[]{:S(2)}) async-start(f32[8,64,256]{2,1,0:T(8,128)} %broadcast_in_dim.137), calls=%async_computation.11 | async-start | bytes 1048576 | tf_op jit(solution)/shard_map/all_to_all | solution.py:26
  413.1 2.5 copy-start.13
  416.3 56.0 %copy-start.35 = (s32[1152]{0:T(1024)S(1)}, s32[1152]{0:T(1024)}, u32[]{:S(2)}) copy-start(s32[1152]{0:T(1024)} %fusion.99) | copy-start | bytes 13828
  447.6 39.9 %copy-start.17 = (f32[128,128]{1,0:T(8,128)}, f32[128,128]{1,0:T(8,128)S(1)}, u32[]{:S(2)}) copy-start(f32[128,128]{1,0:T(8,128)S(1)} %fusion.48) | copy-start | bytes 196612
  472.1 15.3 %copy-start.24 = (f32[128,128]{1,0:T(8,128)}, f32[128,128]{1,0:T(8,128)S(1)}, u32[]{:S(2)}) copy-start(f32[128,128]{1,0:T(8,128)S(1)} %copy.84) | copy-start | bytes 196612
  472.3 15.1 %copy-start.22 = (f32[128,128]{1,0:T(8,128)}, f32[128,128]{1,0:T(8,128)S(1)}, u32[]{:S(2)}) copy-start(f32[128,128]{1,0:T(8,128)S(1)} %convolution_negate_fusion.1) | copy-start | bytes 196612
  473.1 14.4 %copy-start.4 = (f32[1152,256]{0,1:T(8,128)}, f32[1152,256]{0,1:T(8,128)S(1)}, u32[]{:S(2)}) copy-start(f32[1152,256]{0,1:T(8,128)S(1)} %convolution_add_fusion) | copy-start | bytes 3538948
  487.5 4.8 copy-start.1
  487.5 36.7 %all-to-all-start.12 = ((f32[16,144,256]{2,1,0:T(8,128)}), f32[16,144,256]{2,1,0:T(8,128)}, u32[]{:S(2)}, u32[]{:S(2)}) async-start(f32[16,144,256]{2,1,0:T(8,128)} %bitcast.205), calls=%async_computation.12 | async-start | bytes 4718592 | tf_op jit(solution)/shard_map/all_to_all | solution.py:26
  495.9 1.4 copy-start.2
  506.0 24.4 %copy-start.18 = (f32[128,128]{1,0:T(8,128)S(1)}, f32[128,128]{1,0:T(8,128)}, u32[]{:S(2)}) copy-start(f32[128,128]{1,0:T(8,128)} %copy-done.17) | copy-start | bytes 196612
  506.0 24.4 %copy-start.23 = (f32[128,128]{1,0:T(8,128)S(1)}, f32[128,128]{1,0:T(8,128)}, u32[]{:S(2)}) copy-start(f32[128,128]{1,0:T(8,128)} %copy-done.22) | copy-start | bytes 196612
  506.0 24.4 %copy-start.25 = (f32[128,128]{1,0:T(8,128)S(1)}, f32[128,128]{1,0:T(8,128)}, u32[]{:S(2)}) copy-start(f32[128,128]{1,0:T(8,128)} %copy-done.24) | copy-start | bytes 196612
  506.0 24.5 %copy-start.30 = (f32[4,64,256]{2,1,0:T(8,128)S(1)}, f32[4,64,256]{2,1,0:T(8,128)}, u32[]{:S(2)}) copy-start(f32[4,64,256]{2,1,0:T(8,128)} %get-tuple-element.14) | copy-start | bytes 786436
  524.2 22.8 %all-to-all-start.16 = ((f32[8,144,256]{2,1,0:T(8,128)}), f32[8,144,256]{2,1,0:T(8,128)S(1)}, u32[]{:S(2)}, u32[]{:S(2)}) async-start(f32[8,144,256]{2,1,0:T(8,128)} %bitcast.48), calls=%async_computation.16 | async-start | bytes 2359296 | tf_op jit(solution)/shard_map/all_to_all | solution.py:26
  530.9 16.1 %copy-start.14 = (f32[256,256]{1,0:T(8,128)}, f32[256,256]{1,0:T(8,128)S(1)}, u32[]{:S(2)}) copy-start(f32[256,256]{1,0:T(8,128)S(1)} %convolution_add_fusion.2) | copy-start | bytes 786436
  531.2 15.8 %copy-start.26 = (f32[256,256]{1,0:T(8,128)}, f32[256,256]{1,0:T(8,128)S(1)}, u32[]{:S(2)}) copy-start(f32[256,256]{1,0:T(8,128)S(1)} %fusion.138) | copy-start | bytes 786436
  543.7 0.6 copy-start.34
  548.6 58.2 %copy-start.5 = (f32[1152,256]{0,1:T(8,128)S(1)}, f32[1152,256]{0,1:T(8,128)}, u32[]{:S(2)}) copy-start(f32[1152,256]{0,1:T(8,128)} %copy-done.4) | copy-start | bytes 3538948
  548.6 59.9 %all-to-all-start.13 = ((f32[16,144,256]{2,1,0:T(8,128)}), f32[16,144,256]{2,1,0:T(8,128)}, u32[]{:S(2)}, u32[]{:S(2)}) async-start(f32[16,144,256]{2,1,0:T(8,128)} %broadcast_in_dim.138), calls=%async_computation.13 | async-start | bytes 4718592 | tf_op jit(solution)/shard_map/all_to_all | solution.py:26
  570.0 0.6 copy-start.31
  571.7 0.6 copy-start.27
  608.5 5.6 copy-start.28
  608.5 5.6 copy-start.33
  609.7 20.9 %all-to-all-start.17 = ((f32[8,144,256]{2,1,0:T(8,128)}), f32[8,144,256]{2,1,0:T(8,128)S(1)}, u32[]{:S(2)}, u32[]{:S(2)}) async-start(f32[8,144,256]{2,1,0:T(8,128)} %broadcast_in_dim.140), calls=%async_computation.17 | async-start | bytes 2359296 | tf_op jit(solution)/shard_map/all_to_all | solution.py:26
  614.4 3.1 copy-start.32
  614.4 3.7 copy-start.15
  630.6 11.0 %all-to-all-start.14 = ((f32[8,32,256]{2,1,0:T(8,128)}), f32[8,32,256]{2,1,0:T(8,128)S(1)}, u32[]{:S(2)}, u32[]{:S(2)}) async-start(f32[8,32,256]{2,1,0:T(8,128)} %fusion.142), calls=%async_computation.14 | async-start | bytes 524288 | tf_op jit(solution)/shard_map/all_to_all | solution.py:26
  642.3 10.9 %all-to-all-start.15 = ((f32[8,32,256]{2,1,0:T(8,128)}), f32[8,32,256]{2,1,0:T(8,128)S(1)}, u32[]{:S(2)}, u32[]{:S(2)}) async-start(f32[8,32,256]{2,1,0:T(8,128)} %broadcast_in_dim.139), calls=%async_computation.15 | async-start | bytes 524288 | tf_op jit(solution)/shard_map/all_to_all | solution.py:26
  646.6 7.2 %copy-start.10 = (f32[1152,256]{1,0:T(8,128)S(1)}, f32[1152,256]{1,0:T(8,128)}, u32[]{:S(2)}) copy-start(f32[1152,256]{1,0:T(8,128)} %fusion.145) | copy-start | bytes 3538948
  653.2 1.8 copy-start.9
  653.4 2.2 copy-start.3
Sparse Core Ops, SparseCore 0:
  51.3 110.0 all-reduce.5
